TPU v7x, 128 devices: a whole 4x4x4 slice. The times are simulated.
128 devices in a mesh: seq: 32 (over x, z_lo, y), head: 2 (over core), dp: 2 (over z_hi).
Axes of the slice: x: 4, y: 4, z: 4 (z_hi: 2, z_lo: 2; z = z_hi * 2 + z_lo), core: 2. Of those that a mesh axis runs over, the one named last changes fastest.
Arguments:
- queries: bfloat16 [16384, 2048], P(('dp', 'seq'), 'head'), parts along dimension 0, may hold values from -32 to 32
- keys: bfloat16 [16384, 2048], P(('dp', 'seq'), 'head'), parts along dimension 0, may hold values from -32 to 32
- values: bfloat16 [16384, 2048], P(('dp', 'seq'), 'head'), parts along dimension 0, may hold values from -6 to 6
- out_grad: bfloat16 [16384, 4096], P(('dp', 'seq')), parts along dimension 0, may hold values from -6 to 6
- proj_weight: bfloat16 [4096, 2048], P(None, 'head'), may hold values from -0.09375 to 0.09375
- layout: int32 [64, 12], replicated, may hold values from -1 to 63, as said below
Outputs:
- query_grad: bfloat16 [16384, 2048], P(('dp', 'seq'), 'head'), parts along dimension 0
- key_grad: bfloat16 [16384, 2048], P(('dp', 'seq'), 'head'), parts along dimension 0
- value_grad: bfloat16 [16384, 2048], P(('dp', 'seq'), 'head'), parts along dimension 0
- proj_grad: float32 [8192, 2048], P(('dp', 'seq'), 'head'), parts along dimension 0
There are 2 independent parts, one for each index of `dp`. A program takes and returns all parts, laid end to end along the dimension named above; an argument that names none is the same for every part. Nothing has to cross between parts.
Inputs may be any that keep to these rules, and one draw needn't show every extreme that they name: `layout`: row i lists, in increasing order, some of the blocks j < i - 7 whose remainder modulo 16 equals one offset, below 8 and shared by all rows (the last row lists all of them), then the blocks max(0, i - w + 1) to i for a window w of its own between 1 and 8, and ends with -1 in the unused entries; a row whose block follows a block of that remainder has w = 8.
All inputs are finite; a program needn't handle non-finite values.
Results may differ from a plain program's by a relative error of at most 0.03.
Values may be sent and summed in bfloat16 or wider, within the bound.
A program may use at most 192 MiB of HBM per device.

v0:
```python
import jax
import jax.numpy as jnp
from jax import lax
from jax.sharding import PartitionSpec as P

HD = 128
BLK = 128
LOCAL = 8
STRIDE = 16


def passed_along(block, axis, distance):
    devices = range(lax.axis_size(axis))
    route = [(i - distance, i) for i in devices if i - distance in devices]
    return lax.ppermute(block, axis, route)


def broadcast(array, axis, root):
    mine = lax.axis_index(axis) == root
    return lax.psum(jnp.where(mine, array, jnp.zeros_like(array)), axis)


def listed(table_row, block_ids):
    return jnp.any(table_row[None, :] == block_ids[:, None], axis=1) & (block_ids >= 0)


def local(queries, keys, values, out_grad, proj_weight, layout):
    tok_dev = queries.shape[0]
    width = queries.shape[1]
    heads_here = width // HD
    blocks_dev = tok_dev // BLK
    block_count = layout.shape[0]
    summary_count = block_count // STRIDE
    score_scale = HD ** (-0.5)
    first_block = lax.axis_index("seq") * blocks_dev
    offset_block = layout[block_count - 1, 0] % STRIDE
    reach_back = (LOCAL - 2) // blocks_dev + 1
    span_blocks = [
        min(blocks_dev, LOCAL - 1 - hop_index * blocks_dev) for hop_index in range(reach_back)
    ]
    attn_grad = jnp.dot(out_grad, proj_weight, preferred_element_type=jnp.float32).astype(
        jnp.bfloat16
    )
    near_keys = []
    near_values = []
    for distance in range(reach_back, 0, -1):
        rows_needed = span_blocks[distance - 1] * BLK
        moved_keys, moved_values = passed_along(
            (keys[tok_dev - rows_needed :], values[tok_dev - rows_needed :]), "seq", distance
        )
        near_keys.append(moved_keys)
        near_values.append(moved_values)
    pool_keys = jnp.concatenate(near_keys + [keys], axis=0).reshape(-1, heads_here, HD)
    pool_values = jnp.concatenate(near_values + [values], axis=0).reshape(-1, heads_here, HD)

    def fetch_summary(scan_state, summary_index):
        block_id = summary_index * STRIDE + offset_block
        start_row = block_id % blocks_dev * BLK
        owner_rank = block_id // blocks_dev
        piece_keys = lax.dynamic_slice_in_dim(keys, start_row, BLK, 0)
        piece_values = lax.dynamic_slice_in_dim(values, start_row, BLK, 0)
        received = (
            broadcast(piece_keys, "seq", owner_rank),
            broadcast(piece_values, "seq", owner_rank),
        )
        return (scan_state, received)

    ignored, fetched = lax.scan(fetch_summary, None, jnp.arange(summary_count, dtype=jnp.int32))
    far_keys = fetched[0].reshape(summary_count * BLK, heads_here, HD)
    far_values = fetched[1].reshape(summary_count * BLK, heads_here, HD)
    far_ids = jnp.arange(summary_count, dtype=jnp.int32) * STRIDE + offset_block
    query_blocks = queries.reshape(blocks_dev, BLK, heads_here, HD)
    grad_blocks = attn_grad.reshape(blocks_dev, BLK, heads_here, HD)
    window_offsets = jnp.arange(LOCAL, dtype=jnp.int32)
    causal_local = jnp.arange(LOCAL * BLK)[None, :] <= (LOCAL - 1) * BLK + jnp.arange(BLK)[:, None]

    def query_step(scan_state, local_block):
        query_rows = query_blocks[local_block]
        grad_rows = grad_blocks[local_block]
        block_id = first_block + local_block
        table_row = layout[block_id]
        window_key_rows = lax.dynamic_slice_in_dim(pool_keys, local_block * BLK, LOCAL * BLK, 0)
        window_value_rows = lax.dynamic_slice_in_dim(pool_values, local_block * BLK, LOCAL * BLK, 0)
        window_ids = block_id - (LOCAL - 1) + window_offsets
        plain_window = (window_ids % STRIDE != offset_block) | (window_ids == block_id)
        local_allowed = (
            causal_local & jnp.repeat(listed(table_row, window_ids) & plain_window, BLK)[None, :]
        )
        far_allowed = jnp.repeat(listed(table_row, far_ids) & (far_ids < block_id), BLK)[None, :]
        near_scores = (
            jnp.einsum(
                "ahd,chd->hac", query_rows, window_key_rows, preferred_element_type=jnp.float32
            )
            * score_scale
        )
        far_scores = (
            jnp.einsum("ahd,chd->hac", query_rows, far_keys, preferred_element_type=jnp.float32)
            * score_scale
        )
        near_scores = jnp.where(local_allowed[None], near_scores, -jnp.inf)
        far_scores = jnp.where(far_allowed[None], far_scores, -jnp.inf)
        row_top = jnp.maximum(jnp.max(near_scores, axis=-1), jnp.max(far_scores, axis=-1))[
            ..., None
        ]
        row_total = jnp.sum(jnp.exp(near_scores - row_top), axis=-1, keepdims=True) + jnp.sum(
            jnp.exp(far_scores - row_top), axis=-1, keepdims=True
        )
        log_total = row_top + jnp.log(row_total)
        near_probs = jnp.exp(near_scores - log_total)
        far_probs = jnp.exp(far_scores - log_total)
        near_low = near_probs.astype(jnp.bfloat16)
        far_low = far_probs.astype(jnp.bfloat16)
        out_rows = (
            jnp.einsum(
                "hac,chd->ahd", near_low, window_value_rows, preferred_element_type=jnp.float32
            )
            + jnp.einsum("hac,chd->ahd", far_low, far_values, preferred_element_type=jnp.float32)
        ).astype(jnp.bfloat16)
        delta_rows = jnp.transpose(
            jnp.sum(out_rows.astype(jnp.float32) * grad_rows.astype(jnp.float32), axis=-1)
        )[..., None]
        near_dprob = jnp.einsum(
            "ahd,chd->hac", grad_rows, window_value_rows, preferred_element_type=jnp.float32
        )
        far_dprob = jnp.einsum(
            "ahd,chd->hac", grad_rows, far_values, preferred_element_type=jnp.float32
        )
        near_dscore = (score_scale * near_probs * (near_dprob - delta_rows)).astype(jnp.bfloat16)
        far_dscore = (score_scale * far_probs * (far_dprob - delta_rows)).astype(jnp.bfloat16)
        query_grad_rows = (
            jnp.einsum(
                "hac,chd->ahd", near_dscore, window_key_rows, preferred_element_type=jnp.float32
            )
            + jnp.einsum("hac,chd->ahd", far_dscore, far_keys, preferred_element_type=jnp.float32)
        ).astype(jnp.bfloat16)
        far_key_grad = scan_state[0] + jnp.einsum(
            "hac,ahd->chd", far_dscore, query_rows, preferred_element_type=jnp.float32
        )
        far_value_grad = scan_state[1] + jnp.einsum(
            "hac,ahd->chd", far_low, grad_rows, preferred_element_type=jnp.float32
        )
        start_row = local_block * BLK
        old_keys = lax.dynamic_slice_in_dim(scan_state[2], start_row, LOCAL * BLK, 0)
        old_values = lax.dynamic_slice_in_dim(scan_state[3], start_row, LOCAL * BLK, 0)
        new_keys = old_keys + jnp.einsum(
            "hac,ahd->chd", near_dscore, query_rows, preferred_element_type=jnp.float32
        )
        new_values = old_values + jnp.einsum(
            "hac,ahd->chd", near_low, grad_rows, preferred_element_type=jnp.float32
        )
        pool_key_grad = lax.dynamic_update_slice_in_dim(scan_state[2], new_keys, start_row, 0)
        pool_value_grad = lax.dynamic_update_slice_in_dim(scan_state[3], new_values, start_row, 0)
        new_state = (far_key_grad, far_value_grad, pool_key_grad, pool_value_grad)
        return (new_state, (out_rows, query_grad_rows, log_total[..., 0], delta_rows[..., 0]))

    far_zeros = jnp.zeros((summary_count * BLK, heads_here, HD), jnp.float32)
    pool_zeros = jnp.zeros((pool_keys.shape[0], heads_here, HD), jnp.float32)
    init_state = (far_zeros, far_zeros, pool_zeros, pool_zeros)
    state_out, scanned = lax.scan(query_step, init_state, jnp.arange(blocks_dev, dtype=jnp.int32))
    out_blocks, query_parts, log_blocks, delta_blocks = scanned
    attn_out = out_blocks.reshape(tok_dev, width)
    query_grad = query_parts.reshape(tok_dev, width)
    own_ids = first_block + jnp.arange(blocks_dev, dtype=jnp.int32)
    is_summary = own_ids % STRIDE == offset_block
    summary_slot = jnp.minimum(own_ids // STRIDE, summary_count - 1)
    summed = lax.psum((state_out[0], state_out[1]), "seq")
    far_key_sum = summed[0].reshape(summary_count, BLK, width)
    far_value_sum = summed[1].reshape(summary_count, BLK, width)
    far_key_add = jnp.take(far_key_sum, summary_slot, axis=0)
    far_value_add = jnp.take(far_value_sum, summary_slot, axis=0)
    own_start = (LOCAL - 1) * BLK
    key_grad = state_out[2][own_start:]
    value_grad = state_out[3][own_start:]
    pool_start = 0
    for distance in range(reach_back, 0, -1):
        rows_needed = span_blocks[distance - 1] * BLK
        back_keys, back_values = passed_along(
            (
                state_out[2][pool_start : pool_start + rows_needed],
                state_out[3][pool_start : pool_start + rows_needed],
            ),
            "seq",
            -distance,
        )
        key_grad = key_grad.at[tok_dev - rows_needed :].add(back_keys)
        value_grad = value_grad.at[tok_dev - rows_needed :].add(back_values)
        pool_start = pool_start + rows_needed
    key_total = key_grad.reshape(blocks_dev, BLK, width) + jnp.where(
        is_summary[:, None, None], far_key_add, 0.0
    )
    value_total = value_grad.reshape(blocks_dev, BLK, width) + jnp.where(
        is_summary[:, None, None], far_value_add, 0.0
    )
    proj_grad = lax.psum_scatter(
        lax.dot_general(
            out_grad, attn_out, (((0,), (0,)), ((), ())), preferred_element_type=jnp.float32
        ),
        "seq",
        scatter_dimension=0,
        tiled=True,
    )
    key_out = key_total.reshape(tok_dev, width).astype(jnp.bfloat16)
    value_out = value_total.reshape(tok_dev, width).astype(jnp.bfloat16)
    return (query_grad, key_out, value_out, proj_grad)


def solution(mesh):
    return jax.shard_map(
        local,
        mesh=mesh,
        in_specs=(
            P(("dp", "seq"), "head"),
            P(("dp", "seq"), "head"),
            P(("dp", "seq"), "head"),
            P(("dp", "seq"), None),
            P(None, "head"),
            P(),
        ),
        out_specs=(
            P(("dp", "seq"), "head"),
            P(("dp", "seq"), "head"),
            P(("dp", "seq"), "head"),
            P(("dp", "seq"), "head"),
        ),
        check_vma=False,
    )
```

profile of v0, /device:TPU:40, one launch (start us, length us, event | category | flops | bytes accessed | tf_op | source)
XLA Modules:
  0.0 2063.3 jit_solution(11944361138026221976)
XLA Ops:
  10.2 2.8 collective-permute-start.1
  13.1 4.5 collective-permute-start.2
  17.6 3.8 collective-permute-start.3
  23.0 3.8 collective-permute-start
  28.5 2.9 collective-permute-start.4
  36.5 6.6 fusion.40
  43.1 1248.2 %while.53 = (s32[]{:T(128)}, bf16[4,128,1024]{2,1,0:T(8,128)(2,1)}, bf16[4,128,1024]{2,1,0:T(8,128)(2,1)}, s32[4]{0:T(128)S(1)}, s32[]{:T(128)}, /*index=5*/bf16...) while((s32[]{:T(128)}, bf16[4,128,1024]{2,1,0:T(8,128)(2,1)}, ...), condition=%wide.region_3.4_spmd, body=%wide.region_0.3_spmd.sunk | while | flops 524319 | bytes 5243400 | solution.py:68
  45.2 301.6 %all-reduce.9.cloned.1.call-done = (bf16[1,128,1024]{2,1,0:T(8,128)(2,1)}, bf16[1,128,1024]{2,1,0:T(8,128)(2,1)}) async-done(((bf16[1,128,1024]{2,1,0:T(8,128)(2,1)}, bf16[1,128,1024]{2,1,0:T(8,128)(2,1)}), (bf16[1,128,1024]{2,1,0:T(8,128)(2,1)}, bf16[1,128,1024]{2,1,0:T(8,128)(2,1)})) %all-reduce.9.cloned.1.call-update) | async-done | bytes 524304 | tf_op jit(solution)/shard_map/while/body/eval_jaxpr/psum | solution.py:20
  352.3 308.3 %all-reduce.9.cloned.1.call-done = (bf16[1,128,1024]{2,1,0:T(8,128)(2,1)}, bf16[1,128,1024]{2,1,0:T(8,128)(2,1)}) async-done(((bf16[1,128,1024]{2,1,0:T(8,128)(2,1)}, bf16[1,128,1024]{2,1,0:T(8,128)(2,1)}), (bf16[1,128,1024]{2,1,0:T(8,128)(2,1)}, bf16[1,128,1024]{2,1,0:T(8,128)(2,1)})) %all-reduce.9.cloned.1.call-update) | async-done | bytes 524304 | tf_op jit(solution)/shard_map/while/body/eval_jaxpr/psum | solution.py:20
  666.1 308.3 %all-reduce.9.cloned.1.call-done = (bf16[1,128,1024]{2,1,0:T(8,128)(2,1)}, bf16[1,128,1024]{2,1,0:T(8,128)(2,1)}) async-done(((bf16[1,128,1024]{2,1,0:T(8,128)(2,1)}, bf16[1,128,1024]{2,1,0:T(8,128)(2,1)}), (bf16[1,128,1024]{2,1,0:T(8,128)(2,1)}, bf16[1,128,1024]{2,1,0:T(8,128)(2,1)})) %all-reduce.9.cloned.1.call-update) | async-done | bytes 524304 | tf_op jit(solution)/shard_map/while/body/eval_jaxpr/psum | solution.py:20
  979.9 308.0 %all-reduce.9.cloned.1.call-done = (bf16[1,128,1024]{2,1,0:T(8,128)(2,1)}, bf16[1,128,1024]{2,1,0:T(8,128)(2,1)}) async-done(((bf16[1,128,1024]{2,1,0:T(8,128)(2,1)}, bf16[1,128,1024]{2,1,0:T(8,128)(2,1)}), (bf16[1,128,1024]{2,1,0:T(8,128)(2,1)}, bf16[1,128,1024]{2,1,0:T(8,128)(2,1)})) %all-reduce.9.cloned.1.call-update) | async-done | bytes 524304 | tf_op jit(solution)/shard_map/while/body/eval_jaxpr/psum | solution.py:20
  1296.2 2.4 copy.99
  1305.1 3.4 collective-permute-start.7
  1317.0 3.5 collective-permute-done.6
  1323.0 4.4 copy.75
  1327.4 2.5 broadcast_in_dim.123
  1329.9 2.5 broadcast_in_dim.123.clone
  1332.4 88.2 %while.54 = (s32[]{:T(128)}, f32[512,8,128]{0,2,1:T(8,128)}, f32[512,8,128]{0,2,1:T(8,128)}, f32[1152,8,128]{0,2,1:T(8,128)}, f32[1152,8,128]{0,2,1:T(8,128)}, /...) while((s32[]{:T(128)}, f32[512,8,128]{0,2,1:T(8,128)}, ...), condition=%wide.region_12.13_spmd.clone.clone.clone, body=%wide.region_4.12_spmd.clone.clone.clone.sunk | while | flops 2451831296 | bytes 213504784 | solution.py:159
  1336.9 3.0 fusion.100
  1342.0 2.6 fusion.102
  1360.9 5.0 fusion.104
  1367.8 3.9 fusion.106
  1371.7 2.5 fusion.107
  1380.7 3.0 fusion.100
  1385.7 2.6 fusion.102
  1396.3 3.5 bitcast_add_fusion.6
  1405.2 5.1 fusion.104
  1412.2 3.9 fusion.106
  1416.1 2.5 fusion.107
  1420.6 2.9 reshape.422
  1423.5 2.9 copy.101
  1426.5 2.9 reshape.424
  1429.4 3.0 copy.103
  1433.4 8.1 convolution_bitcast_fusion.2
  1441.6 2.7 fusion.49
  1444.3 7.7 collective-permute-start.15
  1458.0 2.7 collective-permute-start.14
  1464.6 11.3 collective-permute-done.12
  1476.0 76.1 %collective-permute-start.11 = (f32[256,8,128]{0,2,1:T(8,128)}, f32[256,8,128]{0,2,1:T(8,128)}, u32[]{:S(2)}, u32[]{:S(2)}) collective-permute-start(f32[256,8,128]{0,2,1:T(8,128)} %get-tuple-element.790), channel_id=1, source_target_pairs={{4,0},{8,4},{12,8},{16,12},{20,16},{24,20},{28,24},{32,28},{36,32}... | collective-permute-start | bytes 3145736 | tf_op jit(solution)/shard_map/ppermute | solution.py:15
  1552.1 23.2 %collective-permute-start.10 = (f32[256,8,128]{0,2,1:T(8,128)}, f32[256,8,128]{0,2,1:T(8,128)}, u32[]{:S(2)}, u32[]{:S(2)}) collective-permute-start(f32[256,8,128]{0,2,1:T(8,128)} %get-tuple-element.791), channel_id=1, source_target_pairs={{8,0},{12,4},{16,8},{20,12},{24,16},{28,20},{32,24},{36,28},{40,32... | collective-permute-start | bytes 3145736 | tf_op jit(solution)/shard_map/ppermute | solution.py:15
  1580.4 87.1 %collective-permute-done.13 = f32[256,8,128]{0,2,1:T(8,128)S(1)} collective-permute-done((f32[256,8,128]{0,2,1:T(8,128)S(1)}, f32[256,8,128]{0,2,1:T(8,128)S(1)}, u32[]{:S(2)}, u32[]{:S(2)}) %collective-permute-start.13) | collective-permute-done | bytes 1048608 | tf_op jit(solution)/shard_map/ppermute | solution.py:15
  1671.5 43.8 %collective-permute-done.9 = f32[256,8,128]{0,2,1:T(8,128)} collective-permute-done((f32[256,8,128]{0,2,1:T(8,128)}, f32[256,8,128]{0,2,1:T(8,128)}, u32[]{:S(2)}, u32[]{:S(2)}) %collective-permute-start.9) | collective-permute-done | bytes 1048608 | tf_op jit(solution)/shard_map/ppermute | solution.py:15
  1715.3 2.5 add_add_fusion.1
  1719.3 2.3 copy.100
  1721.6 130.2 %all-reduce.7.cloned.1.call-done = (f32[4,128,1024]{2,1,0:T(8,128)}, f32[4,128,1024]{2,1,0:T(8,128)}) async-done(((f32[4,128,1024]{2,1,0:T(8,128)}, f32[4,128,1024]{2,1,0:T(8,128)}), (f32[4,128,1024]{2,1,0:T(8,128)}, f32[4,128,1024]{2,1,0:T(8,128)})) %all-reduce.7.cloned.1.call-update) | async-done | bytes 4194320 | tf_op jit(solution)/shard_map/psum | solution.py:166
  1854.1 3.2 gather_fusion
  1857.3 3.4 fusion.42
  1860.7 193.5 %reduce-scatter.2.cloned.1.call-done = f32[128,1024]{0,1:T(8,128)} async-done(((f32[4096,1024]{0,1:T(8,128)}), f32[128,1024]{0,1:T(8,128)}) %reduce-scatter.2.cloned.1.call-update) | async-done | bytes 524304 | tf_op jit(solution)/shard_map/reduce_scatter | solution.py:194
  (234 shorter events, 119.8 us)
Async XLA Ops:
  8.0 28.5 %copy-start = (bf16[256,4096]{1,0:T(8,128)(2,1)S(1)}, bf16[256,4096]{1,0:T(8,128)(2,1)}, u32[]{:S(2)}) copy-start(bf16[256,4096]{1,0:T(8,128)(2,1)} %param.43) | copy-start | bytes 6291460
  8.0 27.5 %copy-start.19 = (bf16[256,1024]{1,0:T(8,128)(2,1)S(1)}, bf16[256,1024]{1,0:T(8,128)(2,1)}, u32[]{:S(2)}) copy-start(bf16[256,1024]{1,0:T(8,128)(2,1)} %param.40) | copy-start | bytes 1572868
  10.2 1294.8 %collective-permute-start.1 = (bf16[256,1024]{0,1:T(8,128)(2,1)}, bf16[256,1024]{0,1:T(8,128)(2,1)}, u32[]{:S(2)}, u32[]{:S(2)}) collective-permute-start(bf16[256,1024]{0,1:T(8,128)(2,1)} %copy.69), channel_id=1, source_target_pairs={{0,12},{4,16},{8,20},{12,24},{16,28},{20,32},{24,36},{28,40},{32,4... | collective-permute-start | bytes 1572872 | tf_op jit(solution)/shard_map/ppermute | solution.py:15
  13.1 1297.3 %collective-permute-start.2 = (bf16[256,1024]{0,1:T(8,128)(2,1)}, bf16[256,1024]{0,1:T(8,128)(2,1)}, u32[]{:S(2)}, u32[]{:S(2)}) collective-permute-start(bf16[256,1024]{0,1:T(8,128)(2,1)} %copy.69), channel_id=1, source_target_pairs={{0,8},{4,12},{8,16},{12,20},{16,24},{20,28},{24,32},{28,36},{32,40... | collective-permute-start | bytes 1572872 | tf_op jit(solution)/shard_map/ppermute | solution.py:15
  17.6 1294.7 %collective-permute-start.3 = (bf16[256,1024]{0,1:T(8,128)(2,1)}, bf16[256,1024]{0,1:T(8,128)(2,1)}, u32[]{:S(2)}, u32[]{:S(2)}) collective-permute-start(bf16[256,1024]{0,1:T(8,128)(2,1)} %copy.69), channel_id=1, source_target_pairs={{0,4},{4,8},{8,12},{12,16},{16,20},{20,24},{24,28},{28,32},{32,36}... | collective-permute-start | bytes 1572872 | tf_op jit(solution)/shard_map/ppermute | solution.py:15
  23.0 1275.6 %collective-permute-start = (bf16[128,1024]{0,1:T(8,128)(2,1)}, bf16[128,1024]{0,1:T(8,128)(2,1)}, u32[]{:S(2)}, u32[]{:S(2)}) collective-permute-start(bf16[128,1024]{0,1:T(8,128)(2,1)} %slice.222), channel_id=1, source_target_pairs={{0,16},{4,20},{8,24},{12,28},{16,32},{20,36},{24,40},{28,44},{32,4... | collective-permute-start | bytes 786440 | tf_op jit(solution)/shard_map/ppermute | solution.py:15
  28.5 1273.9 %collective-permute-start.4 = (bf16[128,1024]{1,0:T(8,128)(2,1)}, bf16[128,1024]{1,0:T(8,128)(2,1)S(1)}, u32[]{:S(2)}, u32[]{:S(2)}) collective-permute-start(bf16[128,1024]{1,0:T(8,128)(2,1)} %slice.205), channel_id=1, source_target_pairs={{0,16},{4,20},{8,24},{12,28},{16,32},{20,36},{24,40},{28,44},{32,4... | collective-permute-start | bytes 786440 | tf_op jit(solution)/shard_map/ppermute | solution.py:15
  36.5 6.6 copy-start.12
  36.5 6.6 copy-start.13
  43.1 303.8 %all-reduce.9.cloned.1.call-start = ((), (), s32[]{:S(2)}) async-start(), calls=%async_computation.3 | async-start | bytes 1048576 | tf_op jit(solution)/shard_map/while/body/eval_jaxpr/psum | solution.py:20
  350.2 310.4 %all-reduce.9.cloned.1.call-start = ((), (), s32[]{:S(2)}) async-start(), calls=%async_computation.3 | async-start | bytes 1048576 | tf_op jit(solution)/shard_map/while/body/eval_jaxpr/psum | solution.py:20
  664.0 310.4 %all-reduce.9.cloned.1.call-start = ((), (), s32[]{:S(2)}) async-start(), calls=%async_computation.3 | async-start | bytes 1048576 | tf_op jit(solution)/shard_map/while/body/eval_jaxpr/psum | solution.py:20
  977.8 310.1 %all-reduce.9.cloned.1.call-start = ((), (), s32[]{:S(2)}) async-start(), calls=%async_computation.3 | async-start | bytes 1048576 | tf_op jit(solution)/shard_map/while/body/eval_jaxpr/psum | solution.py:20
  1291.3 560.6 %all-reduce.7.cloned.1.call-start = ((), (), s32[]{:S(2)}) async-start(), calls=%async_computation.2 | async-start | bytes 8388608 | tf_op jit(solution)/shard_map/psum | solution.py:166
  1291.3 3.7 copy-start.17
  1298.6 17.5 collective-permute-start.5
  1302.4 18.0 collective-permute-start.6
  1305.1 16.3 collective-permute-start.7
  1332.4 9.3 copy-start.22
  1340.8 8.7 copy-start.6
  1344.6 3.8 copy-start.3
  1344.6 3.8 copy-start.15
  1355.5 3.7 copy-start.16
  1359.2 6.7 slice-start
  1360.9 5.0 slice-start.1
  1367.7 3.9 copy-start.5
  1371.6 4.6 copy-start.23
  1376.2 9.3 copy-start.22
  1384.6 8.7 copy-start.6
  1388.4 3.8 copy-start.3
  1388.4 3.8 copy-start.15
  1399.8 3.7 copy-start.16
  1403.5 6.8 slice-start
  1405.2 5.1 slice-start.1
  1412.2 3.9 copy-start.5
  1416.1 4.6 copy-start.23
  1432.4 621.8 %reduce-scatter.2.cloned.1.call-start = ((), (), s32[]{:S(2)}) async-start(), calls=%async_computation.1 | async-start | bytes 17301504 | tf_op jit(solution)/shard_map/reduce_scatter | solution.py:194
  1441.6 21.2 %slice-start.2 = ((s8[4718592]{0:T(1024)(128)(4,1)}), s8[4194304]{0:T(1024)(128)(4,1)S(1)}, s32[]{:S(2)}) async-start(s8[4718592]{0:T(1024)(128)(4,1)} %bitcast.181), calls=%async_computation.6 | async-start | bytes 8388608
  1441.6 21.2 %slice-start.3 = ((s8[4718592]{0:T(1024)(128)(4,1)}), s8[524288]{0:T(1024)(128)(4,1)S(1)}, s32[]{:S(2)}) async-start(s8[4718592]{0:T(1024)(128)(4,1)} %bitcast.181), calls=%async_computation.7 | async-start | bytes 1048576
  1444.3 131.0 %collective-permute-start.15 = (f32[256,8,128]{0,2,1:T(8,128)S(1)}, f32[256,8,128]{0,2,1:T(8,128)S(1)}, u32[]{:S(2)}, u32[]{:S(2)}) collective-permute-start(f32[256,8,128]{0,2,1:T(8,128)S(1)} %get-tuple-element.786), channel_id=1, source_target_pairs={{4,0},{8,4},{12,8},{16,12},{20,16},{24,20},{28,24},{32,28},{36,32}... | collective-permute-start | bytes 3145736 | tf_op jit(solution)/shard_map/ppermute | solution.py:15
  1453.0 22.9 %collective-permute-start.12 = (f32[128,8,128]{0,2,1:T(8,128)S(1)}, f32[128,8,128]{0,2,1:T(8,128)S(1)}, u32[]{:S(2)}, u32[]{:S(2)}) collective-permute-start(f32[128,8,128]{0,2,1:T(8,128)S(1)} %slice.214), channel_id=1, source_target_pairs={{16,0},{20,4},{24,8},{28,12},{32,16},{36,20},{40,24},{44,28},{48,3... | collective-permute-start | bytes 1572872 | tf_op jit(solution)/shard_map/ppermute | solution.py:15
  1456.0 96.0 %collective-permute-start.8 = (f32[128,8,128]{0,2,1:T(8,128)S(1)}, f32[128,8,128]{0,2,1:T(8,128)S(1)}, u32[]{:S(2)}, u32[]{:S(2)}) collective-permute-start(f32[128,8,128]{0,2,1:T(8,128)S(1)} %slice.208), channel_id=1, source_target_pairs={{16,0},{20,4},{24,8},{28,12},{32,16},{36,20},{40,24},{44,28},{48,3... | collective-permute-start | bytes 1572872 | tf_op jit(solution)/shard_map/ppermute | solution.py:15
  1458.0 121.4 %collective-permute-start.14 = (f32[256,8,128]{0,2,1:T(8,128)S(1)}, f32[256,8,128]{0,2,1:T(8,128)S(1)}, u32[]{:S(2)}, u32[]{:S(2)}) collective-permute-start(f32[256,8,128]{0,2,1:T(8,128)S(1)} %get-tuple-element.787), channel_id=1, source_target_pairs={{8,0},{12,4},{16,8},{20,12},{24,16},{28,20},{32,24},{36,28},{40,32... | collective-permute-start | bytes 3145736 | tf_op jit(solution)/shard_map/ppermute | solution.py:15
  1460.7 116.6 %copy-start.20 = (bf16[2,128,8,128]{3,2,1,0:T(8,128)(2,1)S(1)}, bf16[2,128,8,128]{3,2,1,0:T(8,128)(2,1)}, u32[]{:S(2)}) copy-start(bf16[2,128,8,128]{3,2,1,0:T(8,128)(2,1)} %get-tuple-element.496) | copy-start | bytes 1572868
  1460.7 206.7 %collective-permute-start.13 = (f32[256,8,128]{0,2,1:T(8,128)S(1)}, f32[256,8,128]{0,2,1:T(8,128)S(1)}, u32[]{:S(2)}, u32[]{:S(2)}) collective-permute-start(f32[256,8,128]{0,2,1:T(8,128)S(1)} %get-tuple-element.784), channel_id=1, source_target_pairs={{12,0},{16,4},{20,8},{24,12},{28,16},{32,20},{36,24},{40,28},{44,3... | collective-permute-start | bytes 3145736 | tf_op jit(solution)/shard_map/ppermute | solution.py:15
  1476.0 195.6 %collective-permute-start.11 = (f32[256,8,128]{0,2,1:T(8,128)}, f32[256,8,128]{0,2,1:T(8,128)}, u32[]{:S(2)}, u32[]{:S(2)}) collective-permute-start(f32[256,8,128]{0,2,1:T(8,128)} %get-tuple-element.790), channel_id=1, source_target_pairs={{4,0},{8,4},{12,8},{16,12},{20,16},{24,20},{28,24},{32,28},{36,32}... | collective-permute-start | bytes 3145736 | tf_op jit(solution)/shard_map/ppermute | solution.py:15
  1552.1 119.5 %collective-permute-start.10 = (f32[256,8,128]{0,2,1:T(8,128)}, f32[256,8,128]{0,2,1:T(8,128)}, u32[]{:S(2)}, u32[]{:S(2)}) collective-permute-start(f32[256,8,128]{0,2,1:T(8,128)} %get-tuple-element.791), channel_id=1, source_target_pairs={{8,0},{12,4},{16,8},{20,12},{24,16},{28,20},{32,24},{36,28},{40,32... | collective-permute-start | bytes 3145736 | tf_op jit(solution)/shard_map/ppermute | solution.py:15
  1575.3 140.0 %collective-permute-start.9 = (f32[256,8,128]{0,2,1:T(8,128)}, f32[256,8,128]{0,2,1:T(8,128)}, u32[]{:S(2)}, u32[]{:S(2)}) collective-permute-start(f32[256,8,128]{0,2,1:T(8,128)} %get-tuple-element.788), channel_id=1, source_target_pairs={{12,0},{16,4},{20,8},{24,12},{28,16},{32,20},{36,24},{40,28},{44,3... | collective-permute-start | bytes 3145736 | tf_op jit(solution)/shard_map/ppermute | solution.py:15
  (19 other events, 46.6 us)
Sparse Core Ops, SparseCore 0:
  46.4 300.4 all-reduce.8
  353.5 307.0 all-reduce.8
  667.3 307.0 all-reduce.8
  980.8 307.0 all-reduce.8
Sparse Core Ops, SparseCore 1:
  1432.5 419.4 all-reduce.6
  1854.1 200.0 reduce-scatter.1
where the time goes:
time: 2080 us; the launch traced here: 2060 us
  waiting for transfers between devices  1700 us (82%)
  starting transfers between devices  143 us (7%)
  local copies, waits for them, and re-layouts  111 us (5%)
  matrix products  70.8 us (3%)
    psum x4, waiting for transfers between devices, broadcast(): return lax.psum(jnp.where(mine, array, jnp.zeros_like(array)), axis)  1230 us
    reduce_scatter x1, waiting for transfers between devices, local(): lax.psum_scatter(lax.dot_general(out_grad, attn_out, (((0,), (0,)), ((),...  194 us
    ppermute x16, waiting for transfers between devices, passed_along(): return lax.ppermute(block, axis, route)  146 us
    ppermute x16, starting transfers between devices, passed_along(): return lax.ppermute(block, axis, route)  143 us
    psum x1, waiting for transfers between devices, local(): summed = lax.psum((state_out[0], state_out[1]), 'seq')  130 us
  transfers between devices with their start and end apart: 22, of which 10 were waited for; matrix products, arithmetic and copies ran while one was open for 4% of the time, Pallas kernels for 0%

commit v1 on v0

v1 whole, which is shorter than its diff:
```python
import jax
import jax.numpy as jnp
from jax import lax
from jax.sharding import PartitionSpec as P

HD = 128
BLK = 128
LOCAL = 8
STRIDE = 16


def passed_along(block, axis, distance):
    devices = range(lax.axis_size(axis))
    route = [(i - distance, i) for i in devices if i - distance in devices]
    return lax.ppermute(block, axis, route)


def listed(table_rows, block_ids):
    hit = jnp.any(table_rows[:, None, :] == block_ids[:, :, None], axis=2)
    return hit & (block_ids >= 0)


def local(queries, keys, values, out_grad, proj_weight, layout):
    tok_dev = queries.shape[0]
    width = queries.shape[1]
    heads_here = width // HD
    blocks_dev = tok_dev // BLK
    block_count = layout.shape[0]
    summary_count = block_count // STRIDE
    score_scale = HD ** (-0.5)
    me = lax.axis_index("seq")
    first_block = me * blocks_dev
    offset_block = layout[block_count - 1, 0] % STRIDE
    reach_back = (LOCAL - 2) // blocks_dev + 1
    span_blocks = [
        min(blocks_dev, LOCAL - 1 - hop_index * blocks_dev) for hop_index in range(reach_back)
    ]
    back_blocks = sum(span_blocks)
    pool_blocks = back_blocks + blocks_dev

    attn_grad = jnp.dot(out_grad, proj_weight, preferred_element_type=jnp.float32).astype(
        jnp.bfloat16
    )
    kv = jnp.concatenate([keys, values], axis=1)

    near = []
    for distance in range(reach_back, 0, -1):
        rows_needed = span_blocks[distance - 1] * BLK
        near.append(passed_along(kv[tok_dev - rows_needed :], "seq", distance))
    pool_kv = jnp.concatenate(near + [kv], axis=0)

    far_ids = jnp.arange(summary_count, dtype=jnp.int32) * STRIDE + offset_block
    far_owner = far_ids // blocks_dev
    far_local = far_ids % blocks_dev
    kv_blocks = kv.reshape(blocks_dev, BLK, 2 * width)
    far_mine = jnp.where(
        (far_owner == me)[:, None, None], jnp.take(kv_blocks, far_local, axis=0), jnp.zeros_like(kv_blocks[:1])
    ).reshape(summary_count * BLK, 2 * width)
    far_part = lax.psum_scatter(far_mine, "seq", scatter_dimension=0, tiled=True)
    far_kv = lax.all_gather(far_part, "seq", axis=0, tiled=True)

    all_kv = jnp.concatenate([pool_kv, far_kv], axis=0)
    key_rows = all_kv[:, :width].reshape(-1, heads_here, HD)
    value_rows = all_kv[:, width:].reshape(-1, heads_here, HD)
    query_rows = queries.reshape(tok_dev, heads_here, HD)
    grad_rows = attn_grad.reshape(tok_dev, heads_here, HD)

    own_ids = first_block + jnp.arange(blocks_dev, dtype=jnp.int32)
    table_rows = lax.dynamic_slice_in_dim(layout, first_block, blocks_dev, 0)
    pool_ids = first_block - back_blocks + jnp.arange(pool_blocks, dtype=jnp.int32)
    pool_ids_b = jnp.broadcast_to(pool_ids[None, :], (blocks_dev, pool_blocks))
    plain = (pool_ids_b % STRIDE != offset_block) | (pool_ids_b == own_ids[:, None])
    pool_ok = listed(table_rows, pool_ids_b) & plain
    far_ids_b = jnp.broadcast_to(far_ids[None, :], (blocks_dev, summary_count))
    far_ok = listed(table_rows, far_ids_b) & (far_ids_b < own_ids[:, None])
    block_ok = jnp.concatenate([pool_ok, far_ok], axis=1)
    token_ok = jnp.repeat(jnp.repeat(block_ok, BLK, axis=0), BLK, axis=1)
    query_pos = jnp.arange(tok_dev, dtype=jnp.int32)
    pool_pos = jnp.arange(pool_blocks * BLK, dtype=jnp.int32) - back_blocks * BLK
    causal = jnp.concatenate(
        [
            pool_pos[None, :] <= query_pos[:, None],
            jnp.ones((tok_dev, summary_count * BLK), jnp.bool_),
        ],
        axis=1,
    )
    allowed = token_ok & causal

    scores = (
        jnp.einsum("qhd,khd->hqk", query_rows, key_rows, preferred_element_type=jnp.float32)
        * score_scale
    )
    scores = jnp.where(allowed[None], scores, -jnp.inf)
    row_top = jnp.max(scores, axis=-1, keepdims=True)
    log_total = row_top + jnp.log(jnp.sum(jnp.exp(scores - row_top), axis=-1, keepdims=True))
    probs = jnp.exp(scores - log_total)
    probs_low = probs.astype(jnp.bfloat16)
    attn_out = jnp.einsum(
        "hqk,khd->qhd", probs_low, value_rows, preferred_element_type=jnp.float32
    ).astype(jnp.bfloat16)
    delta = jnp.transpose(
        jnp.sum(attn_out.astype(jnp.float32) * grad_rows.astype(jnp.float32), axis=-1)
    )[..., None]
    dprobs = jnp.einsum("qhd,khd->hqk", grad_rows, value_rows, preferred_element_type=jnp.float32)
    dscores = (score_scale * probs * (dprobs - delta)).astype(jnp.bfloat16)
    query_grad = jnp.einsum(
        "hqk,khd->qhd", dscores, key_rows, preferred_element_type=jnp.float32
    ).astype(jnp.bfloat16)
    key_part = jnp.einsum("hqk,qhd->khd", dscores, query_rows, preferred_element_type=jnp.float32)
    value_part = jnp.einsum(
        "hqk,qhd->khd", probs_low, grad_rows, preferred_element_type=jnp.float32
    )
    grad_kv = jnp.concatenate(
        [key_part.reshape(-1, width), value_part.reshape(-1, width)], axis=1
    )

    far_grad = grad_kv[pool_blocks * BLK :]
    far_sum = lax.all_gather(
        lax.psum_scatter(far_grad, "seq", scatter_dimension=0, tiled=True), "seq", axis=0, tiled=True
    ).reshape(summary_count, BLK, 2 * width)
    is_summary = own_ids % STRIDE == offset_block
    summary_slot = jnp.minimum(own_ids // STRIDE, summary_count - 1)
    far_add = jnp.where(is_summary[:, None, None], jnp.take(far_sum, summary_slot, axis=0), 0.0)

    own_grad = grad_kv[back_blocks * BLK : pool_blocks * BLK]
    pool_start = 0
    for distance in range(reach_back, 0, -1):
        rows_needed = span_blocks[distance - 1] * BLK
        back = passed_along(grad_kv[pool_start : pool_start + rows_needed], "seq", -distance)
        own_grad = own_grad.at[tok_dev - rows_needed :].add(back)
        pool_start = pool_start + rows_needed
    total = own_grad.reshape(blocks_dev, BLK, 2 * width) + far_add
    total = total.reshape(tok_dev, 2 * width).astype(jnp.bfloat16)

    proj_grad = lax.psum_scatter(
        lax.dot_general(
            out_grad,
            attn_out.reshape(tok_dev, width),
            (((0,), (0,)), ((), ())),
            preferred_element_type=jnp.float32,
        ),
        "seq",
        scatter_dimension=0,
        tiled=True,
    )
    return (
        query_grad.reshape(tok_dev, width),
        total[:, :width],
        total[:, width:],
        proj_grad,
    )


def solution(mesh):
    return jax.shard_map(
        local,
        mesh=mesh,
        in_specs=(
            P(("dp", "seq"), "head"),
            P(("dp", "seq"), "head"),
            P(("dp", "seq"), "head"),
            P(("dp", "seq"), None),
            P(None, "head"),
            P(),
        ),
        out_specs=(
            P(("dp", "seq"), "head"),
            P(("dp", "seq"), "head"),
            P(("dp", "seq"), "head"),
            P(("dp", "seq"), "head"),
        ),
        check_vma=False,
    )
```

time: 2080 us -> 1130 us (0.54)
  waiting for transfers between devices: 1700 us -> 903 us
  starting transfers between devices: 143 us -> 37.6 us
  local copies, waits for them, and re-layouts: 111 us -> 66 us
  other arithmetic: 15.5 us -> 36.7 us
    psum x5 -> x0, waiting for transfers between devices: 1360 us -> none  [the longest x4 1230 us: broadcast(): return lax.psum(jnp.where(mine, array, jnp.zeros_like(array)), axis)]
    reduce_scatter x1 -> x3, waiting for transfers between devices: 194 us -> 508 us  [the longest x1 181 us: local(): lax.psum_scatter(lax.dot_general(out_grad, attn_out.reshape(tok_dev, widt...]
    all_gather x0 -> x2, waiting for transfers between devices: none -> 196 us  [the longest x1 136 us: local(): far_kv = lax.all_gather(far_part, 'seq', axis=0, tiled=True)]
    ppermute x16 -> x8, starting transfers between devices: 143 us -> 37.4 us  [passed_along(): return lax.ppermute(block, axis, route)]
    ppermute x16 -> x8, waiting for transfers between devices: 146 us -> 199 us  [passed_along(): return lax.ppermute(block, axis, route)]
    dot_general x25 -> x7, matrix products: 64.2 us -> 53.8 us  [the longest x1 10.4 us: local(): jnp.einsum('hqk,khd->qhd', probs_low, value_rows, preferred_element_type=...]
  transfers between devices with their start and end apart: 22 -> 13, of which waited for: 10 -> 7; matrix products, arithmetic and copies ran while one was open for 4% -> 5% of each run, Pallas kernels for 0% -> 0%
where the time goes in v1:
time: 1130 us; the launch traced here: 1120 us
  waiting for transfers between devices  903 us (80%)
  local copies, waits for them, and re-layouts  66 us (6%)
  matrix products  60.3 us (5%)
  starting transfers between devices  37.6 us (3%)
  other arithmetic  36.7 us (3%)
  between operations  16.1 us (1%)
    ppermute x8, waiting for transfers between devices, passed_along(): return lax.ppermute(block, axis, route)  199 us
    reduce_scatter x1, waiting for transfers between devices, local(): lax.psum_scatter(lax.dot_general(out_grad, attn_out.reshape(tok_dev, widt...  181 us
    reduce_scatter x1, waiting for transfers between devices, local(): lax.psum_scatter(far_mine, 'seq', scatter_dimension=0, tiled=True)  166 us
    reduce_scatter x1, waiting for transfers between devices, local(): lax.psum_scatter(far_grad, 'seq', scatter_dimension=0, tiled=True)  161 us
    all_gather x1, waiting for transfers between devices, local(): far_kv = lax.all_gather(far_part, 'seq', axis=0, tiled=True)  136 us
    all_gather x1, waiting for transfers between devices, local(): lax.all_gather(lax.psum_scatter(far_grad, 'seq', scatter_dimension=0, til...  59.7 us
    ppermute x8, starting transfers between devices, passed_along(): return lax.ppermute(block, axis, route)  37.4 us
  transfers between devices with their start and end apart: 13, of which 7 were waited for; matrix products, arithmetic and copies ran while one was open for 5% of the time, Pallas kernels for 0%

profile of v1, /device:TPU:40, one launch (start us, length us, event | category | flops | bytes accessed | tf_op | source)
XLA Modules:
  0.0 1119.6 jit_solution(14929468038700556082)
XLA Ops:
  11.9 1.4 copy.96
  15.1 1.5 copy.97
  16.7 2.0 gather_fusion
  18.7 4.0 copy.98
  22.9 3.1 select_select_fusion
  26.0 4.0 copy.127
  30.0 2.8 collective-permute-start.1
  32.9 4.5 collective-permute-start.2
  37.4 3.8 collective-permute-start.3
  42.0 3.8 collective-permute-start
  46.0 166.1 %reduce-scatter.10.cloned.1.call-done = bf16[16,2048]{1,0:T(8,128)(2,1)} async-done(((bf16[512,2048]{1,0:T(8,128)(2,1)}), bf16[16,2048]{1,0:T(8,128)(2,1)}) %reduce-scatter.10.cloned.1.call-update) | async-done | bytes 65552 | tf_op jit(solution)/shard_map/reduce_scatter | solution.py:59
  212.8 6.5 convolution_convert_fusion.2
  219.6 2.0 copy.129
  221.7 2.0 copy.130
  224.9 1.9 constant_dynamic-update-slice_fusion.5
  226.8 2.3 constant_dynamic-update-slice_fusion.4
  229.2 2.3 constant_dynamic-update-slice_fusion.3
  231.5 2.3 constant_dynamic-update-slice_fusion.2
  234.9 136.3 %all-gather.3.cloned.1.call-done = bf16[512,2048]{1,0:T(8,128)(2,1)} async-done(((bf16[16,2048]{1,0:T(8,128)(2,1)}), bf16[512,2048]{1,0:T(8,128)(2,1)}) %all-gather.3.cloned.1.call-update) | async-done | bytes 2097168 | tf_op jit(solution)/shard_map/all_gather | solution.py:60
  371.2 3.9 copy.100
  375.1 3.1 constant_dynamic-update-slice_fusion
  378.2 5.3 fusion.23
  383.4 7.5 fusion.1
  390.9 7.8 exponential_reduce_fusion
  398.8 10.4 multiply_reduce_fusion
  409.2 5.8 fusion.20
  415.0 10.1 multiply_convert_fusion
  425.2 7.7 copy.117
  432.9 7.9 fusion.25
  440.7 7.7 copy.116
  448.4 4.7 pad_maximum_fusion
  453.2 161.3 %reduce-scatter.6.cloned.1.call-done = f32[16,2048]{1,0:T(8,128)} async-done(((f32[512,2048]{1,0:T(8,128)}), f32[16,2048]{1,0:T(8,128)}) %reduce-scatter.6.cloned.1.call-update) | async-done | bytes 131088 | tf_op jit(solution)/shard_map/reduce_scatter | solution.py:119
  614.5 8.1 convolution_bitcast_fusion
  622.6 6.1 fusion.4
  628.7 7.6 collective-permute-start.7
  636.3 7.0 collective-permute-start.6
  643.3 5.9 collective-permute-start.5
  649.3 2.4 fusion.12
  651.7 1.9 collective-permute-start.4
  653.8 4.1 convolution_convert_fusion
  658.9 190.7 %collective-permute-done.4 = f32[128,2048]{1,0:T(8,128)} collective-permute-done((f32[128,2048]{1,0:T(8,128)}, f32[128,2048]{1,0:T(8,128)}, u32[]{:S(2)}, u32[]{:S(2)}) %collective-permute-start.4) | collective-permute-done | bytes 1048608 | tf_op jit(solution)/shard_map/ppermute | solution.py:15
  849.6 2.6 fusion.11
  852.3 59.7 %all-gather.5.cloned.1.call-done = f32[512,2048]{1,0:T(8,128)} async-done(((f32[16,2048]{1,0:T(8,128)}), f32[512,2048]{1,0:T(8,128)}) %all-gather.5.cloned.1.call-update) | async-done | bytes 4194320 | tf_op jit(solution)/shard_map/all_gather | solution.py:118
  912.0 4.2 gather_fusion.1
  916.2 7.8 collective-permute-done.5
  924.0 5.0 fusion.8
  930.1 181.0 %reduce-scatter.8.cloned.1.call-done = f32[128,1024]{0,1:T(8,128)} async-done(((f32[4096,1024]{0,1:T(8,128)}), f32[128,1024]{0,1:T(8,128)}) %reduce-scatter.8.cloned.1.call-update) | async-done | bytes 524304 | tf_op jit(solution)/shard_map/reduce_scatter | solution.py:135
  1111.1 2.0 copy.119
  (89 shorter events, 11.4 us)
Async XLA Ops:
  7.2 205.6 %copy-start = (bf16[256,4096]{1,0:T(8,128)(2,1)S(1)}, bf16[256,4096]{1,0:T(8,128)(2,1)}, u32[]{:S(2)}) copy-start(bf16[256,4096]{1,0:T(8,128)(2,1)} %param.23) | copy-start | bytes 6291460
  7.2 204.9 %reduce-scatter.10.cloned.1.call-start = ((), (), s32[]{:S(2)}) async-start(), calls=%async_computation.7 | async-start | bytes 2162688 | tf_op jit(solution)/shard_map/reduce_scatter | solution.py:59
  11.8 1.5 copy-start.3
  13.3 0.8 copy-start.5
  18.7 22.5 %copy-start.4 = (bf16[256,1024]{0,1:T(8,128)(2,1)S(1)}, bf16[256,1024]{0,1:T(8,128)(2,1)}, u32[]{:S(2)}) copy-start(bf16[256,1024]{0,1:T(8,128)(2,1)} %copy-done.3) | copy-start | bytes 1572868
  18.7 22.5 %copy-start.6 = (bf16[256,1024]{0,1:T(8,128)(2,1)S(1)}, bf16[256,1024]{0,1:T(8,128)(2,1)}, u32[]{:S(2)}) copy-start(bf16[256,1024]{0,1:T(8,128)(2,1)} %copy-done.5) | copy-start | bytes 1572868
  22.7 23.2 %copy-start.12 = (s32[64,12]{0,1:T(8,128)S(1)}, s32[64,12]{0,1:T(8,128)}, u32[]{:S(2)}) copy-start(s32[64,12]{0,1:T(8,128)} %param.25) | copy-start | bytes 9220
  30.0 341.2 %all-gather.3.cloned.1.call-start = ((), (), s32[]{:S(2)}) async-start(), calls=%async_computation.3 | async-start | bytes 2162688 | tf_op jit(solution)/shard_map/all_gather | solution.py:60
  30.0 196.8 %collective-permute-start.1 = (bf16[256,2048]{0,1:T(8,128)(2,1)}, bf16[256,2048]{0,1:T(8,128)(2,1)}, u32[]{:S(2)}, u32[]{:S(2)}) collective-permute-start(bf16[256,2048]{0,1:T(8,128)(2,1)} %pad_maximum_fusion.1), channel_id=1, source_target_pairs={{0,12},{4,16},{8,20},{12,24},{16,28},{20,32},{24,36},{28,40},{32,4... | collective-permute-start | bytes 3145736 | tf_op jit(solution)/shard_map/ppermute | solution.py:15
  32.9 196.3 %collective-permute-start.2 = (bf16[256,2048]{0,1:T(8,128)(2,1)}, bf16[256,2048]{0,1:T(8,128)(2,1)}, u32[]{:S(2)}, u32[]{:S(2)}) collective-permute-start(bf16[256,2048]{0,1:T(8,128)(2,1)} %pad_maximum_fusion.1), channel_id=1, source_target_pairs={{0,8},{4,12},{8,16},{12,20},{16,24},{20,28},{24,32},{28,36},{32,40... | collective-permute-start | bytes 3145736 | tf_op jit(solution)/shard_map/ppermute | solution.py:15
  37.4 194.1 %collective-permute-start.3 = (bf16[256,2048]{0,1:T(8,128)(2,1)}, bf16[256,2048]{0,1:T(8,128)(2,1)}, u32[]{:S(2)}, u32[]{:S(2)}) collective-permute-start(bf16[256,2048]{0,1:T(8,128)(2,1)} %pad_maximum_fusion.1), channel_id=1, source_target_pairs={{0,4},{4,8},{8,12},{12,16},{16,20},{20,24},{24,28},{28,32},{32,36}... | collective-permute-start | bytes 3145736 | tf_op jit(solution)/shard_map/ppermute | solution.py:15
  42.0 182.9 %collective-permute-start = (bf16[128,2048]{0,1:T(8,128)(2,1)}, bf16[128,2048]{0,1:T(8,128)(2,1)}, u32[]{:S(2)}, u32[]{:S(2)}) collective-permute-start(bf16[128,2048]{0,1:T(8,128)(2,1)} %fusion.13), channel_id=1, source_target_pairs={{0,16},{4,20},{8,24},{12,28},{16,32},{20,36},{24,40},{28,44},{32,4... | collective-permute-start | bytes 1572872 | tf_op jit(solution)/shard_map/ppermute | solution.py:15
  212.1 402.4 %reduce-scatter.6.cloned.1.call-start = ((), (), s32[]{:S(2)}) async-start(), calls=%async_computation.4 | async-start | bytes 4325376 | tf_op jit(solution)/shard_map/reduce_scatter | solution.py:119
  378.2 5.3 copy-start.7
  378.2 5.3 copy-start.8
  383.4 7.5 copy-start.1
  390.9 18.2 %slice-start = ((s8[13631488]{0:T(1024)(128)(4,1)}), s8[4194304]{0:T(1024)(128)(4,1)S(1)}, s32[]{:S(2)}) async-start(s8[13631488]{0:T(1024)(128)(4,1)} %bitcast.82), calls=%async_computation.8 | async-start | bytes 8388608
  390.9 18.2 %slice-start.1 = ((s8[13631488]{0:T(1024)(128)(4,1)}), s8[1048576]{0:T(1024)(128)(4,1)S(1)}, s32[]{:S(2)}) async-start(s8[13631488]{0:T(1024)(128)(4,1)} %bitcast.82), calls=%async_computation.9 | async-start | bytes 2097152
  398.7 10.4 slice-start.2
  398.7 10.4 slice-start.3
  398.8 10.4 copy-start.10
  425.2 7.7 copy-start.9
  448.4 166.1 %copy-start.11 = (bf16[8,128,256]{2,1,0:T(8,128)(2,1)S(1)}, bf16[8,128,256]{2,1,0:T(8,128)(2,1)}, u32[]{:S(2)}) copy-start(bf16[8,128,256]{2,1,0:T(8,128)(2,1)} %get-tuple-element.107) | copy-start | bytes 1572868
  453.2 458.8 %all-gather.5.cloned.1.call-start = ((), (), s32[]{:S(2)}) async-start(), calls=%async_computation.5 | async-start | bytes 4325376 | tf_op jit(solution)/shard_map/all_gather | solution.py:118
  614.5 496.6 %reduce-scatter.8.cloned.1.call-start = ((), (), s32[]{:S(2)}) async-start(), calls=%async_computation.6 | async-start | bytes 17301504 | tf_op jit(solution)/shard_map/reduce_scatter | solution.py:135
  628.7 287.5 %collective-permute-start.7 = (f32[256,2048]{1,0:T(8,128)}, f32[256,2048]{1,0:T(8,128)}, u32[]{:S(2)}, u32[]{:S(2)}) collective-permute-start(f32[256,2048]{1,0:T(8,128)} %get-tuple-element.99), channel_id=1, source_target_pairs={{4,0},{8,4},{12,8},{16,12},{20,16},{24,20},{28,24},{32,28},{36,32}... | collective-permute-start | bytes 6291464 | tf_op jit(solution)/shard_map/ppermute | solution.py:15
  636.3 279.9 %collective-permute-start.6 = (f32[256,2048]{1,0:T(8,128)}, f32[256,2048]{1,0:T(8,128)}, u32[]{:S(2)}, u32[]{:S(2)}) collective-permute-start(f32[256,2048]{1,0:T(8,128)} %get-tuple-element.98), channel_id=1, source_target_pairs={{8,0},{12,4},{16,8},{20,12},{24,16},{28,20},{32,24},{36,28},{40,32... | collective-permute-start | bytes 6291464 | tf_op jit(solution)/shard_map/ppermute | solution.py:15
  643.3 280.7 %collective-permute-start.5 = (f32[256,2048]{1,0:T(8,128)}, f32[256,2048]{1,0:T(8,128)}, u32[]{:S(2)}, u32[]{:S(2)}) collective-permute-start(f32[256,2048]{1,0:T(8,128)} %get-tuple-element.96), channel_id=1, source_target_pairs={{12,0},{16,4},{20,8},{24,12},{28,16},{32,20},{36,24},{40,28},{44,3... | collective-permute-start | bytes 6291464 | tf_op jit(solution)/shard_map/ppermute | solution.py:15
  649.3 4.5 copy-start.2
  651.7 197.9 %collective-permute-start.4 = (f32[128,2048]{1,0:T(8,128)}, f32[128,2048]{1,0:T(8,128)}, u32[]{:S(2)}, u32[]{:S(2)}) collective-permute-start(f32[128,2048]{1,0:T(8,128)} %fusion.12), channel_id=1, source_target_pairs={{16,0},{20,4},{24,8},{28,12},{32,16},{36,20},{40,24},{44,28},{48,3... | collective-permute-start | bytes 3145736 | tf_op jit(solution)/shard_map/ppermute | solution.py:15
Sparse Core Ops, SparseCore 0:
  30.1 181.9 reduce-scatter.9
  213.8 157.3 all-gather.2
  453.3 161.1 reduce-scatter.5
  616.1 295.8 all-gather.4
  914.3 196.6 reduce-scatter.7

commit v2 on v1

--- a/solution.py
+++ b/solution.py
@@ -49,15 +49,34 @@
         near.append(passed_along(kv[tok_dev - rows_needed :], "seq", distance))
     pool_kv = jnp.concatenate(near + [kv], axis=0)
 
+    seq_size = lax.axis_size("seq")
+    group = STRIDE // blocks_dev
+    groups = seq_size // group
+    assert groups == summary_count and blocks_dev <= STRIDE
     far_ids = jnp.arange(summary_count, dtype=jnp.int32) * STRIDE + offset_block
-    far_owner = far_ids // blocks_dev
-    far_local = far_ids % blocks_dev
-    kv_blocks = kv.reshape(blocks_dev, BLK, 2 * width)
-    far_mine = jnp.where(
-        (far_owner == me)[:, None, None], jnp.take(kv_blocks, far_local, axis=0), jnp.zeros_like(kv_blocks[:1])
-    ).reshape(summary_count * BLK, 2 * width)
-    far_part = lax.psum_scatter(far_mine, "seq", scatter_dimension=0, tiled=True)
-    far_kv = lax.all_gather(far_part, "seq", axis=0, tiled=True)
+    lead = offset_block // blocks_dev
+    sum_local = offset_block % blocks_dev
+    in_group = me % group
+    my_group = me // group
+    rel = (in_group - lead) % group
+    held = lax.dynamic_index_in_dim(kv.reshape(blocks_dev, BLK, 2 * width), sum_local, 0, keepdims=False)
+    hop = 1
+    while hop < group:
+        route = [(g * group + (r - hop) % group, g * group + r) for g in range(groups) for r in range(group)]
+        moved = lax.ppermute(held, "seq", route)
+        held = jnp.where((rel >= hop) & (rel < 2 * hop), moved, held)
+        hop *= 2
+    gathered = held[None]
+    span = 1
+    while span < groups:
+        route = [(d, d ^ (span * group)) for d in range(seq_size)]
+        moved = lax.ppermute(gathered, "seq", route)
+        upper = (my_group // span) % 2 == 1
+        gathered = jnp.where(
+            upper, jnp.concatenate([moved, gathered], 0), jnp.concatenate([gathered, moved], 0)
+        )
+        span *= 2
+    far_kv = gathered.reshape(summary_count * BLK, 2 * width)
 
     all_kv = jnp.concatenate([pool_kv, far_kv], axis=0)
     key_rows = all_kv[:, :width].reshape(-1, heads_here, HD)
@@ -114,13 +133,26 @@
         [key_part.reshape(-1, width), value_part.reshape(-1, width)], axis=1
     )
 
-    far_grad = grad_kv[pool_blocks * BLK :]
-    far_sum = lax.all_gather(
-        lax.psum_scatter(far_grad, "seq", scatter_dimension=0, tiled=True), "seq", axis=0, tiled=True
-    ).reshape(summary_count, BLK, 2 * width)
-    is_summary = own_ids % STRIDE == offset_block
-    summary_slot = jnp.minimum(own_ids // STRIDE, summary_count - 1)
-    far_add = jnp.where(is_summary[:, None, None], jnp.take(far_sum, summary_slot, axis=0), 0.0)
+    part = grad_kv[pool_blocks * BLK :].reshape(summary_count, BLK, 2 * width)
+    span = groups // 2
+    while span >= 1:
+        half = part.shape[0] // 2
+        upper = (my_group // span) % 2 == 1
+        keep = jnp.where(upper, part[half:], part[:half])
+        send = jnp.where(upper, part[:half], part[half:])
+        route = [(d, d ^ (span * group)) for d in range(seq_size)]
+        part = keep + lax.ppermute(send, "seq", route)
+        span //= 2
+    part = part[0]
+    hop = group // 2
+    while hop >= 1:
+        route = [(g * group + (r + hop) % group, g * group + r) for g in range(groups) for r in range(group)]
+        moved = lax.ppermute(part, "seq", route)
+        part = jnp.where(rel < hop, part + moved, part)
+        hop //= 2
+    own_local = jnp.arange(blocks_dev, dtype=jnp.int32)
+    far_here = (rel == 0) & (own_local == sum_local)
+    far_add = jnp.where(far_here[:, None, None], part[None], 0.0)
 
     own_grad = grad_kv[back_blocks * BLK : pool_blocks * BLK]
     pool_start = 0

time: 1130 us -> 815 us (0.72)
  waiting for transfers between devices: 903 us -> 456 us
  starting transfers between devices: 37.6 us -> 193 us
  local copies, waits for them, and re-layouts: 66 us -> 51.2 us
    reduce_scatter x2 -> x0, waiting for transfers between devices: 327 us -> none  [the longest x1 166 us: local(): lax.psum_scatter(far_mine, 'seq', scatter_dimension=0, tiled=True)]
    all_gather x2 -> x0, waiting for transfers between devices: 196 us -> none  [the longest x1 136 us: local(): far_kv = lax.all_gather(far_part, 'seq', axis=0, tiled=True)]
    reduce_scatter x1, waiting for transfers between devices: 181 us -> 0.01 us  [local(): lax.psum_scatter(lax.dot_general(out_grad, attn_out.reshape(tok_dev, widt...]
    ppermute x0 -> x10, waiting for transfers between devices: none -> 177 us  [the longest x3 78.6 us: local(): moved = lax.ppermute(held, 'seq', route)]
    ppermute x0 -> x10, starting transfers between devices: none -> 166 us  [the longest x3 153 us: local(): moved = lax.ppermute(part, 'seq', route)]
    ppermute x8, waiting for transfers between devices: 199 us -> 279 us  [passed_along(): return lax.ppermute(block, axis, route)]
    select_n x3 -> x10, other arithmetic: 3.15 us -> 15.7 us  [the longest x1 5.24 us: local(): keep = jnp.where(upper, part[half:], part[:half])]
    concatenate x3 -> x1, other arithmetic: 13.2 us -> 1.9 us  [local(): jnp.concatenate([key_part.reshape(-1, width), value_part.reshape(-1, widt...]
  transfers between devices with their start and end apart: 13 -> 19, of which waited for: 7 -> 11; matrix products, arithmetic and copies ran while one was open for 5% -> 11% of each run, Pallas kernels for 0% -> 0%
where the time goes in v2:
time: 815 us; the launch traced here: 812 us
  waiting for transfers between devices  456 us (56%)
  starting transfers between devices  193 us (24%)
  matrix products  58 us (7%)
  local copies, waits for them, and re-layouts  51.2 us (6%)
  other arithmetic  37.6 us (5%)
  between operations  16.5 us (2%)
    ppermute x8, waiting for transfers between devices, passed_along(): return lax.ppermute(block, axis, route)  279 us
    ppermute x3, starting transfers between devices, local(): moved = lax.ppermute(part, 'seq', route)  153 us
    ppermute x3, waiting for transfers between devices, local(): moved = lax.ppermute(held, 'seq', route)  78.6 us
    ppermute x2, waiting for transfers between devices, local(): part = keep + lax.ppermute(send, 'seq', route)  57.7 us
    ppermute x8, starting transfers between devices, passed_along(): return lax.ppermute(block, axis, route)  26.3 us
    ppermute x3, waiting for transfers between devices, local(): moved = lax.ppermute(part, 'seq', route)  25.3 us
  transfers between devices with their start and end apart: 19, of which 11 were waited for; matrix products, arithmetic and copies ran while one was open for 11% of the time, Pallas kernels for 0%

profile of v2, /device:TPU:40, one launch (start us, length us, event | category | flops | bytes accessed | tf_op | source)
XLA Modules:
  0.0 811.8 jit_solution(7252010278204093263)
XLA Ops:
  11.0 2.8 collective-permute-start.1
  13.8 4.5 collective-permute-start.2
  18.3 3.8 collective-permute-start.3
  22.9 3.8 collective-permute-start
  26.7 2.3 copy.95
  31.6 1.9 dynamic-slice_bitcast_fusion
  34.2 41.8 %collective-permute-done.4 = bf16[128,2048]{1,0:T(8,128)(2,1)} collective-permute-done((bf16[128,2048]{1,0:T(8,128)(2,1)}, bf16[128,2048]{1,0:T(8,128)(2,1)}, u32[]{:S(2)}, u32[]{:S(2)}) %collective-permute-start.4) | collective-permute-done | bytes 524320 | tf_op jit(solution)/shard_map/ppermute | solution.py:66
  77.2 6.5 convolution_convert_fusion.2
  83.7 23.8 %collective-permute-done.5 = bf16[128,2048]{1,0:T(8,128)(2,1)S(1)} collective-permute-done((bf16[128,2048]{1,0:T(8,128)(2,1)S(1)}, bf16[128,2048]{1,0:T(8,128)(2,1)S(1)}, u32[]{:S(2)}, u32[]{:S(2)}) %collective-permute-start.5) | collective-permute-done | bytes 524320 | tf_op jit(solution)/shard_map/ppermute | solution.py:66
  107.8 13.1 %collective-permute-done.6 = bf16[128,2048]{1,0:T(8,128)(2,1)S(1)} collective-permute-done((bf16[128,2048]{1,0:T(8,128)(2,1)S(1)}, bf16[128,2048]{1,0:T(8,128)(2,1)S(1)}, u32[]{:S(2)}, u32[]{:S(2)}) %collective-permute-start.6) | collective-permute-done | bytes 524320 | tf_op jit(solution)/shard_map/ppermute | solution.py:66
  121.8 7.4 collective-permute-start.7
  129.6 2.0 copy.123
  131.7 2.0 copy.124
  134.7 3.5 collective-permute-done.7
  138.2 1.8 maximum_select_fusion.1
  140.0 3.6 collective-permute-start.8
  148.7 2.8 copy-done.6
  151.5 12.1 %collective-permute-done.8 = bf16[2,128,2048]{2,1,0:T(8,128)(2,1)S(1)} collective-permute-done((bf16[2,128,2048]{2,1,0:T(8,128)(2,1)S(1)}, bf16[2,128,2048]{2,1,0:T(8,128)(2,1)S(1)}, u32[]{:S(2)}, u32[]{:S(2)}) %collective-permute-start.8) | collective-permute-done | bytes 1048608 | tf_op jit(solution)/shard_map/ppermute | solution.py:73
  165.2 4.0 copy.96
  169.2 3.1 constant_dynamic-update-slice_fusion
  172.3 3.6 fusion.18
  175.9 7.5 fusion.1
  183.4 7.7 exponential_reduce_fusion
  191.1 8.4 %multiply_reduce_fusion = (f32[256,8]{0,1:T(8,128)S(1)}, bf16[8,128,256]{2,1,0:T(8,128)(2,1)S(1)}) fusion(bf16[256,1024]{0,1:T(8,128)(2,1)S(1)} %copy-done.10, bf16[1664,8,128]{0,2,1:T(8,128)(2,1)S(1)} %bitcast.90, f32[8,1664,256]{2,1,0:T(8,128)} %get-tuple-element.108, f32[8,256]{1,0:T(8,128)S(1)} %log_add_fusion, pred[256,1664]{0,1:T(8,128)(4,1)S(1)} %copy-done.7), kind=kOutput, calls=%fused_computation.48 | convolution fusion | flops 887355392 | bytes 18530304 | tf_op jit(solution)/shard_map/hqk,khd->qhd/dot_general | solution.py:117
  199.6 8.1 convolution_bitcast_fusion
  208.7 11.4 %fusion.15 = f32[8,128,1664]{2,1,0:T(8,128)} fusion(bf16[256,8,128]{0,2,1:T(8,128)(2,1)S(1)} %bitcast.94, f32[8,1664,256]{2,1,0:T(8,128)} %get-tuple-element.108, f32[8,256]{1,0:T(8,128)S(1)} %log_add_fusion, pred[256,1664]{0,1:T(8,128)(4,1)S(1)} %copy-done.7), kind=kOutput, calls=%fused_computation.84 | convolution fusion | flops 886046720 | bytes 21405696 | tf_op jit(solution)/shard_map/hqk,qhd->khd/dot_general | solution.py:129
  220.1 7.9 copy.113
  228.0 9.9 %multiply_convert_fusion = bf16[8,256,1664]{1,2,0:T(8,128)(2,1)S(1)} fusion(f32[8,1664,256]{2,1,0:T(8,128)} %get-tuple-element.108, f32[8,256]{1,0:T(8,128)S(1)} %bitcast.99, f32[8,256]{1,0:T(8,128)S(1)} %log_add_fusion, pred[256,1664]{0,1:T(8,128)(4,1)S(1)} %copy-done.7, bf16[256,8,128]{0,2,1:T(8,128)(2,1)S(1)} %bitcast.95, bf16[1664,8,128]{0,2,1:T(8,128)(2,1)} %bitcast.91), kind=kOutput, calls=%fused_computation.15 | convolution fusion | flops 896270336 | bytes 24821760 | tf_op jit(solution)/shard_map/qhd,khd->hqk/dot_general | solution.py:123
  238.0 5.0 fusion.20
  243.0 7.7 copy.112
  250.7 2.8 broadcast_select_fusion
  253.5 1.8 collective-permute-start.13
  255.3 5.2 broadcast_select_fusion.1
  260.5 42.0 %collective-permute-done.13 = f32[2,128,2048]{2,1,0:T(8,128)S(1)} collective-permute-done((f32[2,128,2048]{2,1,0:T(8,128)S(1)}, f32[2,128,2048]{2,1,0:T(8,128)S(1)}, u32[]{:S(2)}, u32[]{:S(2)}) %collective-permute-start.13) | collective-permute-done | bytes 2097184 | tf_op jit(solution)/shard_map/ppermute | solution.py:144
  303.1 15.6 %collective-permute-done.14 = f32[1,128,2048]{2,1,0:T(8,128)S(1)} collective-permute-done((f32[1,128,2048]{2,1,0:T(8,128)S(1)}, f32[1,128,2048]{2,1,0:T(8,128)S(1)}, u32[]{:S(2)}, u32[]{:S(2)}) %collective-permute-start.14) | collective-permute-done | bytes 1048608 | tf_op jit(solution)/shard_map/ppermute | solution.py:144
  320.5 13.5 %collective-permute-done.15 = f32[128,2048]{1,0:T(8,128)S(1)} collective-permute-done((f32[128,2048]{1,0:T(8,128)S(1)}, f32[128,2048]{1,0:T(8,128)S(1)}, u32[]{:S(2)}, u32[]{:S(2)}) %collective-permute-start.15) | collective-permute-done | bytes 1048608 | tf_op jit(solution)/shard_map/ppermute | solution.py:150
  334.2 151.3 %collective-permute-start.16 = (f32[128,2048]{1,0:T(8,128)S(1)}, f32[128,2048]{1,0:T(8,128)}, u32[]{:S(2)}, u32[]{:S(2)}) collective-permute-start(f32[128,2048]{1,0:T(8,128)S(1)} %add_select_fusion.2), channel_id=1, source_target_pairs={{8,0},{12,4},{16,8},{20,12},{24,16},{28,20},{0,24},{4,28},{40,32},... | collective-permute-start | bytes 3145736 | tf_op jit(solution)/shard_map/ppermute | solution.py:150
  485.6 1.9 collective-permute-start.12
  487.5 2.3 collective-permute-start.11
  489.8 1.9 fusion.12
  491.8 3.7 collective-permute-start.9
  495.5 3.4 collective-permute-start.10
  498.9 11.8 %collective-permute-done.16 = f32[128,2048]{1,0:T(8,128)} collective-permute-done((f32[128,2048]{1,0:T(8,128)S(1)}, f32[128,2048]{1,0:T(8,128)}, u32[]{:S(2)}, u32[]{:S(2)}) %collective-permute-start.16) | collective-permute-done | bytes 1048608 | tf_op jit(solution)/shard_map/ppermute | solution.py:150
  514.6 132.4 %collective-permute-done.9 = f32[128,2048]{1,0:T(8,128)} collective-permute-done((f32[128,2048]{1,0:T(8,128)S(1)}, f32[128,2048]{1,0:T(8,128)}, u32[]{:S(2)}, u32[]{:S(2)}) %collective-permute-start.9) | collective-permute-done | bytes 1048608 | tf_op jit(solution)/shard_map/ppermute | solution.py:15
  647.0 2.6 fusion.11
  651.1 146.2 %collective-permute-done.10 = f32[256,2048]{1,0:T(8,128)} collective-permute-done((f32[256,2048]{1,0:T(8,128)}, f32[256,2048]{1,0:T(8,128)}, u32[]{:S(2)}, u32[]{:S(2)}) %collective-permute-start.10) | collective-permute-done | bytes 2097184 | tf_op jit(solution)/shard_map/ppermute | solution.py:15
  797.4 4.5 fusion.8
  802.9 2.0 copy.115
  (92 shorter events, 26.3 us)
Async XLA Ops:
  7.2 70.0 %copy-start = (bf16[256,4096]{1,0:T(8,128)(2,1)S(1)}, bf16[256,4096]{1,0:T(8,128)(2,1)}, u32[]{:S(2)}) copy-start(bf16[256,4096]{1,0:T(8,128)(2,1)} %param.23) | copy-start | bytes 6291460
  7.2 21.8 %copy-start.12 = (s32[64,12]{0,1:T(8,128)S(1)}, s32[64,12]{0,1:T(8,128)}, u32[]{:S(2)}) copy-start(s32[64,12]{0,1:T(8,128)} %param.25) | copy-start | bytes 9220
  7.2 795.8 %reduce-scatter.2.cloned.1.call-start = ((), (), s32[]{:S(2)}) async-start(), calls=%async_computation.1 | async-start | bytes 17301504 | tf_op jit(solution)/shard_map/reduce_scatter | solution.py:167
  11.0 133.7 %collective-permute-start.1 = (bf16[256,2048]{0,1:T(8,128)(2,1)}, bf16[256,2048]{0,1:T(8,128)(2,1)}, u32[]{:S(2)}, u32[]{:S(2)}) collective-permute-start(bf16[256,2048]{0,1:T(8,128)(2,1)} %pad_maximum_fusion.1), channel_id=1, source_target_pairs={{0,12},{4,16},{8,20},{12,24},{16,28},{20,32},{24,36},{28,40},{32,4... | collective-permute-start | bytes 3145736 | tf_op jit(solution)/shard_map/ppermute | solution.py:15
  13.8 132.2 %collective-permute-start.2 = (bf16[256,2048]{0,1:T(8,128)(2,1)}, bf16[256,2048]{0,1:T(8,128)(2,1)}, u32[]{:S(2)}, u32[]{:S(2)}) collective-permute-start(bf16[256,2048]{0,1:T(8,128)(2,1)} %pad_maximum_fusion.1), channel_id=1, source_target_pairs={{0,8},{4,12},{8,16},{12,20},{16,24},{20,28},{24,32},{28,36},{32,40... | collective-permute-start | bytes 3145736 | tf_op jit(solution)/shard_map/ppermute | solution.py:15
  18.3 129.0 %collective-permute-start.3 = (bf16[256,2048]{0,1:T(8,128)(2,1)}, bf16[256,2048]{0,1:T(8,128)(2,1)}, u32[]{:S(2)}, u32[]{:S(2)}) collective-permute-start(bf16[256,2048]{0,1:T(8,128)(2,1)} %pad_maximum_fusion.1), channel_id=1, source_target_pairs={{0,4},{4,8},{8,12},{12,16},{16,20},{20,24},{24,28},{28,32},{32,36}... | collective-permute-start | bytes 3145736 | tf_op jit(solution)/shard_map/ppermute | solution.py:15
  22.9 120.6 %collective-permute-start = (bf16[128,2048]{0,1:T(8,128)(2,1)}, bf16[128,2048]{0,1:T(8,128)(2,1)}, u32[]{:S(2)}, u32[]{:S(2)}) collective-permute-start(bf16[128,2048]{0,1:T(8,128)(2,1)} %fusion.13), channel_id=1, source_target_pairs={{0,16},{4,20},{8,24},{12,28},{16,32},{20,36},{24,40},{28,44},{32,4... | collective-permute-start | bytes 1572872 | tf_op jit(solution)/shard_map/ppermute | solution.py:15
  33.5 42.5 %collective-permute-start.4 = (bf16[128,2048]{1,0:T(8,128)(2,1)}, bf16[128,2048]{1,0:T(8,128)(2,1)}, u32[]{:S(2)}, u32[]{:S(2)}) collective-permute-start(bf16[128,2048]{1,0:T(8,128)(2,1)} %dynamic-slice_bitcast_fusion), channel_id=1, source_target_pairs={{28,0},{0,4},{4,8},{8,12},{12,16},{16,20},{20,24},{24,28},{60,32},... | collective-permute-start | bytes 1572872 | tf_op jit(solution)/shard_map/ppermute | solution.py:66
  77.1 30.4 %collective-permute-start.5 = (bf16[128,2048]{1,0:T(8,128)(2,1)S(1)}, bf16[128,2048]{1,0:T(8,128)(2,1)S(1)}, u32[]{:S(2)}, u32[]{:S(2)}) collective-permute-start(bf16[128,2048]{1,0:T(8,128)(2,1)S(1)} %broadcast_select_fusion.2), channel_id=1, source_target_pairs={{24,0},{28,4},{0,8},{4,12},{8,16},{12,20},{16,24},{20,28},{56,32},... | collective-permute-start | bytes 1572872 | tf_op jit(solution)/shard_map/ppermute | solution.py:66
  107.5 13.4 %collective-permute-start.6 = (bf16[128,2048]{1,0:T(8,128)(2,1)S(1)}, bf16[128,2048]{1,0:T(8,128)(2,1)S(1)}, u32[]{:S(2)}, u32[]{:S(2)}) collective-permute-start(bf16[128,2048]{1,0:T(8,128)(2,1)S(1)} %broadcast_select_fusion.3), channel_id=1, source_target_pairs={{16,0},{20,4},{24,8},{28,12},{0,16},{4,20},{8,24},{12,28},{48,32},... | collective-permute-start | bytes 1572872 | tf_op jit(solution)/shard_map/ppermute | solution.py:66
  121.8 16.4 %collective-permute-start.7 = (bf16[1,128,2048]{2,1,0:T(8,128)(2,1)}, bf16[1,128,2048]{2,1,0:T(8,128)(2,1)}, u32[]{:S(2)}, u32[]{:S(2)}) collective-permute-start(bf16[1,128,2048]{2,1,0:T(8,128)(2,1)} %select_bitcast_fusion), channel_id=1, source_target_pairs={{0,32},{4,36},{8,40},{12,44},{16,48},{20,52},{24,56},{28,60},{32,0... | collective-permute-start | bytes 1572872 | tf_op jit(solution)/shard_map/ppermute | solution.py:73
  140.0 23.6 %collective-permute-start.8 = (bf16[2,128,2048]{2,1,0:T(8,128)(2,1)S(1)}, bf16[2,128,2048]{2,1,0:T(8,128)(2,1)S(1)}, u32[]{:S(2)}, u32[]{:S(2)}) collective-permute-start(bf16[2,128,2048]{2,1,0:T(8,128)(2,1)S(1)} %maximum_select_fusion.1), channel_id=1, source_target_pairs={{0,64},{4,68},{8,72},{12,76},{16,80},{20,84},{24,88},{28,92},{32,9... | collective-permute-start | bytes 3145736 | tf_op jit(solution)/shard_map/ppermute | solution.py:73
  148.7 2.8 copy-start.6
  172.3 3.6 copy-start.7
  172.3 3.6 copy-start.8
  175.9 7.5 copy-start.4
  175.9 15.2 %copy-start.9 = (bf16[1664,1024]{0,1:T(8,128)(2,1)}, bf16[1664,1024]{0,1:T(8,128)(2,1)S(1)}, u32[]{:S(2)}) copy-start(bf16[1664,1024]{0,1:T(8,128)(2,1)S(1)} %get-tuple-element.103) | copy-start | bytes 10223620
  183.4 7.7 copy-start.10
  207.6 1.0 copy-start.11
  237.9 5.0 copy-start.3
  250.7 4.6 copy-start.2
  253.5 49.1 %collective-permute-start.13 = (f32[2,128,2048]{2,1,0:T(8,128)S(1)}, f32[2,128,2048]{2,1,0:T(8,128)S(1)}, u32[]{:S(2)}, u32[]{:S(2)}) collective-permute-start(f32[2,128,2048]{2,1,0:T(8,128)S(1)} %bitcast.93), channel_id=1, source_target_pairs={{0,64},{4,68},{8,72},{12,76},{16,80},{20,84},{24,88},{28,92},{32,9... | collective-permute-start | bytes 6291464 | tf_op jit(solution)/shard_map/ppermute | solution.py:144
  303.0 15.7 %collective-permute-start.14 = (f32[1,128,2048]{2,1,0:T(8,128)S(1)}, f32[1,128,2048]{2,1,0:T(8,128)S(1)}, u32[]{:S(2)}, u32[]{:S(2)}) collective-permute-start(f32[1,128,2048]{2,1,0:T(8,128)S(1)} %slice_select_fusion), channel_id=1, source_target_pairs={{0,32},{4,36},{8,40},{12,44},{16,48},{20,52},{24,56},{28,60},{32,0... | collective-permute-start | bytes 3145736 | tf_op jit(solution)/shard_map/ppermute | solution.py:144
  318.9 15.1 %collective-permute-start.15 = (f32[128,2048]{1,0:T(8,128)S(1)}, f32[128,2048]{1,0:T(8,128)S(1)}, u32[]{:S(2)}, u32[]{:S(2)}) collective-permute-start(f32[128,2048]{1,0:T(8,128)S(1)} %add_bitcast_fusion), channel_id=1, source_target_pairs={{16,0},{20,4},{24,8},{28,12},{0,16},{4,20},{8,24},{12,28},{48,32},... | collective-permute-start | bytes 3145736 | tf_op jit(solution)/shard_map/ppermute | solution.py:150
  334.2 176.5 %collective-permute-start.16 = (f32[128,2048]{1,0:T(8,128)S(1)}, f32[128,2048]{1,0:T(8,128)}, u32[]{:S(2)}, u32[]{:S(2)}) collective-permute-start(f32[128,2048]{1,0:T(8,128)S(1)} %add_select_fusion.2), channel_id=1, source_target_pairs={{8,0},{12,4},{16,8},{20,12},{24,16},{28,20},{0,24},{4,28},{40,32},... | collective-permute-start | bytes 3145736 | tf_op jit(solution)/shard_map/ppermute | solution.py:150
  485.6 165.6 %collective-permute-start.12 = (f32[256,2048]{1,0:T(8,128)}, f32[256,2048]{1,0:T(8,128)}, u32[]{:S(2)}, u32[]{:S(2)}) collective-permute-start(f32[256,2048]{1,0:T(8,128)} %get-tuple-element.102), channel_id=1, source_target_pairs={{4,0},{8,4},{12,8},{16,12},{20,16},{24,20},{28,24},{32,28},{36,32}... | collective-permute-start | bytes 6291464 | tf_op jit(solution)/shard_map/ppermute | solution.py:15
  487.5 24.9 %slice-start = ((s8[6815744]{0:T(1024)(128)(4,1)}), s8[4194304]{0:T(1024)(128)(4,1)S(1)}, s32[]{:S(2)}) async-start(s8[6815744]{0:T(1024)(128)(4,1)} %bitcast.78), calls=%async_computation.2 | async-start | bytes 8388608
  487.5 24.9 %slice-start.1 = ((s8[6815744]{0:T(1024)(128)(4,1)}), s8[2621440]{0:T(1024)(128)(4,1)S(1)}, s32[]{:S(2)}) async-start(s8[6815744]{0:T(1024)(128)(4,1)} %bitcast.78), calls=%async_computation.3 | async-start | bytes 5242880
  487.5 24.9 %copy-start.5 = (bf16[1664,1024]{0,1:T(8,128)(2,1)S(1)}, bf16[1664,1024]{0,1:T(8,128)(2,1)}, u32[]{:S(2)}) copy-start(bf16[1664,1024]{0,1:T(8,128)(2,1)} %copy-done.4) | copy-start | bytes 10223620
  487.5 163.6 %collective-permute-start.11 = (f32[256,2048]{1,0:T(8,128)}, f32[256,2048]{1,0:T(8,128)}, u32[]{:S(2)}, u32[]{:S(2)}) collective-permute-start(f32[256,2048]{1,0:T(8,128)} %get-tuple-element.101), channel_id=1, source_target_pairs={{8,0},{12,4},{16,8},{20,12},{24,16},{28,20},{32,24},{36,28},{40,32... | collective-permute-start | bytes 6291464 | tf_op jit(solution)/shard_map/ppermute | solution.py:15
  491.8 155.2 %collective-permute-start.9 = (f32[128,2048]{1,0:T(8,128)S(1)}, f32[128,2048]{1,0:T(8,128)}, u32[]{:S(2)}, u32[]{:S(2)}) collective-permute-start(f32[128,2048]{1,0:T(8,128)S(1)} %fusion.12), channel_id=1, source_target_pairs={{16,0},{20,4},{24,8},{28,12},{32,16},{36,20},{40,24},{44,28},{48,3... | collective-permute-start | bytes 3145736 | tf_op jit(solution)/shard_map/ppermute | solution.py:15
  495.5 301.9 %collective-permute-start.10 = (f32[256,2048]{1,0:T(8,128)}, f32[256,2048]{1,0:T(8,128)}, u32[]{:S(2)}, u32[]{:S(2)}) collective-permute-start(f32[256,2048]{1,0:T(8,128)} %get-tuple-element.100), channel_id=1, source_target_pairs={{12,0},{16,4},{20,8},{24,12},{28,16},{32,20},{36,24},{40,28},{44,3... | collective-permute-start | bytes 6291464 | tf_op jit(solution)/shard_map/ppermute | solution.py:15
  512.1 137.6 %collective-permute-start.17 = (f32[128,2048]{1,0:T(8,128)S(1)}, f32[128,2048]{1,0:T(8,128)}, u32[]{:S(2)}, u32[]{:S(2)}) collective-permute-start(f32[128,2048]{1,0:T(8,128)S(1)} %add_select_fusion.1), channel_id=1, source_target_pairs={{4,0},{8,4},{12,8},{16,12},{20,16},{24,20},{28,24},{0,28},{36,32},... | collective-permute-start | bytes 3145736 | tf_op jit(solution)/shard_map/ppermute | solution.py:150
  649.6 155.4 %copy-start.1 = (bf16[256,4096]{1,0:T(8,128)(2,1)S(1)}, bf16[256,4096]{1,0:T(8,128)(2,1)}, u32[]{:S(2)}) copy-start(bf16[256,4096]{1,0:T(8,128)(2,1)} %param.23) | copy-start | bytes 6291460
Sparse Core Ops, SparseCore 0:
  207.8 257.2 reduce-scatter.1

commit v3 on v2

--- a/solution.py
+++ b/solution.py
@@ -141,13 +141,13 @@
         keep = jnp.where(upper, part[half:], part[:half])
         send = jnp.where(upper, part[:half], part[half:])
         route = [(d, d ^ (span * group)) for d in range(seq_size)]
-        part = keep + lax.ppermute(send, "seq", route)
+        part = keep + lax.ppermute(send.astype(jnp.bfloat16), "seq", route).astype(jnp.float32)
         span //= 2
     part = part[0]
     hop = group // 2
     while hop >= 1:
         route = [(g * group + (r + hop) % group, g * group + r) for g in range(groups) for r in range(group)]
-        moved = lax.ppermute(part, "seq", route)
+        moved = lax.ppermute(part.astype(jnp.bfloat16), "seq", route).astype(jnp.float32)
         part = jnp.where(rel < hop, part + moved, part)
         hop //= 2
     own_local = jnp.arange(blocks_dev, dtype=jnp.int32)
@@ -158,7 +158,9 @@
     pool_start = 0
     for distance in range(reach_back, 0, -1):
         rows_needed = span_blocks[distance - 1] * BLK
-        back = passed_along(grad_kv[pool_start : pool_start + rows_needed], "seq", -distance)
+        back = passed_along(
+            grad_kv[pool_start : pool_start + rows_needed].astype(jnp.bfloat16), "seq", -distance
+        ).astype(jnp.float32)
         own_grad = own_grad.at[tok_dev - rows_needed :].add(back)
         pool_start = pool_start + rows_needed
     total = own_grad.reshape(blocks_dev, BLK, 2 * width) + far_add

time: 815 us -> 612 us (0.75)
  waiting for transfers between devices: 456 us -> 259 us
  starting transfers between devices: 193 us -> 183 us
    ppermute x8, waiting for transfers between devices: 279 us -> 131 us  [passed_along(): return lax.ppermute(block, axis, route)]
    ppermute x5, waiting for transfers between devices: 83 us -> 32.8 us  [the longest x2 30.3 us: local(): lax.ppermute(send.astype(jnp.bfloat16), 'seq', route).astype(jnp.float32)]
    ppermute x5, starting transfers between devices: 155 us -> 146 us  [the longest x3 144 us: local(): lax.ppermute(part.astype(jnp.bfloat16), 'seq', route).astype(jnp.float32)]
  transfers between devices with their start and end apart: 19 -> 19, of which waited for: 11 -> 11; matrix products, arithmetic and copies ran while one was open for 11% -> 16% of each run, Pallas kernels for 0% -> 0%
where the time goes in v3:
time: 612 us; the launch traced here: 609 us
  waiting for transfers between devices  259 us (42%)
  starting transfers between devices  183 us (30%)
  matrix products  58 us (9%)
  local copies, waits for them, and re-layouts  53.7 us (9%)
  other arithmetic  39.6 us (6%)
  between operations  16.6 us (3%)
    ppermute x3, starting transfers between devices, local(): lax.ppermute(part.astype(jnp.bfloat16), 'seq', route).astype(jnp.float32)  144 us
    ppermute x8, waiting for transfers between devices, passed_along(): return lax.ppermute(block, axis, route)  131 us
    ppermute x3, waiting for transfers between devices, local(): moved = lax.ppermute(held, 'seq', route)  78.6 us
    ppermute x2, waiting for transfers between devices, local(): lax.ppermute(send.astype(jnp.bfloat16), 'seq', route).astype(jnp.float32)  30.3 us
    ppermute x8, starting transfers between devices, passed_along(): return lax.ppermute(block, axis, route)  26.2 us
    ppermute x2, waiting for transfers between devices, local(): moved = lax.ppermute(gathered, 'seq', route)  15.6 us
    unnamed x51, local copies, waits for them, and re-layouts  15.5 us
  transfers between devices with their start and end apart: 19, of which 11 were waited for; matrix products, arithmetic and copies ran while one was open for 16% of the time, Pallas kernels for 0%

profile of v3, /device:TPU:40, one launch (start us, length us, event | category | flops | bytes accessed | tf_op | source)
XLA Modules:
  0.0 609.4 jit_solution(7648803409838081880)
XLA Ops:
  10.9 2.8 collective-permute-start.1
  13.8 4.5 collective-permute-start.2
  18.3 3.8 collective-permute-start.3
  22.9 3.8 collective-permute-start
  26.7 2.3 copy.95
  31.6 1.9 dynamic-slice_bitcast_fusion
  34.2 41.7 %collective-permute-done.4 = bf16[128,2048]{1,0:T(8,128)(2,1)} collective-permute-done((bf16[128,2048]{1,0:T(8,128)(2,1)}, bf16[128,2048]{1,0:T(8,128)(2,1)}, u32[]{:S(2)}, u32[]{:S(2)}) %collective-permute-start.4) | collective-permute-done | bytes 524320 | tf_op jit(solution)/shard_map/ppermute | solution.py:66
  77.1 6.5 %convolution_convert_fusion.2 = bf16[256,1024]{1,0:T(8,128)(2,1)} fusion(bf16[256,4096]{1,0:T(8,128)(2,1)S(1)} %copy-done, bf16[4096,1024]{1,0:T(8,128)(2,1)} %param.24), kind=kOutput, calls=%fused_computation.32 | convolution fusion | flops 2147745792 | bytes 11010048 | tf_op jit(solution)/shard_map/dot_general | solution.py:41
  83.7 23.8 %collective-permute-done.5 = bf16[128,2048]{1,0:T(8,128)(2,1)S(1)} collective-permute-done((bf16[128,2048]{1,0:T(8,128)(2,1)S(1)}, bf16[128,2048]{1,0:T(8,128)(2,1)S(1)}, u32[]{:S(2)}, u32[]{:S(2)}) %collective-permute-start.5) | collective-permute-done | bytes 524320 | tf_op jit(solution)/shard_map/ppermute | solution.py:66
  107.8 13.1 %collective-permute-done.6 = bf16[128,2048]{1,0:T(8,128)(2,1)S(1)} collective-permute-done((bf16[128,2048]{1,0:T(8,128)(2,1)S(1)}, bf16[128,2048]{1,0:T(8,128)(2,1)S(1)}, u32[]{:S(2)}, u32[]{:S(2)}) %collective-permute-start.6) | collective-permute-done | bytes 524320 | tf_op jit(solution)/shard_map/ppermute | solution.py:66
  121.7 7.4 %collective-permute-start.7 = (bf16[1,128,2048]{2,1,0:T(8,128)(2,1)}, bf16[1,128,2048]{2,1,0:T(8,128)(2,1)}, u32[]{:S(2)}, u32[]{:S(2)}) collective-permute-start(bf16[1,128,2048]{2,1,0:T(8,128)(2,1)} %select_bitcast_fusion), channel_id=1, source_target_pairs={{0,32},{4,36},{8,40},{12,44},{16,48},{20,52},{24,56},{28,60},{32,0... | collective-permute-start | bytes 1572872 | tf_op jit(solution)/shard_map/ppermute | solution.py:73
  129.6 2.0 copy.123
  131.7 2.0 copy.124
  134.6 3.5 collective-permute-done.7
  138.2 1.7 maximum_select_fusion.1
  139.9 3.6 collective-permute-start.8
  148.7 2.8 copy-done.6
  151.4 12.1 %collective-permute-done.8 = bf16[2,128,2048]{2,1,0:T(8,128)(2,1)S(1)} collective-permute-done((bf16[2,128,2048]{2,1,0:T(8,128)(2,1)S(1)}, bf16[2,128,2048]{2,1,0:T(8,128)(2,1)S(1)}, u32[]{:S(2)}, u32[]{:S(2)}) %collective-permute-start.8) | collective-permute-done | bytes 1048608 | tf_op jit(solution)/shard_map/ppermute | solution.py:73
  165.2 4.0 copy.96
  169.2 3.1 constant_dynamic-update-slice_fusion
  172.3 3.6 fusion.19
  175.9 7.5 %fusion.2 = (f32[8,256]{1,0:T(8,128)S(1)}, f32[8,1664,256]{2,1,0:T(8,128)}) fusion(pred[256,1664]{0,1:T(8,128)(4,1)S(1)} %copy-done.7, bf16[1664,8,128]{0,2,1:T(8,128)(2,1)S(1)} %bitcast.89, bf16[256,8,128]{0,2,1:T(8,128)(2,1)S(1)} %bitcast.95), kind=kOutput, calls=%fused_computation.15 | convolution fusion | flops 882636800 | bytes 17997824 | tf_op jit(solution)/shard_map/qhd,khd->hqk/dot_general | solution.py:109
  183.4 7.7 %exponential_reduce_fusion = f32[8,256]{1,0:T(8,128)S(1)} fusion(f32[8,1664,256]{2,1,0:T(8,128)} %get-tuple-element.108, f32[8,256]{1,0:T(8,128)S(1)} %get-tuple-element.107, pred[256,1664]{0,1:T(8,128)(4,1)S(1)} %copy-done.7), kind=kLoop, calls=%fused_computation.13 | loop fusion | flops 13629440 | bytes 14073856 | tf_op jit(solution)/shard_map/reduce_sum | solution.py:114
  191.1 8.4 %multiply_reduce_fusion = (f32[256,8]{0,1:T(8,128)S(1)}, bf16[8,128,256]{2,1,0:T(8,128)(2,1)S(1)}) fusion(bf16[256,1024]{0,1:T(8,128)(2,1)S(1)} %copy-done.12, bf16[1664,8,128]{0,2,1:T(8,128)(2,1)S(1)} %bitcast.99, f32[8,1664,256]{2,1,0:T(8,128)} %get-tuple-element.108, f32[8,256]{1,0:T(8,128)S(1)} %log_add_fusion, pred[256,1664]{0,1:T(8,128)(4,1)S(1)} %copy-done.7), kind=kOutput, calls=%fused_computation.44 | convolution fusion | flops 887355392 | bytes 18530304 | tf_op jit(solution)/shard_map/hqk,khd->qhd/dot_general | solution.py:117
  199.5 8.1 %convolution_bitcast_fusion = f32[4096,1024]{0,1:T(8,128)} fusion(bf16[256,1024]{0,1:T(8,128)(2,1)S(1)} %bitcast.105, bf16[256,4096]{1,0:T(8,128)(2,1)S(1)} %copy-done), kind=kOutput, calls=%fused_computation.16 | convolution fusion | flops 2147483648 | bytes 19398656 | tf_op jit(solution)/shard_map/dot_general | solution.py:170
  208.7 11.4 %fusion.15 = f32[8,128,1664]{2,1,0:T(8,128)} fusion(bf16[256,8,128]{0,2,1:T(8,128)(2,1)S(1)} %bitcast.102, f32[8,1664,256]{2,1,0:T(8,128)} %get-tuple-element.108, f32[8,256]{1,0:T(8,128)S(1)} %log_add_fusion, pred[256,1664]{0,1:T(8,128)(4,1)S(1)} %copy-done.7), kind=kOutput, calls=%fused_computation.80 | convolution fusion | flops 886046720 | bytes 21405696 | tf_op jit(solution)/shard_map/hqk,qhd->khd/dot_general | solution.py:129
  220.0 7.9 %copy.113 = f32[1664,1024]{1,0:T(8,128)} copy(f32[1664,1024]{0,1:T(8,128)} %bitcast.92) | data formatting | bytes 13631488 | tf_op jit(solution)/shard_map/reshape | solution.py:133
  227.9 9.9 %multiply_convert_fusion = bf16[8,256,1664]{1,2,0:T(8,128)(2,1)S(1)} fusion(f32[8,1664,256]{2,1,0:T(8,128)} %get-tuple-element.108, f32[8,256]{1,0:T(8,128)S(1)} %bitcast.108, f32[8,256]{1,0:T(8,128)S(1)} %log_add_fusion, pred[256,1664]{0,1:T(8,128)(4,1)S(1)} %copy-done.7, bf16[256,8,128]{0,2,1:T(8,128)(2,1)S(1)} %bitcast.103, ...), kind=kOutput, calls=%fused_computation.11 | convolution fusion | flops 896270336 | bytes 24821760 | tf_op jit(solution)/shard_map/qhd,khd->hqk/dot_general | solution.py:123
  237.9 5.0 fusion.21
  242.9 7.7 %copy.112 = f32[1664,1024]{1,0:T(8,128)} copy(f32[1664,1024]{0,1:T(8,128)} %bitcast.91) | data formatting | bytes 13631488 | tf_op jit(solution)/shard_map/reshape | solution.py:133
  250.6 2.6 select_convert_fusion
  253.3 1.8 collective-permute-start.13
  255.0 3.8 broadcast_select_fusion
  258.8 21.1 %collective-permute-done.13 = bf16[2,128,2048]{2,1,0:T(8,128)(2,1)S(1)} collective-permute-done((bf16[2,128,2048]{2,1,0:T(8,128)(2,1)S(1)}, bf16[2,128,2048]{2,1,0:T(8,128)(2,1)S(1)}, u32[]{:S(2)}, u32[]{:S(2)}) %collective-permute-start.13) | collective-permute-done | bytes 1048608 | tf_op jit(solution)/shard_map/ppermute | solution.py:144
  280.5 9.2 %collective-permute-done.14 = bf16[1,128,2048]{2,1,0:T(8,128)(2,1)} collective-permute-done((bf16[1,128,2048]{2,1,0:T(8,128)(2,1)S(1)}, bf16[1,128,2048]{2,1,0:T(8,128)(2,1)}, u32[]{:S(2)}, u32[]{:S(2)}) %collective-permute-start.14) | collective-permute-done | bytes 524320 | tf_op jit(solution)/shard_map/ppermute | solution.py:144
  292.1 6.3 %fusion = bf16[1664,2048]{1,0:T(8,128)(2,1)S(1)} fusion(f32[1664,1024]{1,0:T(8,128)} %copy.113, f32[1664,1024]{1,0:T(8,128)} %copy.112), kind=kLoop, calls=%fused_computation.9 | loop fusion | flops 13631488 | bytes 20447232 | tf_op jit(solution)/shard_map/convert.3
  300.3 140.7 %collective-permute-start.16 = (bf16[128,2048]{1,0:T(8,128)(2,1)S(1)}, bf16[128,2048]{1,0:T(8,128)(2,1)S(1)}, u32[]{:S(2)}, u32[]{:S(2)}) collective-permute-start(bf16[128,2048]{1,0:T(8,128)(2,1)S(1)} %fusion.11), channel_id=1, source_target_pairs={{8,0},{12,4},{16,8},{20,12},{24,16},{28,20},{0,24},{4,28},{40,32},... | collective-permute-start | bytes 1572872 | tf_op jit(solution)/shard_map/ppermute | solution.py:150
  441.0 1.8 fusion.18
  442.7 1.9 collective-permute-start.12
  444.7 1.9 collective-permute-start.11
  446.6 4.0 collective-permute-start.9
  450.6 3.4 collective-permute-start.10
  455.9 1.8 collective-permute-start.17
  459.9 65.8 %collective-permute-done.9 = bf16[128,2048]{1,0:T(8,128)(2,1)S(1)} collective-permute-done((bf16[128,2048]{1,0:T(8,128)(2,1)S(1)}, bf16[128,2048]{1,0:T(8,128)(2,1)S(1)}, u32[]{:S(2)}, u32[]{:S(2)}) %collective-permute-start.9) | collective-permute-done | bytes 524320 | tf_op jit(solution)/shard_map/ppermute | solution.py:15
  526.5 2.6 fusion.10
  530.5 65.6 %collective-permute-done.10 = bf16[256,2048]{1,0:T(8,128)(2,1)} collective-permute-done((bf16[256,2048]{1,0:T(8,128)(2,1)}, bf16[256,2048]{1,0:T(8,128)(2,1)}, u32[]{:S(2)}, u32[]{:S(2)}) %collective-permute-start.10) | collective-permute-done | bytes 1048608 | tf_op jit(solution)/shard_map/ppermute | solution.py:15
  596.2 3.3 fusion.7
  600.5 2.0 copy.115
  (104 shorter events, 29.5 us)
Async XLA Ops:
  7.2 70.0 %copy-start = (bf16[256,4096]{1,0:T(8,128)(2,1)S(1)}, bf16[256,4096]{1,0:T(8,128)(2,1)}, u32[]{:S(2)}) copy-start(bf16[256,4096]{1,0:T(8,128)(2,1)} %param.23) | copy-start | bytes 6291460
  7.2 21.8 %copy-start.17 = (s32[64,12]{0,1:T(8,128)S(1)}, s32[64,12]{0,1:T(8,128)}, u32[]{:S(2)}) copy-start(s32[64,12]{0,1:T(8,128)} %param.25) | copy-start | bytes 9220
  7.2 593.3 %reduce-scatter.2.cloned.1.call-start = ((), (), s32[]{:S(2)}) async-start(), calls=%async_computation.1 | async-start | bytes 17301504 | tf_op jit(solution)/shard_map/reduce_scatter | solution.py:169
  10.9 133.7 %collective-permute-start.1 = (bf16[256,2048]{0,1:T(8,128)(2,1)}, bf16[256,2048]{0,1:T(8,128)(2,1)}, u32[]{:S(2)}, u32[]{:S(2)}) collective-permute-start(bf16[256,2048]{0,1:T(8,128)(2,1)} %pad_maximum_fusion.1), channel_id=1, source_target_pairs={{0,12},{4,16},{8,20},{12,24},{16,28},{20,32},{24,36},{28,40},{32,4... | collective-permute-start | bytes 3145736 | tf_op jit(solution)/shard_map/ppermute | solution.py:15
  13.8 132.2 %collective-permute-start.2 = (bf16[256,2048]{0,1:T(8,128)(2,1)}, bf16[256,2048]{0,1:T(8,128)(2,1)}, u32[]{:S(2)}, u32[]{:S(2)}) collective-permute-start(bf16[256,2048]{0,1:T(8,128)(2,1)} %pad_maximum_fusion.1), channel_id=1, source_target_pairs={{0,8},{4,12},{8,16},{12,20},{16,24},{20,28},{24,32},{28,36},{32,40... | collective-permute-start | bytes 3145736 | tf_op jit(solution)/shard_map/ppermute | solution.py:15
  18.3 129.0 %collective-permute-start.3 = (bf16[256,2048]{0,1:T(8,128)(2,1)}, bf16[256,2048]{0,1:T(8,128)(2,1)}, u32[]{:S(2)}, u32[]{:S(2)}) collective-permute-start(bf16[256,2048]{0,1:T(8,128)(2,1)} %pad_maximum_fusion.1), channel_id=1, source_target_pairs={{0,4},{4,8},{8,12},{12,16},{16,20},{20,24},{24,28},{28,32},{32,36}... | collective-permute-start | bytes 3145736 | tf_op jit(solution)/shard_map/ppermute | solution.py:15
  22.9 120.6 %collective-permute-start = (bf16[128,2048]{0,1:T(8,128)(2,1)}, bf16[128,2048]{0,1:T(8,128)(2,1)}, u32[]{:S(2)}, u32[]{:S(2)}) collective-permute-start(bf16[128,2048]{0,1:T(8,128)(2,1)} %fusion.12), channel_id=1, source_target_pairs={{0,16},{4,20},{8,24},{12,28},{16,32},{20,36},{24,40},{28,44},{32,4... | collective-permute-start | bytes 1572872 | tf_op jit(solution)/shard_map/ppermute | solution.py:15
  33.5 42.5 %collective-permute-start.4 = (bf16[128,2048]{1,0:T(8,128)(2,1)}, bf16[128,2048]{1,0:T(8,128)(2,1)}, u32[]{:S(2)}, u32[]{:S(2)}) collective-permute-start(bf16[128,2048]{1,0:T(8,128)(2,1)} %dynamic-slice_bitcast_fusion), channel_id=1, source_target_pairs={{28,0},{0,4},{4,8},{8,12},{12,16},{16,20},{20,24},{24,28},{60,32},... | collective-permute-start | bytes 1572872 | tf_op jit(solution)/shard_map/ppermute | solution.py:66
  77.1 30.4 %collective-permute-start.5 = (bf16[128,2048]{1,0:T(8,128)(2,1)S(1)}, bf16[128,2048]{1,0:T(8,128)(2,1)S(1)}, u32[]{:S(2)}, u32[]{:S(2)}) collective-permute-start(bf16[128,2048]{1,0:T(8,128)(2,1)S(1)} %broadcast_select_fusion.1), channel_id=1, source_target_pairs={{24,0},{28,4},{0,8},{4,12},{8,16},{12,20},{16,24},{20,28},{56,32},... | collective-permute-start | bytes 1572872 | tf_op jit(solution)/shard_map/ppermute | solution.py:66
  107.5 13.4 %collective-permute-start.6 = (bf16[128,2048]{1,0:T(8,128)(2,1)S(1)}, bf16[128,2048]{1,0:T(8,128)(2,1)S(1)}, u32[]{:S(2)}, u32[]{:S(2)}) collective-permute-start(bf16[128,2048]{1,0:T(8,128)(2,1)S(1)} %broadcast_select_fusion.2), channel_id=1, source_target_pairs={{16,0},{20,4},{24,8},{28,12},{0,16},{4,20},{8,24},{12,28},{48,32},... | collective-permute-start | bytes 1572872 | tf_op jit(solution)/shard_map/ppermute | solution.py:66
  121.7 16.4 %collective-permute-start.7 = (bf16[1,128,2048]{2,1,0:T(8,128)(2,1)}, bf16[1,128,2048]{2,1,0:T(8,128)(2,1)}, u32[]{:S(2)}, u32[]{:S(2)}) collective-permute-start(bf16[1,128,2048]{2,1,0:T(8,128)(2,1)} %select_bitcast_fusion), channel_id=1, source_target_pairs={{0,32},{4,36},{8,40},{12,44},{16,48},{20,52},{24,56},{28,60},{32,0... | collective-permute-start | bytes 1572872 | tf_op jit(solution)/shard_map/ppermute | solution.py:73
  139.9 23.7 %collective-permute-start.8 = (bf16[2,128,2048]{2,1,0:T(8,128)(2,1)S(1)}, bf16[2,128,2048]{2,1,0:T(8,128)(2,1)S(1)}, u32[]{:S(2)}, u32[]{:S(2)}) collective-permute-start(bf16[2,128,2048]{2,1,0:T(8,128)(2,1)S(1)} %maximum_select_fusion.1), channel_id=1, source_target_pairs={{0,64},{4,68},{8,72},{12,76},{16,80},{20,84},{24,88},{28,92},{32,9... | collective-permute-start | bytes 3145736 | tf_op jit(solution)/shard_map/ppermute | solution.py:73
  148.6 2.8 copy-start.6
  172.2 3.6 copy-start.7
  172.3 3.6 copy-start.8
  175.8 7.5 %copy-start.4 = (bf16[1664,1024]{0,1:T(8,128)(2,1)}, bf16[1664,1024]{0,1:T(8,128)(2,1)S(1)}, u32[]{:S(2)}) copy-start(bf16[1664,1024]{0,1:T(8,128)(2,1)S(1)} %get-tuple-element.104) | copy-start | bytes 10223620
  175.8 15.2 %copy-start.11 = (bf16[1664,1024]{0,1:T(8,128)(2,1)}, bf16[1664,1024]{0,1:T(8,128)(2,1)S(1)}, u32[]{:S(2)}) copy-start(bf16[1664,1024]{0,1:T(8,128)(2,1)S(1)} %get-tuple-element.103) | copy-start | bytes 10223620
  183.3 7.7 %copy-start.12 = (bf16[256,1024]{0,1:T(8,128)(2,1)S(1)}, bf16[256,1024]{0,1:T(8,128)(2,1)}, u32[]{:S(2)}) copy-start(bf16[256,1024]{0,1:T(8,128)(2,1)} %copy.124) | copy-start | bytes 1572868
  207.6 1.0 copy-start.13
  237.9 5.0 copy-start.3
  250.6 4.4 copy-start.2
  253.3 26.6 %collective-permute-start.13 = (bf16[2,128,2048]{2,1,0:T(8,128)(2,1)S(1)}, bf16[2,128,2048]{2,1,0:T(8,128)(2,1)S(1)}, u32[]{:S(2)}, u32[]{:S(2)}) collective-permute-start(bf16[2,128,2048]{2,1,0:T(8,128)(2,1)S(1)} %bitcast.104), channel_id=1, source_target_pairs={{0,64},{4,68},{8,72},{12,76},{16,80},{20,84},{24,88},{28,92},{32,9... | collective-permute-start | bytes 3145736 | tf_op jit(solution)/shard_map/ppermute | solution.py:144
  280.3 9.4 %collective-permute-start.14 = (bf16[1,128,2048]{2,1,0:T(8,128)(2,1)S(1)}, bf16[1,128,2048]{2,1,0:T(8,128)(2,1)}, u32[]{:S(2)}, u32[]{:S(2)}) collective-permute-start(bf16[1,128,2048]{2,1,0:T(8,128)(2,1)S(1)} %select_convert_fusion.1), channel_id=1, source_target_pairs={{0,32},{4,36},{8,40},{12,44},{16,48},{20,52},{24,56},{28,60},{32,0... | collective-permute-start | bytes 1572872 | tf_op jit(solution)/shard_map/ppermute | solution.py:144
  290.9 166.9 %slice-start = ((s8[6815744]{0:T(1024)(128)(4,1)}), s8[4194304]{0:T(1024)(128)(4,1)S(1)}, s32[]{:S(2)}) async-start(s8[6815744]{0:T(1024)(128)(4,1)} %bitcast.87), calls=%async_computation.2 | async-start | bytes 8388608
  290.9 166.9 %slice-start.1 = ((s8[6815744]{0:T(1024)(128)(4,1)}), s8[2621440]{0:T(1024)(128)(4,1)S(1)}, s32[]{:S(2)}) async-start(s8[6815744]{0:T(1024)(128)(4,1)} %bitcast.87), calls=%async_computation.3 | async-start | bytes 5242880
  290.9 9.3 %collective-permute-start.15 = (bf16[128,2048]{1,0:T(8,128)(2,1)S(1)}, bf16[128,2048]{1,0:T(8,128)(2,1)S(1)}, u32[]{:S(2)}, u32[]{:S(2)}) collective-permute-start(bf16[128,2048]{1,0:T(8,128)(2,1)S(1)} %get-tuple-element.96), channel_id=1, source_target_pairs={{16,0},{20,4},{24,8},{28,12},{0,16},{4,20},{8,24},{12,28},{48,32},... | collective-permute-start | bytes 1572872 | tf_op jit(solution)/shard_map/ppermute | solution.py:150
  298.4 159.3 %copy-start.5 = (bf16[1664,1024]{0,1:T(8,128)(2,1)S(1)}, bf16[1664,1024]{0,1:T(8,128)(2,1)}, u32[]{:S(2)}) copy-start(bf16[1664,1024]{0,1:T(8,128)(2,1)} %copy-done.4) | copy-start | bytes 10223620
  300.2 154.7 %copy-start.9 = (bf16[128,2048]{1,0:T(8,128)(2,1)}, bf16[128,2048]{1,0:T(8,128)(2,1)S(1)}, u32[]{:S(2)}) copy-start(bf16[128,2048]{1,0:T(8,128)(2,1)S(1)} %collective-permute-done.15) | copy-start | bytes 1572868
  300.3 154.6 %collective-permute-start.16 = (bf16[128,2048]{1,0:T(8,128)(2,1)S(1)}, bf16[128,2048]{1,0:T(8,128)(2,1)S(1)}, u32[]{:S(2)}, u32[]{:S(2)}) collective-permute-start(bf16[128,2048]{1,0:T(8,128)(2,1)S(1)} %fusion.11), channel_id=1, source_target_pairs={{8,0},{12,4},{16,8},{20,12},{24,16},{28,20},{0,24},{4,28},{40,32},... | collective-permute-start | bytes 1572872 | tf_op jit(solution)/shard_map/ppermute | solution.py:150
  442.7 87.8 %collective-permute-start.12 = (bf16[256,2048]{1,0:T(8,128)(2,1)}, bf16[256,2048]{1,0:T(8,128)(2,1)}, u32[]{:S(2)}, u32[]{:S(2)}) collective-permute-start(bf16[256,2048]{1,0:T(8,128)(2,1)} %get-tuple-element.101), channel_id=1, source_target_pairs={{4,0},{8,4},{12,8},{16,12},{20,16},{24,20},{28,24},{32,28},{36,32}... | collective-permute-start | bytes 3145736 | tf_op jit(solution)/shard_map/ppermute | solution.py:15
  444.7 85.9 %collective-permute-start.11 = (bf16[256,2048]{1,0:T(8,128)(2,1)}, bf16[256,2048]{1,0:T(8,128)(2,1)}, u32[]{:S(2)}, u32[]{:S(2)}) collective-permute-start(bf16[256,2048]{1,0:T(8,128)(2,1)} %get-tuple-element.102), channel_id=1, source_target_pairs={{8,0},{12,4},{16,8},{20,12},{24,16},{28,20},{32,24},{36,28},{40,32... | collective-permute-start | bytes 3145736 | tf_op jit(solution)/shard_map/ppermute | solution.py:15
  446.6 79.1 %collective-permute-start.9 = (bf16[128,2048]{1,0:T(8,128)(2,1)S(1)}, bf16[128,2048]{1,0:T(8,128)(2,1)S(1)}, u32[]{:S(2)}, u32[]{:S(2)}) collective-permute-start(bf16[128,2048]{1,0:T(8,128)(2,1)S(1)} %slice.144), channel_id=1, source_target_pairs={{16,0},{20,4},{24,8},{28,12},{32,16},{36,20},{40,24},{44,28},{48,3... | collective-permute-start | bytes 1572872 | tf_op jit(solution)/shard_map/ppermute | solution.py:15
  450.6 145.5 %collective-permute-start.10 = (bf16[256,2048]{1,0:T(8,128)(2,1)}, bf16[256,2048]{1,0:T(8,128)(2,1)}, u32[]{:S(2)}, u32[]{:S(2)}) collective-permute-start(bf16[256,2048]{1,0:T(8,128)(2,1)} %get-tuple-element.100), channel_id=1, source_target_pairs={{12,0},{16,4},{20,8},{24,12},{28,16},{32,20},{36,24},{40,28},{44,3... | collective-permute-start | bytes 3145736 | tf_op jit(solution)/shard_map/ppermute | solution.py:15
  454.9 1.0 copy-start.14
  455.9 73.2 %collective-permute-start.17 = (bf16[128,2048]{1,0:T(8,128)(2,1)}, bf16[128,2048]{1,0:T(8,128)(2,1)}, u32[]{:S(2)}, u32[]{:S(2)}) collective-permute-start(bf16[128,2048]{1,0:T(8,128)(2,1)} %fusion.13), channel_id=1, source_target_pairs={{4,0},{8,4},{12,8},{16,12},{20,16},{24,20},{28,24},{0,28},{36,32},... | collective-permute-start | bytes 1572872 | tf_op jit(solution)/shard_map/ppermute | solution.py:150
  525.7 0.8 copy-start.16
  526.5 2.6 copy-start.10
  526.5 2.6 copy-start.15
  526.5 76.0 %copy-start.1 = (bf16[256,4096]{1,0:T(8,128)(2,1)S(1)}, bf16[256,4096]{1,0:T(8,128)(2,1)}, u32[]{:S(2)}) copy-start(bf16[256,4096]{1,0:T(8,128)(2,1)} %param.23) | copy-start | bytes 6291460
Sparse Core Ops, SparseCore 0:
  207.8 224.3 reduce-scatter.1

commit v4 on v3

--- a/solution.py
+++ b/solution.py
@@ -172,11 +172,11 @@
             attn_out.reshape(tok_dev, width),
             (((0,), (0,)), ((), ())),
             preferred_element_type=jnp.float32,
-        ),
+        ).astype(jnp.bfloat16),
         "seq",
         scatter_dimension=0,
         tiled=True,
-    )
+    ).astype(jnp.float32)
     return (
         query_grad.reshape(tok_dev, width),
         total[:, :width],

time: 612 us -> 523 us (0.85)
  waiting for transfers between devices: 259 us -> 185 us
  starting transfers between devices: 183 us -> 156 us
  local copies, waits for them, and re-layouts: 53.7 us -> 65.6 us
    ppermute x8, waiting for transfers between devices: 131 us -> 59.1 us  [passed_along(): return lax.ppermute(block, axis, route)]
    ppermute x3, starting transfers between devices: 144 us -> 117 us  [local(): lax.ppermute(part.astype(jnp.bfloat16), 'seq', route).astype(jnp.float32)]
    unnamed x51 -> x53, local copies, waits for them, and re-layouts: 15.5 us -> 27.5 us
  transfers between devices with their start and end apart: 19 -> 19, of which waited for: 11 -> 10; matrix products, arithmetic and copies ran while one was open for 16% -> 19% of each run, Pallas kernels for 0% -> 0%
where the time goes in v4:
time: 523 us; the launch traced here: 518 us
  waiting for transfers between devices  185 us (35%)
  starting transfers between devices  156 us (30%)
  local copies, waits for them, and re-layouts  65.6 us (13%)
  matrix products  55.3 us (11%)
  other arithmetic  39.6 us (8%)
  between operations  16.6 us (3%)
    ppermute x3, starting transfers between devices, local(): lax.ppermute(part.astype(jnp.bfloat16), 'seq', route).astype(jnp.float32)  117 us
    ppermute x3, waiting for transfers between devices, local(): moved = lax.ppermute(held, 'seq', route)  78.6 us
    ppermute x8, waiting for transfers between devices, passed_along(): return lax.ppermute(block, axis, route)  59.1 us
    ppermute x2, waiting for transfers between devices, local(): lax.ppermute(send.astype(jnp.bfloat16), 'seq', route).astype(jnp.float32)  30.1 us
    unnamed x53, local copies, waits for them, and re-layouts  27.5 us
    ppermute x8, starting transfers between devices, passed_along(): return lax.ppermute(block, axis, route)  25.9 us
    ppermute x2, waiting for transfers between devices, local(): moved = lax.ppermute(gathered, 'seq', route)  15.6 us
    dot_general x1, matrix products, local(): jnp.einsum('hqk,qhd->khd', probs_low, grad_rows, preferred_element_type=j...  11.1 us
  transfers between devices with their start and end apart: 19, of which 10 were waited for; matrix products, arithmetic and copies ran while one was open for 19% of the time, Pallas kernels for 0%

profile of v4, /device:TPU:40, one launch (start us, length us, event | category | flops | bytes accessed | tf_op | source)
XLA Modules:
  0.0 517.8 jit_solution(1700766964033680099)
XLA Ops:
  10.9 2.8 collective-permute-start.1
  13.8 4.5 collective-permute-start.2
  18.3 3.8 collective-permute-start.3
  22.9 3.8 collective-permute-start
  26.7 2.3 copy.95
  31.6 1.9 dynamic-slice_bitcast_fusion
  34.2 41.7 %collective-permute-done.4 = bf16[128,2048]{1,0:T(8,128)(2,1)} collective-permute-done((bf16[128,2048]{1,0:T(8,128)(2,1)}, bf16[128,2048]{1,0:T(8,128)(2,1)}, u32[]{:S(2)}, u32[]{:S(2)}) %collective-permute-start.4) | collective-permute-done | bytes 524320 | tf_op jit(solution)/shard_map/ppermute | solution.py:66
  77.1 6.5 %convolution_convert_fusion.2 = bf16[256,1024]{1,0:T(8,128)(2,1)} fusion(bf16[256,4096]{1,0:T(8,128)(2,1)S(1)} %copy-done, bf16[4096,1024]{1,0:T(8,128)(2,1)} %param.24), kind=kOutput, calls=%fused_computation.32 | convolution fusion | flops 2147745792 | bytes 11010048 | tf_op jit(solution)/shard_map/dot_general | solution.py:41
  83.7 23.8 %collective-permute-done.5 = bf16[128,2048]{1,0:T(8,128)(2,1)S(1)} collective-permute-done((bf16[128,2048]{1,0:T(8,128)(2,1)S(1)}, bf16[128,2048]{1,0:T(8,128)(2,1)S(1)}, u32[]{:S(2)}, u32[]{:S(2)}) %collective-permute-start.5) | collective-permute-done | bytes 524320 | tf_op jit(solution)/shard_map/ppermute | solution.py:66
  107.8 13.1 %collective-permute-done.6 = bf16[128,2048]{1,0:T(8,128)(2,1)S(1)} collective-permute-done((bf16[128,2048]{1,0:T(8,128)(2,1)S(1)}, bf16[128,2048]{1,0:T(8,128)(2,1)S(1)}, u32[]{:S(2)}, u32[]{:S(2)}) %collective-permute-start.6) | collective-permute-done | bytes 524320 | tf_op jit(solution)/shard_map/ppermute | solution.py:66
  121.7 7.4 %collective-permute-start.7 = (bf16[1,128,2048]{2,1,0:T(8,128)(2,1)}, bf16[1,128,2048]{2,1,0:T(8,128)(2,1)}, u32[]{:S(2)}, u32[]{:S(2)}) collective-permute-start(bf16[1,128,2048]{2,1,0:T(8,128)(2,1)} %select_bitcast_fusion), channel_id=1, source_target_pairs={{0,32},{4,36},{8,40},{12,44},{16,48},{20,52},{24,56},{28,60},{32,0... | collective-permute-start | bytes 1572872 | tf_op jit(solution)/shard_map/ppermute | solution.py:73
  129.6 2.0 copy.125
  131.7 2.0 copy.126
  134.6 3.5 collective-permute-done.7
  138.2 1.7 maximum_select_fusion.1
  139.9 3.6 collective-permute-start.8
  148.6 2.8 copy-done.6
  151.4 12.1 %collective-permute-done.8 = bf16[2,128,2048]{2,1,0:T(8,128)(2,1)S(1)} collective-permute-done((bf16[2,128,2048]{2,1,0:T(8,128)(2,1)S(1)}, bf16[2,128,2048]{2,1,0:T(8,128)(2,1)S(1)}, u32[]{:S(2)}, u32[]{:S(2)}) %collective-permute-start.8) | collective-permute-done | bytes 1048608 | tf_op jit(solution)/shard_map/ppermute | solution.py:73
  165.2 4.0 copy.96
  169.2 3.1 constant_dynamic-update-slice_fusion
  172.3 3.6 fusion.19
  175.9 7.5 %fusion.2 = (f32[8,256]{1,0:T(8,128)S(1)}, f32[8,1664,256]{2,1,0:T(8,128)}) fusion(pred[256,1664]{0,1:T(8,128)(4,1)S(1)} %copy-done.7, bf16[1664,8,128]{0,2,1:T(8,128)(2,1)S(1)} %bitcast.90, bf16[256,8,128]{0,2,1:T(8,128)(2,1)S(1)} %bitcast.96), kind=kOutput, calls=%fused_computation.15 | convolution fusion | flops 882636800 | bytes 17997824 | tf_op jit(solution)/shard_map/qhd,khd->hqk/dot_general | solution.py:109
  183.4 7.7 %exponential_reduce_fusion = f32[8,256]{1,0:T(8,128)S(1)} fusion(f32[8,1664,256]{2,1,0:T(8,128)} %get-tuple-element.108, f32[8,256]{1,0:T(8,128)S(1)} %get-tuple-element.107, pred[256,1664]{0,1:T(8,128)(4,1)S(1)} %copy-done.7), kind=kLoop, calls=%fused_computation.13 | loop fusion | flops 13629440 | bytes 14073856 | tf_op jit(solution)/shard_map/reduce_sum | solution.py:114
  191.1 8.4 %multiply_reduce_fusion = (f32[256,8]{0,1:T(8,128)S(1)}, bf16[8,128,256]{2,1,0:T(8,128)(2,1)S(1)}) fusion(bf16[256,1024]{0,1:T(8,128)(2,1)S(1)} %copy-done.12, bf16[1664,8,128]{0,2,1:T(8,128)(2,1)S(1)} %bitcast.100, f32[8,1664,256]{2,1,0:T(8,128)} %get-tuple-element.108, f32[8,256]{1,0:T(8,128)S(1)} %log_add_fusion, pred[256,1664]{0,1:T(8,128)(4,1)S(1)} %copy-done.7), kind=kOutput, calls=%fused_computation.44 | convolution fusion | flops 887355392 | bytes 18530304 | tf_op jit(solution)/shard_map/hqk,khd->qhd/dot_general | solution.py:117
  199.5 5.7 %convert_bitcast_fusion = bf16[4096,1024]{0,1:T(8,128)(2,1)} fusion(bf16[256,1024]{0,1:T(8,128)(2,1)S(1)} %bitcast.106, bf16[256,4096]{1,0:T(8,128)(2,1)S(1)} %copy-done), kind=kOutput, calls=%fused_computation.16 | convolution fusion | flops 2151677952 | bytes 11010048 | tf_op jit(solution)/shard_map/dot_general | solution.py:170
  205.2 12.0 %copy.123 = bf16[4096,1024]{1,0:T(8,128)(2,1)} copy(bf16[4096,1024]{0,1:T(8,128)(2,1)} %convert_bitcast_fusion) | data formatting | bytes 16777216
  218.2 11.1 %fusion.15 = f32[8,128,1664]{2,1,0:T(8,128)} fusion(bf16[256,8,128]{0,2,1:T(8,128)(2,1)S(1)} %bitcast.103, f32[8,1664,256]{2,1,0:T(8,128)} %get-tuple-element.108, f32[8,256]{1,0:T(8,128)S(1)} %log_add_fusion, pred[256,1664]{0,1:T(8,128)(4,1)S(1)} %copy-done.7), kind=kOutput, calls=%fused_computation.80 | convolution fusion | flops 886046720 | bytes 21405696 | tf_op jit(solution)/shard_map/hqk,qhd->khd/dot_general | solution.py:129
  229.4 7.7 %copy.113 = f32[1664,1024]{1,0:T(8,128)} copy(f32[1664,1024]{0,1:T(8,128)} %bitcast.93) | data formatting | bytes 13631488 | tf_op jit(solution)/shard_map/reshape | solution.py:133
  237.1 9.9 %multiply_convert_fusion = bf16[8,256,1664]{1,2,0:T(8,128)(2,1)S(1)} fusion(f32[8,1664,256]{2,1,0:T(8,128)} %get-tuple-element.108, f32[8,256]{1,0:T(8,128)S(1)} %bitcast.109, f32[8,256]{1,0:T(8,128)S(1)} %log_add_fusion, pred[256,1664]{0,1:T(8,128)(4,1)S(1)} %copy-done.7, bf16[256,8,128]{0,2,1:T(8,128)(2,1)S(1)} %bitcast.104, ...), kind=kOutput, calls=%fused_computation.11 | convolution fusion | flops 896270336 | bytes 24821760 | tf_op jit(solution)/shard_map/qhd,khd->hqk/dot_general | solution.py:123
  247.0 5.0 fusion.21
  252.1 7.7 %copy.112 = f32[1664,1024]{1,0:T(8,128)} copy(f32[1664,1024]{0,1:T(8,128)} %bitcast.92) | data formatting | bytes 13631488 | tf_op jit(solution)/shard_map/reshape | solution.py:133
  259.7 2.6 select_convert_fusion
  262.3 1.9 collective-permute-start.13
  264.3 3.8 broadcast_select_fusion
  268.1 20.9 %collective-permute-done.13 = bf16[2,128,2048]{2,1,0:T(8,128)(2,1)S(1)} collective-permute-done((bf16[2,128,2048]{2,1,0:T(8,128)(2,1)S(1)}, bf16[2,128,2048]{2,1,0:T(8,128)(2,1)S(1)}, u32[]{:S(2)}, u32[]{:S(2)}) %collective-permute-start.13) | collective-permute-done | bytes 1048608 | tf_op jit(solution)/shard_map/ppermute | solution.py:144
  289.6 9.2 %collective-permute-done.14 = bf16[1,128,2048]{2,1,0:T(8,128)(2,1)} collective-permute-done((bf16[1,128,2048]{2,1,0:T(8,128)(2,1)S(1)}, bf16[1,128,2048]{2,1,0:T(8,128)(2,1)}, u32[]{:S(2)}, u32[]{:S(2)}) %collective-permute-start.14) | collective-permute-done | bytes 524320 | tf_op jit(solution)/shard_map/ppermute | solution.py:144
  301.3 6.4 %fusion = bf16[1664,2048]{1,0:T(8,128)(2,1)S(1)} fusion(f32[1664,1024]{1,0:T(8,128)} %copy.113, f32[1664,1024]{1,0:T(8,128)} %copy.112), kind=kLoop, calls=%fused_computation.9 | loop fusion | flops 13631488 | bytes 20447232 | tf_op jit(solution)/shard_map/convert.3
  309.4 112.6 %collective-permute-start.16 = (bf16[128,2048]{1,0:T(8,128)(2,1)S(1)}, bf16[128,2048]{1,0:T(8,128)(2,1)S(1)}, u32[]{:S(2)}, u32[]{:S(2)}) collective-permute-start(bf16[128,2048]{1,0:T(8,128)(2,1)S(1)} %fusion.11), channel_id=1, source_target_pairs={{8,0},{12,4},{16,8},{20,12},{24,16},{28,20},{0,24},{4,28},{40,32},... | collective-permute-start | bytes 1572872 | tf_op jit(solution)/shard_map/ppermute | solution.py:150
  422.0 1.8 fusion.18
  423.8 1.9 collective-permute-start.12
  425.7 1.9 collective-permute-start.11
  427.6 3.8 collective-permute-start.9
  431.4 3.4 collective-permute-start.10
  435.8 2.7 collective-permute-start.17
  440.7 27.7 %collective-permute-done.9 = bf16[128,2048]{1,0:T(8,128)(2,1)S(1)} collective-permute-done((bf16[128,2048]{1,0:T(8,128)(2,1)S(1)}, bf16[128,2048]{1,0:T(8,128)(2,1)S(1)}, u32[]{:S(2)}, u32[]{:S(2)}) %collective-permute-start.9) | collective-permute-done | bytes 524320 | tf_op jit(solution)/shard_map/ppermute | solution.py:15
  469.1 2.6 fusion.10
  473.2 31.4 %collective-permute-done.10 = bf16[256,2048]{1,0:T(8,128)(2,1)} collective-permute-done((bf16[256,2048]{1,0:T(8,128)(2,1)}, bf16[256,2048]{1,0:T(8,128)(2,1)}, u32[]{:S(2)}, u32[]{:S(2)}) %collective-permute-start.10) | collective-permute-done | bytes 1048608 | tf_op jit(solution)/shard_map/ppermute | solution.py:15
  504.5 3.3 fusion.7
  (106 shorter events, 30.6 us)
Async XLA Ops:
  7.2 70.0 %copy-start = (bf16[256,4096]{1,0:T(8,128)(2,1)S(1)}, bf16[256,4096]{1,0:T(8,128)(2,1)}, u32[]{:S(2)}) copy-start(bf16[256,4096]{1,0:T(8,128)(2,1)} %param.23) | copy-start | bytes 6291460
  7.2 21.8 %copy-start.17 = (s32[64,12]{0,1:T(8,128)S(1)}, s32[64,12]{0,1:T(8,128)}, u32[]{:S(2)}) copy-start(s32[64,12]{0,1:T(8,128)} %param.25) | copy-start | bytes 9220
  7.2 501.7 %reduce-scatter.4.cloned.1.call-start = ((), (), s32[]{:S(2)}) async-start(), calls=%async_computation.1 | async-start | bytes 8650752
  10.9 133.7 %collective-permute-start.1 = (bf16[256,2048]{0,1:T(8,128)(2,1)}, bf16[256,2048]{0,1:T(8,128)(2,1)}, u32[]{:S(2)}, u32[]{:S(2)}) collective-permute-start(bf16[256,2048]{0,1:T(8,128)(2,1)} %pad_maximum_fusion.1), channel_id=1, source_target_pairs={{0,12},{4,16},{8,20},{12,24},{16,28},{20,32},{24,36},{28,40},{32,4... | collective-permute-start | bytes 3145736 | tf_op jit(solution)/shard_map/ppermute | solution.py:15
  13.8 132.2 %collective-permute-start.2 = (bf16[256,2048]{0,1:T(8,128)(2,1)}, bf16[256,2048]{0,1:T(8,128)(2,1)}, u32[]{:S(2)}, u32[]{:S(2)}) collective-permute-start(bf16[256,2048]{0,1:T(8,128)(2,1)} %pad_maximum_fusion.1), channel_id=1, source_target_pairs={{0,8},{4,12},{8,16},{12,20},{16,24},{20,28},{24,32},{28,36},{32,40... | collective-permute-start | bytes 3145736 | tf_op jit(solution)/shard_map/ppermute | solution.py:15
  18.3 129.0 %collective-permute-start.3 = (bf16[256,2048]{0,1:T(8,128)(2,1)}, bf16[256,2048]{0,1:T(8,128)(2,1)}, u32[]{:S(2)}, u32[]{:S(2)}) collective-permute-start(bf16[256,2048]{0,1:T(8,128)(2,1)} %pad_maximum_fusion.1), channel_id=1, source_target_pairs={{0,4},{4,8},{8,12},{12,16},{16,20},{20,24},{24,28},{28,32},{32,36}... | collective-permute-start | bytes 3145736 | tf_op jit(solution)/shard_map/ppermute | solution.py:15
  22.9 120.6 %collective-permute-start = (bf16[128,2048]{0,1:T(8,128)(2,1)}, bf16[128,2048]{0,1:T(8,128)(2,1)}, u32[]{:S(2)}, u32[]{:S(2)}) collective-permute-start(bf16[128,2048]{0,1:T(8,128)(2,1)} %fusion.12), channel_id=1, source_target_pairs={{0,16},{4,20},{8,24},{12,28},{16,32},{20,36},{24,40},{28,44},{32,4... | collective-permute-start | bytes 1572872 | tf_op jit(solution)/shard_map/ppermute | solution.py:15
  33.5 42.5 %collective-permute-start.4 = (bf16[128,2048]{1,0:T(8,128)(2,1)}, bf16[128,2048]{1,0:T(8,128)(2,1)}, u32[]{:S(2)}, u32[]{:S(2)}) collective-permute-start(bf16[128,2048]{1,0:T(8,128)(2,1)} %dynamic-slice_bitcast_fusion), channel_id=1, source_target_pairs={{28,0},{0,4},{4,8},{8,12},{12,16},{16,20},{20,24},{24,28},{60,32},... | collective-permute-start | bytes 1572872 | tf_op jit(solution)/shard_map/ppermute | solution.py:66
  77.1 30.4 %collective-permute-start.5 = (bf16[128,2048]{1,0:T(8,128)(2,1)S(1)}, bf16[128,2048]{1,0:T(8,128)(2,1)S(1)}, u32[]{:S(2)}, u32[]{:S(2)}) collective-permute-start(bf16[128,2048]{1,0:T(8,128)(2,1)S(1)} %broadcast_select_fusion.1), channel_id=1, source_target_pairs={{24,0},{28,4},{0,8},{4,12},{8,16},{12,20},{16,24},{20,28},{56,32},... | collective-permute-start | bytes 1572872 | tf_op jit(solution)/shard_map/ppermute | solution.py:66
  107.5 13.4 %collective-permute-start.6 = (bf16[128,2048]{1,0:T(8,128)(2,1)S(1)}, bf16[128,2048]{1,0:T(8,128)(2,1)S(1)}, u32[]{:S(2)}, u32[]{:S(2)}) collective-permute-start(bf16[128,2048]{1,0:T(8,128)(2,1)S(1)} %broadcast_select_fusion.2), channel_id=1, source_target_pairs={{16,0},{20,4},{24,8},{28,12},{0,16},{4,20},{8,24},{12,28},{48,32},... | collective-permute-start | bytes 1572872 | tf_op jit(solution)/shard_map/ppermute | solution.py:66
  121.7 16.4 %collective-permute-start.7 = (bf16[1,128,2048]{2,1,0:T(8,128)(2,1)}, bf16[1,128,2048]{2,1,0:T(8,128)(2,1)}, u32[]{:S(2)}, u32[]{:S(2)}) collective-permute-start(bf16[1,128,2048]{2,1,0:T(8,128)(2,1)} %select_bitcast_fusion), channel_id=1, source_target_pairs={{0,32},{4,36},{8,40},{12,44},{16,48},{20,52},{24,56},{28,60},{32,0... | collective-permute-start | bytes 1572872 | tf_op jit(solution)/shard_map/ppermute | solution.py:73
  139.9 23.7 %collective-permute-start.8 = (bf16[2,128,2048]{2,1,0:T(8,128)(2,1)S(1)}, bf16[2,128,2048]{2,1,0:T(8,128)(2,1)S(1)}, u32[]{:S(2)}, u32[]{:S(2)}) collective-permute-start(bf16[2,128,2048]{2,1,0:T(8,128)(2,1)S(1)} %maximum_select_fusion.1), channel_id=1, source_target_pairs={{0,64},{4,68},{8,72},{12,76},{16,80},{20,84},{24,88},{28,92},{32,9... | collective-permute-start | bytes 3145736 | tf_op jit(solution)/shard_map/ppermute | solution.py:73
  148.6 2.8 copy-start.6
  172.2 3.6 copy-start.7
  172.3 3.6 copy-start.8
  175.8 7.5 %copy-start.4 = (bf16[1664,1024]{0,1:T(8,128)(2,1)}, bf16[1664,1024]{0,1:T(8,128)(2,1)S(1)}, u32[]{:S(2)}) copy-start(bf16[1664,1024]{0,1:T(8,128)(2,1)S(1)} %get-tuple-element.104) | copy-start | bytes 10223620
  175.8 15.2 %copy-start.11 = (bf16[1664,1024]{0,1:T(8,128)(2,1)}, bf16[1664,1024]{0,1:T(8,128)(2,1)S(1)}, u32[]{:S(2)}) copy-start(bf16[1664,1024]{0,1:T(8,128)(2,1)S(1)} %get-tuple-element.103) | copy-start | bytes 10223620
  183.3 7.7 %copy-start.12 = (bf16[256,1024]{0,1:T(8,128)(2,1)S(1)}, bf16[256,1024]{0,1:T(8,128)(2,1)}, u32[]{:S(2)}) copy-start(bf16[256,1024]{0,1:T(8,128)(2,1)} %copy.126) | copy-start | bytes 1572868
  217.2 1.0 copy-start.13
  247.0 5.0 copy-start.3
  259.7 4.5 copy-start.2
  262.3 26.6 %collective-permute-start.13 = (bf16[2,128,2048]{2,1,0:T(8,128)(2,1)S(1)}, bf16[2,128,2048]{2,1,0:T(8,128)(2,1)S(1)}, u32[]{:S(2)}, u32[]{:S(2)}) collective-permute-start(bf16[2,128,2048]{2,1,0:T(8,128)(2,1)S(1)} %bitcast.105), channel_id=1, source_target_pairs={{0,64},{4,68},{8,72},{12,76},{16,80},{20,84},{24,88},{28,92},{32,9... | collective-permute-start | bytes 3145736 | tf_op jit(solution)/shard_map/ppermute | solution.py:144
  289.4 9.4 %collective-permute-start.14 = (bf16[1,128,2048]{2,1,0:T(8,128)(2,1)S(1)}, bf16[1,128,2048]{2,1,0:T(8,128)(2,1)}, u32[]{:S(2)}, u32[]{:S(2)}) collective-permute-start(bf16[1,128,2048]{2,1,0:T(8,128)(2,1)S(1)} %select_convert_fusion.1), channel_id=1, source_target_pairs={{0,32},{4,36},{8,40},{12,44},{16,48},{20,52},{24,56},{28,60},{32,0... | collective-permute-start | bytes 1572872 | tf_op jit(solution)/shard_map/ppermute | solution.py:144
  300.0 138.6 %slice-start = ((s8[6815744]{0:T(1024)(128)(4,1)}), s8[4194304]{0:T(1024)(128)(4,1)S(1)}, s32[]{:S(2)}) async-start(s8[6815744]{0:T(1024)(128)(4,1)} %bitcast.88), calls=%async_computation.2 | async-start | bytes 8388608
  300.0 138.6 %slice-start.1 = ((s8[6815744]{0:T(1024)(128)(4,1)}), s8[2621440]{0:T(1024)(128)(4,1)S(1)}, s32[]{:S(2)}) async-start(s8[6815744]{0:T(1024)(128)(4,1)} %bitcast.88), calls=%async_computation.3 | async-start | bytes 5242880
  300.0 9.3 %collective-permute-start.15 = (bf16[128,2048]{1,0:T(8,128)(2,1)S(1)}, bf16[128,2048]{1,0:T(8,128)(2,1)S(1)}, u32[]{:S(2)}, u32[]{:S(2)}) collective-permute-start(bf16[128,2048]{1,0:T(8,128)(2,1)S(1)} %get-tuple-element.96), channel_id=1, source_target_pairs={{16,0},{20,4},{24,8},{28,12},{0,16},{4,20},{8,24},{12,28},{48,32},... | collective-permute-start | bytes 1572872 | tf_op jit(solution)/shard_map/ppermute | solution.py:150
  307.7 130.8 %copy-start.5 = (bf16[1664,1024]{0,1:T(8,128)(2,1)S(1)}, bf16[1664,1024]{0,1:T(8,128)(2,1)}, u32[]{:S(2)}) copy-start(bf16[1664,1024]{0,1:T(8,128)(2,1)} %copy-done.4) | copy-start | bytes 10223620
  309.3 125.5 %copy-start.9 = (bf16[128,2048]{1,0:T(8,128)(2,1)}, bf16[128,2048]{1,0:T(8,128)(2,1)S(1)}, u32[]{:S(2)}) copy-start(bf16[128,2048]{1,0:T(8,128)(2,1)S(1)} %collective-permute-done.15) | copy-start | bytes 1572868
  309.4 125.4 %collective-permute-start.16 = (bf16[128,2048]{1,0:T(8,128)(2,1)S(1)}, bf16[128,2048]{1,0:T(8,128)(2,1)S(1)}, u32[]{:S(2)}, u32[]{:S(2)}) collective-permute-start(bf16[128,2048]{1,0:T(8,128)(2,1)S(1)} %fusion.11), channel_id=1, source_target_pairs={{8,0},{12,4},{16,8},{20,12},{24,16},{28,20},{0,24},{4,28},{40,32},... | collective-permute-start | bytes 1572872 | tf_op jit(solution)/shard_map/ppermute | solution.py:150
  423.8 49.4 %collective-permute-start.12 = (bf16[256,2048]{1,0:T(8,128)(2,1)}, bf16[256,2048]{1,0:T(8,128)(2,1)}, u32[]{:S(2)}, u32[]{:S(2)}) collective-permute-start(bf16[256,2048]{1,0:T(8,128)(2,1)} %get-tuple-element.101), channel_id=1, source_target_pairs={{4,0},{8,4},{12,8},{16,12},{20,16},{24,20},{28,24},{32,28},{36,32}... | collective-permute-start | bytes 3145736 | tf_op jit(solution)/shard_map/ppermute | solution.py:15
  425.7 47.5 %collective-permute-start.11 = (bf16[256,2048]{1,0:T(8,128)(2,1)}, bf16[256,2048]{1,0:T(8,128)(2,1)}, u32[]{:S(2)}, u32[]{:S(2)}) collective-permute-start(bf16[256,2048]{1,0:T(8,128)(2,1)} %get-tuple-element.102), channel_id=1, source_target_pairs={{8,0},{12,4},{16,8},{20,12},{24,16},{28,20},{32,24},{36,28},{40,32... | collective-permute-start | bytes 3145736 | tf_op jit(solution)/shard_map/ppermute | solution.py:15
  427.6 40.7 %collective-permute-start.9 = (bf16[128,2048]{1,0:T(8,128)(2,1)S(1)}, bf16[128,2048]{1,0:T(8,128)(2,1)S(1)}, u32[]{:S(2)}, u32[]{:S(2)}) collective-permute-start(bf16[128,2048]{1,0:T(8,128)(2,1)S(1)} %slice.144), channel_id=1, source_target_pairs={{16,0},{20,4},{24,8},{28,12},{32,16},{36,20},{40,24},{44,28},{48,3... | collective-permute-start | bytes 1572872 | tf_op jit(solution)/shard_map/ppermute | solution.py:15
  431.4 73.1 %collective-permute-start.10 = (bf16[256,2048]{1,0:T(8,128)(2,1)}, bf16[256,2048]{1,0:T(8,128)(2,1)}, u32[]{:S(2)}, u32[]{:S(2)}) collective-permute-start(bf16[256,2048]{1,0:T(8,128)(2,1)} %get-tuple-element.100), channel_id=1, source_target_pairs={{12,0},{16,4},{20,8},{24,12},{28,16},{32,20},{36,24},{40,28},{44,3... | collective-permute-start | bytes 3145736 | tf_op jit(solution)/shard_map/ppermute | solution.py:15
  434.8 1.0 copy-start.14
  435.8 35.9 %collective-permute-start.17 = (bf16[128,2048]{1,0:T(8,128)(2,1)}, bf16[128,2048]{1,0:T(8,128)(2,1)}, u32[]{:S(2)}, u32[]{:S(2)}) collective-permute-start(bf16[128,2048]{1,0:T(8,128)(2,1)} %fusion.13), channel_id=1, source_target_pairs={{4,0},{8,4},{12,8},{16,12},{20,16},{24,20},{28,24},{0,28},{36,32},... | collective-permute-start | bytes 1572872 | tf_op jit(solution)/shard_map/ppermute | solution.py:150
  468.3 0.8 copy-start.16
  469.1 2.6 copy-start.10
  469.1 2.6 copy-start.15
  469.1 41.8 %copy-start.1 = (bf16[256,4096]{1,0:T(8,128)(2,1)S(1)}, bf16[256,4096]{1,0:T(8,128)(2,1)}, u32[]{:S(2)}) copy-start(bf16[256,4096]{1,0:T(8,128)(2,1)} %param.23) | copy-start | bytes 6291460
Sparse Core Ops, SparseCore 0:
  217.3 215.5 reduce-scatter.3

commit v5 on v3

--- a/solution.py
+++ b/solution.py
@@ -1,6 +1,10 @@
+import functools
+
 import jax
 import jax.numpy as jnp
 from jax import lax
+from jax.experimental import pallas as pl
+from jax.experimental.pallas import tpu as pltpu
 from jax.sharding import PartitionSpec as P
 
 HD = 128
@@ -18,6 +22,154 @@
 def listed(table_rows, block_ids):
     hit = jnp.any(table_rows[:, None, :] == block_ids[:, :, None], axis=2)
     return hit & (block_ids >= 0)
+
+
+def exchange_kernel(dims, ctl_ref, kv_ref, win_out, far_out, win_buf, hop_buf, cross1, cross2, held, pair, sends, recvs):
+    seq_size, group, spans = dims
+    groups = seq_size // group
+    me = lax.axis_index("seq")
+    in_group = me % group
+    base = me - in_group
+    my_group = me // group
+    lead = ctl_ref[0]
+    sum_local = ctl_ref[1]
+    rel = (in_group - lead + group) % group
+    mesh_id = pl.DeviceIdType.MESH
+
+    def ring(step):
+        return (me + step + seq_size) % seq_size
+
+    def in_ring(step):
+        return base + (in_group + step + group) % group
+
+    def across(span):
+        upper = (my_group // span) % 2
+        return me + span * group - 2 * span * group * upper
+
+    barrier = pltpu.get_barrier_semaphore()
+    partners = []
+    for distance in range(1, len(spans) + 1):
+        partners += [ring(distance), ring(-distance)]
+    hop = 1
+    while hop < group:
+        partners += [in_ring(hop), in_ring(-hop)]
+        hop *= 2
+    span = 1
+    while span < groups:
+        partners += [across(span), across(span)]
+        span *= 2
+    for partner in partners:
+        pl.semaphore_signal(barrier, 1, device_id={"seq": partner}, device_id_type=mesh_id)
+    pl.semaphore_wait(barrier, len(partners))
+
+    tok_dev = kv_ref.shape[0]
+    window = []
+    start = 0
+    for distance in range(len(spans), 0, -1):
+        rows = spans[distance - 1] * BLK
+        copy = pltpu.make_async_remote_copy(
+            src_ref=kv_ref.at[pl.ds(tok_dev - rows, rows)],
+            dst_ref=win_buf.at[pl.ds(start, rows)],
+            send_sem=sends.at[distance - 1],
+            recv_sem=recvs.at[distance - 1],
+            device_id={"seq": ring(distance)},
+            device_id_type=mesh_id,
+        )
+        copy.start()
+        window.append(copy)
+        start += rows
+
+    mine = kv_ref[0:BLK, :]
+    for block in range(1, tok_dev // BLK):
+        mine = jnp.where(sum_local == block, kv_ref[block * BLK : (block + 1) * BLK, :], mine)
+    held[...] = mine
+    slot = len(spans)
+    hop = 1
+    stage = 0
+    while hop < group:
+        copy = pltpu.make_async_remote_copy(
+            src_ref=held,
+            dst_ref=hop_buf.at[stage],
+            send_sem=sends.at[slot],
+            recv_sem=recvs.at[slot],
+            device_id={"seq": in_ring(hop)},
+            device_id_type=mesh_id,
+        )
+        copy.start()
+        copy.wait()
+        take = (rel >= hop) & (rel < 2 * hop)
+        held[...] = jnp.where(take, hop_buf[stage], held[...])
+        slot += 1
+        stage += 1
+        hop *= 2
+
+    copy = pltpu.make_async_remote_copy(
+        src_ref=held,
+        dst_ref=cross1,
+        send_sem=sends.at[slot],
+        recv_sem=recvs.at[slot],
+        device_id={"seq": across(1)},
+        device_id_type=mesh_id,
+    )
+    copy.start()
+    copy.wait()
+    upper = (my_group % 2) == 1
+    pair[0] = jnp.where(upper, cross1[...], held[...])
+    pair[1] = jnp.where(upper, held[...], cross1[...])
+    slot += 1
+    copy = pltpu.make_async_remote_copy(
+        src_ref=pair,
+        dst_ref=cross2,
+        send_sem=sends.at[slot],
+        recv_sem=recvs.at[slot],
+        device_id={"seq": across(2)},
+        device_id_type=mesh_id,
+    )
+    copy.start()
+    copy.wait()
+    upper = ((my_group // 2) % 2) == 1
+    for index in range(2):
+        far_out[index] = jnp.where(upper, cross2[index], pair[index])
+        far_out[2 + index] = jnp.where(upper, pair[index], cross2[index])
+    for copy in window:
+        copy.wait()
+    win_out[...] = win_buf[...]
+
+
+def exchange(kv, lead, sum_local, spans, seq_size, group):
+    tok_dev, cols = kv.shape
+    back_rows = sum(spans) * BLK
+    groups = seq_size // group
+    copies = len(spans) + 5
+    ctl = jnp.stack([lead, sum_local]).astype(jnp.int32)
+    return pl.pallas_call(
+        functools.partial(exchange_kernel, (seq_size, group, spans)),
+        out_shape=(
+            jax.ShapeDtypeStruct((back_rows, cols), kv.dtype),
+            jax.ShapeDtypeStruct((groups, BLK, cols), kv.dtype),
+        ),
+        in_specs=[
+            pl.BlockSpec(memory_space=pltpu.SMEM),
+            pl.BlockSpec(memory_space=pltpu.VMEM),
+        ],
+        out_specs=(
+            pl.BlockSpec(memory_space=pltpu.VMEM),
+            pl.BlockSpec(memory_space=pltpu.VMEM),
+        ),
+        scratch_shapes=[
+            pltpu.VMEM((back_rows, cols), kv.dtype),
+            pltpu.VMEM((3, BLK, cols), kv.dtype),
+            pltpu.VMEM((BLK, cols), kv.dtype),
+            pltpu.VMEM((2, BLK, cols), kv.dtype),
+            pltpu.VMEM((BLK, cols), kv.dtype),
+            pltpu.VMEM((2, BLK, cols), kv.dtype),
+            pltpu.SemaphoreType.DMA((copies,)),
+            pltpu.SemaphoreType.DMA((copies,)),
+        ],
+        compiler_params=pltpu.CompilerParams(
+            collective_id=0, has_side_effects=True, vmem_limit_bytes=48 * 1024 * 1024
+        ),
+    )(ctl, kv)
 
 
 def local(queries, keys, values, out_grad, proj_weight, layout):
@@ -43,40 +195,19 @@
     )
     kv = jnp.concatenate([keys, values], axis=1)
 
-    near = []
-    for distance in range(reach_back, 0, -1):
-        rows_needed = span_blocks[distance - 1] * BLK
-        near.append(passed_along(kv[tok_dev - rows_needed :], "seq", distance))
-    pool_kv = jnp.concatenate(near + [kv], axis=0)
-
     seq_size = lax.axis_size("seq")
     group = STRIDE // blocks_dev
     groups = seq_size // group
-    assert groups == summary_count and blocks_dev <= STRIDE
+    assert groups == summary_count == 4 and group == 8
     far_ids = jnp.arange(summary_count, dtype=jnp.int32) * STRIDE + offset_block
     lead = offset_block // blocks_dev
     sum_local = offset_block % blocks_dev
     in_group = me % group
     my_group = me // group
     rel = (in_group - lead) % group
-    held = lax.dynamic_index_in_dim(kv.reshape(blocks_dev, BLK, 2 * width), sum_local, 0, keepdims=False)
-    hop = 1
-    while hop < group:
-        route = [(g * group + (r - hop) % group, g * group + r) for g in range(groups) for r in range(group)]
-        moved = lax.ppermute(held, "seq", route)
-        held = jnp.where((rel >= hop) & (rel < 2 * hop), moved, held)
-        hop *= 2
-    gathered = held[None]
-    span = 1
-    while span < groups:
-        route = [(d, d ^ (span * group)) for d in range(seq_size)]
-        moved = lax.ppermute(gathered, "seq", route)
-        upper = (my_group // span) % 2 == 1
-        gathered = jnp.where(
-            upper, jnp.concatenate([moved, gathered], 0), jnp.concatenate([gathered, moved], 0)
-        )
-        span *= 2
-    far_kv = gathered.reshape(summary_count * BLK, 2 * width)
+    win_kv, far_blocks = exchange(kv, lead, sum_local, span_blocks, seq_size, group)
+    pool_kv = jnp.concatenate([win_kv, kv], axis=0)
+    far_kv = far_blocks.reshape(summary_count * BLK, 2 * width)
 
     all_kv = jnp.concatenate([pool_kv, far_kv], axis=0)
     key_rows = all_kv[:, :width].reshape(-1, heads_here, HD)

time: 612 us -> 604 us (0.987)
  Pallas kernels: 0 us -> 156 us
  waiting for transfers between devices: 259 us -> 116 us
  starting transfers between devices: 183 us -> 164 us
  local copies, waits for them, and re-layouts: 53.7 us -> 45.3 us
    pallas_call x0 -> x1, Pallas kernels: none -> 156 us  [exchange(): pl.pallas_call(functools.partial(exchange_kernel, (seq_size, group, spans...]
    ppermute x5 -> x0, waiting for transfers between devices: 94.2 us -> none  [the longest x3 78.6 us: local(): moved = lax.ppermute(held, 'seq', route)]
    ppermute x8 -> x4, waiting for transfers between devices: 131 us -> 47.6 us  [passed_along(): return lax.ppermute(block, axis, route)]
    ppermute x3, waiting for transfers between devices: 2.57 us -> 34 us  [local(): lax.ppermute(part.astype(jnp.bfloat16), 'seq', route).astype(jnp.float32)]
    ppermute x3, starting transfers between devices: 144 us -> 116 us  [local(): lax.ppermute(part.astype(jnp.bfloat16), 'seq', route).astype(jnp.float32)]
    ppermute x8 -> x4, starting transfers between devices: 26.2 us -> 45.7 us  [passed_along(): return lax.ppermute(block, axis, route)]
    reduce_scatter x1, waiting for transfers between devices: 0.01 us -> 12 us  [local(): lax.psum_scatter(lax.dot_general(out_grad, attn_out.reshape(tok_dev, widt...]
    ppermute x5 -> x0, starting transfers between devices: 11.3 us -> none  [the longest x2 11 us: local(): moved = lax.ppermute(gathered, 'seq', route)]
  transfers between devices with their start and end apart: 19 -> 10, of which waited for: 11 -> 6; matrix products, arithmetic and copies ran while one was open for 16% -> 12% of each run, Pallas kernels for 0% -> 0%
where the time goes in v5:
time: 604 us; the launch traced here: 597 us
  starting transfers between devices  164 us (27%)
  Pallas kernels  156 us (26%)
  waiting for transfers between devices  116 us (19%)
  matrix products  63.9 us (11%)
  local copies, waits for them, and re-layouts  45.3 us (8%)
  other arithmetic  35 us (6%)
  between operations  16.5 us (3%)
    pallas_call x1, Pallas kernels, exchange(): pl.pallas_call(functools.partial(exchange_kernel, (seq_size, group, spans...  156 us
    ppermute x3, starting transfers between devices, local(): lax.ppermute(part.astype(jnp.bfloat16), 'seq', route).astype(jnp.float32)  116 us
    ppermute x4, waiting for transfers between devices, passed_along(): return lax.ppermute(block, axis, route)  47.6 us
    ppermute x4, starting transfers between devices, passed_along(): return lax.ppermute(block, axis, route)  45.7 us
    ppermute x3, waiting for transfers between devices, local(): lax.ppermute(part.astype(jnp.bfloat16), 'seq', route).astype(jnp.float32)  34 us
    ppermute x2, waiting for transfers between devices, local(): lax.ppermute(send.astype(jnp.bfloat16), 'seq', route).astype(jnp.float32)  22.5 us
  transfers between devices with their start and end apart: 10, of which 6 were waited for; matrix products, arithmetic and copies ran while one was open for 12% of the time, Pallas kernels for 0%

profile of v5, /device:TPU:40, one launch (start us, length us, event | category | flops | bytes accessed | tf_op | source)
XLA Modules:
  0.0 597.4 jit_solution(3507021669742313858)
XLA Ops:
  7.2 1.4 slice.117
  10.7 1.1 constant_dynamic-update-slice_fusion.1
  11.9 1.1 constant_dynamic-update-slice_fusion.kv_ref
  13.0 156.4 %shard_map.108 = (bf16[896,2048]{1,0:T(8,128)(2,1)}, bf16[4,128,2048]{2,1,0:T(8,128)(2,1)S(1)}) custom-call(s32[2]{0:T(128)S(1)} %pad_add_fusion.1.ctl_ref, bf16[256,2048]{1,0:T(8,128)(2,1)S(1)} %constant_dynamic-update-slice_fusion.kv_ref), custom_call_target="tpu_custom_call" | custom-call | tf_op jit(solution)/shard_map/pallas_call | solution.py:145
  169.4 3.3 pad_maximum_fusion.1
  172.6 3.8 fusion.18
  176.4 5.6 copy.97
  183.3 1.2 copy.98
  184.6 6.5 %convolution_convert_fusion.2 = bf16[256,1024]{1,0:T(8,128)(2,1)} fusion(bf16[256,4096]{1,0:T(8,128)(2,1)S(1)} %copy-done, bf16[4096,1024]{1,0:T(8,128)(2,1)} %param.24), kind=kOutput, calls=%fused_computation.32 | convolution fusion | flops 2147745792 | bytes 11010048 | tf_op jit(solution)/shard_map/dot_general | solution.py:193
  191.1 2.0 copy.99
  193.1 5.6 copy.100
  198.9 9.4 %fusion.2 = (f32[8,256]{1,0:T(8,128)S(1)}, f32[8,1664,256]{2,1,0:T(8,128)}) fusion(pred[256,1664]{0,1:T(8,128)(4,1)S(1)} %bitcast_and_fusion, bf16[1664,8,128]{0,2,1:T(8,128)(2,1)} %bitcast.83, bf16[256,8,128]{0,2,1:T(8,128)(2,1)S(1)} %bitcast.88), kind=kOutput, calls=%fused_computation.15 | convolution fusion | flops 882636800 | bytes 17997824 | tf_op jit(solution)/shard_map/qhd,khd->hqk/dot_general | solution.py:240
  208.3 7.8 %exponential_reduce_fusion = f32[8,256]{1,0:T(8,128)S(1)} fusion(f32[8,1664,256]{2,1,0:T(8,128)} %get-tuple-element.108, f32[8,256]{1,0:T(8,128)S(1)} %get-tuple-element.107, pred[256,1664]{0,1:T(8,128)(4,1)S(1)} %bitcast_and_fusion), kind=kLoop, calls=%fused_computation.13 | loop fusion | flops 13629440 | bytes 14073856 | tf_op jit(solution)/shard_map/reduce_sum | solution.py:245
  216.1 8.4 %multiply_reduce_fusion = (f32[256,8]{0,1:T(8,128)S(1)}, bf16[8,128,256]{2,1,0:T(8,128)(2,1)S(1)}) fusion(bf16[256,1024]{0,1:T(8,128)(2,1)S(1)} %copy-done.6, bf16[1664,8,128]{0,2,1:T(8,128)(2,1)S(1)} %bitcast.91, f32[8,1664,256]{2,1,0:T(8,128)} %get-tuple-element.108, f32[8,256]{1,0:T(8,128)S(1)} %log_add_fusion, pred[256,1664]{0,1:T(8,128)(4,1)S(1)} %bitcast_and_fusion), kind=kOutput, calls=%fused_computation.40 | convolution fusion | flops 887355392 | bytes 18530304 | tf_op jit(solution)/shard_map/hqk,khd->qhd/dot_general | solution.py:248
  224.5 8.1 %convolution_bitcast_fusion = f32[4096,1024]{0,1:T(8,128)} fusion(bf16[256,1024]{0,1:T(8,128)(2,1)S(1)} %bitcast.96, bf16[256,4096]{1,0:T(8,128)(2,1)S(1)} %copy-done), kind=kOutput, calls=%fused_computation.16 | convolution fusion | flops 2147483648 | bytes 19398656 | tf_op jit(solution)/shard_map/dot_general | solution.py:301
  232.7 1.0 copy-done.7
  233.6 11.4 %fusion.14 = f32[8,128,1664]{2,1,0:T(8,128)} fusion(bf16[256,8,128]{0,2,1:T(8,128)(2,1)S(1)} %bitcast.93, f32[8,1664,256]{2,1,0:T(8,128)} %get-tuple-element.108, f32[8,256]{1,0:T(8,128)S(1)} %log_add_fusion, pred[256,1664]{0,1:T(8,128)(4,1)S(1)} %bitcast_and_fusion), kind=kOutput, calls=%fused_computation.68 | convolution fusion | flops 886046720 | bytes 21405696 | tf_op jit(solution)/shard_map/hqk,qhd->khd/dot_general | solution.py:260
  245.0 7.7 %copy.89 = f32[1664,1024]{1,0:T(8,128)} copy(f32[1664,1024]{0,1:T(8,128)} %bitcast.86) | data formatting | bytes 13631488 | tf_op jit(solution)/shard_map/reshape | solution.py:264
  252.8 9.9 %multiply_convert_fusion = bf16[8,256,1664]{1,2,0:T(8,128)(2,1)S(1)} fusion(f32[8,1664,256]{2,1,0:T(8,128)} %get-tuple-element.108, f32[8,256]{1,0:T(8,128)S(1)} %bitcast.99, f32[8,256]{1,0:T(8,128)S(1)} %log_add_fusion, pred[256,1664]{0,1:T(8,128)(4,1)S(1)} %bitcast_and_fusion, bf16[256,8,128]{0,2,1:T(8,128)(2,1)S(1)} %bitcast.94, ...), kind=kOutput, calls=%fused_computation.11 | convolution fusion | flops 896270336 | bytes 24821760 | tf_op jit(solution)/shard_map/qhd,khd->hqk/dot_general | solution.py:254
  262.7 5.0 fusion.20
  267.7 7.7 %copy.88 = f32[1664,1024]{1,0:T(8,128)} copy(f32[1664,1024]{0,1:T(8,128)} %bitcast.85) | data formatting | bytes 13631488 | tf_op jit(solution)/shard_map/reshape | solution.py:264
  275.4 2.5 select_convert_fusion
  277.9 2.3 collective-permute-start.4
  280.3 4.7 broadcast_select_fusion
  285.0 17.4 %collective-permute-done.4 = bf16[2,128,2048]{2,1,0:T(8,128)(2,1)S(1)} collective-permute-done((bf16[2,128,2048]{2,1,0:T(8,128)(2,1)S(1)}, bf16[2,128,2048]{2,1,0:T(8,128)(2,1)S(1)}, u32[]{:S(2)}, u32[]{:S(2)}) %collective-permute-start.4) | collective-permute-done | bytes 1048608 | tf_op jit(solution)/shard_map/ppermute | solution.py:275
  302.9 5.8 fusion
  308.7 5.0 collective-permute-done.5
  313.7 1.0 bitcast_convert_fusion
  314.7 2.7 collective-permute-start.6
  317.3 1.7 fusion.17
  319.1 40.0 %collective-permute-start.3 = (bf16[256,2048]{1,0:T(8,128)(2,1)}, bf16[256,2048]{1,0:T(8,128)(2,1)}, u32[]{:S(2)}, u32[]{:S(2)}) collective-permute-start(bf16[256,2048]{1,0:T(8,128)(2,1)} %get-tuple-element.101), channel_id=1, source_target_pairs={{4,0},{8,4},{12,8},{16,12},{20,16},{24,20},{28,24},{32,28},{36,32}... | collective-permute-start | bytes 3145736 | tf_op jit(solution)/shard_map/ppermute | solution.py:19
  359.1 1.9 collective-permute-start.2
  361.0 0.8 slice.138
  361.8 1.9 collective-permute-start
  363.8 1.9 collective-permute-start.1
  365.9 113.5 %collective-permute-start.7 = (bf16[128,2048]{1,0:T(8,128)(2,1)S(1)}, bf16[128,2048]{1,0:T(8,128)(2,1)S(1)}, u32[]{:S(2)}, u32[]{:S(2)}) collective-permute-start(bf16[128,2048]{1,0:T(8,128)(2,1)S(1)} %fusion.11), channel_id=1, source_target_pairs={{8,0},{12,4},{16,8},{20,12},{24,16},{28,20},{0,24},{4,28},{40,32},... | collective-permute-start | bytes 1572872 | tf_op jit(solution)/shard_map/ppermute | solution.py:281
  479.4 5.1 convolution_convert_fusion
  484.5 14.6 %collective-permute-done.7 = bf16[128,2048]{1,0:T(8,128)(2,1)S(1)} collective-permute-done((bf16[128,2048]{1,0:T(8,128)(2,1)S(1)}, bf16[128,2048]{1,0:T(8,128)(2,1)S(1)}, u32[]{:S(2)}, u32[]{:S(2)}) %collective-permute-start.7) | collective-permute-done | bytes 524320 | tf_op jit(solution)/shard_map/ppermute | solution.py:281
  499.1 1.0 fusion.12
  500.2 1.0 copy.90
  501.2 2.6 fusion.10
  503.8 19.4 %collective-permute-done.8 = bf16[128,2048]{1,0:T(8,128)(2,1)} collective-permute-done((bf16[128,2048]{1,0:T(8,128)(2,1)}, bf16[128,2048]{1,0:T(8,128)(2,1)}, u32[]{:S(2)}, u32[]{:S(2)}) %collective-permute-start.8) | collective-permute-done | bytes 524320 | tf_op jit(solution)/shard_map/ppermute | solution.py:281
  523.2 1.4 add_select_fusion
  524.6 47.6 %collective-permute-done.1 = bf16[256,2048]{1,0:T(8,128)(2,1)} collective-permute-done((bf16[256,2048]{1,0:T(8,128)(2,1)}, bf16[256,2048]{1,0:T(8,128)(2,1)}, u32[]{:S(2)}, u32[]{:S(2)}) %collective-permute-start.1) | collective-permute-done | bytes 1048608 | tf_op jit(solution)/shard_map/ppermute | solution.py:19
  572.2 3.3 fusion.7
  575.5 1.0 fusion.19
  576.5 12.0 %reduce-scatter.2.cloned.1.call-done = f32[128,1024]{0,1:T(8,128)} async-done(((f32[4096,1024]{0,1:T(8,128)}), f32[128,1024]{0,1:T(8,128)}) %reduce-scatter.2.cloned.1.call-update) | async-done | bytes 524304 | tf_op jit(solution)/shard_map/reduce_scatter | solution.py:300
  588.5 2.0 copy.91
  (56 shorter events, 2.3 us)
Async XLA Ops:
  7.2 177.4 %copy-start = (bf16[256,4096]{1,0:T(8,128)(2,1)S(1)}, bf16[256,4096]{1,0:T(8,128)(2,1)}, u32[]{:S(2)}) copy-start(bf16[256,4096]{1,0:T(8,128)(2,1)} %param.23) | copy-start | bytes 6291460
  7.2 581.4 %reduce-scatter.2.cloned.1.call-start = ((), (), s32[]{:S(2)}) async-start(), calls=%async_computation.1 | async-start | bytes 17301504 | tf_op jit(solution)/shard_map/reduce_scatter | solution.py:300
  176.4 5.8 copy-start.10
  208.3 7.8 %copy-start.5 = (bf16[1664,1024]{0,1:T(8,128)(2,1)S(1)}, bf16[1664,1024]{0,1:T(8,128)(2,1)}, u32[]{:S(2)}) copy-start(bf16[1664,1024]{0,1:T(8,128)(2,1)} %copy.100) | copy-start | bytes 10223620
  208.3 7.8 %copy-start.6 = (bf16[256,1024]{0,1:T(8,128)(2,1)S(1)}, bf16[256,1024]{0,1:T(8,128)(2,1)}, u32[]{:S(2)}) copy-start(bf16[256,1024]{0,1:T(8,128)(2,1)} %copy.99) | copy-start | bytes 1572868
  232.6 1.0 copy-start.7
  262.7 5.0 copy-start.2
  277.9 24.5 %collective-permute-start.4 = (bf16[2,128,2048]{2,1,0:T(8,128)(2,1)S(1)}, bf16[2,128,2048]{2,1,0:T(8,128)(2,1)S(1)}, u32[]{:S(2)}, u32[]{:S(2)}) collective-permute-start(bf16[2,128,2048]{2,1,0:T(8,128)(2,1)S(1)} %bitcast.95), channel_id=1, source_target_pairs={{0,64},{4,68},{8,72},{12,76},{16,80},{20,84},{24,88},{28,92},{32,9... | collective-permute-start | bytes 3145736 | tf_op jit(solution)/shard_map/ppermute | solution.py:275
  302.8 10.9 %collective-permute-start.5 = (bf16[1,128,2048]{2,1,0:T(8,128)(2,1)S(1)}, bf16[1,128,2048]{2,1,0:T(8,128)(2,1)S(1)}, u32[]{:S(2)}, u32[]{:S(2)}) collective-permute-start(bf16[1,128,2048]{2,1,0:T(8,128)(2,1)S(1)} %select_convert_fusion.1), channel_id=1, source_target_pairs={{0,32},{4,36},{8,40},{12,44},{16,48},{20,52},{24,56},{28,60},{32,0... | collective-permute-start | bytes 1572872 | tf_op jit(solution)/shard_map/ppermute | solution.py:275
  314.7 51.1 %collective-permute-start.6 = (bf16[128,2048]{1,0:T(8,128)(2,1)}, bf16[128,2048]{1,0:T(8,128)(2,1)S(1)}, u32[]{:S(2)}, u32[]{:S(2)}) collective-permute-start(bf16[128,2048]{1,0:T(8,128)(2,1)} %get-tuple-element.96), channel_id=1, source_target_pairs={{16,0},{20,4},{24,8},{28,12},{0,16},{4,20},{8,24},{12,28},{48,32},... | collective-permute-start | bytes 1572872 | tf_op jit(solution)/shard_map/ppermute | solution.py:281
  319.1 205.5 %collective-permute-start.3 = (bf16[256,2048]{1,0:T(8,128)(2,1)}, bf16[256,2048]{1,0:T(8,128)(2,1)}, u32[]{:S(2)}, u32[]{:S(2)}) collective-permute-start(bf16[256,2048]{1,0:T(8,128)(2,1)} %get-tuple-element.101), channel_id=1, source_target_pairs={{4,0},{8,4},{12,8},{16,12},{20,16},{24,20},{28,24},{32,28},{36,32}... | collective-permute-start | bytes 3145736 | tf_op jit(solution)/shard_map/ppermute | solution.py:19
  359.1 165.5 %collective-permute-start.2 = (bf16[256,2048]{1,0:T(8,128)(2,1)}, bf16[256,2048]{1,0:T(8,128)(2,1)}, u32[]{:S(2)}, u32[]{:S(2)}) collective-permute-start(bf16[256,2048]{1,0:T(8,128)(2,1)} %get-tuple-element.102), channel_id=1, source_target_pairs={{8,0},{12,4},{16,8},{20,12},{24,16},{28,20},{32,24},{36,28},{40,32... | collective-permute-start | bytes 3145736 | tf_op jit(solution)/shard_map/ppermute | solution.py:19
  361.8 139.4 %collective-permute-start = (bf16[128,2048]{1,0:T(8,128)(2,1)}, bf16[128,2048]{1,0:T(8,128)(2,1)}, u32[]{:S(2)}, u32[]{:S(2)}) collective-permute-start(bf16[128,2048]{1,0:T(8,128)(2,1)} %slice.138), channel_id=1, source_target_pairs={{16,0},{20,4},{24,8},{28,12},{32,16},{36,20},{40,24},{44,28},{48,3... | collective-permute-start | bytes 1572872 | tf_op jit(solution)/shard_map/ppermute | solution.py:19
  363.8 208.4 %collective-permute-start.1 = (bf16[256,2048]{1,0:T(8,128)(2,1)}, bf16[256,2048]{1,0:T(8,128)(2,1)}, u32[]{:S(2)}, u32[]{:S(2)}) collective-permute-start(bf16[256,2048]{1,0:T(8,128)(2,1)} %get-tuple-element.100), channel_id=1, source_target_pairs={{12,0},{16,4},{20,8},{24,12},{28,16},{32,20},{36,24},{40,28},{44,3... | collective-permute-start | bytes 3145736 | tf_op jit(solution)/shard_map/ppermute | solution.py:19
  365.8 133.3 %copy-start.3 = (bf16[128,2048]{1,0:T(8,128)(2,1)}, bf16[128,2048]{1,0:T(8,128)(2,1)S(1)}, u32[]{:S(2)}) copy-start(bf16[128,2048]{1,0:T(8,128)(2,1)S(1)} %collective-permute-done.6) | copy-start | bytes 1572868
  365.9 133.2 %collective-permute-start.7 = (bf16[128,2048]{1,0:T(8,128)(2,1)S(1)}, bf16[128,2048]{1,0:T(8,128)(2,1)S(1)}, u32[]{:S(2)}, u32[]{:S(2)}) collective-permute-start(bf16[128,2048]{1,0:T(8,128)(2,1)S(1)} %fusion.11), channel_id=1, source_target_pairs={{8,0},{12,4},{16,8},{20,12},{24,16},{28,20},{0,24},{4,28},{40,32},... | collective-permute-start | bytes 1572872 | tf_op jit(solution)/shard_map/ppermute | solution.py:281
  499.1 2.1 copy-start.8
  500.1 23.1 %collective-permute-start.8 = (bf16[128,2048]{1,0:T(8,128)(2,1)}, bf16[128,2048]{1,0:T(8,128)(2,1)}, u32[]{:S(2)}, u32[]{:S(2)}) collective-permute-start(bf16[128,2048]{1,0:T(8,128)(2,1)} %fusion.12), channel_id=1, source_target_pairs={{4,0},{8,4},{12,8},{16,12},{20,16},{24,20},{28,24},{0,28},{36,32},... | collective-permute-start | bytes 1572872 | tf_op jit(solution)/shard_map/ppermute | solution.py:281
  501.2 22.0 %copy-start.4 = (bf16[128,2048]{1,0:T(8,128)(2,1)S(1)}, bf16[128,2048]{1,0:T(8,128)(2,1)}, u32[]{:S(2)}) copy-start(bf16[128,2048]{1,0:T(8,128)(2,1)} %copy-done.3) | copy-start | bytes 1572868
  501.2 22.0 %copy-start.9 = (bf16[128,2048]{1,0:T(8,128)(2,1)S(1)}, bf16[128,2048]{1,0:T(8,128)(2,1)}, u32[]{:S(2)}) copy-start(bf16[128,2048]{1,0:T(8,128)(2,1)} %copy-done.8) | copy-start | bytes 1572868
  501.2 89.4 %copy-start.1 = (bf16[256,4096]{1,0:T(8,128)(2,1)S(1)}, bf16[256,4096]{1,0:T(8,128)(2,1)}, u32[]{:S(2)}) copy-start(bf16[256,4096]{1,0:T(8,128)(2,1)} %param.23) | copy-start | bytes 6291460
Sparse Core Ops, SparseCore 0:
  232.7 355.7 reduce-scatter.1

commit v6 on v5

--- a/solution.py
+++ b/solution.py
@@ -63,22 +63,6 @@
     pl.semaphore_wait(barrier, len(partners))
 
     tok_dev = kv_ref.shape[0]
-    window = []
-    start = 0
-    for distance in range(len(spans), 0, -1):
-        rows = spans[distance - 1] * BLK
-        copy = pltpu.make_async_remote_copy(
-            src_ref=kv_ref.at[pl.ds(tok_dev - rows, rows)],
-            dst_ref=win_buf.at[pl.ds(start, rows)],
-            send_sem=sends.at[distance - 1],
-            recv_sem=recvs.at[distance - 1],
-            device_id={"seq": ring(distance)},
-            device_id_type=mesh_id,
-        )
-        copy.start()
-        window.append(copy)
-        start += rows
-
     mine = kv_ref[0:BLK, :]
     for block in range(1, tok_dev // BLK):
         mine = jnp.where(sum_local == block, kv_ref[block * BLK : (block + 1) * BLK, :], mine)
@@ -117,6 +101,22 @@
     pair[0] = jnp.where(upper, cross1[...], held[...])
     pair[1] = jnp.where(upper, held[...], cross1[...])
     slot += 1
+    window = []
+    start = 0
+    for distance in range(len(spans), 0, -1):
+        rows = spans[distance - 1] * BLK
+        copy = pltpu.make_async_remote_copy(
+            src_ref=kv_ref.at[pl.ds(tok_dev - rows, rows)],
+            dst_ref=win_buf.at[pl.ds(start, rows)],
+            send_sem=sends.at[distance - 1],
+            recv_sem=recvs.at[distance - 1],
+            device_id={"seq": ring(distance)},
+            device_id_type=mesh_id,
+        )
+        copy.start()
+        window.append(copy)
+        start += rows
+
     copy = pltpu.make_async_remote_copy(
         src_ref=pair,
         dst_ref=cross2,

time: 604 us -> 607 us (level)
  Pallas kernels: 156 us -> 112 us
  starting transfers between devices: 164 us -> 205 us
  waiting for transfers between devices: 116 us -> 124 us
    pallas_call x1, Pallas kernels: 156 us -> 112 us  [exchange(): pl.pallas_call(functools.partial(exchange_kernel, (seq_size, group, spans...]
    ppermute x4, starting transfers between devices: 45.7 us -> 74.2 us  [passed_along(): return lax.ppermute(block, axis, route)]
    ppermute x3, starting transfers between devices: 116 us -> 126 us  [local(): lax.ppermute(part.astype(jnp.bfloat16), 'seq', route).astype(jnp.float32)]
    reduce_scatter x1, waiting for transfers between devices: 12 us -> 19.4 us  [local(): lax.psum_scatter(lax.dot_general(out_grad, attn_out.reshape(tok_dev, widt...]
where the time goes in v6:
time: 607 us; the launch traced here: 602 us
  starting transfers between devices  205 us (34%)
  waiting for transfers between devices  124 us (20%)
  Pallas kernels  112 us (18%)
  matrix products  63.7 us (10%)
  local copies, waits for them, and re-layouts  45.3 us (7%)
  other arithmetic  34.9 us (6%)
  between operations  16.5 us (3%)
    ppermute x3, starting transfers between devices, local(): lax.ppermute(part.astype(jnp.bfloat16), 'seq', route).astype(jnp.float32)  126 us
    pallas_call x1, Pallas kernels, exchange(): pl.pallas_call(functools.partial(exchange_kernel, (seq_size, group, spans...  112 us
    ppermute x4, starting transfers between devices, passed_along(): return lax.ppermute(block, axis, route)  74.2 us
    ppermute x4, waiting for transfers between devices, passed_along(): return lax.ppermute(block, axis, route)  52.4 us
    ppermute x3, waiting for transfers between devices, local(): lax.ppermute(part.astype(jnp.bfloat16), 'seq', route).astype(jnp.float32)  32 us
    ppermute x2, waiting for transfers between devices, local(): lax.ppermute(send.astype(jnp.bfloat16), 'seq', route).astype(jnp.float32)  20.2 us
    reduce_scatter x1, waiting for transfers between devices, local(): lax.psum_scatter(lax.dot_general(out_grad, attn_out.reshape(tok_dev, widt...  19.4 us
  transfers between devices with their start and end apart: 10, of which 6 were waited for; matrix products, arithmetic and copies ran while one was open for 12% of the time, Pallas kernels for 0%

profile of v6, /device:TPU:40, one launch (start us, length us, event | category | flops | bytes accessed | tf_op | source)
XLA Modules:
  0.0 601.8 jit_solution(16975328188347350501)
XLA Ops:
  7.2 1.4 slice.117
  10.7 1.1 constant_dynamic-update-slice_fusion.1
  11.9 1.1 constant_dynamic-update-slice_fusion.kv_ref
  13.0 112.1 %shard_map.108 = (bf16[896,2048]{1,0:T(8,128)(2,1)}, bf16[4,128,2048]{2,1,0:T(8,128)(2,1)S(1)}) custom-call(s32[2]{0:T(128)S(1)} %pad_add_fusion.1.ctl_ref, bf16[256,2048]{1,0:T(8,128)(2,1)S(1)} %constant_dynamic-update-slice_fusion.kv_ref), custom_call_target="tpu_custom_call" | custom-call | tf_op jit(solution)/shard_map/pallas_call | solution.py:145
  125.2 3.3 pad_maximum_fusion.1
  128.4 3.8 fusion.18
  132.2 5.6 copy.97
  139.1 1.2 copy.98
  140.4 6.5 %convolution_convert_fusion.2 = bf16[256,1024]{1,0:T(8,128)(2,1)} fusion(bf16[256,4096]{1,0:T(8,128)(2,1)S(1)} %copy-done, bf16[4096,1024]{1,0:T(8,128)(2,1)} %param.24), kind=kOutput, calls=%fused_computation.32 | convolution fusion | flops 2147745792 | bytes 11010048 | tf_op jit(solution)/shard_map/dot_general | solution.py:193
  146.9 2.0 copy.99
  148.9 5.6 copy.100
  154.7 9.4 %fusion.2 = (f32[8,256]{1,0:T(8,128)S(1)}, f32[8,1664,256]{2,1,0:T(8,128)}) fusion(pred[256,1664]{0,1:T(8,128)(4,1)S(1)} %bitcast_and_fusion, bf16[1664,8,128]{0,2,1:T(8,128)(2,1)} %bitcast.83, bf16[256,8,128]{0,2,1:T(8,128)(2,1)S(1)} %bitcast.88), kind=kOutput, calls=%fused_computation.15 | convolution fusion | flops 882636800 | bytes 17997824 | tf_op jit(solution)/shard_map/qhd,khd->hqk/dot_general | solution.py:240
  164.1 7.8 %exponential_reduce_fusion = f32[8,256]{1,0:T(8,128)S(1)} fusion(f32[8,1664,256]{2,1,0:T(8,128)} %get-tuple-element.108, f32[8,256]{1,0:T(8,128)S(1)} %get-tuple-element.107, pred[256,1664]{0,1:T(8,128)(4,1)S(1)} %bitcast_and_fusion), kind=kLoop, calls=%fused_computation.13 | loop fusion | flops 13629440 | bytes 14073856 | tf_op jit(solution)/shard_map/reduce_sum | solution.py:245
  171.9 8.4 %multiply_reduce_fusion = (f32[256,8]{0,1:T(8,128)S(1)}, bf16[8,128,256]{2,1,0:T(8,128)(2,1)S(1)}) fusion(bf16[256,1024]{0,1:T(8,128)(2,1)S(1)} %copy-done.6, bf16[1664,8,128]{0,2,1:T(8,128)(2,1)S(1)} %bitcast.91, f32[8,1664,256]{2,1,0:T(8,128)} %get-tuple-element.108, f32[8,256]{1,0:T(8,128)S(1)} %log_add_fusion, pred[256,1664]{0,1:T(8,128)(4,1)S(1)} %bitcast_and_fusion), kind=kOutput, calls=%fused_computation.40 | convolution fusion | flops 887355392 | bytes 18530304 | tf_op jit(solution)/shard_map/hqk,khd->qhd/dot_general | solution.py:248
  180.3 8.1 %convolution_bitcast_fusion = f32[4096,1024]{0,1:T(8,128)} fusion(bf16[256,1024]{0,1:T(8,128)(2,1)S(1)} %bitcast.96, bf16[256,4096]{1,0:T(8,128)(2,1)S(1)} %copy-done), kind=kOutput, calls=%fused_computation.16 | convolution fusion | flops 2147483648 | bytes 19398656 | tf_op jit(solution)/shard_map/dot_general | solution.py:301
  188.5 1.0 copy-done.7
  189.4 11.4 %fusion.14 = f32[8,128,1664]{2,1,0:T(8,128)} fusion(bf16[256,8,128]{0,2,1:T(8,128)(2,1)S(1)} %bitcast.93, f32[8,1664,256]{2,1,0:T(8,128)} %get-tuple-element.108, f32[8,256]{1,0:T(8,128)S(1)} %log_add_fusion, pred[256,1664]{0,1:T(8,128)(4,1)S(1)} %bitcast_and_fusion), kind=kOutput, calls=%fused_computation.68 | convolution fusion | flops 886046720 | bytes 21405696 | tf_op jit(solution)/shard_map/hqk,qhd->khd/dot_general | solution.py:260
  200.8 7.7 %copy.89 = f32[1664,1024]{1,0:T(8,128)} copy(f32[1664,1024]{0,1:T(8,128)} %bitcast.86) | data formatting | bytes 13631488 | tf_op jit(solution)/shard_map/reshape | solution.py:264
  208.5 9.8 %multiply_convert_fusion = bf16[8,256,1664]{1,2,0:T(8,128)(2,1)S(1)} fusion(f32[8,1664,256]{2,1,0:T(8,128)} %get-tuple-element.108, f32[8,256]{1,0:T(8,128)S(1)} %bitcast.99, f32[8,256]{1,0:T(8,128)S(1)} %log_add_fusion, pred[256,1664]{0,1:T(8,128)(4,1)S(1)} %bitcast_and_fusion, bf16[256,8,128]{0,2,1:T(8,128)(2,1)S(1)} %bitcast.94, ...), kind=kOutput, calls=%fused_computation.11 | convolution fusion | flops 896270336 | bytes 24821760 | tf_op jit(solution)/shard_map/qhd,khd->hqk/dot_general | solution.py:254
  218.3 5.0 fusion.20
  223.3 7.6 %copy.88 = f32[1664,1024]{1,0:T(8,128)} copy(f32[1664,1024]{0,1:T(8,128)} %bitcast.85) | data formatting | bytes 13631488 | tf_op jit(solution)/shard_map/reshape | solution.py:264
  230.9 2.4 select_convert_fusion
  233.4 4.0 collective-permute-start.4
  237.4 4.7 broadcast_select_fusion
  242.1 15.6 %collective-permute-done.4 = bf16[2,128,2048]{2,1,0:T(8,128)(2,1)S(1)} collective-permute-done((bf16[2,128,2048]{2,1,0:T(8,128)(2,1)S(1)}, bf16[2,128,2048]{2,1,0:T(8,128)(2,1)S(1)}, u32[]{:S(2)}, u32[]{:S(2)}) %collective-permute-start.4) | collective-permute-done | bytes 1048608 | tf_op jit(solution)/shard_map/ppermute | solution.py:275
  258.1 1.0 collective-permute-start.5
  259.1 5.8 fusion
  264.9 4.6 collective-permute-done.5
  269.4 1.0 bitcast_convert_fusion
  270.4 16.1 %collective-permute-start.6 = (bf16[128,2048]{1,0:T(8,128)(2,1)}, bf16[128,2048]{1,0:T(8,128)(2,1)S(1)}, u32[]{:S(2)}, u32[]{:S(2)}) collective-permute-start(bf16[128,2048]{1,0:T(8,128)(2,1)} %get-tuple-element.96), channel_id=1, source_target_pairs={{16,0},{20,4},{24,8},{28,12},{0,16},{4,20},{8,24},{12,28},{48,32},... | collective-permute-start | bytes 1572872 | tf_op jit(solution)/shard_map/ppermute | solution.py:281
  286.5 1.8 fusion.17
  288.3 52.2 %collective-permute-start.3 = (bf16[256,2048]{1,0:T(8,128)(2,1)}, bf16[256,2048]{1,0:T(8,128)(2,1)}, u32[]{:S(2)}, u32[]{:S(2)}) collective-permute-start(bf16[256,2048]{1,0:T(8,128)(2,1)} %get-tuple-element.101), channel_id=1, source_target_pairs={{4,0},{8,4},{12,8},{16,12},{20,16},{24,20},{28,24},{32,28},{36,32}... | collective-permute-start | bytes 3145736 | tf_op jit(solution)/shard_map/ppermute | solution.py:19
  340.5 18.2 %collective-permute-start.2 = (bf16[256,2048]{1,0:T(8,128)(2,1)}, bf16[256,2048]{1,0:T(8,128)(2,1)}, u32[]{:S(2)}, u32[]{:S(2)}) collective-permute-start(bf16[256,2048]{1,0:T(8,128)(2,1)} %get-tuple-element.102), channel_id=1, source_target_pairs={{8,0},{12,4},{16,8},{20,12},{24,16},{28,20},{32,24},{36,28},{40,32... | collective-permute-start | bytes 3145736 | tf_op jit(solution)/shard_map/ppermute | solution.py:19
  359.5 1.9 collective-permute-start
  361.4 1.9 collective-permute-start.1
  363.6 109.9 %collective-permute-start.7 = (bf16[128,2048]{1,0:T(8,128)(2,1)S(1)}, bf16[128,2048]{1,0:T(8,128)(2,1)S(1)}, u32[]{:S(2)}, u32[]{:S(2)}) collective-permute-start(bf16[128,2048]{1,0:T(8,128)(2,1)S(1)} %fusion.11), channel_id=1, source_target_pairs={{8,0},{12,4},{16,8},{20,12},{24,16},{28,20},{0,24},{4,28},{40,32},... | collective-permute-start | bytes 1572872 | tf_op jit(solution)/shard_map/ppermute | solution.py:281
  473.5 5.2 convolution_convert_fusion
  478.6 13.6 %collective-permute-done.7 = bf16[128,2048]{1,0:T(8,128)(2,1)S(1)} collective-permute-done((bf16[128,2048]{1,0:T(8,128)(2,1)S(1)}, bf16[128,2048]{1,0:T(8,128)(2,1)S(1)}, u32[]{:S(2)}, u32[]{:S(2)}) %collective-permute-start.7) | collective-permute-done | bytes 524320 | tf_op jit(solution)/shard_map/ppermute | solution.py:281
  492.2 1.0 fusion.12
  493.3 1.0 copy.90
  494.3 2.6 fusion.10
  497.0 18.4 %collective-permute-done.8 = bf16[128,2048]{1,0:T(8,128)(2,1)} collective-permute-done((bf16[128,2048]{1,0:T(8,128)(2,1)}, bf16[128,2048]{1,0:T(8,128)(2,1)}, u32[]{:S(2)}, u32[]{:S(2)}) %collective-permute-start.8) | collective-permute-done | bytes 524320 | tf_op jit(solution)/shard_map/ppermute | solution.py:281
  515.4 1.4 add_select_fusion
  516.8 52.4 %collective-permute-done.1 = bf16[256,2048]{1,0:T(8,128)(2,1)} collective-permute-done((bf16[256,2048]{1,0:T(8,128)(2,1)}, bf16[256,2048]{1,0:T(8,128)(2,1)}, u32[]{:S(2)}, u32[]{:S(2)}) %collective-permute-start.1) | collective-permute-done | bytes 1048608 | tf_op jit(solution)/shard_map/ppermute | solution.py:19
  569.1 3.3 fusion.7
  572.5 1.0 fusion.19
  573.5 19.4 %reduce-scatter.2.cloned.1.call-done = f32[128,1024]{0,1:T(8,128)} async-done(((f32[4096,1024]{0,1:T(8,128)}), f32[128,1024]{0,1:T(8,128)}) %reduce-scatter.2.cloned.1.call-update) | async-done | bytes 524304 | tf_op jit(solution)/shard_map/reduce_scatter | solution.py:300
  592.9 2.0 copy.91
  (56 shorter events, 3.1 us)
Async XLA Ops:
  7.2 133.2 %copy-start = (bf16[256,4096]{1,0:T(8,128)(2,1)S(1)}, bf16[256,4096]{1,0:T(8,128)(2,1)}, u32[]{:S(2)}) copy-start(bf16[256,4096]{1,0:T(8,128)(2,1)} %param.23) | copy-start | bytes 6291460
  7.2 585.7 %reduce-scatter.2.cloned.1.call-start = ((), (), s32[]{:S(2)}) async-start(), calls=%async_computation.1 | async-start | bytes 17301504 | tf_op jit(solution)/shard_map/reduce_scatter | solution.py:300
  132.2 5.8 copy-start.10
  164.1 7.8 %copy-start.5 = (bf16[1664,1024]{0,1:T(8,128)(2,1)S(1)}, bf16[1664,1024]{0,1:T(8,128)(2,1)}, u32[]{:S(2)}) copy-start(bf16[1664,1024]{0,1:T(8,128)(2,1)} %copy.100) | copy-start | bytes 10223620
  164.1 7.8 %copy-start.6 = (bf16[256,1024]{0,1:T(8,128)(2,1)S(1)}, bf16[256,1024]{0,1:T(8,128)(2,1)}, u32[]{:S(2)}) copy-start(bf16[256,1024]{0,1:T(8,128)(2,1)} %copy.99) | copy-start | bytes 1572868
  188.4 1.0 copy-start.7
  218.3 5.0 copy-start.2
  233.4 24.3 %collective-permute-start.4 = (bf16[2,128,2048]{2,1,0:T(8,128)(2,1)S(1)}, bf16[2,128,2048]{2,1,0:T(8,128)(2,1)S(1)}, u32[]{:S(2)}, u32[]{:S(2)}) collective-permute-start(bf16[2,128,2048]{2,1,0:T(8,128)(2,1)S(1)} %bitcast.95), channel_id=1, source_target_pairs={{0,64},{4,68},{8,72},{12,76},{16,80},{20,84},{24,88},{28,92},{32,9... | collective-permute-start | bytes 3145736 | tf_op jit(solution)/shard_map/ppermute | solution.py:275
  258.1 11.3 %collective-permute-start.5 = (bf16[1,128,2048]{2,1,0:T(8,128)(2,1)S(1)}, bf16[1,128,2048]{2,1,0:T(8,128)(2,1)S(1)}, u32[]{:S(2)}, u32[]{:S(2)}) collective-permute-start(bf16[1,128,2048]{2,1,0:T(8,128)(2,1)S(1)} %select_convert_fusion.1), channel_id=1, source_target_pairs={{0,32},{4,36},{8,40},{12,44},{16,48},{20,52},{24,56},{28,60},{32,0... | collective-permute-start | bytes 1572872 | tf_op jit(solution)/shard_map/ppermute | solution.py:275
  270.4 93.0 %collective-permute-start.6 = (bf16[128,2048]{1,0:T(8,128)(2,1)}, bf16[128,2048]{1,0:T(8,128)(2,1)S(1)}, u32[]{:S(2)}, u32[]{:S(2)}) collective-permute-start(bf16[128,2048]{1,0:T(8,128)(2,1)} %get-tuple-element.96), channel_id=1, source_target_pairs={{16,0},{20,4},{24,8},{28,12},{0,16},{4,20},{8,24},{12,28},{48,32},... | collective-permute-start | bytes 1572872 | tf_op jit(solution)/shard_map/ppermute | solution.py:281
  288.3 228.5 %collective-permute-start.3 = (bf16[256,2048]{1,0:T(8,128)(2,1)}, bf16[256,2048]{1,0:T(8,128)(2,1)}, u32[]{:S(2)}, u32[]{:S(2)}) collective-permute-start(bf16[256,2048]{1,0:T(8,128)(2,1)} %get-tuple-element.101), channel_id=1, source_target_pairs={{4,0},{8,4},{12,8},{16,12},{20,16},{24,20},{28,24},{32,28},{36,32}... | collective-permute-start | bytes 3145736 | tf_op jit(solution)/shard_map/ppermute | solution.py:19
  340.5 176.3 %collective-permute-start.2 = (bf16[256,2048]{1,0:T(8,128)(2,1)}, bf16[256,2048]{1,0:T(8,128)(2,1)}, u32[]{:S(2)}, u32[]{:S(2)}) collective-permute-start(bf16[256,2048]{1,0:T(8,128)(2,1)} %get-tuple-element.102), channel_id=1, source_target_pairs={{8,0},{12,4},{16,8},{20,12},{24,16},{28,20},{32,24},{36,28},{40,32... | collective-permute-start | bytes 3145736 | tf_op jit(solution)/shard_map/ppermute | solution.py:19
  359.5 134.8 %collective-permute-start = (bf16[128,2048]{1,0:T(8,128)(2,1)}, bf16[128,2048]{1,0:T(8,128)(2,1)}, u32[]{:S(2)}, u32[]{:S(2)}) collective-permute-start(bf16[128,2048]{1,0:T(8,128)(2,1)} %slice.138), channel_id=1, source_target_pairs={{16,0},{20,4},{24,8},{28,12},{32,16},{36,20},{40,24},{44,28},{48,3... | collective-permute-start | bytes 1572872 | tf_op jit(solution)/shard_map/ppermute | solution.py:19
  361.4 207.7 %collective-permute-start.1 = (bf16[256,2048]{1,0:T(8,128)(2,1)}, bf16[256,2048]{1,0:T(8,128)(2,1)}, u32[]{:S(2)}, u32[]{:S(2)}) collective-permute-start(bf16[256,2048]{1,0:T(8,128)(2,1)} %get-tuple-element.100), channel_id=1, source_target_pairs={{12,0},{16,4},{20,8},{24,12},{28,16},{32,20},{36,24},{40,28},{44,3... | collective-permute-start | bytes 3145736 | tf_op jit(solution)/shard_map/ppermute | solution.py:19
  363.4 128.8 %copy-start.3 = (bf16[128,2048]{1,0:T(8,128)(2,1)}, bf16[128,2048]{1,0:T(8,128)(2,1)S(1)}, u32[]{:S(2)}) copy-start(bf16[128,2048]{1,0:T(8,128)(2,1)S(1)} %collective-permute-done.6) | copy-start | bytes 1572868
  363.6 128.7 %collective-permute-start.7 = (bf16[128,2048]{1,0:T(8,128)(2,1)S(1)}, bf16[128,2048]{1,0:T(8,128)(2,1)S(1)}, u32[]{:S(2)}, u32[]{:S(2)}) collective-permute-start(bf16[128,2048]{1,0:T(8,128)(2,1)S(1)} %fusion.11), channel_id=1, source_target_pairs={{8,0},{12,4},{16,8},{20,12},{24,16},{28,20},{0,24},{4,28},{40,32},... | collective-permute-start | bytes 1572872 | tf_op jit(solution)/shard_map/ppermute | solution.py:281
  492.2 2.1 copy-start.8
  493.2 22.1 %collective-permute-start.8 = (bf16[128,2048]{1,0:T(8,128)(2,1)}, bf16[128,2048]{1,0:T(8,128)(2,1)}, u32[]{:S(2)}, u32[]{:S(2)}) collective-permute-start(bf16[128,2048]{1,0:T(8,128)(2,1)} %fusion.12), channel_id=1, source_target_pairs={{4,0},{8,4},{12,8},{16,12},{20,16},{24,20},{28,24},{0,28},{36,32},... | collective-permute-start | bytes 1572872 | tf_op jit(solution)/shard_map/ppermute | solution.py:281
  494.3 21.0 %copy-start.4 = (bf16[128,2048]{1,0:T(8,128)(2,1)S(1)}, bf16[128,2048]{1,0:T(8,128)(2,1)}, u32[]{:S(2)}) copy-start(bf16[128,2048]{1,0:T(8,128)(2,1)} %copy-done.3) | copy-start | bytes 1572868
  494.3 21.0 %copy-start.9 = (bf16[128,2048]{1,0:T(8,128)(2,1)S(1)}, bf16[128,2048]{1,0:T(8,128)(2,1)}, u32[]{:S(2)}) copy-start(bf16[128,2048]{1,0:T(8,128)(2,1)} %copy-done.8) | copy-start | bytes 1572868
  494.3 100.6 %copy-start.1 = (bf16[256,4096]{1,0:T(8,128)(2,1)S(1)}, bf16[256,4096]{1,0:T(8,128)(2,1)}, u32[]{:S(2)}) copy-start(bf16[256,4096]{1,0:T(8,128)(2,1)} %param.23) | copy-start | bytes 6291460
Sparse Core Ops, SparseCore 0:
  188.5 404.3 reduce-scatter.1

commit v7 on v6

--- a/solution.py
+++ b/solution.py
@@ -172,6 +172,40 @@
     )(ctl, kv)
 
 
+def forward_kernel(scale, q_ref, k_ref, v_ref, bias_ref, o_ref):
+    scores = lax.dot_general(
+        q_ref[...], k_ref[...], (((1,), (1,)), ((), ())), preferred_element_type=jnp.float32
+    )
+    scores = scores * scale + bias_ref[...]
+    row_top = jnp.max(scores, axis=1, keepdims=True)
+    log_total = row_top + jnp.log(jnp.sum(jnp.exp(scores - row_top), axis=1, keepdims=True))
+    probs_low = jnp.exp(scores - log_total).astype(jnp.bfloat16)
+    o_ref[...] = jnp.dot(probs_low, v_ref[...], preferred_element_type=jnp.float32).astype(o_ref.dtype)
+
+
+def attention_out(queries, all_kv, bias, scale):
+    rows, width = queries.shape
+    keys_total = all_kv.shape[0]
+    heads_here = width // HD
+    return pl.pallas_call(
+        functools.partial(forward_kernel, scale),
+        out_shape=jax.ShapeDtypeStruct((rows, width), jnp.bfloat16),
+        grid=(heads_here,),
+        in_specs=[
+            pl.BlockSpec((rows, HD), lambda h: (0, h)),
+            pl.BlockSpec((keys_total, HD), lambda h: (0, h)),
+            pl.BlockSpec((keys_total, HD), lambda h: (0, h + heads_here)),
+            pl.BlockSpec((rows, keys_total), lambda h: (0, 0)),
+        ],
+        out_specs=pl.BlockSpec((rows, HD), lambda h: (0, h)),
+        cost_estimate=pl.CostEstimate(
+            flops=4 * rows * keys_total * width,
+            transcendentals=2 * rows * keys_total * heads_here,
+            bytes_accessed=2 * (2 * rows * width + 2 * keys_total * width) + 4 * rows * keys_total,
+        ),
+    )(queries, all_kv, all_kv, bias)
+
+
 def local(queries, keys, values, out_grad, proj_weight, layout):
     tok_dev = queries.shape[0]
     width = queries.shape[1]
@@ -245,9 +279,8 @@
     log_total = row_top + jnp.log(jnp.sum(jnp.exp(scores - row_top), axis=-1, keepdims=True))
     probs = jnp.exp(scores - log_total)
     probs_low = probs.astype(jnp.bfloat16)
-    attn_out = jnp.einsum(
-        "hqk,khd->qhd", probs_low, value_rows, preferred_element_type=jnp.float32
-    ).astype(jnp.bfloat16)
+    bias = jnp.where(allowed, 0.0, -jnp.inf).astype(jnp.float32)
+    attn_out = attention_out(queries, all_kv, bias, score_scale).reshape(tok_dev, heads_here, HD)
     delta = jnp.transpose(
         jnp.sum(attn_out.astype(jnp.float32) * grad_rows.astype(jnp.float32), axis=-1)
     )[..., None]

time: 607 us -> 580 us (0.956)
  waiting for transfers between devices: 124 us -> 81 us
  Pallas kernels: 112 us -> 124 us
  starting transfers between devices: 205 us -> 214 us
  matrix products: 63.7 us -> 54.8 us
    reduce_scatter x1, waiting for transfers between devices: 19.4 us -> 0.01 us  [local(): lax.psum_scatter(lax.dot_general(out_grad, attn_out.reshape(tok_dev, widt...]
    ppermute x4, waiting for transfers between devices: 52.4 us -> 33.4 us  [passed_along(): return lax.ppermute(block, axis, route)]
    pallas_call x0 -> x1, Pallas kernels: none -> 12.3 us  [attention_out(): pl.pallas_call(functools.partial(forward_kernel, scale), out_shape=jax.Sh...]
    unnamed x28 -> x33, local copies, waits for them, and re-layouts: 5.24 us -> 13.9 us
    ppermute x3, starting transfers between devices: 126 us -> 135 us  [local(): lax.ppermute(part.astype(jnp.bfloat16), 'seq', route).astype(jnp.float32)]
    dot_general x1 -> x0, matrix products: 8.42 us -> none  [local(): jnp.einsum('hqk,khd->qhd', probs_low, value_rows, preferred_element_type=...]
  transfers between devices with their start and end apart: 10 -> 10, of which waited for: 6 -> 5; matrix products, arithmetic and copies ran while one was open for 12% -> 20% of each run, Pallas kernels for 0% -> 0%
where the time goes in v7:
time: 580 us; the launch traced here: 579 us
  starting transfers between devices  214 us (37%)
  Pallas kernels  124 us (21%)
  waiting for transfers between devices  81 us (14%)
  matrix products  54.8 us (9%)
  local copies, waits for them, and re-layouts  47.7 us (8%)
  other arithmetic  40.9 us (7%)
  between operations  16.4 us (3%)
    ppermute x3, starting transfers between devices, local(): lax.ppermute(part.astype(jnp.bfloat16), 'seq', route).astype(jnp.float32)  135 us
    pallas_call x1, Pallas kernels, exchange(): pl.pallas_call(functools.partial(exchange_kernel, (seq_size, group, spans...  112 us
    ppermute x4, starting transfers between devices, passed_along(): return lax.ppermute(block, axis, route)  73.9 us
    ppermute x4, waiting for transfers between devices, passed_along(): return lax.ppermute(block, axis, route)  33.4 us
    ppermute x3, waiting for transfers between devices, local(): lax.ppermute(part.astype(jnp.bfloat16), 'seq', route).astype(jnp.float32)  27.6 us
    ppermute x2, waiting for transfers between devices, local(): lax.ppermute(send.astype(jnp.bfloat16), 'seq', route).astype(jnp.float32)  19.9 us
    unnamed x33, local copies, waits for them, and re-layouts  13.9 us
    pallas_call x1, Pallas kernels, attention_out(): pl.pallas_call(functools.partial(forward_kernel, scale), out_shape=jax.Sh...  12.3 us
  transfers between devices with their start and end apart: 10, of which 5 were waited for; matrix products, arithmetic and copies ran while one was open for 20% of the time, Pallas kernels for 0%

profile of v7, /device:TPU:40, one launch (start us, length us, event | category | flops | bytes accessed | tf_op | source)
XLA Modules:
  0.0 579.1 jit_solution(10160762727411694919)
XLA Ops:
  7.2 1.4 slice.117
  10.7 1.1 constant_dynamic-update-slice_fusion.1
  14.4 2.2 copy.90
  17.6 1.1 constant_dynamic-update-slice_fusion.kv_ref
  18.7 112.1 %shard_map.108 = (bf16[896,2048]{1,0:T(8,128)(2,1)}, bf16[4,128,2048]{2,1,0:T(8,128)(2,1)S(1)}) custom-call(s32[2]{0:T(128)S(1)} %pad_add_fusion.1.ctl_ref, bf16[256,2048]{1,0:T(8,128)(2,1)S(1)} %constant_dynamic-update-slice_fusion.kv_ref), custom_call_target="tpu_custom_call" | custom-call | tf_op jit(solution)/shard_map/pallas_call | solution.py:145
  130.8 5.6 pad_maximum_fusion.1.k_ref.v_ref
  136.5 1.6 broadcast_select_fusion.1
  138.1 12.3 %shard_map.109 = bf16[256,1024]{1,0:T(8,128)(2,1)} custom-call(bf16[256,1024]{1,0:T(8,128)(2,1)} %q_ref.1, bf16[1664,2048]{1,0:T(8,128)(2,1)} %pad_maximum_fusion.1.k_ref.v_ref, bf16[1664,2048]{1,0:T(8,128)(2,1)} %pad_maximum_fusion.1.k_ref.v_ref, f32[256,1664]{1,0:T(8,128)} %get-tuple-element.102.bias_ref), custom_call_target="tpu_custom_call" | custom-call | flops 1744830464 | bytes 9568256 | tf_op jit(solution)/shard_map/pallas_call | solution.py:190
  150.3 9.2 %convolution_bitcast_fusion = f32[4096,1024]{0,1:T(8,128)} fusion(bf16[256,1024]{1,0:T(8,128)(2,1)} %shard_map.109, bf16[256,4096]{1,0:T(8,128)(2,1)S(1)} %copy-done), kind=kOutput, calls=%fused_computation.16 | convolution fusion | flops 2147483648 | bytes 19398656 | tf_op jit(solution)/shard_map/dot_general | solution.py:334
  159.5 1.0 copy-done.7
  160.6 1.0 copy.113
  161.6 7.4 %slice_bitcast_fusion = (bf16[208,8,8,128]{3,2,1,0:T(8,128)(2,1)}, bf16[1664,1024]{1,0:T(8,128)(2,1)}) fusion(bf16[1664,2048]{1,0:T(8,128)(2,1)} %pad_maximum_fusion.1.k_ref.v_ref), kind=kLoop, calls=%fused_computation.25 | loop fusion | bytes 13631488
  168.9 5.7 copy.112
  174.6 1.1 copy.91
  175.8 1.2 copy.117
  177.0 5.8 fusion.16
  183.2 1.6 multiply_reduce_fusion
  184.8 9.4 %fusion.2 = (f32[8,256]{1,0:T(8,128)S(1)}, f32[8,1664,256]{2,1,0:T(8,128)}) fusion(pred[256,1664]{0,1:T(8,128)(4,1)S(1)} %copy.91, bf16[1664,8,128]{0,2,1:T(8,128)(2,1)} %bitcast.81, bf16[256,8,128]{0,2,1:T(8,128)(2,1)S(1)} %bitcast.86), kind=kOutput, calls=%fused_computation.15 | convolution fusion | flops 882636800 | bytes 17997824 | tf_op jit(solution)/shard_map/qhd,khd->hqk/dot_general | solution.py:274
  194.2 7.6 %exponential_reduce_fusion = f32[8,256]{1,0:T(8,128)S(1)} fusion(f32[8,1664,256]{2,1,0:T(8,128)} %get-tuple-element.114, f32[8,256]{1,0:T(8,128)S(1)} %get-tuple-element.113, pred[256,1664]{0,1:T(8,128)(4,1)S(1)} %copy.91), kind=kLoop, calls=%fused_computation.13 | loop fusion | flops 13629440 | bytes 14073856 | tf_op jit(solution)/shard_map/reduce_sum | solution.py:279
  201.9 11.2 %fusion.3 = f32[8,128,1664]{2,1,0:T(8,128)} fusion(bf16[256,8,128]{0,2,1:T(8,128)(2,1)S(1)} %copy.102, f32[8,1664,256]{2,1,0:T(8,128)} %get-tuple-element.114, f32[8,256]{1,0:T(8,128)S(1)} %log_add_fusion, pred[256,1664]{0,1:T(8,128)(4,1)S(1)} %copy.91), kind=kOutput, calls=%fused_computation.17 | convolution fusion | flops 886046720 | bytes 21405696 | tf_op jit(solution)/shard_map/hqk,qhd->khd/dot_general | solution.py:293
  213.1 7.7 %copy.105 = f32[1664,1024]{1,0:T(8,128)} copy(f32[1664,1024]{0,1:T(8,128)} %bitcast.84) | data formatting | bytes 13631488 | tf_op jit(solution)/shard_map/reshape | solution.py:297
  220.8 9.1 %multiply_convert_fusion = bf16[8,256,1664]{1,2,0:T(8,128)(2,1)S(1)} fusion(f32[8,1664,256]{2,1,0:T(8,128)} %get-tuple-element.114, f32[8,256]{1,0:T(8,128)S(1)} %copy.96, f32[8,256]{1,0:T(8,128)S(1)} %log_add_fusion, pred[256,1664]{0,1:T(8,128)(4,1)S(1)} %copy.91, bf16[256,8,128]{0,2,1:T(8,128)(2,1)S(1)} %copy.102, ...), kind=kOutput, calls=%fused_computation.11 | convolution fusion | flops 896270336 | bytes 24821760 | tf_op jit(solution)/shard_map/qhd,khd->hqk/dot_general | solution.py:287
  229.9 5.0 fusion.27
  234.9 7.7 %copy.104 = f32[1664,1024]{1,0:T(8,128)} copy(f32[1664,1024]{0,1:T(8,128)} %bitcast.83) | data formatting | bytes 13631488 | tf_op jit(solution)/shard_map/reshape | solution.py:297
  242.6 2.5 select_convert_fusion
  245.1 4.2 collective-permute-start.4
  249.3 4.7 broadcast_select_fusion
  254.0 15.4 %collective-permute-done.4 = bf16[2,128,2048]{2,1,0:T(8,128)(2,1)S(1)} collective-permute-done((bf16[2,128,2048]{2,1,0:T(8,128)(2,1)S(1)}, bf16[2,128,2048]{2,1,0:T(8,128)(2,1)S(1)}, u32[]{:S(2)}, u32[]{:S(2)}) %collective-permute-start.4) | collective-permute-done | bytes 1048608 | tf_op jit(solution)/shard_map/ppermute | solution.py:308
  270.8 5.8 %fusion = bf16[1664,2048]{1,0:T(8,128)(2,1)S(1)} fusion(f32[1664,1024]{1,0:T(8,128)} %copy.105, f32[1664,1024]{1,0:T(8,128)} %copy.104), kind=kLoop, calls=%fused_computation.9 | loop fusion | flops 13631488 | bytes 20447232 | tf_op jit(solution)/shard_map/convert.4
  276.6 4.6 collective-permute-done.5
  282.1 15.9 %collective-permute-start.6 = (bf16[128,2048]{1,0:T(8,128)(2,1)}, bf16[128,2048]{1,0:T(8,128)(2,1)S(1)}, u32[]{:S(2)}, u32[]{:S(2)}) collective-permute-start(bf16[128,2048]{1,0:T(8,128)(2,1)} %get-tuple-element.100), channel_id=1, source_target_pairs={{16,0},{20,4},{24,8},{28,12},{0,16},{4,20},{8,24},{12,28},{48,32},... | collective-permute-start | bytes 1572872 | tf_op jit(solution)/shard_map/ppermute | solution.py:314
  298.1 1.7 fusion.25
  299.8 52.7 %collective-permute-start.3 = (bf16[256,2048]{1,0:T(8,128)(2,1)}, bf16[256,2048]{1,0:T(8,128)(2,1)}, u32[]{:S(2)}, u32[]{:S(2)}) collective-permute-start(bf16[256,2048]{1,0:T(8,128)(2,1)} %get-tuple-element.107), channel_id=1, source_target_pairs={{4,0},{8,4},{12,8},{16,12},{20,16},{24,20},{28,24},{32,28},{36,32}... | collective-permute-start | bytes 3145736 | tf_op jit(solution)/shard_map/ppermute | solution.py:19
  352.5 17.4 %collective-permute-start.2 = (bf16[256,2048]{1,0:T(8,128)(2,1)}, bf16[256,2048]{1,0:T(8,128)(2,1)}, u32[]{:S(2)}, u32[]{:S(2)}) collective-permute-start(bf16[256,2048]{1,0:T(8,128)(2,1)} %get-tuple-element.108), channel_id=1, source_target_pairs={{8,0},{12,4},{16,8},{20,12},{24,16},{28,20},{32,24},{36,28},{40,32... | collective-permute-start | bytes 3145736 | tf_op jit(solution)/shard_map/ppermute | solution.py:19
  370.7 1.9 collective-permute-start
  372.6 1.9 collective-permute-start.1
  374.8 118.8 %collective-permute-start.7 = (bf16[128,2048]{1,0:T(8,128)(2,1)S(1)}, bf16[128,2048]{1,0:T(8,128)(2,1)S(1)}, u32[]{:S(2)}, u32[]{:S(2)}) collective-permute-start(bf16[128,2048]{1,0:T(8,128)(2,1)S(1)} %fusion.20), channel_id=1, source_target_pairs={{8,0},{12,4},{16,8},{20,12},{24,16},{28,20},{0,24},{4,28},{40,32},... | collective-permute-start | bytes 1572872 | tf_op jit(solution)/shard_map/ppermute | solution.py:314
  493.5 5.1 convolution_convert_fusion
  498.7 17.5 %collective-permute-done.7 = bf16[128,2048]{1,0:T(8,128)(2,1)S(1)} collective-permute-done((bf16[128,2048]{1,0:T(8,128)(2,1)S(1)}, bf16[128,2048]{1,0:T(8,128)(2,1)S(1)}, u32[]{:S(2)}, u32[]{:S(2)}) %collective-permute-start.7) | collective-permute-done | bytes 524320 | tf_op jit(solution)/shard_map/ppermute | solution.py:314
  516.2 1.0 fusion.21
  517.3 1.0 copy.106
  518.3 2.6 fusion.19
  520.9 10.1 %collective-permute-done.8 = bf16[128,2048]{1,0:T(8,128)(2,1)} collective-permute-done((bf16[128,2048]{1,0:T(8,128)(2,1)}, bf16[128,2048]{1,0:T(8,128)(2,1)}, u32[]{:S(2)}, u32[]{:S(2)}) %collective-permute-start.8) | collective-permute-done | bytes 524320 | tf_op jit(solution)/shard_map/ppermute | solution.py:314
  531.0 1.4 add_select_fusion
  532.4 33.4 %collective-permute-done.1 = bf16[256,2048]{1,0:T(8,128)(2,1)} collective-permute-done((bf16[256,2048]{1,0:T(8,128)(2,1)}, bf16[256,2048]{1,0:T(8,128)(2,1)}, u32[]{:S(2)}, u32[]{:S(2)}) %collective-permute-start.1) | collective-permute-done | bytes 1048608 | tf_op jit(solution)/shard_map/ppermute | solution.py:19
  565.8 3.3 fusion.15
  569.1 1.0 fusion.26
  570.2 2.0 copy.107
  (65 shorter events, 7.6 us)
Async XLA Ops:
  7.2 143.2 %copy-start = (bf16[256,4096]{1,0:T(8,128)(2,1)S(1)}, bf16[256,4096]{1,0:T(8,128)(2,1)}, u32[]{:S(2)}) copy-start(bf16[256,4096]{1,0:T(8,128)(2,1)} %param.23) | copy-start | bytes 6291460
  7.2 563.0 %reduce-scatter.2.cloned.1.call-start = ((), (), s32[]{:S(2)}) async-start(), calls=%async_computation.1 | async-start | bytes 17301504 | tf_op jit(solution)/shard_map/reduce_scatter | solution.py:333
  130.8 5.7 copy-start.10
  130.8 5.6 copy-start.11
  159.5 1.0 copy-start.7
  168.9 6.7 %copy-start.3 = (bf16[256,1024]{1,0:T(8,128)(2,1)S(1)}, bf16[256,1024]{1,0:T(8,128)(2,1)}, u32[]{:S(2)}) copy-start(bf16[256,1024]{1,0:T(8,128)(2,1)} %shard_map.109) | copy-start | bytes 1572868
  177.0 7.9 %copy-start.4 = (bf16[256,1024]{0,1:T(8,128)(2,1)S(1)}, bf16[256,1024]{0,1:T(8,128)(2,1)}, u32[]{:S(2)}) copy-start(bf16[256,1024]{0,1:T(8,128)(2,1)} %copy.113) | copy-start | bytes 1572868
  229.9 5.1 copy-start.2
  245.1 24.3 %collective-permute-start.4 = (bf16[2,128,2048]{2,1,0:T(8,128)(2,1)S(1)}, bf16[2,128,2048]{2,1,0:T(8,128)(2,1)S(1)}, u32[]{:S(2)}, u32[]{:S(2)}) collective-permute-start(bf16[2,128,2048]{2,1,0:T(8,128)(2,1)S(1)} %bitcast.93), channel_id=1, source_target_pairs={{0,64},{4,68},{8,72},{12,76},{16,80},{20,84},{24,88},{28,92},{32,9... | collective-permute-start | bytes 3145736 | tf_op jit(solution)/shard_map/ppermute | solution.py:308
  269.8 11.3 %collective-permute-start.5 = (bf16[1,128,2048]{2,1,0:T(8,128)(2,1)S(1)}, bf16[1,128,2048]{2,1,0:T(8,128)(2,1)S(1)}, u32[]{:S(2)}, u32[]{:S(2)}) collective-permute-start(bf16[1,128,2048]{2,1,0:T(8,128)(2,1)S(1)} %select_convert_fusion.1), channel_id=1, source_target_pairs={{0,32},{4,36},{8,40},{12,44},{16,48},{20,52},{24,56},{28,60},{32,0... | collective-permute-start | bytes 1572872 | tf_op jit(solution)/shard_map/ppermute | solution.py:308
  282.1 92.5 %collective-permute-start.6 = (bf16[128,2048]{1,0:T(8,128)(2,1)}, bf16[128,2048]{1,0:T(8,128)(2,1)S(1)}, u32[]{:S(2)}, u32[]{:S(2)}) collective-permute-start(bf16[128,2048]{1,0:T(8,128)(2,1)} %get-tuple-element.100), channel_id=1, source_target_pairs={{16,0},{20,4},{24,8},{28,12},{0,16},{4,20},{8,24},{12,28},{48,32},... | collective-permute-start | bytes 1572872 | tf_op jit(solution)/shard_map/ppermute | solution.py:314
  299.8 232.6 %collective-permute-start.3 = (bf16[256,2048]{1,0:T(8,128)(2,1)}, bf16[256,2048]{1,0:T(8,128)(2,1)}, u32[]{:S(2)}, u32[]{:S(2)}) collective-permute-start(bf16[256,2048]{1,0:T(8,128)(2,1)} %get-tuple-element.107), channel_id=1, source_target_pairs={{4,0},{8,4},{12,8},{16,12},{20,16},{24,20},{28,24},{32,28},{36,32}... | collective-permute-start | bytes 3145736 | tf_op jit(solution)/shard_map/ppermute | solution.py:19
  352.5 179.9 %collective-permute-start.2 = (bf16[256,2048]{1,0:T(8,128)(2,1)}, bf16[256,2048]{1,0:T(8,128)(2,1)}, u32[]{:S(2)}, u32[]{:S(2)}) collective-permute-start(bf16[256,2048]{1,0:T(8,128)(2,1)} %get-tuple-element.108), channel_id=1, source_target_pairs={{8,0},{12,4},{16,8},{20,12},{24,16},{28,20},{32,24},{36,28},{40,32... | collective-permute-start | bytes 3145736 | tf_op jit(solution)/shard_map/ppermute | solution.py:19
  370.7 147.6 %collective-permute-start = (bf16[128,2048]{1,0:T(8,128)(2,1)}, bf16[128,2048]{1,0:T(8,128)(2,1)}, u32[]{:S(2)}, u32[]{:S(2)}) collective-permute-start(bf16[128,2048]{1,0:T(8,128)(2,1)} %slice.138), channel_id=1, source_target_pairs={{16,0},{20,4},{24,8},{28,12},{32,16},{36,20},{40,24},{44,28},{48,3... | collective-permute-start | bytes 1572872 | tf_op jit(solution)/shard_map/ppermute | solution.py:19
  372.6 193.2 %collective-permute-start.1 = (bf16[256,2048]{1,0:T(8,128)(2,1)}, bf16[256,2048]{1,0:T(8,128)(2,1)}, u32[]{:S(2)}, u32[]{:S(2)}) collective-permute-start(bf16[256,2048]{1,0:T(8,128)(2,1)} %get-tuple-element.106), channel_id=1, source_target_pairs={{12,0},{16,4},{20,8},{24,12},{28,16},{32,20},{36,24},{40,28},{44,3... | collective-permute-start | bytes 3145736 | tf_op jit(solution)/shard_map/ppermute | solution.py:19
  374.6 141.6 %copy-start.5 = (bf16[128,2048]{1,0:T(8,128)(2,1)}, bf16[128,2048]{1,0:T(8,128)(2,1)S(1)}, u32[]{:S(2)}) copy-start(bf16[128,2048]{1,0:T(8,128)(2,1)S(1)} %collective-permute-done.6) | copy-start | bytes 1572868
  374.8 141.4 %collective-permute-start.7 = (bf16[128,2048]{1,0:T(8,128)(2,1)S(1)}, bf16[128,2048]{1,0:T(8,128)(2,1)S(1)}, u32[]{:S(2)}, u32[]{:S(2)}) collective-permute-start(bf16[128,2048]{1,0:T(8,128)(2,1)S(1)} %fusion.20), channel_id=1, source_target_pairs={{8,0},{12,4},{16,8},{20,12},{24,16},{28,20},{0,24},{4,28},{40,32},... | collective-permute-start | bytes 1572872 | tf_op jit(solution)/shard_map/ppermute | solution.py:314
  516.2 2.1 copy-start.8
  517.2 13.8 %collective-permute-start.8 = (bf16[128,2048]{1,0:T(8,128)(2,1)}, bf16[128,2048]{1,0:T(8,128)(2,1)}, u32[]{:S(2)}, u32[]{:S(2)}) collective-permute-start(bf16[128,2048]{1,0:T(8,128)(2,1)} %fusion.21), channel_id=1, source_target_pairs={{4,0},{8,4},{12,8},{16,12},{20,16},{24,20},{28,24},{0,28},{36,32},... | collective-permute-start | bytes 1572872 | tf_op jit(solution)/shard_map/ppermute | solution.py:314
  518.3 12.7 %copy-start.6 = (bf16[128,2048]{1,0:T(8,128)(2,1)S(1)}, bf16[128,2048]{1,0:T(8,128)(2,1)}, u32[]{:S(2)}) copy-start(bf16[128,2048]{1,0:T(8,128)(2,1)} %copy-done.5) | copy-start | bytes 1572868
  518.3 12.7 %copy-start.9 = (bf16[128,2048]{1,0:T(8,128)(2,1)S(1)}, bf16[128,2048]{1,0:T(8,128)(2,1)}, u32[]{:S(2)}) copy-start(bf16[128,2048]{1,0:T(8,128)(2,1)} %copy-done.8) | copy-start | bytes 1572868
  518.3 53.9 %copy-start.1 = (bf16[256,4096]{1,0:T(8,128)(2,1)S(1)}, bf16[256,4096]{1,0:T(8,128)(2,1)}, u32[]{:S(2)}) copy-start(bf16[256,4096]{1,0:T(8,128)(2,1)} %param.23) | copy-start | bytes 6291460
Sparse Core Ops, SparseCore 0:
  159.7 383.3 reduce-scatter.1

commit v8 on v7

--- a/solution.py
+++ b/solution.py
@@ -297,23 +297,30 @@
         [key_part.reshape(-1, width), value_part.reshape(-1, width)], axis=1
     )
 
-    part = grad_kv[pool_blocks * BLK :].reshape(summary_count, BLK, 2 * width)
-    span = groups // 2
-    while span >= 1:
-        half = part.shape[0] // 2
-        upper = (my_group // span) % 2 == 1
-        keep = jnp.where(upper, part[half:], part[:half])
-        send = jnp.where(upper, part[:half], part[half:])
-        route = [(d, d ^ (span * group)) for d in range(seq_size)]
-        part = keep + lax.ppermute(send.astype(jnp.bfloat16), "seq", route).astype(jnp.float32)
-        span //= 2
-    part = part[0]
-    hop = group // 2
-    while hop >= 1:
-        route = [(g * group + (r + hop) % group, g * group + r) for g in range(groups) for r in range(group)]
-        moved = lax.ppermute(part.astype(jnp.bfloat16), "seq", route).astype(jnp.float32)
-        part = jnp.where(rel < hop, part + moved, part)
-        hop //= 2
+    proj_part = lax.dot_general(
+        out_grad,
+        attn_out.reshape(tok_dev, width),
+        (((0,), (0,)), ((), ())),
+        preferred_element_type=jnp.float32,
+    )
+    proj_rows = proj_part.shape[0] // seq_size
+    far_grad = grad_kv[pool_blocks * BLK :].reshape(seq_size, -1, proj_part.shape[1])
+    joined = jnp.concatenate([proj_part.reshape(seq_size, proj_rows, -1), far_grad], axis=1)
+    mine = lax.psum_scatter(
+        joined.reshape(-1, proj_part.shape[1]), "seq", scatter_dimension=0, tiled=True
+    )
+    proj_grad = mine[:proj_rows]
+    chunk = mine[proj_rows:].reshape(1, -1, 2 * width)
+    hop = 1
+    while hop < group:
+        route = [(g * group + r, g * group + (r ^ hop)) for g in range(groups) for r in range(group)]
+        moved = lax.ppermute(chunk, "seq", route)
+        upper = (in_group // hop) % 2 == 1
+        chunk = jnp.where(
+            upper, jnp.concatenate([moved, chunk], 0), jnp.concatenate([chunk, moved], 0)
+        )
+        hop *= 2
+    part = chunk.reshape(BLK, 2 * width)
     own_local = jnp.arange(blocks_dev, dtype=jnp.int32)
     far_here = (rel == 0) & (own_local == sum_local)
     far_add = jnp.where(far_here[:, None, None], part[None], 0.0)
@@ -330,17 +337,6 @@
     total = own_grad.reshape(blocks_dev, BLK, 2 * width) + far_add
     total = total.reshape(tok_dev, 2 * width).astype(jnp.bfloat16)
 
-    proj_grad = lax.psum_scatter(
-        lax.dot_general(
-            out_grad,
-            attn_out.reshape(tok_dev, width),
-            (((0,), (0,)), ((), ())),
-            preferred_element_type=jnp.float32,
-        ),
-        "seq",
-        scatter_dimension=0,
-        tiled=True,
-    )
     return (
         query_grad.reshape(tok_dev, width),
         total[:, :width],

time: 580 us -> 764 us (1.32)
  waiting for transfers between devices: 81 us -> 372 us
  starting transfers between devices: 214 us -> 43.8 us
  local copies, waits for them, and re-layouts: 47.7 us -> 102 us
    reduce_scatter x1, waiting for transfers between devices: 0.01 us -> 361 us  [local(): lax.psum_scatter(joined.reshape(-1, proj_part.shape[1]), 'seq', scatter_d...]
    ppermute x5 -> x3, starting transfers between devices: 140 us -> 8.51 us  [local(): moved = lax.ppermute(chunk, 'seq', route)]
    ppermute x4, starting transfers between devices: 73.9 us -> 35.3 us  [passed_along(): return lax.ppermute(block, axis, route)]
    ppermute x5 -> x3, waiting for transfers between devices: 47.5 us -> 11.6 us  [local(): moved = lax.ppermute(chunk, 'seq', route)]
    ppermute x4, waiting for transfers between devices: 33.4 us -> 0.01 us  [passed_along(): return lax.ppermute(block, axis, route)]
    concatenate x0 -> x1, local copies, waits for them, and re-layouts: none -> 29.3 us  [local(): jnp.concatenate([proj_part.reshape(seq_size, proj_rows, -1), far_grad], a...]
    reshape x0 -> x3, local copies, waits for them, and re-layouts: none -> 19.3 us  [the longest x2 19.3 us: local(): grad_kv[pool_blocks * BLK:].reshape(seq_size, -1, proj_part.shape[1])]
    concatenate x0 -> x3, other arithmetic: none -> 19.1 us  [the longest x1 11.3 us: local(): jnp.concatenate([proj_part.reshape(seq_size, proj_rows, -1), far_grad], a...]
  transfers between devices with their start and end apart: 10 -> 8, of which waited for: 5 -> 3; matrix products, arithmetic and copies ran while one was open for 20% -> 3% of each run, Pallas kernels for 0% -> 0%
where the time goes in v8:
time: 764 us; the launch traced here: 758 us
  waiting for transfers between devices  372 us (49%)
  Pallas kernels  124 us (16%)
  local copies, waits for them, and re-layouts  102 us (13%)
  matrix products  51.8 us (7%)
  other arithmetic  46.9 us (6%)
  starting transfers between devices  43.8 us (6%)
  between operations  16.5 us (2%)
    reduce_scatter x1, waiting for transfers between devices, local(): lax.psum_scatter(joined.reshape(-1, proj_part.shape[1]), 'seq', scatter_d...  361 us
    pallas_call x1, Pallas kernels, exchange(): pl.pallas_call(functools.partial(exchange_kernel, (seq_size, group, spans...  112 us
    ppermute x4, starting transfers between devices, passed_along(): return lax.ppermute(block, axis, route)  35.3 us
    concatenate x1, local copies, waits for them, and re-layouts, local(): jnp.concatenate([proj_part.reshape(seq_size, proj_rows, -1), far_grad], a...  29.3 us
    unnamed x27, local copies, waits for them, and re-layouts  21.3 us
    reshape x2, local copies, waits for them, and re-layouts, local(): grad_kv[pool_blocks * BLK:].reshape(seq_size, -1, proj_part.shape[1])  19.3 us
  transfers between devices with their start and end apart: 8, of which 3 were waited for; matrix products, arithmetic and copies ran while one was open for 3% of the time, Pallas kernels for 0%

profile of v8, /device:TPU:40, one launch (start us, length us, event | category | flops | bytes accessed | tf_op | source)
XLA Modules:
  0.0 757.7 jit_solution(6979594324916705640)
XLA Ops:
  7.2 1.4 slice.105
  10.7 1.1 constant_dynamic-update-slice_fusion.1
  11.9 1.1 constant_dynamic-update-slice_fusion.kv_ref
  13.0 112.2 %shard_map.108 = (bf16[896,2048]{1,0:T(8,128)(2,1)}, bf16[4,128,2048]{2,1,0:T(8,128)(2,1)S(1)}) custom-call(s32[2]{0:T(128)S(1)} %pad_add_fusion.1.ctl_ref, bf16[256,2048]{1,0:T(8,128)(2,1)S(1)} %constant_dynamic-update-slice_fusion.kv_ref), custom_call_target="tpu_custom_call" | custom-call | tf_op jit(solution)/shard_map/pallas_call | solution.py:145
  125.2 3.3 pad_maximum_fusion.2.k_ref.v_ref
  128.4 2.8 copy-done.2
  131.3 4.3 slice_bitcast_fusion
  135.6 5.6 copy.117
  142.4 0.9 copy.94
  143.4 1.6 broadcast_select_fusion
  145.0 0.9 copy.95
  145.9 1.2 copy.118
  147.1 12.3 %shard_map.109 = bf16[256,1024]{1,0:T(8,128)(2,1)} custom-call(bf16[256,1024]{1,0:T(8,128)(2,1)} %q_ref.1, bf16[1664,2048]{1,0:T(8,128)(2,1)} %copy-done.2, bf16[1664,2048]{1,0:T(8,128)(2,1)} %copy-done.2, f32[256,1664]{1,0:T(8,128)} %get-tuple-element.100.bias_ref), custom_call_target="tpu_custom_call" | custom-call | flops 1744830464 | bytes 9568256 | tf_op jit(solution)/shard_map/pallas_call | solution.py:190
  159.4 1.1 convert_bitcast_fusion
  160.6 1.2 copy.122
  161.8 9.6 %convolution_bitcast_fusion = f32[128,8,32,128]{3,1,2,0:T(8,128)} fusion(bf16[256,1024]{1,0:T(8,128)(2,1)} %shard_map.109, bf16[256,4096]{1,0:T(8,128)(2,1)S(1)} %copy-done), kind=kOutput, calls=%fused_computation.15 | convolution fusion | flops 2147483648 | bytes 19398656 | tf_op jit(solution)/shard_map/dot_general | solution.py:300
  171.4 2.4 fusion.15
  174.3 1.6 multiply_reduce_fusion
  175.9 9.4 %fusion.2 = (f32[8,256]{1,0:T(8,128)S(1)}, f32[8,1664,256]{2,1,0:T(8,128)}) fusion(pred[256,1664]{0,1:T(8,128)(4,1)S(1)} %copy.95, bf16[1664,8,128]{0,2,1:T(8,128)(2,1)} %bitcast.76, bf16[256,8,128]{0,2,1:T(8,128)(2,1)S(1)} %bitcast.80), kind=kOutput, calls=%fused_computation.14 | convolution fusion | flops 882636800 | bytes 17997824 | tf_op jit(solution)/shard_map/qhd,khd->hqk/dot_general | solution.py:274
  185.3 7.6 %exponential_reduce_fusion = f32[8,256]{1,0:T(8,128)S(1)} fusion(f32[8,1664,256]{2,1,0:T(8,128)} %get-tuple-element.110, f32[8,256]{1,0:T(8,128)S(1)} %get-tuple-element.109, pred[256,1664]{0,1:T(8,128)(4,1)S(1)} %copy.95), kind=kLoop, calls=%fused_computation.12 | loop fusion | flops 13629440 | bytes 14073856 | tf_op jit(solution)/shard_map/reduce_sum | solution.py:279
  192.9 11.4 %fusion.3 = f32[8,128,1664]{2,1,0:T(8,128)} fusion(bf16[256,8,128]{0,2,1:T(8,128)(2,1)S(1)} %copy.106, f32[8,1664,256]{2,1,0:T(8,128)} %get-tuple-element.110, f32[8,256]{1,0:T(8,128)S(1)} %log_add_fusion, pred[256,1664]{0,1:T(8,128)(4,1)S(1)} %copy.95), kind=kOutput, calls=%fused_computation.16 | convolution fusion | flops 886046720 | bytes 21405696 | tf_op jit(solution)/shard_map/hqk,qhd->khd/dot_general | solution.py:293
  204.3 7.6 %copy.109 = f32[1664,1024]{1,0:T(8,128)} copy(f32[1664,1024]{0,1:T(8,128)} %bitcast.79) | data formatting | bytes 13631488 | tf_op jit(solution)/shard_map/reshape | solution.py:297
  212.0 9.0 %multiply_convert_fusion = bf16[8,256,1664]{1,2,0:T(8,128)(2,1)S(1)} fusion(f32[8,1664,256]{2,1,0:T(8,128)} %get-tuple-element.110, f32[8,256]{1,0:T(8,128)S(1)} %copy.100, f32[8,256]{1,0:T(8,128)S(1)} %log_add_fusion, pred[256,1664]{0,1:T(8,128)(4,1)S(1)} %copy.95, bf16[256,8,128]{0,2,1:T(8,128)(2,1)S(1)} %copy.106, ...), kind=kOutput, calls=%fused_computation.10 | convolution fusion | flops 896270336 | bytes 24821760 | tf_op jit(solution)/shard_map/qhd,khd->hqk/dot_general | solution.py:287
  221.0 4.9 fusion.24
  225.9 7.6 %copy.108 = f32[1664,1024]{1,0:T(8,128)} copy(f32[1664,1024]{0,1:T(8,128)} %bitcast.78) | data formatting | bytes 13631488 | tf_op jit(solution)/shard_map/reshape | solution.py:297
  233.6 4.7 fusion.9
  238.2 5.0 reshape.214
  243.2 14.3 %copy.110 = f32[32,32,1024]{1,0,2:T(8,128)} copy(f32[32,32,1024]{2,1,0:T(8,128)} %reshape.214) | data formatting | bytes 8388608 | tf_op jit(solution)/shard_map/reshape | solution.py:307
  257.5 9.8 %copy.123 = f32[128,8,32,128]{3,2,1,0:T(8,128)S(1)} copy(f32[128,8,32,128]{3,1,2,0:T(8,128)} %convolution_bitcast_fusion) | data formatting | bytes 33554432
  268.2 11.3 %pad_maximum_fusion = f32[32,160,1024]{1,0,2:T(8,128)} fusion(f32[32,32,1024]{1,0,2:T(8,128)S(1)} %copy-done.3, f32[32,128,1024]{1,0,2:T(8,128)S(1)} %bitcast.75), kind=kLoop, calls=%fused_computation | loop fusion | flops 5242880 | bytes 41943040 | tf_op jit(solution)/shard_map/concatenate | solution.py:308
  279.5 29.3 %copy.111 = f32[32,160,1024]{2,1,0:T(8,128)} copy(f32[32,160,1024]{1,0,2:T(8,128)} %pad_maximum_fusion) | data formatting | bytes 41943040 | tf_op jit(solution)/shard_map/concatenate | solution.py:308
  308.9 5.7 fusion
  314.6 1.7 fusion.22
  316.3 23.2 %collective-permute-start.3 = (bf16[256,2048]{1,0:T(8,128)(2,1)}, bf16[256,2048]{1,0:T(8,128)(2,1)}, u32[]{:S(2)}, u32[]{:S(2)}) collective-permute-start(bf16[256,2048]{1,0:T(8,128)(2,1)} %get-tuple-element.103), channel_id=1, source_target_pairs={{4,0},{8,4},{12,8},{16,12},{20,16},{24,20},{28,24},{32,28},{36,32}... | collective-permute-start | bytes 3145736 | tf_op jit(solution)/shard_map/ppermute | solution.py:19
  339.5 1.9 collective-permute-start.2
  341.5 7.7 %collective-permute-start = (bf16[128,2048]{1,0:T(8,128)(2,1)S(1)}, bf16[128,2048]{1,0:T(8,128)(2,1)}, u32[]{:S(2)}, u32[]{:S(2)}) collective-permute-start(bf16[128,2048]{1,0:T(8,128)(2,1)S(1)} %slice.125), channel_id=1, source_target_pairs={{16,0},{20,4},{24,8},{28,12},{32,16},{36,20},{40,24},{44,28},{48,3... | collective-permute-start | bytes 1572872 | tf_op jit(solution)/shard_map/ppermute | solution.py:19
  349.2 2.5 collective-permute-start.1
  351.7 360.7 %reduce-scatter.2.cloned.1.call-done = f32[160,1024]{1,0:T(8,128)} async-done(((f32[5120,1024]{1,0:T(8,128)}), f32[160,1024]{1,0:T(8,128)}) %reduce-scatter.2.cloned.1.call-update) | async-done | bytes 655376 | tf_op jit(solution)/shard_map/reduce_scatter | solution.py:309
  712.4 0.9 slice.131
  713.5 5.1 convolution_convert_fusion
  718.7 8.3 %collective-permute-start.5 = (f32[2,16,2048]{2,1,0:T(8,128)S(1)}, f32[2,16,2048]{2,1,0:T(8,128)S(1)}, u32[]{:S(2)}, u32[]{:S(2)}) collective-permute-start(f32[2,16,2048]{2,1,0:T(8,128)S(1)} %maximum_select_fusion.2), channel_id=1, source_target_pairs={{0,8},{4,12},{8,0},{12,4},{16,24},{20,28},{24,16},{28,20},{32,40},... | collective-permute-start | bytes 786440 | tf_op jit(solution)/shard_map/ppermute | solution.py:317
  727.0 3.1 fusion.12
  730.1 3.1 collective-permute-done.5
  733.5 1.0 copy.112
  734.5 2.6 fusion.18
  737.9 8.5 %collective-permute-done.6 = f32[4,16,2048]{2,1,0:T(8,128)S(1)} collective-permute-done((f32[4,16,2048]{2,1,0:T(8,128)S(1)}, f32[4,16,2048]{2,1,0:T(8,128)S(1)}, u32[]{:S(2)}, u32[]{:S(2)}) %collective-permute-start.6) | collective-permute-done | bytes 524320 | tf_op jit(solution)/shard_map/ppermute | solution.py:317
  746.5 3.3 fusion.14
  749.8 1.0 fusion.23
  (60 shorter events, 4.1 us)
Async XLA Ops:
  7.2 154.6 %copy-start = (bf16[256,4096]{1,0:T(8,128)(2,1)S(1)}, bf16[256,4096]{1,0:T(8,128)(2,1)}, u32[]{:S(2)}) copy-start(bf16[256,4096]{1,0:T(8,128)(2,1)} %param.23) | copy-start | bytes 6291460
  7.2 705.2 %reduce-scatter.2.cloned.1.call-start = ((), (), s32[]{:S(2)}) async-start(), calls=%async_computation.1 | async-start | bytes 21626880 | tf_op jit(solution)/shard_map/reduce_scatter | solution.py:309
  128.4 2.8 copy-start.2
  135.6 5.6 copy-start.6
  160.6 10.8 %slice-start = ((s8[8388608]{0:T(1024)(128)(4,1)}), s8[4194304]{0:T(1024)(128)(4,1)S(1)}, s32[]{:S(2)}) async-start(s8[8388608]{0:T(1024)(128)(4,1)} %bitcast.91), calls=%async_computation.2 | async-start | bytes 8388608
  161.8 9.6 %slice-start.1 = ((s8[8388608]{0:T(1024)(128)(4,1)}), s8[4194304]{0:T(1024)(128)(4,1)S(1)}, s32[]{:S(2)}) async-start(s8[8388608]{0:T(1024)(128)(4,1)} %bitcast.91), calls=%async_computation.3 | async-start | bytes 8388608
  221.0 5.0 copy-start.4
  257.5 10.7 %copy-start.3 = (f32[32,32,1024]{1,0,2:T(8,128)S(1)}, f32[32,32,1024]{1,0,2:T(8,128)}, u32[]{:S(2)}) copy-start(f32[32,32,1024]{1,0,2:T(8,128)} %copy.110) | copy-start | bytes 12582916
  316.3 430.2 %collective-permute-start.3 = (bf16[256,2048]{1,0:T(8,128)(2,1)}, bf16[256,2048]{1,0:T(8,128)(2,1)}, u32[]{:S(2)}, u32[]{:S(2)}) collective-permute-start(bf16[256,2048]{1,0:T(8,128)(2,1)} %get-tuple-element.103), channel_id=1, source_target_pairs={{4,0},{8,4},{12,8},{16,12},{20,16},{24,20},{28,24},{32,28},{36,32}... | collective-permute-start | bytes 3145736 | tf_op jit(solution)/shard_map/ppermute | solution.py:19
  339.5 407.0 %collective-permute-start.2 = (bf16[256,2048]{1,0:T(8,128)(2,1)}, bf16[256,2048]{1,0:T(8,128)(2,1)}, u32[]{:S(2)}, u32[]{:S(2)}) collective-permute-start(bf16[256,2048]{1,0:T(8,128)(2,1)} %get-tuple-element.104), channel_id=1, source_target_pairs={{8,0},{12,4},{16,8},{20,12},{24,16},{28,20},{32,24},{36,28},{40,32... | collective-permute-start | bytes 3145736 | tf_op jit(solution)/shard_map/ppermute | solution.py:19
  341.5 393.0 %collective-permute-start = (bf16[128,2048]{1,0:T(8,128)(2,1)S(1)}, bf16[128,2048]{1,0:T(8,128)(2,1)}, u32[]{:S(2)}, u32[]{:S(2)}) collective-permute-start(bf16[128,2048]{1,0:T(8,128)(2,1)S(1)} %slice.125), channel_id=1, source_target_pairs={{16,0},{20,4},{24,8},{28,12},{32,16},{36,20},{40,24},{44,28},{48,3... | collective-permute-start | bytes 1572872 | tf_op jit(solution)/shard_map/ppermute | solution.py:19
  349.2 397.3 %collective-permute-start.1 = (bf16[256,2048]{1,0:T(8,128)(2,1)}, bf16[256,2048]{1,0:T(8,128)(2,1)}, u32[]{:S(2)}, u32[]{:S(2)}) collective-permute-start(bf16[256,2048]{1,0:T(8,128)(2,1)} %get-tuple-element.102), channel_id=1, source_target_pairs={{12,0},{16,4},{20,8},{24,12},{28,16},{32,20},{36,24},{40,28},{44,3... | collective-permute-start | bytes 3145736 | tf_op jit(solution)/shard_map/ppermute | solution.py:19
  713.4 5.3 collective-permute-start.4
  718.7 14.6 %collective-permute-start.5 = (f32[2,16,2048]{2,1,0:T(8,128)S(1)}, f32[2,16,2048]{2,1,0:T(8,128)S(1)}, u32[]{:S(2)}, u32[]{:S(2)}) collective-permute-start(f32[2,16,2048]{2,1,0:T(8,128)S(1)} %maximum_select_fusion.2), channel_id=1, source_target_pairs={{0,8},{4,12},{8,0},{12,4},{16,24},{20,28},{24,16},{28,20},{32,40},... | collective-permute-start | bytes 786440 | tf_op jit(solution)/shard_map/ppermute | solution.py:317
  733.3 13.1 %collective-permute-start.6 = (f32[4,16,2048]{2,1,0:T(8,128)S(1)}, f32[4,16,2048]{2,1,0:T(8,128)S(1)}, u32[]{:S(2)}, u32[]{:S(2)}) collective-permute-start(f32[4,16,2048]{2,1,0:T(8,128)S(1)} %maximum_select_fusion.1), channel_id=1, source_target_pairs={{0,16},{4,20},{8,24},{12,28},{16,0},{20,4},{24,8},{28,12},{32,48},... | collective-permute-start | bytes 1572872 | tf_op jit(solution)/shard_map/ppermute | solution.py:317
  734.5 2.6 copy-start.5
  734.5 16.4 %copy-start.1 = (bf16[256,4096]{1,0:T(8,128)(2,1)S(1)}, bf16[256,4096]{1,0:T(8,128)(2,1)}, u32[]{:S(2)}) copy-start(bf16[256,4096]{1,0:T(8,128)(2,1)} %param.23) | copy-start | bytes 6291460
Sparse Core Ops, SparseCore 0:
  309.0 403.3 reduce-scatter.1

commit v9 on v7

--- a/solution.py
+++ b/solution.py
@@ -63,6 +63,29 @@
     pl.semaphore_wait(barrier, len(partners))
 
     tok_dev = kv_ref.shape[0]
+    window = []
+    starts = {}
+    start = 0
+    for distance in range(len(spans), 0, -1):
+        starts[distance] = start
+        start += spans[distance - 1] * BLK
+
+    def send_window(distance):
+        rows = spans[distance - 1] * BLK
+        copy = pltpu.make_async_remote_copy(
+            src_ref=kv_ref.at[pl.ds(tok_dev - rows, rows)],
+            dst_ref=win_buf.at[pl.ds(starts[distance], rows)],
+            send_sem=sends.at[distance - 1],
+            recv_sem=recvs.at[distance - 1],
+            device_id={"seq": ring(distance)},
+            device_id_type=mesh_id,
+        )
+        copy.start()
+        window.append(copy)
+
+    for distance in range(len(spans), 2, -1):
+        send_window(distance)
+
     mine = kv_ref[0:BLK, :]
     for block in range(1, tok_dev // BLK):
         mine = jnp.where(sum_local == block, kv_ref[block * BLK : (block + 1) * BLK, :], mine)
@@ -87,6 +110,9 @@
         stage += 1
         hop *= 2
 
+    for distance in range(min(2, len(spans)), 0, -1):
+        send_window(distance)
+
     copy = pltpu.make_async_remote_copy(
         src_ref=held,
         dst_ref=cross1,
@@ -101,22 +127,6 @@
     pair[0] = jnp.where(upper, cross1[...], held[...])
     pair[1] = jnp.where(upper, held[...], cross1[...])
     slot += 1
-    window = []
-    start = 0
-    for distance in range(len(spans), 0, -1):
-        rows = spans[distance - 1] * BLK
-        copy = pltpu.make_async_remote_copy(
-            src_ref=kv_ref.at[pl.ds(tok_dev - rows, rows)],
-            dst_ref=win_buf.at[pl.ds(start, rows)],
-            send_sem=sends.at[distance - 1],
-            recv_sem=recvs.at[distance - 1],
-            device_id={"seq": ring(distance)},
-            device_id_type=mesh_id,
-        )
-        copy.start()
-        window.append(copy)
-        start += rows
-
     copy = pltpu.make_async_remote_copy(
         src_ref=pair,
         dst_ref=cross2,

time: 580 us -> 584 us (level)
  starting transfers between devices: 214 us -> 175 us
  Pallas kernels: 124 us -> 159 us
  waiting for transfers between devices: 81 us -> 87.6 us
    pallas_call x1, Pallas kernels: 112 us -> 147 us  [exchange(): pl.pallas_call(functools.partial(exchange_kernel, (seq_size, group, spans...]
    ppermute x4, starting transfers between devices: 73.9 us -> 41.8 us  [passed_along(): return lax.ppermute(block, axis, route)]
    ppermute x3, starting transfers between devices: 135 us -> 109 us  [local(): lax.ppermute(part.astype(jnp.bfloat16), 'seq', route).astype(jnp.float32)]
    ppermute x2, starting transfers between devices: 5.18 us -> 24.2 us  [local(): lax.ppermute(send.astype(jnp.bfloat16), 'seq', route).astype(jnp.float32)]
where the time goes in v9:
time: 584 us; the launch traced here: 582 us
  starting transfers between devices  175 us (30%)
  Pallas kernels  159 us (27%)
  waiting for transfers between devices  87.6 us (15%)
  matrix products  55 us (9%)
  local copies, waits for them, and re-layouts  47.7 us (8%)
  other arithmetic  41.1 us (7%)
  between operations  16.4 us (3%)
    pallas_call x1, Pallas kernels, exchange(): pl.pallas_call(functools.partial(exchange_kernel, (seq_size, group, spans...  147 us
    ppermute x3, starting transfers between devices, local(): lax.ppermute(part.astype(jnp.bfloat16), 'seq', route).astype(jnp.float32)  109 us
    ppermute x4, starting transfers between devices, passed_along(): return lax.ppermute(block, axis, route)  41.8 us
    ppermute x4, waiting for transfers between devices, passed_along(): return lax.ppermute(block, axis, route)  33.8 us
    ppermute x3, waiting for transfers between devices, local(): lax.ppermute(part.astype(jnp.bfloat16), 'seq', route).astype(jnp.float32)  31.7 us
    ppermute x2, starting transfers between devices, local(): lax.ppermute(send.astype(jnp.bfloat16), 'seq', route).astype(jnp.float32)  24.2 us
    ppermute x2, waiting for transfers between devices, local(): lax.ppermute(send.astype(jnp.bfloat16), 'seq', route).astype(jnp.float32)  22.1 us
    unnamed x33, local copies, waits for them, and re-layouts  13.9 us
  transfers between devices with their start and end apart: 10, of which 5 were waited for; matrix products, arithmetic and copies ran while one was open for 20% of the time, Pallas kernels for 0%

profile of v9, /device:TPU:40, one launch (start us, length us, event | category | flops | bytes accessed | tf_op | source)
XLA Modules:
  0.0 581.8 jit_solution(16697988184813761418)
XLA Ops:
  7.2 1.4 slice.117
  10.7 1.1 constant_dynamic-update-slice_fusion.1
  14.4 2.2 copy.90
  17.6 1.1 constant_dynamic-update-slice_fusion.kv_ref
  18.7 146.9 %shard_map.108 = (bf16[896,2048]{1,0:T(8,128)(2,1)}, bf16[4,128,2048]{2,1,0:T(8,128)(2,1)S(1)}) custom-call(s32[2]{0:T(128)S(1)} %pad_add_fusion.1.ctl_ref, bf16[256,2048]{1,0:T(8,128)(2,1)S(1)} %constant_dynamic-update-slice_fusion.kv_ref), custom_call_target="tpu_custom_call" | custom-call | tf_op jit(solution)/shard_map/pallas_call | solution.py:155
  165.6 5.6 pad_maximum_fusion.1.k_ref.v_ref
  171.3 1.6 broadcast_select_fusion.1
  172.8 12.3 %shard_map.109 = bf16[256,1024]{1,0:T(8,128)(2,1)} custom-call(bf16[256,1024]{1,0:T(8,128)(2,1)} %q_ref.1, bf16[1664,2048]{1,0:T(8,128)(2,1)} %pad_maximum_fusion.1.k_ref.v_ref, bf16[1664,2048]{1,0:T(8,128)(2,1)} %pad_maximum_fusion.1.k_ref.v_ref, f32[256,1664]{1,0:T(8,128)} %get-tuple-element.102.bias_ref), custom_call_target="tpu_custom_call" | custom-call | flops 1744830464 | bytes 9568256 | tf_op jit(solution)/shard_map/pallas_call | solution.py:200
  185.1 9.2 %convolution_bitcast_fusion = f32[4096,1024]{0,1:T(8,128)} fusion(bf16[256,1024]{1,0:T(8,128)(2,1)} %shard_map.109, bf16[256,4096]{1,0:T(8,128)(2,1)S(1)} %copy-done), kind=kOutput, calls=%fused_computation.16 | convolution fusion | flops 2147483648 | bytes 19398656 | tf_op jit(solution)/shard_map/dot_general | solution.py:344
  194.3 1.0 copy-done.7
  195.3 1.0 copy.113
  196.3 7.4 %slice_bitcast_fusion = (bf16[208,8,8,128]{3,2,1,0:T(8,128)(2,1)}, bf16[1664,1024]{1,0:T(8,128)(2,1)}) fusion(bf16[1664,2048]{1,0:T(8,128)(2,1)} %pad_maximum_fusion.1.k_ref.v_ref), kind=kLoop, calls=%fused_computation.25 | loop fusion | bytes 13631488
  203.7 5.7 copy.112
  209.4 1.1 copy.91
  210.6 1.2 copy.117
  211.7 5.8 fusion.16
  217.9 1.6 multiply_reduce_fusion
  219.6 9.4 %fusion.2 = (f32[8,256]{1,0:T(8,128)S(1)}, f32[8,1664,256]{2,1,0:T(8,128)}) fusion(pred[256,1664]{0,1:T(8,128)(4,1)S(1)} %copy.91, bf16[1664,8,128]{0,2,1:T(8,128)(2,1)} %bitcast.81, bf16[256,8,128]{0,2,1:T(8,128)(2,1)S(1)} %bitcast.86), kind=kOutput, calls=%fused_computation.15 | convolution fusion | flops 882636800 | bytes 17997824 | tf_op jit(solution)/shard_map/qhd,khd->hqk/dot_general | solution.py:284
  229.0 7.8 %exponential_reduce_fusion = f32[8,256]{1,0:T(8,128)S(1)} fusion(f32[8,1664,256]{2,1,0:T(8,128)} %get-tuple-element.114, f32[8,256]{1,0:T(8,128)S(1)} %get-tuple-element.113, pred[256,1664]{0,1:T(8,128)(4,1)S(1)} %copy.91), kind=kLoop, calls=%fused_computation.13 | loop fusion | flops 13629440 | bytes 14073856 | tf_op jit(solution)/shard_map/reduce_sum | solution.py:289
  236.8 11.4 %fusion.3 = f32[8,128,1664]{2,1,0:T(8,128)} fusion(bf16[256,8,128]{0,2,1:T(8,128)(2,1)S(1)} %copy.102, f32[8,1664,256]{2,1,0:T(8,128)} %get-tuple-element.114, f32[8,256]{1,0:T(8,128)S(1)} %log_add_fusion, pred[256,1664]{0,1:T(8,128)(4,1)S(1)} %copy.91), kind=kOutput, calls=%fused_computation.17 | convolution fusion | flops 886046720 | bytes 21405696 | tf_op jit(solution)/shard_map/hqk,qhd->khd/dot_general | solution.py:303
  248.1 7.7 %copy.105 = f32[1664,1024]{1,0:T(8,128)} copy(f32[1664,1024]{0,1:T(8,128)} %bitcast.84) | data formatting | bytes 13631488 | tf_op jit(solution)/shard_map/reshape | solution.py:307
  255.8 9.1 %multiply_convert_fusion = bf16[8,256,1664]{1,2,0:T(8,128)(2,1)S(1)} fusion(f32[8,1664,256]{2,1,0:T(8,128)} %get-tuple-element.114, f32[8,256]{1,0:T(8,128)S(1)} %copy.96, f32[8,256]{1,0:T(8,128)S(1)} %log_add_fusion, pred[256,1664]{0,1:T(8,128)(4,1)S(1)} %copy.91, bf16[256,8,128]{0,2,1:T(8,128)(2,1)S(1)} %copy.102, ...), kind=kOutput, calls=%fused_computation.11 | convolution fusion | flops 896270336 | bytes 24821760 | tf_op jit(solution)/shard_map/qhd,khd->hqk/dot_general | solution.py:297
  264.9 5.1 fusion.27
  270.0 7.7 %copy.104 = f32[1664,1024]{1,0:T(8,128)} copy(f32[1664,1024]{0,1:T(8,128)} %bitcast.83) | data formatting | bytes 13631488 | tf_op jit(solution)/shard_map/reshape | solution.py:307
  277.7 2.5 select_convert_fusion
  280.2 22.6 %collective-permute-start.4 = (bf16[2,128,2048]{2,1,0:T(8,128)(2,1)S(1)}, bf16[2,128,2048]{2,1,0:T(8,128)(2,1)S(1)}, u32[]{:S(2)}, u32[]{:S(2)}) collective-permute-start(bf16[2,128,2048]{2,1,0:T(8,128)(2,1)S(1)} %bitcast.93), channel_id=1, source_target_pairs={{0,64},{4,68},{8,72},{12,76},{16,80},{20,84},{24,88},{28,92},{32,9... | collective-permute-start | bytes 3145736 | tf_op jit(solution)/shard_map/ppermute | solution.py:318
  302.8 4.8 broadcast_select_fusion
  307.5 17.4 %collective-permute-done.4 = bf16[2,128,2048]{2,1,0:T(8,128)(2,1)S(1)} collective-permute-done((bf16[2,128,2048]{2,1,0:T(8,128)(2,1)S(1)}, bf16[2,128,2048]{2,1,0:T(8,128)(2,1)S(1)}, u32[]{:S(2)}, u32[]{:S(2)}) %collective-permute-start.4) | collective-permute-done | bytes 1048608 | tf_op jit(solution)/shard_map/ppermute | solution.py:318
  325.3 1.6 collective-permute-start.5
  326.9 5.8 fusion
  332.7 4.7 collective-permute-done.5
  338.4 1.7 fusion.25
  340.1 36.0 %collective-permute-start.3 = (bf16[256,2048]{1,0:T(8,128)(2,1)}, bf16[256,2048]{1,0:T(8,128)(2,1)}, u32[]{:S(2)}, u32[]{:S(2)}) collective-permute-start(bf16[256,2048]{1,0:T(8,128)(2,1)} %get-tuple-element.107), channel_id=1, source_target_pairs={{4,0},{8,4},{12,8},{16,12},{20,16},{24,20},{28,24},{32,28},{36,32}... | collective-permute-start | bytes 3145736 | tf_op jit(solution)/shard_map/ppermute | solution.py:19
  376.2 1.9 collective-permute-start.2
  378.9 1.9 collective-permute-start
  380.9 1.9 collective-permute-start.1
  383.0 108.7 %collective-permute-start.7 = (bf16[128,2048]{1,0:T(8,128)(2,1)S(1)}, bf16[128,2048]{1,0:T(8,128)(2,1)S(1)}, u32[]{:S(2)}, u32[]{:S(2)}) collective-permute-start(bf16[128,2048]{1,0:T(8,128)(2,1)S(1)} %fusion.20), channel_id=1, source_target_pairs={{8,0},{12,4},{16,8},{20,12},{24,16},{28,20},{0,24},{4,28},{40,32},... | collective-permute-start | bytes 1572872 | tf_op jit(solution)/shard_map/ppermute | solution.py:324
  491.7 5.2 convolution_convert_fusion
  496.9 13.3 %collective-permute-done.7 = bf16[128,2048]{1,0:T(8,128)(2,1)S(1)} collective-permute-done((bf16[128,2048]{1,0:T(8,128)(2,1)S(1)}, bf16[128,2048]{1,0:T(8,128)(2,1)S(1)}, u32[]{:S(2)}, u32[]{:S(2)}) %collective-permute-start.7) | collective-permute-done | bytes 524320 | tf_op jit(solution)/shard_map/ppermute | solution.py:324
  510.2 1.0 fusion.21
  511.3 1.0 copy.106
  512.3 2.6 fusion.19
  514.9 18.5 %collective-permute-done.8 = bf16[128,2048]{1,0:T(8,128)(2,1)} collective-permute-done((bf16[128,2048]{1,0:T(8,128)(2,1)}, bf16[128,2048]{1,0:T(8,128)(2,1)}, u32[]{:S(2)}, u32[]{:S(2)}) %collective-permute-start.8) | collective-permute-done | bytes 524320 | tf_op jit(solution)/shard_map/ppermute | solution.py:324
  533.4 1.4 add_select_fusion
  534.8 33.8 %collective-permute-done.1 = bf16[256,2048]{1,0:T(8,128)(2,1)} collective-permute-done((bf16[256,2048]{1,0:T(8,128)(2,1)}, bf16[256,2048]{1,0:T(8,128)(2,1)}, u32[]{:S(2)}, u32[]{:S(2)}) %collective-permute-start.1) | collective-permute-done | bytes 1048608 | tf_op jit(solution)/shard_map/ppermute | solution.py:19
  568.6 3.3 fusion.15
  571.9 1.0 fusion.26
  572.9 2.0 copy.107
  (65 shorter events, 6.7 us)
Async XLA Ops:
  7.2 177.9 %copy-start = (bf16[256,4096]{1,0:T(8,128)(2,1)S(1)}, bf16[256,4096]{1,0:T(8,128)(2,1)}, u32[]{:S(2)}) copy-start(bf16[256,4096]{1,0:T(8,128)(2,1)} %param.23) | copy-start | bytes 6291460
  7.2 565.7 %reduce-scatter.2.cloned.1.call-start = ((), (), s32[]{:S(2)}) async-start(), calls=%async_computation.1 | async-start | bytes 17301504 | tf_op jit(solution)/shard_map/reduce_scatter | solution.py:343
  165.6 5.7 copy-start.10
  165.6 5.6 copy-start.11
  194.3 1.0 copy-start.7
  203.7 6.7 %copy-start.3 = (bf16[256,1024]{1,0:T(8,128)(2,1)S(1)}, bf16[256,1024]{1,0:T(8,128)(2,1)}, u32[]{:S(2)}) copy-start(bf16[256,1024]{1,0:T(8,128)(2,1)} %shard_map.109) | copy-start | bytes 1572868
  211.7 7.9 %copy-start.4 = (bf16[256,1024]{0,1:T(8,128)(2,1)S(1)}, bf16[256,1024]{0,1:T(8,128)(2,1)}, u32[]{:S(2)}) copy-start(bf16[256,1024]{0,1:T(8,128)(2,1)} %copy.113) | copy-start | bytes 1572868
  264.9 5.1 copy-start.2
  280.2 44.7 %collective-permute-start.4 = (bf16[2,128,2048]{2,1,0:T(8,128)(2,1)S(1)}, bf16[2,128,2048]{2,1,0:T(8,128)(2,1)S(1)}, u32[]{:S(2)}, u32[]{:S(2)}) collective-permute-start(bf16[2,128,2048]{2,1,0:T(8,128)(2,1)S(1)} %bitcast.93), channel_id=1, source_target_pairs={{0,64},{4,68},{8,72},{12,76},{16,80},{20,84},{24,88},{28,92},{32,9... | collective-permute-start | bytes 3145736 | tf_op jit(solution)/shard_map/ppermute | solution.py:318
  325.3 12.1 %collective-permute-start.5 = (bf16[1,128,2048]{2,1,0:T(8,128)(2,1)S(1)}, bf16[1,128,2048]{2,1,0:T(8,128)(2,1)S(1)}, u32[]{:S(2)}, u32[]{:S(2)}) collective-permute-start(bf16[1,128,2048]{2,1,0:T(8,128)(2,1)S(1)} %select_convert_fusion.1), channel_id=1, source_target_pairs={{0,32},{4,36},{8,40},{12,44},{16,48},{20,52},{24,56},{28,60},{32,0... | collective-permute-start | bytes 1572872 | tf_op jit(solution)/shard_map/ppermute | solution.py:318
  338.4 44.4 %collective-permute-start.6 = (bf16[128,2048]{1,0:T(8,128)(2,1)}, bf16[128,2048]{1,0:T(8,128)(2,1)S(1)}, u32[]{:S(2)}, u32[]{:S(2)}) collective-permute-start(bf16[128,2048]{1,0:T(8,128)(2,1)} %get-tuple-element.100), channel_id=1, source_target_pairs={{16,0},{20,4},{24,8},{28,12},{0,16},{4,20},{8,24},{12,28},{48,32},... | collective-permute-start | bytes 1572872 | tf_op jit(solution)/shard_map/ppermute | solution.py:324
  340.1 194.6 %collective-permute-start.3 = (bf16[256,2048]{1,0:T(8,128)(2,1)}, bf16[256,2048]{1,0:T(8,128)(2,1)}, u32[]{:S(2)}, u32[]{:S(2)}) collective-permute-start(bf16[256,2048]{1,0:T(8,128)(2,1)} %get-tuple-element.107), channel_id=1, source_target_pairs={{4,0},{8,4},{12,8},{16,12},{20,16},{24,20},{28,24},{32,28},{36,32}... | collective-permute-start | bytes 3145736 | tf_op jit(solution)/shard_map/ppermute | solution.py:19
  376.2 158.6 %collective-permute-start.2 = (bf16[256,2048]{1,0:T(8,128)(2,1)}, bf16[256,2048]{1,0:T(8,128)(2,1)}, u32[]{:S(2)}, u32[]{:S(2)}) collective-permute-start(bf16[256,2048]{1,0:T(8,128)(2,1)} %get-tuple-element.108), channel_id=1, source_target_pairs={{8,0},{12,4},{16,8},{20,12},{24,16},{28,20},{32,24},{36,28},{40,32... | collective-permute-start | bytes 3145736 | tf_op jit(solution)/shard_map/ppermute | solution.py:19
  378.9 133.3 %collective-permute-start = (bf16[128,2048]{1,0:T(8,128)(2,1)}, bf16[128,2048]{1,0:T(8,128)(2,1)}, u32[]{:S(2)}, u32[]{:S(2)}) collective-permute-start(bf16[128,2048]{1,0:T(8,128)(2,1)} %slice.138), channel_id=1, source_target_pairs={{16,0},{20,4},{24,8},{28,12},{32,16},{36,20},{40,24},{44,28},{48,3... | collective-permute-start | bytes 1572872 | tf_op jit(solution)/shard_map/ppermute | solution.py:19
  380.9 187.7 %collective-permute-start.1 = (bf16[256,2048]{1,0:T(8,128)(2,1)}, bf16[256,2048]{1,0:T(8,128)(2,1)}, u32[]{:S(2)}, u32[]{:S(2)}) collective-permute-start(bf16[256,2048]{1,0:T(8,128)(2,1)} %get-tuple-element.106), channel_id=1, source_target_pairs={{12,0},{16,4},{20,8},{24,12},{28,16},{32,20},{36,24},{40,28},{44,3... | collective-permute-start | bytes 3145736 | tf_op jit(solution)/shard_map/ppermute | solution.py:19
  382.9 127.3 %copy-start.5 = (bf16[128,2048]{1,0:T(8,128)(2,1)}, bf16[128,2048]{1,0:T(8,128)(2,1)S(1)}, u32[]{:S(2)}) copy-start(bf16[128,2048]{1,0:T(8,128)(2,1)S(1)} %collective-permute-done.6) | copy-start | bytes 1572868
  383.0 127.2 %collective-permute-start.7 = (bf16[128,2048]{1,0:T(8,128)(2,1)S(1)}, bf16[128,2048]{1,0:T(8,128)(2,1)S(1)}, u32[]{:S(2)}, u32[]{:S(2)}) collective-permute-start(bf16[128,2048]{1,0:T(8,128)(2,1)S(1)} %fusion.20), channel_id=1, source_target_pairs={{8,0},{12,4},{16,8},{20,12},{24,16},{28,20},{0,24},{4,28},{40,32},... | collective-permute-start | bytes 1572872 | tf_op jit(solution)/shard_map/ppermute | solution.py:324
  510.2 2.1 copy-start.8
  511.2 22.2 %collective-permute-start.8 = (bf16[128,2048]{1,0:T(8,128)(2,1)}, bf16[128,2048]{1,0:T(8,128)(2,1)}, u32[]{:S(2)}, u32[]{:S(2)}) collective-permute-start(bf16[128,2048]{1,0:T(8,128)(2,1)} %fusion.21), channel_id=1, source_target_pairs={{4,0},{8,4},{12,8},{16,12},{20,16},{24,20},{28,24},{0,28},{36,32},... | collective-permute-start | bytes 1572872 | tf_op jit(solution)/shard_map/ppermute | solution.py:324
  512.3 21.1 %copy-start.6 = (bf16[128,2048]{1,0:T(8,128)(2,1)S(1)}, bf16[128,2048]{1,0:T(8,128)(2,1)}, u32[]{:S(2)}) copy-start(bf16[128,2048]{1,0:T(8,128)(2,1)} %copy-done.5) | copy-start | bytes 1572868
  512.3 21.1 %copy-start.9 = (bf16[128,2048]{1,0:T(8,128)(2,1)S(1)}, bf16[128,2048]{1,0:T(8,128)(2,1)}, u32[]{:S(2)}) copy-start(bf16[128,2048]{1,0:T(8,128)(2,1)} %copy-done.8) | copy-start | bytes 1572868
  512.3 62.7 %copy-start.1 = (bf16[256,4096]{1,0:T(8,128)(2,1)S(1)}, bf16[256,4096]{1,0:T(8,128)(2,1)}, u32[]{:S(2)}) copy-start(bf16[256,4096]{1,0:T(8,128)(2,1)} %param.23) | copy-start | bytes 6291460
Sparse Core Ops, SparseCore 0:
  194.4 343.4 reduce-scatter.1

commit v10 on v9

--- a/solution.py
+++ b/solution.py
@@ -82,9 +82,6 @@
         )
         copy.start()
         window.append(copy)
-
-    for distance in range(len(spans), 2, -1):
-        send_window(distance)
 
     mine = kv_ref[0:BLK, :]
     for block in range(1, tok_dev // BLK):
@@ -110,9 +107,6 @@
         stage += 1
         hop *= 2
 
-    for distance in range(min(2, len(spans)), 0, -1):
-        send_window(distance)
-
     copy = pltpu.make_async_remote_copy(
         src_ref=held,
         dst_ref=cross1,
@@ -137,6 +131,8 @@
     )
     copy.start()
     copy.wait()
+    for distance in range(len(spans), 0, -1):
+        send_window(distance)
     upper = ((my_group // 2) % 2) == 1
     for index in range(2):
         far_out[index] = jnp.where(upper, cross2[index], pair[index])

time: 584 us -> 575 us (0.985)
  Pallas kernels: 159 us -> 144 us
  starting transfers between devices: 175 us -> 184 us
    ppermute x2, starting transfers between devices: 24.2 us -> 5.51 us  [local(): lax.ppermute(send.astype(jnp.bfloat16), 'seq', route).astype(jnp.float32)]
    ppermute x3, starting transfers between devices: 109 us -> 125 us  [local(): lax.ppermute(part.astype(jnp.bfloat16), 'seq', route).astype(jnp.float32)]
    pallas_call x1, Pallas kernels: 147 us -> 132 us  [exchange(): pl.pallas_call(functools.partial(exchange_kernel, (seq_size, group, spans...]
    ppermute x4, starting transfers between devices: 41.8 us -> 53.6 us  [passed_along(): return lax.ppermute(block, axis, route)]
where the time goes in v10:
time: 575 us; the launch traced here: 574 us
  starting transfers between devices  184 us (32%)
  Pallas kernels  144 us (25%)
  waiting for transfers between devices  86.1 us (15%)
  matrix products  54.9 us (10%)
  local copies, waits for them, and re-layouts  47.7 us (8%)
  other arithmetic  41.3 us (7%)
  between operations  16.4 us (3%)
    pallas_call x1, Pallas kernels, exchange(): pl.pallas_call(functools.partial(exchange_kernel, (seq_size, group, spans...  132 us
    ppermute x3, starting transfers between devices, local(): lax.ppermute(part.astype(jnp.bfloat16), 'seq', route).astype(jnp.float32)  125 us
    ppermute x4, starting transfers between devices, passed_along(): return lax.ppermute(block, axis, route)  53.6 us
    ppermute x4, waiting for transfers between devices, passed_along(): return lax.ppermute(block, axis, route)  32 us
    ppermute x3, waiting for transfers between devices, local(): lax.ppermute(part.astype(jnp.bfloat16), 'seq', route).astype(jnp.float32)  30.2 us
    ppermute x2, waiting for transfers between devices, local(): lax.ppermute(send.astype(jnp.bfloat16), 'seq', route).astype(jnp.float32)  23.9 us
    unnamed x33, local copies, waits for them, and re-layouts  13.9 us
    pallas_call x1, Pallas kernels, attention_out(): pl.pallas_call(functools.partial(forward_kernel, scale), out_shape=jax.Sh...  12.3 us
  transfers between devices with their start and end apart: 10, of which 5 were waited for; matrix products, arithmetic and copies ran while one was open for 20% of the time, Pallas kernels for 0%

profile of v10, /device:TPU:40, one launch (start us, length us, event | category | flops | bytes accessed | tf_op | source)
XLA Modules:
  0.0 574.1 jit_solution(10882923611052190624)
XLA Ops:
  7.2 1.4 slice.117
  10.7 1.1 constant_dynamic-update-slice_fusion.1
  14.4 2.2 copy.90
  17.6 1.1 constant_dynamic-update-slice_fusion.kv_ref
  18.7 131.6 %shard_map.108 = (bf16[896,2048]{1,0:T(8,128)(2,1)}, bf16[4,128,2048]{2,1,0:T(8,128)(2,1)S(1)}) custom-call(s32[2]{0:T(128)S(1)} %pad_add_fusion.1.ctl_ref, bf16[256,2048]{1,0:T(8,128)(2,1)S(1)} %constant_dynamic-update-slice_fusion.kv_ref), custom_call_target="tpu_custom_call" | custom-call | tf_op jit(solution)/shard_map/pallas_call | solution.py:151
  150.4 5.6 pad_maximum_fusion.1.k_ref.v_ref
  156.0 1.6 broadcast_select_fusion.1
  157.6 12.3 %shard_map.109 = bf16[256,1024]{1,0:T(8,128)(2,1)} custom-call(bf16[256,1024]{1,0:T(8,128)(2,1)} %q_ref.1, bf16[1664,2048]{1,0:T(8,128)(2,1)} %pad_maximum_fusion.1.k_ref.v_ref, bf16[1664,2048]{1,0:T(8,128)(2,1)} %pad_maximum_fusion.1.k_ref.v_ref, f32[256,1664]{1,0:T(8,128)} %get-tuple-element.102.bias_ref), custom_call_target="tpu_custom_call" | custom-call | flops 1744830464 | bytes 9568256 | tf_op jit(solution)/shard_map/pallas_call | solution.py:196
  169.8 9.2 %convolution_bitcast_fusion = f32[4096,1024]{0,1:T(8,128)} fusion(bf16[256,1024]{1,0:T(8,128)(2,1)} %shard_map.109, bf16[256,4096]{1,0:T(8,128)(2,1)S(1)} %copy-done), kind=kOutput, calls=%fused_computation.16 | convolution fusion | flops 2147483648 | bytes 19398656 | tf_op jit(solution)/shard_map/dot_general | solution.py:340
  179.0 1.0 copy-done.7
  181.1 7.4 %slice_bitcast_fusion = (bf16[208,8,8,128]{3,2,1,0:T(8,128)(2,1)}, bf16[1664,1024]{1,0:T(8,128)(2,1)}) fusion(bf16[1664,2048]{1,0:T(8,128)(2,1)} %pad_maximum_fusion.1.k_ref.v_ref), kind=kLoop, calls=%fused_computation.25 | loop fusion | bytes 13631488
  188.4 5.7 copy.112
  194.1 1.1 copy.91
  195.3 1.2 copy.117
  196.5 5.8 %fusion.16 = bf16[32,8,8,128]{3,1,2,0:T(8,128)(2,1)S(1)} fusion(bf16[256,4096]{1,0:T(8,128)(2,1)S(1)} %copy-done, bf16[4096,1024]{1,0:T(8,128)(2,1)} %param.24), kind=kOutput, calls=%fused_computation.40 | convolution fusion | flops 2147745792 | bytes 11010048 | tf_op jit(solution)/shard_map/dot_general | solution.py:233
  202.7 1.6 multiply_reduce_fusion
  204.3 9.4 %fusion.2 = (f32[8,256]{1,0:T(8,128)S(1)}, f32[8,1664,256]{2,1,0:T(8,128)}) fusion(pred[256,1664]{0,1:T(8,128)(4,1)S(1)} %copy.91, bf16[1664,8,128]{0,2,1:T(8,128)(2,1)} %bitcast.81, bf16[256,8,128]{0,2,1:T(8,128)(2,1)S(1)} %bitcast.86), kind=kOutput, calls=%fused_computation.15 | convolution fusion | flops 882636800 | bytes 17997824 | tf_op jit(solution)/shard_map/qhd,khd->hqk/dot_general | solution.py:280
  213.7 8.0 %exponential_reduce_fusion = f32[8,256]{1,0:T(8,128)S(1)} fusion(f32[8,1664,256]{2,1,0:T(8,128)} %get-tuple-element.114, f32[8,256]{1,0:T(8,128)S(1)} %get-tuple-element.113, pred[256,1664]{0,1:T(8,128)(4,1)S(1)} %copy.91), kind=kLoop, calls=%fused_computation.13 | loop fusion | flops 13629440 | bytes 14073856 | tf_op jit(solution)/shard_map/reduce_sum | solution.py:285
  221.8 11.4 %fusion.3 = f32[8,128,1664]{2,1,0:T(8,128)} fusion(bf16[256,8,128]{0,2,1:T(8,128)(2,1)S(1)} %copy.102, f32[8,1664,256]{2,1,0:T(8,128)} %get-tuple-element.114, f32[8,256]{1,0:T(8,128)S(1)} %log_add_fusion, pred[256,1664]{0,1:T(8,128)(4,1)S(1)} %copy.91), kind=kOutput, calls=%fused_computation.17 | convolution fusion | flops 886046720 | bytes 21405696 | tf_op jit(solution)/shard_map/hqk,qhd->khd/dot_general | solution.py:299
  233.1 7.7 %copy.105 = f32[1664,1024]{1,0:T(8,128)} copy(f32[1664,1024]{0,1:T(8,128)} %bitcast.84) | data formatting | bytes 13631488 | tf_op jit(solution)/shard_map/reshape | solution.py:303
  240.8 9.1 %multiply_convert_fusion = bf16[8,256,1664]{1,2,0:T(8,128)(2,1)S(1)} fusion(f32[8,1664,256]{2,1,0:T(8,128)} %get-tuple-element.114, f32[8,256]{1,0:T(8,128)S(1)} %copy.96, f32[8,256]{1,0:T(8,128)S(1)} %log_add_fusion, pred[256,1664]{0,1:T(8,128)(4,1)S(1)} %copy.91, bf16[256,8,128]{0,2,1:T(8,128)(2,1)S(1)} %copy.102, ...), kind=kOutput, calls=%fused_computation.11 | convolution fusion | flops 896270336 | bytes 24821760 | tf_op jit(solution)/shard_map/qhd,khd->hqk/dot_general | solution.py:293
  250.0 5.0 fusion.27
  255.0 7.7 %copy.104 = f32[1664,1024]{1,0:T(8,128)} copy(f32[1664,1024]{0,1:T(8,128)} %bitcast.83) | data formatting | bytes 13631488 | tf_op jit(solution)/shard_map/reshape | solution.py:303
  262.7 2.5 select_convert_fusion
  265.2 4.0 collective-permute-start.4
  269.2 4.7 broadcast_select_fusion
  273.9 18.2 %collective-permute-done.4 = bf16[2,128,2048]{2,1,0:T(8,128)(2,1)S(1)} collective-permute-done((bf16[2,128,2048]{2,1,0:T(8,128)(2,1)S(1)}, bf16[2,128,2048]{2,1,0:T(8,128)(2,1)S(1)}, u32[]{:S(2)}, u32[]{:S(2)}) %collective-permute-start.4) | collective-permute-done | bytes 1048608 | tf_op jit(solution)/shard_map/ppermute | solution.py:314
  292.5 1.5 collective-permute-start.5
  294.0 5.8 %fusion = bf16[1664,2048]{1,0:T(8,128)(2,1)S(1)} fusion(f32[1664,1024]{1,0:T(8,128)} %copy.105, f32[1664,1024]{1,0:T(8,128)} %copy.104), kind=kLoop, calls=%fused_computation.9 | loop fusion | flops 13631488 | bytes 20447232 | tf_op jit(solution)/shard_map/convert.4
  299.8 5.6 collective-permute-done.5
  306.5 17.0 %collective-permute-start.6 = (bf16[128,2048]{1,0:T(8,128)(2,1)}, bf16[128,2048]{1,0:T(8,128)(2,1)S(1)}, u32[]{:S(2)}, u32[]{:S(2)}) collective-permute-start(bf16[128,2048]{1,0:T(8,128)(2,1)} %get-tuple-element.100), channel_id=1, source_target_pairs={{16,0},{20,4},{24,8},{28,12},{0,16},{4,20},{8,24},{12,28},{48,32},... | collective-permute-start | bytes 1572872 | tf_op jit(solution)/shard_map/ppermute | solution.py:320
  323.4 1.7 fusion.25
  325.1 47.8 %collective-permute-start.3 = (bf16[256,2048]{1,0:T(8,128)(2,1)}, bf16[256,2048]{1,0:T(8,128)(2,1)}, u32[]{:S(2)}, u32[]{:S(2)}) collective-permute-start(bf16[256,2048]{1,0:T(8,128)(2,1)} %get-tuple-element.107), channel_id=1, source_target_pairs={{4,0},{8,4},{12,8},{16,12},{20,16},{24,20},{28,24},{32,28},{36,32}... | collective-permute-start | bytes 3145736 | tf_op jit(solution)/shard_map/ppermute | solution.py:19
  372.9 1.9 collective-permute-start.2
  375.7 1.9 collective-permute-start
  377.6 1.9 collective-permute-start.1
  379.8 107.6 %collective-permute-start.7 = (bf16[128,2048]{1,0:T(8,128)(2,1)S(1)}, bf16[128,2048]{1,0:T(8,128)(2,1)S(1)}, u32[]{:S(2)}, u32[]{:S(2)}) collective-permute-start(bf16[128,2048]{1,0:T(8,128)(2,1)S(1)} %fusion.20), channel_id=1, source_target_pairs={{8,0},{12,4},{16,8},{20,12},{24,16},{28,20},{0,24},{4,28},{40,32},... | collective-permute-start | bytes 1572872 | tf_op jit(solution)/shard_map/ppermute | solution.py:320
  487.4 5.1 convolution_convert_fusion
  492.5 14.0 %collective-permute-done.7 = bf16[128,2048]{1,0:T(8,128)(2,1)S(1)} collective-permute-done((bf16[128,2048]{1,0:T(8,128)(2,1)S(1)}, bf16[128,2048]{1,0:T(8,128)(2,1)S(1)}, u32[]{:S(2)}, u32[]{:S(2)}) %collective-permute-start.7) | collective-permute-done | bytes 524320 | tf_op jit(solution)/shard_map/ppermute | solution.py:320
  506.5 1.0 fusion.21
  507.6 1.0 copy.106
  508.7 2.6 fusion.19
  511.3 16.2 %collective-permute-done.8 = bf16[128,2048]{1,0:T(8,128)(2,1)} collective-permute-done((bf16[128,2048]{1,0:T(8,128)(2,1)}, bf16[128,2048]{1,0:T(8,128)(2,1)}, u32[]{:S(2)}, u32[]{:S(2)}) %collective-permute-start.8) | collective-permute-done | bytes 524320 | tf_op jit(solution)/shard_map/ppermute | solution.py:320
  527.5 1.4 add_select_fusion
  528.9 32.0 %collective-permute-done.1 = bf16[256,2048]{1,0:T(8,128)(2,1)} collective-permute-done((bf16[256,2048]{1,0:T(8,128)(2,1)}, bf16[256,2048]{1,0:T(8,128)(2,1)}, u32[]{:S(2)}, u32[]{:S(2)}) %collective-permute-start.1) | collective-permute-done | bytes 1048608 | tf_op jit(solution)/shard_map/ppermute | solution.py:19
  560.9 3.3 fusion.15
  564.2 1.0 fusion.26
  565.2 2.0 copy.107
  (65 shorter events, 7.7 us)
Async XLA Ops:
  7.2 162.7 %copy-start = (bf16[256,4096]{1,0:T(8,128)(2,1)S(1)}, bf16[256,4096]{1,0:T(8,128)(2,1)}, u32[]{:S(2)}) copy-start(bf16[256,4096]{1,0:T(8,128)(2,1)} %param.23) | copy-start | bytes 6291460
  7.2 558.0 %reduce-scatter.2.cloned.1.call-start = ((), (), s32[]{:S(2)}) async-start(), calls=%async_computation.1 | async-start | bytes 17301504 | tf_op jit(solution)/shard_map/reduce_scatter | solution.py:339
  150.3 5.7 copy-start.10
  150.3 5.6 copy-start.11
  179.0 1.0 copy-start.7
  188.4 6.7 %copy-start.3 = (bf16[256,1024]{1,0:T(8,128)(2,1)S(1)}, bf16[256,1024]{1,0:T(8,128)(2,1)}, u32[]{:S(2)}) copy-start(bf16[256,1024]{1,0:T(8,128)(2,1)} %shard_map.109) | copy-start | bytes 1572868
  196.5 7.9 %copy-start.4 = (bf16[256,1024]{0,1:T(8,128)(2,1)S(1)}, bf16[256,1024]{0,1:T(8,128)(2,1)}, u32[]{:S(2)}) copy-start(bf16[256,1024]{0,1:T(8,128)(2,1)} %copy.113) | copy-start | bytes 1572868
  250.0 5.0 copy-start.2
  265.2 27.0 %collective-permute-start.4 = (bf16[2,128,2048]{2,1,0:T(8,128)(2,1)S(1)}, bf16[2,128,2048]{2,1,0:T(8,128)(2,1)S(1)}, u32[]{:S(2)}, u32[]{:S(2)}) collective-permute-start(bf16[2,128,2048]{2,1,0:T(8,128)(2,1)S(1)} %bitcast.93), channel_id=1, source_target_pairs={{0,64},{4,68},{8,72},{12,76},{16,80},{20,84},{24,88},{28,92},{32,9... | collective-permute-start | bytes 3145736 | tf_op jit(solution)/shard_map/ppermute | solution.py:314
  292.5 13.0 %collective-permute-start.5 = (bf16[1,128,2048]{2,1,0:T(8,128)(2,1)S(1)}, bf16[1,128,2048]{2,1,0:T(8,128)(2,1)S(1)}, u32[]{:S(2)}, u32[]{:S(2)}) collective-permute-start(bf16[1,128,2048]{2,1,0:T(8,128)(2,1)S(1)} %select_convert_fusion.1), channel_id=1, source_target_pairs={{0,32},{4,36},{8,40},{12,44},{16,48},{20,52},{24,56},{28,60},{32,0... | collective-permute-start | bytes 1572872 | tf_op jit(solution)/shard_map/ppermute | solution.py:314
  306.5 73.1 %collective-permute-start.6 = (bf16[128,2048]{1,0:T(8,128)(2,1)}, bf16[128,2048]{1,0:T(8,128)(2,1)S(1)}, u32[]{:S(2)}, u32[]{:S(2)}) collective-permute-start(bf16[128,2048]{1,0:T(8,128)(2,1)} %get-tuple-element.100), channel_id=1, source_target_pairs={{16,0},{20,4},{24,8},{28,12},{0,16},{4,20},{8,24},{12,28},{48,32},... | collective-permute-start | bytes 1572872 | tf_op jit(solution)/shard_map/ppermute | solution.py:320
  325.1 203.7 %collective-permute-start.3 = (bf16[256,2048]{1,0:T(8,128)(2,1)}, bf16[256,2048]{1,0:T(8,128)(2,1)}, u32[]{:S(2)}, u32[]{:S(2)}) collective-permute-start(bf16[256,2048]{1,0:T(8,128)(2,1)} %get-tuple-element.107), channel_id=1, source_target_pairs={{4,0},{8,4},{12,8},{16,12},{20,16},{24,20},{28,24},{32,28},{36,32}... | collective-permute-start | bytes 3145736 | tf_op jit(solution)/shard_map/ppermute | solution.py:19
  372.9 155.9 %collective-permute-start.2 = (bf16[256,2048]{1,0:T(8,128)(2,1)}, bf16[256,2048]{1,0:T(8,128)(2,1)}, u32[]{:S(2)}, u32[]{:S(2)}) collective-permute-start(bf16[256,2048]{1,0:T(8,128)(2,1)} %get-tuple-element.108), channel_id=1, source_target_pairs={{8,0},{12,4},{16,8},{20,12},{24,16},{28,20},{32,24},{36,28},{40,32... | collective-permute-start | bytes 3145736 | tf_op jit(solution)/shard_map/ppermute | solution.py:19
  375.7 132.9 %collective-permute-start = (bf16[128,2048]{1,0:T(8,128)(2,1)}, bf16[128,2048]{1,0:T(8,128)(2,1)}, u32[]{:S(2)}, u32[]{:S(2)}) collective-permute-start(bf16[128,2048]{1,0:T(8,128)(2,1)} %slice.138), channel_id=1, source_target_pairs={{16,0},{20,4},{24,8},{28,12},{32,16},{36,20},{40,24},{44,28},{48,3... | collective-permute-start | bytes 1572872 | tf_op jit(solution)/shard_map/ppermute | solution.py:19
  377.6 183.2 %collective-permute-start.1 = (bf16[256,2048]{1,0:T(8,128)(2,1)}, bf16[256,2048]{1,0:T(8,128)(2,1)}, u32[]{:S(2)}, u32[]{:S(2)}) collective-permute-start(bf16[256,2048]{1,0:T(8,128)(2,1)} %get-tuple-element.106), channel_id=1, source_target_pairs={{12,0},{16,4},{20,8},{24,12},{28,16},{32,20},{36,24},{40,28},{44,3... | collective-permute-start | bytes 3145736 | tf_op jit(solution)/shard_map/ppermute | solution.py:19
  379.6 126.9 %copy-start.5 = (bf16[128,2048]{1,0:T(8,128)(2,1)}, bf16[128,2048]{1,0:T(8,128)(2,1)S(1)}, u32[]{:S(2)}) copy-start(bf16[128,2048]{1,0:T(8,128)(2,1)S(1)} %collective-permute-done.6) | copy-start | bytes 1572868
  379.8 126.7 %collective-permute-start.7 = (bf16[128,2048]{1,0:T(8,128)(2,1)S(1)}, bf16[128,2048]{1,0:T(8,128)(2,1)S(1)}, u32[]{:S(2)}, u32[]{:S(2)}) collective-permute-start(bf16[128,2048]{1,0:T(8,128)(2,1)S(1)} %fusion.20), channel_id=1, source_target_pairs={{8,0},{12,4},{16,8},{20,12},{24,16},{28,20},{0,24},{4,28},{40,32},... | collective-permute-start | bytes 1572872 | tf_op jit(solution)/shard_map/ppermute | solution.py:320
  506.5 2.1 copy-start.8
  507.5 19.9 %collective-permute-start.8 = (bf16[128,2048]{1,0:T(8,128)(2,1)}, bf16[128,2048]{1,0:T(8,128)(2,1)}, u32[]{:S(2)}, u32[]{:S(2)}) collective-permute-start(bf16[128,2048]{1,0:T(8,128)(2,1)} %fusion.21), channel_id=1, source_target_pairs={{4,0},{8,4},{12,8},{16,12},{20,16},{24,20},{28,24},{0,28},{36,32},... | collective-permute-start | bytes 1572872 | tf_op jit(solution)/shard_map/ppermute | solution.py:320
  508.6 18.9 %copy-start.6 = (bf16[128,2048]{1,0:T(8,128)(2,1)S(1)}, bf16[128,2048]{1,0:T(8,128)(2,1)}, u32[]{:S(2)}) copy-start(bf16[128,2048]{1,0:T(8,128)(2,1)} %copy-done.5) | copy-start | bytes 1572868
  508.6 18.9 %copy-start.9 = (bf16[128,2048]{1,0:T(8,128)(2,1)S(1)}, bf16[128,2048]{1,0:T(8,128)(2,1)}, u32[]{:S(2)}) copy-start(bf16[128,2048]{1,0:T(8,128)(2,1)} %copy-done.8) | copy-start | bytes 1572868
  508.6 58.6 %copy-start.1 = (bf16[256,4096]{1,0:T(8,128)(2,1)S(1)}, bf16[256,4096]{1,0:T(8,128)(2,1)}, u32[]{:S(2)}) copy-start(bf16[256,4096]{1,0:T(8,128)(2,1)} %param.23) | copy-start | bytes 6291460
Sparse Core Ops, SparseCore 0:
  179.2 350.5 reduce-scatter.1

commit v11 on v10

--- a/solution.py
+++ b/solution.py
@@ -33,14 +33,20 @@
     my_group = me // group
     lead = ctl_ref[0]
     sum_local = ctl_ref[1]
-    rel = (in_group - lead + group) % group
+    lanes = group // 2
+    lane = in_group % lanes
+    lane_base = in_group - lane
+    rel_lane = (lane - lead + lanes) % lanes
     mesh_id = pl.DeviceIdType.MESH
 
     def ring(step):
         return (me + step + seq_size) % seq_size
 
     def in_ring(step):
-        return base + (in_group + step + group) % group
+        return base + lane_base + (lane + step + lanes) % lanes
+
+    def flip():
+        return me + lanes - 2 * lanes * (in_group // lanes)
 
     def across(span):
         upper = (my_group // span) % 2
@@ -50,10 +56,9 @@
     partners = []
     for distance in range(1, len(spans) + 1):
         partners += [ring(distance), ring(-distance)]
-    hop = 1
-    while hop < group:
+    for hop in (1, 2):
         partners += [in_ring(hop), in_ring(-hop)]
-        hop *= 2
+    partners += [flip(), flip()]
     span = 1
     while span < groups:
         partners += [across(span), across(span)]
@@ -88,24 +93,20 @@
         mine = jnp.where(sum_local == block, kv_ref[block * BLK : (block + 1) * BLK, :], mine)
     held[...] = mine
     slot = len(spans)
-    hop = 1
-    stage = 0
-    while hop < group:
+    steps = [(in_ring(1), rel_lane == 1), (in_ring(2), rel_lane >= 2), (flip(), in_group >= lanes)]
+    for stage, (target, take) in enumerate(steps):
         copy = pltpu.make_async_remote_copy(
             src_ref=held,
             dst_ref=hop_buf.at[stage],
             send_sem=sends.at[slot],
             recv_sem=recvs.at[slot],
-            device_id={"seq": in_ring(hop)},
+            device_id={"seq": target},
             device_id_type=mesh_id,
         )
         copy.start()
         copy.wait()
-        take = (rel >= hop) & (rel < 2 * hop)
         held[...] = jnp.where(take, hop_buf[stage], held[...])
         slot += 1
-        stage += 1
-        hop *= 2
 
     copy = pltpu.make_async_remote_copy(
         src_ref=held,
@@ -239,6 +240,7 @@
     group = STRIDE // blocks_dev
     groups = seq_size // group
     assert groups == summary_count == 4 and group == 8
+    assert (STRIDE - LOCAL) // blocks_dev <= group // 2
     far_ids = jnp.arange(summary_count, dtype=jnp.int32) * STRIDE + offset_block
     lead = offset_block // blocks_dev
     sum_local = offset_block % blocks_dev
@@ -314,12 +316,20 @@
         part = keep + lax.ppermute(send.astype(jnp.bfloat16), "seq", route).astype(jnp.float32)
         span //= 2
     part = part[0]
-    hop = group // 2
-    while hop >= 1:
-        route = [(g * group + (r + hop) % group, g * group + r) for g in range(groups) for r in range(group)]
+    lanes = group // 2
+    lane = in_group % lanes
+    rel_lane = (lane - lead) % lanes
+    route = [(g * group + (r ^ lanes), g * group + r) for g in range(groups) for r in range(group)]
+    moved = lax.ppermute(part.astype(jnp.bfloat16), "seq", route).astype(jnp.float32)
+    part = jnp.where(in_group < lanes, part + moved, part)
+    for hop in (2, 1):
+        route = [
+            (g * group + r - r % lanes + (r % lanes + hop) % lanes, g * group + r)
+            for g in range(groups)
+            for r in range(group)
+        ]
         moved = lax.ppermute(part.astype(jnp.bfloat16), "seq", route).astype(jnp.float32)
-        part = jnp.where(rel < hop, part + moved, part)
-        hop //= 2
+        part = jnp.where(rel_lane < hop, part + moved, part)
     own_local = jnp.arange(blocks_dev, dtype=jnp.int32)
     far_here = (rel == 0) & (own_local == sum_local)
     far_add = jnp.where(far_here[:, None, None], part[None], 0.0)

time: 575 us -> 576 us (level)
  no operation moved by 1% of the time
where the time goes in v11:
time: 576 us; the launch traced here: 574 us
  starting transfers between devices  187 us (32%)
  Pallas kernels  143 us (25%)
  waiting for transfers between devices  83.8 us (15%)
  matrix products  55 us (10%)
  local copies, waits for them, and re-layouts  47.7 us (8%)
  other arithmetic  41.3 us (7%)
  between operations  16.5 us (3%)
    pallas_call x1, Pallas kernels, exchange(): pl.pallas_call(functools.partial(exchange_kernel, (seq_size, group, spans...  131 us
    ppermute x3, starting transfers between devices, local(): lax.ppermute(part.astype(jnp.bfloat16), 'seq', route).astype(jnp.float32)  122 us
    ppermute x4, starting transfers between devices, passed_along(): return lax.ppermute(block, axis, route)  59 us
    ppermute x4, waiting for transfers between devices, passed_along(): return lax.ppermute(block, axis, route)  32.3 us
    ppermute x3, waiting for transfers between devices, local(): lax.ppermute(part.astype(jnp.bfloat16), 'seq', route).astype(jnp.float32)  30.1 us
    ppermute x2, waiting for transfers between devices, local(): lax.ppermute(send.astype(jnp.bfloat16), 'seq', route).astype(jnp.float32)  21.3 us
    unnamed x33, local copies, waits for them, and re-layouts  13.9 us
    pallas_call x1, Pallas kernels, attention_out(): pl.pallas_call(functools.partial(forward_kernel, scale), out_shape=jax.Sh...  12.3 us
  transfers between devices with their start and end apart: 10, of which 5 were waited for; matrix products, arithmetic and copies ran while one was open for 20% of the time, Pallas kernels for 0%

profile of v11, /device:TPU:40, one launch (start us, length us, event | category | flops | bytes accessed | tf_op | source)
XLA Modules:
  0.0 574.4 jit_solution(2164992598748019090)
XLA Ops:
  7.2 1.4 slice.117
  10.7 1.1 constant_dynamic-update-slice_fusion.1
  14.4 2.2 copy.90
  17.6 1.1 constant_dynamic-update-slice_fusion.kv_ref
  18.7 130.6 %shard_map.108 = (bf16[896,2048]{1,0:T(8,128)(2,1)}, bf16[4,128,2048]{2,1,0:T(8,128)(2,1)S(1)}) custom-call(s32[2]{0:T(128)S(1)} %pad_add_fusion.1.ctl_ref, bf16[256,2048]{1,0:T(8,128)(2,1)S(1)} %constant_dynamic-update-slice_fusion.kv_ref), custom_call_target="tpu_custom_call" | custom-call | tf_op jit(solution)/shard_map/pallas_call | solution.py:152
  149.3 5.6 pad_maximum_fusion.1.k_ref.v_ref
  154.9 1.6 broadcast_select_fusion.1
  156.5 12.3 %shard_map.109 = bf16[256,1024]{1,0:T(8,128)(2,1)} custom-call(bf16[256,1024]{1,0:T(8,128)(2,1)} %q_ref.1, bf16[1664,2048]{1,0:T(8,128)(2,1)} %pad_maximum_fusion.1.k_ref.v_ref, bf16[1664,2048]{1,0:T(8,128)(2,1)} %pad_maximum_fusion.1.k_ref.v_ref, f32[256,1664]{1,0:T(8,128)} %get-tuple-element.102.bias_ref), custom_call_target="tpu_custom_call" | custom-call | flops 1744830464 | bytes 9568256 | tf_op jit(solution)/shard_map/pallas_call | solution.py:197
  168.8 9.2 %convolution_bitcast_fusion = f32[4096,1024]{0,1:T(8,128)} fusion(bf16[256,1024]{1,0:T(8,128)(2,1)} %shard_map.109, bf16[256,4096]{1,0:T(8,128)(2,1)S(1)} %copy-done), kind=kOutput, calls=%fused_computation.16 | convolution fusion | flops 2147483648 | bytes 19398656 | tf_op jit(solution)/shard_map/dot_general | solution.py:350
  178.0 1.0 copy-done.7
  180.0 7.4 %slice_bitcast_fusion = (bf16[208,8,8,128]{3,2,1,0:T(8,128)(2,1)}, bf16[1664,1024]{1,0:T(8,128)(2,1)}) fusion(bf16[1664,2048]{1,0:T(8,128)(2,1)} %pad_maximum_fusion.1.k_ref.v_ref), kind=kLoop, calls=%fused_computation.25 | loop fusion | bytes 13631488
  187.3 5.7 copy.112
  193.0 1.1 copy.91
  194.2 1.2 copy.117
  195.4 5.8 %fusion.16 = bf16[32,8,8,128]{3,1,2,0:T(8,128)(2,1)S(1)} fusion(bf16[256,4096]{1,0:T(8,128)(2,1)S(1)} %copy-done, bf16[4096,1024]{1,0:T(8,128)(2,1)} %param.24), kind=kOutput, calls=%fused_computation.40 | convolution fusion | flops 2147745792 | bytes 11010048 | tf_op jit(solution)/shard_map/dot_general | solution.py:234
  201.6 1.6 multiply_reduce_fusion
  203.2 9.4 %fusion.2 = (f32[8,256]{1,0:T(8,128)S(1)}, f32[8,1664,256]{2,1,0:T(8,128)}) fusion(pred[256,1664]{0,1:T(8,128)(4,1)S(1)} %copy.91, bf16[1664,8,128]{0,2,1:T(8,128)(2,1)} %bitcast.81, bf16[256,8,128]{0,2,1:T(8,128)(2,1)S(1)} %bitcast.86), kind=kOutput, calls=%fused_computation.15 | convolution fusion | flops 882636800 | bytes 17997824 | tf_op jit(solution)/shard_map/qhd,khd->hqk/dot_general | solution.py:282
  212.6 8.0 %exponential_reduce_fusion = f32[8,256]{1,0:T(8,128)S(1)} fusion(f32[8,1664,256]{2,1,0:T(8,128)} %get-tuple-element.114, f32[8,256]{1,0:T(8,128)S(1)} %get-tuple-element.113, pred[256,1664]{0,1:T(8,128)(4,1)S(1)} %copy.91), kind=kLoop, calls=%fused_computation.13 | loop fusion | flops 13629440 | bytes 14073856 | tf_op jit(solution)/shard_map/reduce_sum | solution.py:287
  220.7 11.4 %fusion.3 = f32[8,128,1664]{2,1,0:T(8,128)} fusion(bf16[256,8,128]{0,2,1:T(8,128)(2,1)S(1)} %copy.102, f32[8,1664,256]{2,1,0:T(8,128)} %get-tuple-element.114, f32[8,256]{1,0:T(8,128)S(1)} %log_add_fusion, pred[256,1664]{0,1:T(8,128)(4,1)S(1)} %copy.91), kind=kOutput, calls=%fused_computation.17 | convolution fusion | flops 886046720 | bytes 21405696 | tf_op jit(solution)/shard_map/hqk,qhd->khd/dot_general | solution.py:301
  232.1 7.7 %copy.105 = f32[1664,1024]{1,0:T(8,128)} copy(f32[1664,1024]{0,1:T(8,128)} %bitcast.84) | data formatting | bytes 13631488 | tf_op jit(solution)/shard_map/reshape | solution.py:305
  239.8 9.1 %multiply_convert_fusion = bf16[8,256,1664]{1,2,0:T(8,128)(2,1)S(1)} fusion(f32[8,1664,256]{2,1,0:T(8,128)} %get-tuple-element.114, f32[8,256]{1,0:T(8,128)S(1)} %copy.96, f32[8,256]{1,0:T(8,128)S(1)} %log_add_fusion, pred[256,1664]{0,1:T(8,128)(4,1)S(1)} %copy.91, bf16[256,8,128]{0,2,1:T(8,128)(2,1)S(1)} %copy.102, ...), kind=kOutput, calls=%fused_computation.11 | convolution fusion | flops 896270336 | bytes 24821760 | tf_op jit(solution)/shard_map/qhd,khd->hqk/dot_general | solution.py:295
  248.9 5.0 fusion.27
  253.9 7.7 %copy.104 = f32[1664,1024]{1,0:T(8,128)} copy(f32[1664,1024]{0,1:T(8,128)} %bitcast.83) | data formatting | bytes 13631488 | tf_op jit(solution)/shard_map/reshape | solution.py:305
  261.6 2.5 select_convert_fusion
  264.1 4.1 collective-permute-start.4
  268.1 4.7 broadcast_select_fusion
  272.9 17.2 %collective-permute-done.4 = bf16[2,128,2048]{2,1,0:T(8,128)(2,1)S(1)} collective-permute-done((bf16[2,128,2048]{2,1,0:T(8,128)(2,1)S(1)}, bf16[2,128,2048]{2,1,0:T(8,128)(2,1)S(1)}, u32[]{:S(2)}, u32[]{:S(2)}) %collective-permute-start.4) | collective-permute-done | bytes 1048608 | tf_op jit(solution)/shard_map/ppermute | solution.py:316
  290.5 1.9 collective-permute-start.5
  292.3 5.8 %fusion = bf16[1664,2048]{1,0:T(8,128)(2,1)S(1)} fusion(f32[1664,1024]{1,0:T(8,128)} %copy.105, f32[1664,1024]{1,0:T(8,128)} %copy.104), kind=kLoop, calls=%fused_computation.9 | loop fusion | flops 13631488 | bytes 20447232 | tf_op jit(solution)/shard_map/convert.4
  298.2 4.1 collective-permute-done.5
  303.3 14.4 %collective-permute-start.6 = (bf16[128,2048]{1,0:T(8,128)(2,1)}, bf16[128,2048]{1,0:T(8,128)(2,1)S(1)}, u32[]{:S(2)}, u32[]{:S(2)}) collective-permute-start(bf16[128,2048]{1,0:T(8,128)(2,1)} %get-tuple-element.100), channel_id=1, source_target_pairs={{16,0},{20,4},{24,8},{28,12},{0,16},{4,20},{8,24},{12,28},{48,32},... | collective-permute-start | bytes 1572872 | tf_op jit(solution)/shard_map/ppermute | solution.py:323
  317.7 1.7 fusion.25
  319.4 53.3 %collective-permute-start.3 = (bf16[256,2048]{1,0:T(8,128)(2,1)}, bf16[256,2048]{1,0:T(8,128)(2,1)}, u32[]{:S(2)}, u32[]{:S(2)}) collective-permute-start(bf16[256,2048]{1,0:T(8,128)(2,1)} %get-tuple-element.107), channel_id=1, source_target_pairs={{4,0},{8,4},{12,8},{16,12},{20,16},{24,20},{28,24},{32,28},{36,32}... | collective-permute-start | bytes 3145736 | tf_op jit(solution)/shard_map/ppermute | solution.py:19
  372.7 1.9 collective-permute-start.2
  375.5 1.9 collective-permute-start
  377.4 1.9 collective-permute-start.1
  379.6 107.9 %collective-permute-start.7 = (bf16[128,2048]{1,0:T(8,128)(2,1)S(1)}, bf16[128,2048]{1,0:T(8,128)(2,1)S(1)}, u32[]{:S(2)}, u32[]{:S(2)}) collective-permute-start(bf16[128,2048]{1,0:T(8,128)(2,1)S(1)} %fusion.20), channel_id=1, source_target_pairs={{8,0},{12,4},{0,8},{4,12},{24,16},{28,20},{16,24},{20,28},{40,32},... | collective-permute-start | bytes 1572872 | tf_op jit(solution)/shard_map/ppermute | solution.py:331
  487.4 5.1 convolution_convert_fusion
  492.6 15.0 %collective-permute-done.7 = bf16[128,2048]{1,0:T(8,128)(2,1)S(1)} collective-permute-done((bf16[128,2048]{1,0:T(8,128)(2,1)S(1)}, bf16[128,2048]{1,0:T(8,128)(2,1)S(1)}, u32[]{:S(2)}, u32[]{:S(2)}) %collective-permute-start.7) | collective-permute-done | bytes 524320 | tf_op jit(solution)/shard_map/ppermute | solution.py:331
  507.6 1.0 fusion.21
  508.7 1.0 copy.106
  509.8 2.6 fusion.19
  512.4 15.1 %collective-permute-done.8 = bf16[128,2048]{1,0:T(8,128)(2,1)} collective-permute-done((bf16[128,2048]{1,0:T(8,128)(2,1)}, bf16[128,2048]{1,0:T(8,128)(2,1)}, u32[]{:S(2)}, u32[]{:S(2)}) %collective-permute-start.8) | collective-permute-done | bytes 524320 | tf_op jit(solution)/shard_map/ppermute | solution.py:331
  527.4 1.4 add_select_fusion
  528.9 32.3 %collective-permute-done.1 = bf16[256,2048]{1,0:T(8,128)(2,1)} collective-permute-done((bf16[256,2048]{1,0:T(8,128)(2,1)}, bf16[256,2048]{1,0:T(8,128)(2,1)}, u32[]{:S(2)}, u32[]{:S(2)}) %collective-permute-start.1) | collective-permute-done | bytes 1048608 | tf_op jit(solution)/shard_map/ppermute | solution.py:19
  561.2 3.3 fusion.15
  564.4 1.0 fusion.26
  565.5 2.0 copy.107
  (65 shorter events, 7.7 us)
Async XLA Ops:
  7.2 161.6 %copy-start = (bf16[256,4096]{1,0:T(8,128)(2,1)S(1)}, bf16[256,4096]{1,0:T(8,128)(2,1)}, u32[]{:S(2)}) copy-start(bf16[256,4096]{1,0:T(8,128)(2,1)} %param.23) | copy-start | bytes 6291460
  7.2 558.3 %reduce-scatter.2.cloned.1.call-start = ((), (), s32[]{:S(2)}) async-start(), calls=%async_computation.1 | async-start | bytes 17301504 | tf_op jit(solution)/shard_map/reduce_scatter | solution.py:349
  149.2 5.7 copy-start.10
  149.3 5.6 copy-start.11
  177.9 1.0 copy-start.7
  187.3 6.7 %copy-start.3 = (bf16[256,1024]{1,0:T(8,128)(2,1)S(1)}, bf16[256,1024]{1,0:T(8,128)(2,1)}, u32[]{:S(2)}) copy-start(bf16[256,1024]{1,0:T(8,128)(2,1)} %shard_map.109) | copy-start | bytes 1572868
  195.4 7.9 %copy-start.4 = (bf16[256,1024]{0,1:T(8,128)(2,1)S(1)}, bf16[256,1024]{0,1:T(8,128)(2,1)}, u32[]{:S(2)}) copy-start(bf16[256,1024]{0,1:T(8,128)(2,1)} %copy.113) | copy-start | bytes 1572868
  248.9 5.0 copy-start.2
  264.1 26.0 %collective-permute-start.4 = (bf16[2,128,2048]{2,1,0:T(8,128)(2,1)S(1)}, bf16[2,128,2048]{2,1,0:T(8,128)(2,1)S(1)}, u32[]{:S(2)}, u32[]{:S(2)}) collective-permute-start(bf16[2,128,2048]{2,1,0:T(8,128)(2,1)S(1)} %bitcast.93), channel_id=1, source_target_pairs={{0,64},{4,68},{8,72},{12,76},{16,80},{20,84},{24,88},{28,92},{32,9... | collective-permute-start | bytes 3145736 | tf_op jit(solution)/shard_map/ppermute | solution.py:316
  290.5 11.9 %collective-permute-start.5 = (bf16[1,128,2048]{2,1,0:T(8,128)(2,1)S(1)}, bf16[1,128,2048]{2,1,0:T(8,128)(2,1)S(1)}, u32[]{:S(2)}, u32[]{:S(2)}) collective-permute-start(bf16[1,128,2048]{2,1,0:T(8,128)(2,1)S(1)} %select_convert_fusion.1), channel_id=1, source_target_pairs={{0,32},{4,36},{8,40},{12,44},{16,48},{20,52},{24,56},{28,60},{32,0... | collective-permute-start | bytes 1572872 | tf_op jit(solution)/shard_map/ppermute | solution.py:316
  303.3 76.1 %collective-permute-start.6 = (bf16[128,2048]{1,0:T(8,128)(2,1)}, bf16[128,2048]{1,0:T(8,128)(2,1)S(1)}, u32[]{:S(2)}, u32[]{:S(2)}) collective-permute-start(bf16[128,2048]{1,0:T(8,128)(2,1)} %get-tuple-element.100), channel_id=1, source_target_pairs={{16,0},{20,4},{24,8},{28,12},{0,16},{4,20},{8,24},{12,28},{48,32},... | collective-permute-start | bytes 1572872 | tf_op jit(solution)/shard_map/ppermute | solution.py:323
  319.4 209.4 %collective-permute-start.3 = (bf16[256,2048]{1,0:T(8,128)(2,1)}, bf16[256,2048]{1,0:T(8,128)(2,1)}, u32[]{:S(2)}, u32[]{:S(2)}) collective-permute-start(bf16[256,2048]{1,0:T(8,128)(2,1)} %get-tuple-element.107), channel_id=1, source_target_pairs={{4,0},{8,4},{12,8},{16,12},{20,16},{24,20},{28,24},{32,28},{36,32}... | collective-permute-start | bytes 3145736 | tf_op jit(solution)/shard_map/ppermute | solution.py:19
  372.7 156.1 %collective-permute-start.2 = (bf16[256,2048]{1,0:T(8,128)(2,1)}, bf16[256,2048]{1,0:T(8,128)(2,1)}, u32[]{:S(2)}, u32[]{:S(2)}) collective-permute-start(bf16[256,2048]{1,0:T(8,128)(2,1)} %get-tuple-element.108), channel_id=1, source_target_pairs={{8,0},{12,4},{16,8},{20,12},{24,16},{28,20},{32,24},{36,28},{40,32... | collective-permute-start | bytes 3145736 | tf_op jit(solution)/shard_map/ppermute | solution.py:19
  375.5 134.3 %collective-permute-start = (bf16[128,2048]{1,0:T(8,128)(2,1)}, bf16[128,2048]{1,0:T(8,128)(2,1)}, u32[]{:S(2)}, u32[]{:S(2)}) collective-permute-start(bf16[128,2048]{1,0:T(8,128)(2,1)} %slice.138), channel_id=1, source_target_pairs={{16,0},{20,4},{24,8},{28,12},{32,16},{36,20},{40,24},{44,28},{48,3... | collective-permute-start | bytes 1572872 | tf_op jit(solution)/shard_map/ppermute | solution.py:19
  377.4 183.8 %collective-permute-start.1 = (bf16[256,2048]{1,0:T(8,128)(2,1)}, bf16[256,2048]{1,0:T(8,128)(2,1)}, u32[]{:S(2)}, u32[]{:S(2)}) collective-permute-start(bf16[256,2048]{1,0:T(8,128)(2,1)} %get-tuple-element.106), channel_id=1, source_target_pairs={{12,0},{16,4},{20,8},{24,12},{28,16},{32,20},{36,24},{40,28},{44,3... | collective-permute-start | bytes 3145736 | tf_op jit(solution)/shard_map/ppermute | solution.py:19
  379.4 128.2 %copy-start.5 = (bf16[128,2048]{1,0:T(8,128)(2,1)}, bf16[128,2048]{1,0:T(8,128)(2,1)S(1)}, u32[]{:S(2)}) copy-start(bf16[128,2048]{1,0:T(8,128)(2,1)S(1)} %collective-permute-done.6) | copy-start | bytes 1572868
  379.6 128.1 %collective-permute-start.7 = (bf16[128,2048]{1,0:T(8,128)(2,1)S(1)}, bf16[128,2048]{1,0:T(8,128)(2,1)S(1)}, u32[]{:S(2)}, u32[]{:S(2)}) collective-permute-start(bf16[128,2048]{1,0:T(8,128)(2,1)S(1)} %fusion.20), channel_id=1, source_target_pairs={{8,0},{12,4},{0,8},{4,12},{24,16},{28,20},{16,24},{20,28},{40,32},... | collective-permute-start | bytes 1572872 | tf_op jit(solution)/shard_map/ppermute | solution.py:331
  507.6 2.1 copy-start.8
  508.6 18.8 %collective-permute-start.8 = (bf16[128,2048]{1,0:T(8,128)(2,1)}, bf16[128,2048]{1,0:T(8,128)(2,1)}, u32[]{:S(2)}, u32[]{:S(2)}) collective-permute-start(bf16[128,2048]{1,0:T(8,128)(2,1)} %fusion.21), channel_id=1, source_target_pairs={{4,0},{8,4},{12,8},{0,12},{20,16},{24,20},{28,24},{16,28},{36,32},... | collective-permute-start | bytes 1572872 | tf_op jit(solution)/shard_map/ppermute | solution.py:331
  509.7 17.7 %copy-start.6 = (bf16[128,2048]{1,0:T(8,128)(2,1)S(1)}, bf16[128,2048]{1,0:T(8,128)(2,1)}, u32[]{:S(2)}) copy-start(bf16[128,2048]{1,0:T(8,128)(2,1)} %copy-done.5) | copy-start | bytes 1572868
  509.7 17.7 %copy-start.9 = (bf16[128,2048]{1,0:T(8,128)(2,1)S(1)}, bf16[128,2048]{1,0:T(8,128)(2,1)}, u32[]{:S(2)}) copy-start(bf16[128,2048]{1,0:T(8,128)(2,1)} %copy-done.8) | copy-start | bytes 1572868
  509.7 57.8 %copy-start.1 = (bf16[256,4096]{1,0:T(8,128)(2,1)S(1)}, bf16[256,4096]{1,0:T(8,128)(2,1)}, u32[]{:S(2)}) copy-start(bf16[256,4096]{1,0:T(8,128)(2,1)} %param.23) | copy-start | bytes 6291460
Sparse Core Ops, SparseCore 0:
  178.1 352.9 reduce-scatter.1

commit v12 on v11

--- a/solution.py
+++ b/solution.py
@@ -240,7 +240,7 @@
     group = STRIDE // blocks_dev
     groups = seq_size // group
     assert groups == summary_count == 4 and group == 8
-    assert (STRIDE - LOCAL) // blocks_dev <= group // 2
+    assert (STRIDE - LOCAL) // blocks_dev <= group // 2 and group == 8
     far_ids = jnp.arange(summary_count, dtype=jnp.int32) * STRIDE + offset_block
     lead = offset_block // blocks_dev
     sum_local = offset_block % blocks_dev
@@ -322,14 +322,19 @@
     route = [(g * group + (r ^ lanes), g * group + r) for g in range(groups) for r in range(group)]
     moved = lax.ppermute(part.astype(jnp.bfloat16), "seq", route).astype(jnp.float32)
     part = jnp.where(in_group < lanes, part + moved, part)
-    for hop in (2, 1):
-        route = [
+    def from_lane(hop):
+        return [
             (g * group + r - r % lanes + (r % lanes + hop) % lanes, g * group + r)
             for g in range(groups)
             for r in range(group)
         ]
-        moved = lax.ppermute(part.astype(jnp.bfloat16), "seq", route).astype(jnp.float32)
-        part = jnp.where(rel_lane < hop, part + moved, part)
+
+    sent = part.astype(jnp.bfloat16)
+    ahead = lax.ppermute(sent, "seq", from_lane(1)).astype(jnp.float32)
+    behind = lax.ppermute(sent, "seq", from_lane(-1)).astype(jnp.float32)
+    part = part + jnp.where(rel_lane == 1, ahead, 0.0) + jnp.where(rel_lane == 0, behind, 0.0)
+    ahead = lax.ppermute(part.astype(jnp.bfloat16), "seq", from_lane(1)).astype(jnp.float32)
+    part = jnp.where(rel_lane == 0, part + ahead, part)
     own_local = jnp.arange(blocks_dev, dtype=jnp.int32)
     far_here = (rel == 0) & (own_local == sum_local)
     far_add = jnp.where(far_here[:, None, None], part[None], 0.0)

time: 576 us -> 553 us (0.960)
  starting transfers between devices: 187 us -> 160 us
    ppermute x3 -> x1, starting transfers between devices: 122 us -> 14.4 us  [local(): lax.ppermute(part.astype(jnp.bfloat16), 'seq', route).astype(jnp.float32)]
    ppermute x4, starting transfers between devices: 59 us -> 120 us  [passed_along(): return lax.ppermute(block, axis, route)]
    ppermute x0 -> x3, waiting for transfers between devices: none -> 33.6 us  [the longest x1 18 us: local(): behind = lax.ppermute(sent, 'seq', from_lane(-1)).astype(jnp.float32)]
    ppermute x3 -> x1, waiting for transfers between devices: 30.1 us -> 0.01 us  [local(): lax.ppermute(part.astype(jnp.bfloat16), 'seq', route).astype(jnp.float32)]
    ppermute x0 -> x3, starting transfers between devices: none -> 19.6 us  [the longest x1 14.8 us: local(): ahead = lax.ppermute(sent, 'seq', from_lane(1)).astype(jnp.float32)]
    unnamed x33 -> x37, local copies, waits for them, and re-layouts: 13.9 us -> 13.9 us
  transfers between devices with their start and end apart: 10 -> 11, of which waited for: 5 -> 6; matrix products, arithmetic and copies ran while one was open for 20% -> 21% of each run, Pallas kernels for 0% -> 0%
where the time goes in v12:
time: 553 us; the launch traced here: 552 us
  starting transfers between devices  160 us (29%)
  Pallas kernels  143 us (26%)
  waiting for transfers between devices  88.2 us (16%)
  matrix products  55 us (10%)
  local copies, waits for them, and re-layouts  47.7 us (9%)
  other arithmetic  41.5 us (8%)
  between operations  16.5 us (3%)
    pallas_call x1, Pallas kernels, exchange(): pl.pallas_call(functools.partial(exchange_kernel, (seq_size, group, spans...  131 us
    ppermute x4, starting transfers between devices, passed_along(): return lax.ppermute(block, axis, route)  120 us
    ppermute x4, waiting for transfers between devices, passed_along(): return lax.ppermute(block, axis, route)  33.3 us
    ppermute x2, waiting for transfers between devices, local(): lax.ppermute(send.astype(jnp.bfloat16), 'seq', route).astype(jnp.float32)  21.3 us
    ppermute x1, waiting for transfers between devices, local(): behind = lax.ppermute(sent, 'seq', from_lane(-1)).astype(jnp.float32)  18 us
    ppermute x1, starting transfers between devices, local(): ahead = lax.ppermute(sent, 'seq', from_lane(1)).astype(jnp.float32)  14.8 us
    ppermute x1, starting transfers between devices, local(): lax.ppermute(part.astype(jnp.bfloat16), 'seq', route).astype(jnp.float32)  14.4 us
    ppermute x1, waiting for transfers between devices, local(): lax.ppermute(part.astype(jnp.bfloat16), 'seq', from_lane(1))  14.1 us
  transfers between devices with their start and end apart: 11, of which 6 were waited for; matrix products, arithmetic and copies ran while one was open for 21% of the time, Pallas kernels for 0%

profile of v12, /device:TPU:40, one launch (start us, length us, event | category | flops | bytes accessed | tf_op | source)
XLA Modules:
  0.0 551.7 jit_solution(6513414591088345051)
XLA Ops:
  7.2 1.4 slice.117
  10.7 1.1 constant_dynamic-update-slice_fusion.1
  14.4 2.2 copy.90
  17.6 1.1 constant_dynamic-update-slice_fusion.kv_ref
  18.7 130.5 %shard_map.108 = (bf16[896,2048]{1,0:T(8,128)(2,1)}, bf16[4,128,2048]{2,1,0:T(8,128)(2,1)S(1)}) custom-call(s32[2]{0:T(128)S(1)} %pad_add_fusion.1.ctl_ref, bf16[256,2048]{1,0:T(8,128)(2,1)S(1)} %constant_dynamic-update-slice_fusion.kv_ref), custom_call_target="tpu_custom_call" | custom-call | tf_op jit(solution)/shard_map/pallas_call | solution.py:152
  149.2 5.6 %pad_maximum_fusion.1.k_ref.v_ref = bf16[1664,2048]{1,0:T(8,128)(2,1)} fusion(bf16[512,2048]{1,0:T(8,128)(2,1)S(1)} %bitcast.80, bf16[256,2048]{1,0:T(8,128)(2,1)S(1)} %constant_dynamic-update-slice_fusion.kv_ref, bf16[896,2048]{1,0:T(8,128)(2,1)} %get-tuple-element.78), kind=kLoop, calls=%fused_computation.18 | loop fusion | flops 20447232 | bytes 13631488 | tf_op jit(solution)/shard_map/concatenate | solution.py:254
  154.9 1.6 broadcast_select_fusion.1
  156.5 12.3 %shard_map.109 = bf16[256,1024]{1,0:T(8,128)(2,1)} custom-call(bf16[256,1024]{1,0:T(8,128)(2,1)} %q_ref.1, bf16[1664,2048]{1,0:T(8,128)(2,1)} %pad_maximum_fusion.1.k_ref.v_ref, bf16[1664,2048]{1,0:T(8,128)(2,1)} %pad_maximum_fusion.1.k_ref.v_ref, f32[256,1664]{1,0:T(8,128)} %get-tuple-element.102.bias_ref), custom_call_target="tpu_custom_call" | custom-call | flops 1744830464 | bytes 9568256 | tf_op jit(solution)/shard_map/pallas_call | solution.py:197
  168.7 9.2 %convolution_bitcast_fusion = f32[4096,1024]{0,1:T(8,128)} fusion(bf16[256,1024]{1,0:T(8,128)(2,1)} %shard_map.109, bf16[256,4096]{1,0:T(8,128)(2,1)S(1)} %copy-done), kind=kOutput, calls=%fused_computation.16 | convolution fusion | flops 2147483648 | bytes 19398656 | tf_op jit(solution)/shard_map/dot_general | solution.py:355
  179.9 7.4 %slice_bitcast_fusion = (bf16[208,8,8,128]{3,2,1,0:T(8,128)(2,1)}, bf16[1664,1024]{1,0:T(8,128)(2,1)}) fusion(bf16[1664,2048]{1,0:T(8,128)(2,1)} %pad_maximum_fusion.1.k_ref.v_ref), kind=kLoop, calls=%fused_computation.25 | loop fusion | bytes 13631488
  187.3 5.7 %copy.112 = bf16[1664,1024]{0,1:T(8,128)(2,1)} copy(bf16[1664,1024]{1,0:T(8,128)(2,1)} %get-tuple-element.110) | data formatting | bytes 6815744 | tf_op jit(solution)/shard_map/reshape | solution.py:255
  193.0 1.1 copy.91
  194.2 1.2 copy.117
  195.3 5.8 %fusion.16 = bf16[32,8,8,128]{3,1,2,0:T(8,128)(2,1)S(1)} fusion(bf16[256,4096]{1,0:T(8,128)(2,1)S(1)} %copy-done, bf16[4096,1024]{1,0:T(8,128)(2,1)} %param.24), kind=kOutput, calls=%fused_computation.39 | convolution fusion | flops 2147745792 | bytes 11010048 | tf_op jit(solution)/shard_map/dot_general | solution.py:234
  201.5 1.6 multiply_reduce_fusion
  203.2 9.4 %fusion.2 = (f32[8,256]{1,0:T(8,128)S(1)}, f32[8,1664,256]{2,1,0:T(8,128)}) fusion(pred[256,1664]{0,1:T(8,128)(4,1)S(1)} %copy.91, bf16[1664,8,128]{0,2,1:T(8,128)(2,1)} %bitcast.81, bf16[256,8,128]{0,2,1:T(8,128)(2,1)S(1)} %bitcast.86), kind=kOutput, calls=%fused_computation.15 | convolution fusion | flops 882636800 | bytes 17997824 | tf_op jit(solution)/shard_map/qhd,khd->hqk/dot_general | solution.py:282
  212.6 8.0 %exponential_reduce_fusion = f32[8,256]{1,0:T(8,128)S(1)} fusion(f32[8,1664,256]{2,1,0:T(8,128)} %get-tuple-element.114, f32[8,256]{1,0:T(8,128)S(1)} %get-tuple-element.113, pred[256,1664]{0,1:T(8,128)(4,1)S(1)} %copy.91), kind=kLoop, calls=%fused_computation.13 | loop fusion | flops 13629440 | bytes 14073856 | tf_op jit(solution)/shard_map/reduce_sum | solution.py:287
  220.6 11.4 %fusion.3 = f32[8,128,1664]{2,1,0:T(8,128)} fusion(bf16[256,8,128]{0,2,1:T(8,128)(2,1)S(1)} %copy.102, f32[8,1664,256]{2,1,0:T(8,128)} %get-tuple-element.114, f32[8,256]{1,0:T(8,128)S(1)} %log_add_fusion, pred[256,1664]{0,1:T(8,128)(4,1)S(1)} %copy.91), kind=kOutput, calls=%fused_computation.17 | convolution fusion | flops 886046720 | bytes 21405696 | tf_op jit(solution)/shard_map/hqk,qhd->khd/dot_general | solution.py:301
  232.0 7.7 %copy.105 = f32[1664,1024]{1,0:T(8,128)} copy(f32[1664,1024]{0,1:T(8,128)} %bitcast.84) | data formatting | bytes 13631488 | tf_op jit(solution)/shard_map/reshape | solution.py:305
  239.7 9.1 %multiply_convert_fusion = bf16[8,256,1664]{1,2,0:T(8,128)(2,1)S(1)} fusion(f32[8,1664,256]{2,1,0:T(8,128)} %get-tuple-element.114, f32[8,256]{1,0:T(8,128)S(1)} %copy.96, f32[8,256]{1,0:T(8,128)S(1)} %log_add_fusion, pred[256,1664]{0,1:T(8,128)(4,1)S(1)} %copy.91, bf16[256,8,128]{0,2,1:T(8,128)(2,1)S(1)} %copy.102, ...), kind=kOutput, calls=%fused_computation.11 | convolution fusion | flops 896270336 | bytes 24821760 | tf_op jit(solution)/shard_map/qhd,khd->hqk/dot_general | solution.py:295
  248.9 5.0 fusion.27
  253.9 7.7 %copy.104 = f32[1664,1024]{1,0:T(8,128)} copy(f32[1664,1024]{0,1:T(8,128)} %bitcast.83) | data formatting | bytes 13631488 | tf_op jit(solution)/shard_map/reshape | solution.py:305
  261.6 2.5 select_convert_fusion
  264.0 4.1 collective-permute-start.4
  268.1 4.7 broadcast_select_fusion
  272.9 17.2 %collective-permute-done.4 = bf16[2,128,2048]{2,1,0:T(8,128)(2,1)S(1)} collective-permute-done((bf16[2,128,2048]{2,1,0:T(8,128)(2,1)S(1)}, bf16[2,128,2048]{2,1,0:T(8,128)(2,1)S(1)}, u32[]{:S(2)}, u32[]{:S(2)}) %collective-permute-start.4) | collective-permute-done | bytes 1048608 | tf_op jit(solution)/shard_map/ppermute | solution.py:316
  290.4 1.9 collective-permute-start.5
  292.4 5.8 %fusion = bf16[1664,2048]{1,0:T(8,128)(2,1)S(1)} fusion(f32[1664,1024]{1,0:T(8,128)} %copy.105, f32[1664,1024]{1,0:T(8,128)} %copy.104), kind=kLoop, calls=%fused_computation.9 | loop fusion | flops 13631488 | bytes 20447232 | tf_op jit(solution)/shard_map/convert.4
  298.2 4.2 collective-permute-done.5
  303.3 14.4 %collective-permute-start.6 = (bf16[128,2048]{1,0:T(8,128)(2,1)}, bf16[128,2048]{1,0:T(8,128)(2,1)S(1)}, u32[]{:S(2)}, u32[]{:S(2)}) collective-permute-start(bf16[128,2048]{1,0:T(8,128)(2,1)} %get-tuple-element.100), channel_id=1, source_target_pairs={{16,0},{20,4},{24,8},{28,12},{0,16},{4,20},{8,24},{12,28},{48,32},... | collective-permute-start | bytes 1572872 | tf_op jit(solution)/shard_map/ppermute | solution.py:323
  317.7 1.7 fusion.25
  319.4 53.4 %collective-permute-start.3 = (bf16[256,2048]{1,0:T(8,128)(2,1)}, bf16[256,2048]{1,0:T(8,128)(2,1)}, u32[]{:S(2)}, u32[]{:S(2)}) collective-permute-start(bf16[256,2048]{1,0:T(8,128)(2,1)} %get-tuple-element.107), channel_id=1, source_target_pairs={{4,0},{8,4},{12,8},{16,12},{20,16},{24,20},{28,24},{32,28},{36,32}... | collective-permute-start | bytes 3145736 | tf_op jit(solution)/shard_map/ppermute | solution.py:19
  372.8 1.9 collective-permute-start.2
  375.5 1.9 collective-permute-start
  377.7 1.5 collective-permute-start.8
  379.2 14.8 %collective-permute-start.7 = (bf16[128,2048]{1,0:T(8,128)(2,1)S(1)}, bf16[128,2048]{1,0:T(8,128)(2,1)S(1)}, u32[]{:S(2)}, u32[]{:S(2)}) collective-permute-start(bf16[128,2048]{1,0:T(8,128)(2,1)S(1)} %fusion.20), channel_id=1, source_target_pairs={{4,0},{8,4},{12,8},{0,12},{20,16},{24,20},{28,24},{16,28},{36,32},... | collective-permute-start | bytes 1572872 | tf_op jit(solution)/shard_map/ppermute | solution.py:333
  394.0 5.2 convolution_convert_fusion
  399.2 18.0 %collective-permute-done.8 = bf16[128,2048]{1,0:T(8,128)(2,1)S(1)} collective-permute-done((bf16[128,2048]{1,0:T(8,128)(2,1)S(1)}, bf16[128,2048]{1,0:T(8,128)(2,1)S(1)}, u32[]{:S(2)}, u32[]{:S(2)}) %collective-permute-start.8) | collective-permute-done | bytes 524320 | tf_op jit(solution)/shard_map/ppermute | solution.py:334
  417.2 62.8 %collective-permute-start.1 = (bf16[256,2048]{1,0:T(8,128)(2,1)}, bf16[256,2048]{1,0:T(8,128)(2,1)}, u32[]{:S(2)}, u32[]{:S(2)}) collective-permute-start(bf16[256,2048]{1,0:T(8,128)(2,1)} %get-tuple-element.106), channel_id=1, source_target_pairs={{12,0},{16,4},{20,8},{24,12},{28,16},{32,20},{36,24},{40,28},{44,3... | collective-permute-start | bytes 3145736 | tf_op jit(solution)/shard_map/ppermute | solution.py:19
  480.0 1.4 collective-permute-done.7
  481.4 1.1 fusion.24
  482.6 3.3 collective-permute-start.9
  487.0 2.6 fusion.19
  489.5 14.1 %collective-permute-done.9 = bf16[128,2048]{1,0:T(8,128)(2,1)} collective-permute-done((bf16[128,2048]{1,0:T(8,128)(2,1)}, bf16[128,2048]{1,0:T(8,128)(2,1)}, u32[]{:S(2)}, u32[]{:S(2)}) %collective-permute-start.9) | collective-permute-done | bytes 524320 | tf_op jit(solution)/shard_map/ppermute | solution.py:336
  503.7 1.5 add_select_fusion
  505.2 33.3 %collective-permute-done.1 = bf16[256,2048]{1,0:T(8,128)(2,1)} collective-permute-done((bf16[256,2048]{1,0:T(8,128)(2,1)}, bf16[256,2048]{1,0:T(8,128)(2,1)}, u32[]{:S(2)}, u32[]{:S(2)}) %collective-permute-start.1) | collective-permute-done | bytes 1048608 | tf_op jit(solution)/shard_map/ppermute | solution.py:19
  538.5 3.3 fusion.15
  542.8 2.0 copy.107
  (71 shorter events, 10.7 us)
Async XLA Ops:
  7.2 161.6 %copy-start = (bf16[256,4096]{1,0:T(8,128)(2,1)S(1)}, bf16[256,4096]{1,0:T(8,128)(2,1)}, u32[]{:S(2)}) copy-start(bf16[256,4096]{1,0:T(8,128)(2,1)} %param.23) | copy-start | bytes 6291460
  7.2 535.6 %reduce-scatter.2.cloned.1.call-start = ((), (), s32[]{:S(2)}) async-start(), calls=%async_computation.1 | async-start | bytes 17301504 | tf_op jit(solution)/shard_map/reduce_scatter | solution.py:354
  149.2 5.6 %copy-start.12 = (pred[256,1664]{1,0:T(8,128)(4,1)S(1)}, pred[256,1664]{1,0:T(8,128)(4,1)}, u32[]{:S(2)}) copy-start(pred[256,1664]{1,0:T(8,128)(4,1)} %copy.90) | copy-start | bytes 1277956
  149.2 5.6 %copy-start.13 = (pred[256,1152]{1,0:T(8,128)(4,1)S(1)}, pred[256,1152]{1,0:T(8,128)(4,1)}, u32[]{:S(2)}) copy-start(pred[256,1152]{1,0:T(8,128)(4,1)} %iota_compare_fusion) | copy-start | bytes 884740
  177.9 1.0 copy-start.11
  187.3 6.7 %copy-start.3 = (bf16[256,1024]{1,0:T(8,128)(2,1)S(1)}, bf16[256,1024]{1,0:T(8,128)(2,1)}, u32[]{:S(2)}) copy-start(bf16[256,1024]{1,0:T(8,128)(2,1)} %shard_map.109) | copy-start | bytes 1572868
  195.3 7.9 %copy-start.4 = (bf16[256,1024]{0,1:T(8,128)(2,1)S(1)}, bf16[256,1024]{0,1:T(8,128)(2,1)}, u32[]{:S(2)}) copy-start(bf16[256,1024]{0,1:T(8,128)(2,1)} %copy.113) | copy-start | bytes 1572868
  248.8 5.1 copy-start.2
  264.0 26.0 %collective-permute-start.4 = (bf16[2,128,2048]{2,1,0:T(8,128)(2,1)S(1)}, bf16[2,128,2048]{2,1,0:T(8,128)(2,1)S(1)}, u32[]{:S(2)}, u32[]{:S(2)}) collective-permute-start(bf16[2,128,2048]{2,1,0:T(8,128)(2,1)S(1)} %bitcast.93), channel_id=1, source_target_pairs={{0,64},{4,68},{8,72},{12,76},{16,80},{20,84},{24,88},{28,92},{32,9... | collective-permute-start | bytes 3145736 | tf_op jit(solution)/shard_map/ppermute | solution.py:316
  290.4 11.9 %collective-permute-start.5 = (bf16[1,128,2048]{2,1,0:T(8,128)(2,1)S(1)}, bf16[1,128,2048]{2,1,0:T(8,128)(2,1)S(1)}, u32[]{:S(2)}, u32[]{:S(2)}) collective-permute-start(bf16[1,128,2048]{2,1,0:T(8,128)(2,1)S(1)} %select_convert_fusion.1), channel_id=1, source_target_pairs={{0,32},{4,36},{8,40},{12,44},{16,48},{20,52},{24,56},{28,60},{32,0... | collective-permute-start | bytes 1572872 | tf_op jit(solution)/shard_map/ppermute | solution.py:316
  303.3 74.2 %collective-permute-start.6 = (bf16[128,2048]{1,0:T(8,128)(2,1)}, bf16[128,2048]{1,0:T(8,128)(2,1)S(1)}, u32[]{:S(2)}, u32[]{:S(2)}) collective-permute-start(bf16[128,2048]{1,0:T(8,128)(2,1)} %get-tuple-element.100), channel_id=1, source_target_pairs={{16,0},{20,4},{24,8},{28,12},{0,16},{4,20},{8,24},{12,28},{48,32},... | collective-permute-start | bytes 1572872 | tf_op jit(solution)/shard_map/ppermute | solution.py:323
  319.4 185.8 %collective-permute-start.3 = (bf16[256,2048]{1,0:T(8,128)(2,1)}, bf16[256,2048]{1,0:T(8,128)(2,1)}, u32[]{:S(2)}, u32[]{:S(2)}) collective-permute-start(bf16[256,2048]{1,0:T(8,128)(2,1)} %get-tuple-element.107), channel_id=1, source_target_pairs={{4,0},{8,4},{12,8},{16,12},{20,16},{24,20},{28,24},{32,28},{36,32}... | collective-permute-start | bytes 3145736 | tf_op jit(solution)/shard_map/ppermute | solution.py:19
  372.8 132.4 %collective-permute-start.2 = (bf16[256,2048]{1,0:T(8,128)(2,1)}, bf16[256,2048]{1,0:T(8,128)(2,1)}, u32[]{:S(2)}, u32[]{:S(2)}) collective-permute-start(bf16[256,2048]{1,0:T(8,128)(2,1)} %get-tuple-element.108), channel_id=1, source_target_pairs={{8,0},{12,4},{16,8},{20,12},{24,16},{28,20},{32,24},{36,28},{40,32... | collective-permute-start | bytes 3145736 | tf_op jit(solution)/shard_map/ppermute | solution.py:19
  375.5 111.4 %collective-permute-start = (bf16[128,2048]{1,0:T(8,128)(2,1)}, bf16[128,2048]{1,0:T(8,128)(2,1)}, u32[]{:S(2)}, u32[]{:S(2)}) collective-permute-start(bf16[128,2048]{1,0:T(8,128)(2,1)} %slice.138), channel_id=1, source_target_pairs={{16,0},{20,4},{24,8},{28,12},{32,16},{36,20},{40,24},{44,28},{48,3... | collective-permute-start | bytes 1572872 | tf_op jit(solution)/shard_map/ppermute | solution.py:19
  377.5 103.9 %copy-start.5 = (bf16[128,2048]{1,0:T(8,128)(2,1)}, bf16[128,2048]{1,0:T(8,128)(2,1)S(1)}, u32[]{:S(2)}) copy-start(bf16[128,2048]{1,0:T(8,128)(2,1)S(1)} %collective-permute-done.6) | copy-start | bytes 1572868
  377.7 39.5 %collective-permute-start.8 = (bf16[128,2048]{1,0:T(8,128)(2,1)S(1)}, bf16[128,2048]{1,0:T(8,128)(2,1)S(1)}, u32[]{:S(2)}, u32[]{:S(2)}) collective-permute-start(bf16[128,2048]{1,0:T(8,128)(2,1)S(1)} %fusion.20), channel_id=1, source_target_pairs={{12,0},{0,4},{4,8},{8,12},{28,16},{16,20},{20,24},{24,28},{44,32},... | collective-permute-start | bytes 1572872 | tf_op jit(solution)/shard_map/ppermute | solution.py:334
  379.2 102.2 %collective-permute-start.7 = (bf16[128,2048]{1,0:T(8,128)(2,1)S(1)}, bf16[128,2048]{1,0:T(8,128)(2,1)S(1)}, u32[]{:S(2)}, u32[]{:S(2)}) collective-permute-start(bf16[128,2048]{1,0:T(8,128)(2,1)S(1)} %fusion.20), channel_id=1, source_target_pairs={{4,0},{8,4},{12,8},{0,12},{20,16},{24,20},{28,24},{16,28},{36,32},... | collective-permute-start | bytes 1572872 | tf_op jit(solution)/shard_map/ppermute | solution.py:333
  417.2 69.7 %copy-start.7 = (bf16[128,2048]{1,0:T(8,128)(2,1)}, bf16[128,2048]{1,0:T(8,128)(2,1)S(1)}, u32[]{:S(2)}) copy-start(bf16[128,2048]{1,0:T(8,128)(2,1)S(1)} %collective-permute-done.8) | copy-start | bytes 1572868
  417.2 121.3 %collective-permute-start.1 = (bf16[256,2048]{1,0:T(8,128)(2,1)}, bf16[256,2048]{1,0:T(8,128)(2,1)}, u32[]{:S(2)}, u32[]{:S(2)}) collective-permute-start(bf16[256,2048]{1,0:T(8,128)(2,1)} %get-tuple-element.106), channel_id=1, source_target_pairs={{12,0},{16,4},{20,8},{24,12},{28,16},{32,20},{36,24},{40,28},{44,3... | collective-permute-start | bytes 3145736 | tf_op jit(solution)/shard_map/ppermute | solution.py:19
  481.4 5.5 copy-start.9
  482.6 21.1 %collective-permute-start.9 = (bf16[128,2048]{1,0:T(8,128)(2,1)}, bf16[128,2048]{1,0:T(8,128)(2,1)}, u32[]{:S(2)}, u32[]{:S(2)}) collective-permute-start(bf16[128,2048]{1,0:T(8,128)(2,1)} %fusion.24), channel_id=1, source_target_pairs={{4,0},{8,4},{12,8},{0,12},{20,16},{24,20},{28,24},{16,28},{36,32},... | collective-permute-start | bytes 1572872 | tf_op jit(solution)/shard_map/ppermute | solution.py:336
  486.9 16.8 %copy-start.6 = (bf16[128,2048]{1,0:T(8,128)(2,1)S(1)}, bf16[128,2048]{1,0:T(8,128)(2,1)}, u32[]{:S(2)}) copy-start(bf16[128,2048]{1,0:T(8,128)(2,1)} %copy-done.5) | copy-start | bytes 1572868
  486.9 16.8 %copy-start.8 = (bf16[128,2048]{1,0:T(8,128)(2,1)S(1)}, bf16[128,2048]{1,0:T(8,128)(2,1)}, u32[]{:S(2)}) copy-start(bf16[128,2048]{1,0:T(8,128)(2,1)} %copy-done.7) | copy-start | bytes 1572868
  486.9 16.8 %copy-start.10 = (bf16[128,2048]{1,0:T(8,128)(2,1)S(1)}, bf16[128,2048]{1,0:T(8,128)(2,1)}, u32[]{:S(2)}) copy-start(bf16[128,2048]{1,0:T(8,128)(2,1)} %copy-done.9) | copy-start | bytes 1572868
  486.9 57.9 %copy-start.1 = (bf16[256,4096]{1,0:T(8,128)(2,1)S(1)}, bf16[256,4096]{1,0:T(8,128)(2,1)}, u32[]{:S(2)}) copy-start(bf16[256,4096]{1,0:T(8,128)(2,1)} %param.23) | copy-start | bytes 6291460
Sparse Core Ops, SparseCore 0:
  178.1 330.9 reduce-scatter.1

commit v13 on v12

--- a/solution.py
+++ b/solution.py
@@ -306,16 +306,31 @@
     )
 
     part = grad_kv[pool_blocks * BLK :].reshape(summary_count, BLK, 2 * width)
-    span = groups // 2
-    while span >= 1:
-        half = part.shape[0] // 2
-        upper = (my_group // span) % 2 == 1
-        keep = jnp.where(upper, part[half:], part[:half])
-        send = jnp.where(upper, part[:half], part[half:])
-        route = [(d, d ^ (span * group)) for d in range(seq_size)]
-        part = keep + lax.ppermute(send.astype(jnp.bfloat16), "seq", route).astype(jnp.float32)
-        span //= 2
-    part = part[0]
+    half_rows = BLK // 2
+    forward_acc = part[:, :half_rows]
+    backward_acc = part[:, half_rows:]
+    to_next = [(d, (d + group) % seq_size) for d in range(seq_size)]
+    to_prev = [(d, (d - group) % seq_size) for d in range(seq_size)]
+    for step in range(groups - 1):
+        out_f = lax.dynamic_index_in_dim(forward_acc, (my_group - step - 1) % groups, 0, keepdims=False)
+        out_b = lax.dynamic_index_in_dim(backward_acc, (my_group + step + 1) % groups, 0, keepdims=False)
+        in_f = lax.ppermute(out_f.astype(jnp.bfloat16), "seq", to_next).astype(jnp.float32)
+        in_b = lax.ppermute(out_b.astype(jnp.bfloat16), "seq", to_prev).astype(jnp.float32)
+        slot_f = (my_group - step - 2) % groups
+        slot_b = (my_group + step + 2) % groups
+        forward_acc = lax.dynamic_update_index_in_dim(
+            forward_acc, lax.dynamic_index_in_dim(forward_acc, slot_f, 0, keepdims=False) + in_f, slot_f, 0
+        )
+        backward_acc = lax.dynamic_update_index_in_dim(
+            backward_acc, lax.dynamic_index_in_dim(backward_acc, slot_b, 0, keepdims=False) + in_b, slot_b, 0
+        )
+    part = jnp.concatenate(
+        [
+            lax.dynamic_index_in_dim(forward_acc, my_group, 0, keepdims=False),
+            lax.dynamic_index_in_dim(backward_acc, my_group, 0, keepdims=False),
+        ],
+        axis=0,
+    )
     lanes = group // 2
     lane = in_group % lanes
     rel_lane = (lane - lead) % lanes

time: 553 us -> 536 us (0.969)
  waiting for transfers between devices: 88.2 us -> 69.6 us
  local copies, waits for them, and re-layouts: 47.7 us -> 54 us
    ppermute x4, starting transfers between devices: 120 us -> 97.8 us  [passed_along(): return lax.ppermute(block, axis, route)]
    ppermute x2 -> x6, waiting for transfers between devices: 21.3 us -> 11.1 us  [the longest x3 5.96 us: local(): lax.ppermute(out_f.astype(jnp.bfloat16), 'seq', to_next).astype(jnp.float32)]
    ppermute x4, waiting for transfers between devices: 33.3 us -> 27.2 us  [passed_along(): return lax.ppermute(block, axis, route)]
    concatenate x0 -> x2, other arithmetic: none -> 5.99 us  [local(): jnp.concatenate([key_part.reshape(-1, width), value_part.reshape(-1, widt...]
    unnamed x37 -> x43, local copies, waits for them, and re-layouts: 13.9 us -> 15.3 us
  transfers between devices with their start and end apart: 11 -> 15, of which waited for: 6 -> 7; matrix products, arithmetic and copies ran while one was open for 21% -> 23% of each run, Pallas kernels for 0% -> 0%
where the time goes in v13:
time: 536 us; the launch traced here: 535 us
  starting transfers between devices  155 us (29%)
  Pallas kernels  143 us (27%)
  waiting for transfers between devices  69.6 us (13%)
  local copies, waits for them, and re-layouts  54 us (10%)
  matrix products  53.8 us (10%)
  other arithmetic  42.8 us (8%)
  between operations  16.7 us (3%)
    pallas_call x1, Pallas kernels, exchange(): pl.pallas_call(functools.partial(exchange_kernel, (seq_size, group, spans...  131 us
    ppermute x4, starting transfers between devices, passed_along(): return lax.ppermute(block, axis, route)  97.8 us
    ppermute x4, waiting for transfers between devices, passed_along(): return lax.ppermute(block, axis, route)  27.2 us
    ppermute x1, starting transfers between devices, local(): lax.ppermute(part.astype(jnp.bfloat16), 'seq', route).astype(jnp.float32)  19 us
    ppermute x1, starting transfers between devices, local(): ahead = lax.ppermute(sent, 'seq', from_lane(1)).astype(jnp.float32)  18.3 us
    ppermute x1, waiting for transfers between devices, local(): behind = lax.ppermute(sent, 'seq', from_lane(-1)).astype(jnp.float32)  17.6 us
    unnamed x43, local copies, waits for them, and re-layouts  15.3 us
    ppermute x1, waiting for transfers between devices, local(): lax.ppermute(part.astype(jnp.bfloat16), 'seq', from_lane(1))  13.6 us
  transfers between devices with their start and end apart: 15, of which 7 were waited for; matrix products, arithmetic and copies ran while one was open for 23% of the time, Pallas kernels for 0%

profile of v13, /device:TPU:40, one launch (start us, length us, event | category | flops | bytes accessed | tf_op | source)
XLA Modules:
  0.0 534.8 jit_solution(10033995992998734717)
XLA Ops:
  7.2 1.4 slice.105
  14.4 2.2 copy.90
  18.7 130.6 %shard_map.108 = (bf16[896,2048]{1,0:T(8,128)(2,1)}, bf16[4,128,2048]{2,1,0:T(8,128)(2,1)S(1)}) custom-call(s32[2]{0:T(128)S(1)} %pad_add_fusion.1.ctl_ref, bf16[256,2048]{1,0:T(8,128)(2,1)S(1)} %constant_dynamic-update-slice_fusion.kv_ref), custom_call_target="tpu_custom_call" | custom-call | tf_op jit(solution)/shard_map/pallas_call | solution.py:152
  149.3 5.6 %pad_maximum_fusion.1.k_ref.v_ref = bf16[1664,2048]{1,0:T(8,128)(2,1)} fusion(bf16[512,2048]{1,0:T(8,128)(2,1)S(1)} %bitcast.120, bf16[256,2048]{1,0:T(8,128)(2,1)S(1)} %constant_dynamic-update-slice_fusion.kv_ref, bf16[896,2048]{1,0:T(8,128)(2,1)} %get-tuple-element.78), kind=kLoop, calls=%fused_computation.16 | loop fusion | flops 20447232 | bytes 13631488 | tf_op jit(solution)/shard_map/concatenate | solution.py:254
  154.9 1.6 broadcast_select_fusion
  156.5 12.3 %shard_map.109 = bf16[256,1024]{1,0:T(8,128)(2,1)} custom-call(bf16[256,1024]{1,0:T(8,128)(2,1)} %q_ref.1, bf16[1664,2048]{1,0:T(8,128)(2,1)} %pad_maximum_fusion.1.k_ref.v_ref, bf16[1664,2048]{1,0:T(8,128)(2,1)} %pad_maximum_fusion.1.k_ref.v_ref, f32[256,1664]{1,0:T(8,128)} %get-tuple-element.100.bias_ref), custom_call_target="tpu_custom_call" | custom-call | flops 1744830464 | bytes 9568256 | tf_op jit(solution)/shard_map/pallas_call | solution.py:197
  168.8 9.1 %convolution_bitcast_fusion = f32[4096,1024]{0,1:T(8,128)} fusion(bf16[256,1024]{1,0:T(8,128)(2,1)} %shard_map.109, bf16[256,4096]{1,0:T(8,128)(2,1)S(1)} %copy-done), kind=kOutput, calls=%fused_computation.14 | convolution fusion | flops 2147483648 | bytes 19398656 | tf_op jit(solution)/shard_map/dot_general | solution.py:370
  179.9 7.4 %slice_bitcast_fusion = (bf16[208,8,8,128]{3,2,1,0:T(8,128)(2,1)}, bf16[1664,1024]{1,0:T(8,128)(2,1)}) fusion(bf16[1664,2048]{1,0:T(8,128)(2,1)} %pad_maximum_fusion.1.k_ref.v_ref), kind=kLoop, calls=%fused_computation.24 | loop fusion | bytes 13631488
  187.3 5.7 %copy.112 = bf16[1664,1024]{0,1:T(8,128)(2,1)} copy(bf16[1664,1024]{1,0:T(8,128)(2,1)} %get-tuple-element.106) | data formatting | bytes 6815744 | tf_op jit(solution)/shard_map/reshape | solution.py:255
  194.2 1.2 copy.117
  195.4 5.7 %fusion.15 = bf16[32,8,8,128]{3,1,2,0:T(8,128)(2,1)S(1)} fusion(bf16[256,4096]{1,0:T(8,128)(2,1)S(1)} %copy-done, bf16[4096,1024]{1,0:T(8,128)(2,1)} %param.24), kind=kOutput, calls=%fused_computation.34 | convolution fusion | flops 2147745792 | bytes 11010048 | tf_op jit(solution)/shard_map/dot_general | solution.py:234
  201.5 1.6 multiply_reduce_fusion
  203.2 9.4 %fusion.2 = (f32[8,256]{1,0:T(8,128)S(1)}, f32[8,1664,256]{2,1,0:T(8,128)}) fusion(pred[256,1664]{0,1:T(8,128)(4,1)S(1)} %copy.91, bf16[1664,8,128]{0,2,1:T(8,128)(2,1)} %bitcast.121, bf16[256,8,128]{0,2,1:T(8,128)(2,1)S(1)} %bitcast.128), kind=kOutput, calls=%fused_computation.13 | convolution fusion | flops 882636800 | bytes 17997824 | tf_op jit(solution)/shard_map/qhd,khd->hqk/dot_general | solution.py:282
  212.6 8.0 %exponential_reduce_fusion = f32[8,256]{1,0:T(8,128)S(1)} fusion(f32[8,1664,256]{2,1,0:T(8,128)} %get-tuple-element.112, f32[8,256]{1,0:T(8,128)S(1)} %get-tuple-element.111, pred[256,1664]{0,1:T(8,128)(4,1)S(1)} %copy.91), kind=kLoop, calls=%fused_computation.11 | loop fusion | flops 13629440 | bytes 14073856 | tf_op jit(solution)/shard_map/reduce_sum | solution.py:287
  220.6 11.3 %fusion.3 = f32[8,128,1664]{2,1,0:T(8,128)} fusion(bf16[256,8,128]{0,2,1:T(8,128)(2,1)S(1)} %copy.102, f32[8,1664,256]{2,1,0:T(8,128)} %get-tuple-element.112, f32[8,256]{1,0:T(8,128)S(1)} %log_add_fusion, pred[256,1664]{0,1:T(8,128)(4,1)S(1)} %copy.91), kind=kOutput, calls=%fused_computation.15 | convolution fusion | flops 886046720 | bytes 21405696 | tf_op jit(solution)/shard_map/hqk,qhd->khd/dot_general | solution.py:301
  232.0 7.7 %copy.105 = f32[1664,1024]{1,0:T(8,128)} copy(f32[1664,1024]{0,1:T(8,128)} %bitcast.124) | data formatting | bytes 13631488 | tf_op jit(solution)/shard_map/reshape | solution.py:305
  239.7 9.1 %multiply_convert_fusion = bf16[8,256,1664]{1,2,0:T(8,128)(2,1)S(1)} fusion(f32[8,1664,256]{2,1,0:T(8,128)} %get-tuple-element.112, f32[8,256]{1,0:T(8,128)S(1)} %copy.96, f32[8,256]{1,0:T(8,128)S(1)} %log_add_fusion, pred[256,1664]{0,1:T(8,128)(4,1)S(1)} %copy.91, bf16[256,8,128]{0,2,1:T(8,128)(2,1)S(1)} %copy.102, ...), kind=kOutput, calls=%fused_computation.9 | convolution fusion | flops 896270336 | bytes 24821760 | tf_op jit(solution)/shard_map/qhd,khd->hqk/dot_general | solution.py:295
  248.8 5.0 fusion.34
  253.8 7.7 %copy.104 = f32[1664,1024]{1,0:T(8,128)} copy(f32[1664,1024]{0,1:T(8,128)} %bitcast.123) | data formatting | bytes 13631488 | tf_op jit(solution)/shard_map/reshape | solution.py:305
  261.5 2.8 fusion.9
  264.6 1.3 copy-done.4
  266.0 2.1 collective-permute-start.7
  269.2 8.1 %fusion = bf16[1664,2048]{1,0:T(8,128)(2,1)} fusion(f32[1664,1024]{1,0:T(8,128)} %copy.105, f32[1664,1024]{1,0:T(8,128)} %copy.104), kind=kLoop, calls=%fused_computation.7 | loop fusion | flops 13631488 | bytes 20447232 | tf_op jit(solution)/shard_map/convert.4
  279.4 1.2 fusion.25
  280.6 2.8 collective-permute-start.8
  284.8 2.6 collective-permute-done.8
  287.5 3.7 collective-permute-start.9
  292.6 2.5 collective-permute-done.9
  295.2 4.9 collective-permute-done.6
  300.3 19.0 %collective-permute-start.10 = (bf16[128,2048]{1,0:T(8,128)(2,1)S(1)}, bf16[128,2048]{1,0:T(8,128)(2,1)S(1)}, u32[]{:S(2)}, u32[]{:S(2)}) collective-permute-start(bf16[128,2048]{1,0:T(8,128)(2,1)S(1)} %fusion.19), channel_id=1, source_target_pairs={{16,0},{20,4},{24,8},{28,12},{0,16},{4,20},{8,24},{12,28},{48,32},... | collective-permute-start | bytes 1572872 | tf_op jit(solution)/shard_map/ppermute | solution.py:338
  319.3 1.8 fusion.31
  321.1 23.0 %collective-permute-start.3 = (bf16[256,2048]{1,0:T(8,128)(2,1)}, bf16[256,2048]{1,0:T(8,128)(2,1)}, u32[]{:S(2)}, u32[]{:S(2)}) collective-permute-start(bf16[256,2048]{1,0:T(8,128)(2,1)} %get-tuple-element.103), channel_id=1, source_target_pairs={{4,0},{8,4},{12,8},{16,12},{20,16},{24,20},{28,24},{32,28},{36,32}... | collective-permute-start | bytes 3145736 | tf_op jit(solution)/shard_map/ppermute | solution.py:19
  344.0 2.8 collective-permute-start.2
  347.7 1.9 collective-permute-start
  349.7 3.2 fusion.12
  353.1 2.7 collective-permute-start.12
  355.8 18.3 %collective-permute-start.11 = (bf16[128,2048]{1,0:T(8,128)(2,1)S(1)}, bf16[128,2048]{1,0:T(8,128)(2,1)S(1)}, u32[]{:S(2)}, u32[]{:S(2)}) collective-permute-start(bf16[128,2048]{1,0:T(8,128)(2,1)S(1)} %fusion.20), channel_id=1, source_target_pairs={{4,0},{8,4},{12,8},{0,12},{20,16},{24,20},{28,24},{16,28},{36,32},... | collective-permute-start | bytes 1572872 | tf_op jit(solution)/shard_map/ppermute | solution.py:348
  374.1 4.1 convolution_convert_fusion
  378.2 17.6 %collective-permute-done.12 = bf16[128,2048]{1,0:T(8,128)(2,1)S(1)} collective-permute-done((bf16[128,2048]{1,0:T(8,128)(2,1)S(1)}, bf16[128,2048]{1,0:T(8,128)(2,1)S(1)}, u32[]{:S(2)}, u32[]{:S(2)}) %collective-permute-start.12) | collective-permute-done | bytes 524320 | tf_op jit(solution)/shard_map/ppermute | solution.py:349
  395.8 70.1 %collective-permute-start.1 = (bf16[256,2048]{1,0:T(8,128)(2,1)}, bf16[256,2048]{1,0:T(8,128)(2,1)}, u32[]{:S(2)}, u32[]{:S(2)}) collective-permute-start(bf16[256,2048]{1,0:T(8,128)(2,1)} %get-tuple-element.102), channel_id=1, source_target_pairs={{12,0},{16,4},{20,8},{24,12},{28,16},{32,20},{36,24},{40,28},{44,3... | collective-permute-start | bytes 3145736 | tf_op jit(solution)/shard_map/ppermute | solution.py:19
  466.0 1.1 fusion.30
  467.1 8.1 %collective-permute-start.13 = (bf16[128,2048]{1,0:T(8,128)(2,1)}, bf16[128,2048]{1,0:T(8,128)(2,1)}, u32[]{:S(2)}, u32[]{:S(2)}) collective-permute-start(bf16[128,2048]{1,0:T(8,128)(2,1)} %fusion.30), channel_id=1, source_target_pairs={{4,0},{8,4},{12,8},{0,12},{20,16},{24,20},{28,24},{16,28},{36,32},... | collective-permute-start | bytes 1572872 | tf_op jit(solution)/shard_map/ppermute | solution.py:351
  476.3 2.5 fusion.18
  478.8 13.6 %collective-permute-done.13 = bf16[128,2048]{1,0:T(8,128)(2,1)} collective-permute-done((bf16[128,2048]{1,0:T(8,128)(2,1)}, bf16[128,2048]{1,0:T(8,128)(2,1)}, u32[]{:S(2)}, u32[]{:S(2)}) %collective-permute-start.13) | collective-permute-done | bytes 524320 | tf_op jit(solution)/shard_map/ppermute | solution.py:351
  492.5 1.9 add_select_fusion
  494.4 27.2 %collective-permute-done.1 = bf16[256,2048]{1,0:T(8,128)(2,1)} collective-permute-done((bf16[256,2048]{1,0:T(8,128)(2,1)}, bf16[256,2048]{1,0:T(8,128)(2,1)}, u32[]{:S(2)}, u32[]{:S(2)}) %collective-permute-start.1) | collective-permute-done | bytes 1048608 | tf_op jit(solution)/shard_map/ppermute | solution.py:19
  521.6 3.3 fusion.14
  526.0 2.0 copy.107
  (105 shorter events, 19.1 us)
Async XLA Ops:
  7.2 161.6 %copy-start = (bf16[256,4096]{1,0:T(8,128)(2,1)S(1)}, bf16[256,4096]{1,0:T(8,128)(2,1)}, u32[]{:S(2)}) copy-start(bf16[256,4096]{1,0:T(8,128)(2,1)} %param.23) | copy-start | bytes 6291460
  7.2 518.8 %reduce-scatter.2.cloned.1.call-start = ((), (), s32[]{:S(2)}) async-start(), calls=%async_computation.1 | async-start | bytes 17301504 | tf_op jit(solution)/shard_map/reduce_scatter | solution.py:369
  149.2 5.6 %copy-start.13 = (pred[256,1664]{1,0:T(8,128)(4,1)S(1)}, pred[256,1664]{1,0:T(8,128)(4,1)}, u32[]{:S(2)}) copy-start(pred[256,1664]{1,0:T(8,128)(4,1)} %copy.90) | copy-start | bytes 1277956
  149.2 5.6 %copy-start.14 = (pred[256,1152]{1,0:T(8,128)(4,1)S(1)}, pred[256,1152]{1,0:T(8,128)(4,1)}, u32[]{:S(2)}) copy-start(pred[256,1152]{1,0:T(8,128)(4,1)} %iota_compare_fusion) | copy-start | bytes 884740
  177.9 1.0 copy-start.12
  187.3 6.7 %copy-start.6 = (bf16[256,1024]{1,0:T(8,128)(2,1)S(1)}, bf16[256,1024]{1,0:T(8,128)(2,1)}, u32[]{:S(2)}) copy-start(bf16[256,1024]{1,0:T(8,128)(2,1)} %shard_map.109) | copy-start | bytes 1572868
  201.1 2.1 copy-start.7
  248.8 5.0 copy-start.2
  264.6 1.3 copy-start.4
  266.0 12.6 %collective-permute-start.7 = (bf16[64,2048]{1,0:T(8,128)(2,1)S(1)}, bf16[64,2048]{1,0:T(8,128)(2,1)S(1)}, u32[]{:S(2)}, u32[]{:S(2)}) collective-permute-start(bf16[64,2048]{1,0:T(8,128)(2,1)S(1)} %fusion.24), channel_id=1, source_target_pairs={{0,96},{4,100},{8,104},{12,108},{16,112},{20,116},{24,120},{28,124... | collective-permute-start | bytes 786440 | tf_op jit(solution)/shard_map/ppermute | solution.py:318
  268.8 15.8 %collective-permute-start.4 = (bf16[64,2048]{1,0:T(8,128)(2,1)}, bf16[64,2048]{1,0:T(8,128)(2,1)S(1)}, u32[]{:S(2)}, u32[]{:S(2)}) collective-permute-start(bf16[64,2048]{1,0:T(8,128)(2,1)} %fusion.21), channel_id=1, source_target_pairs={{0,32},{4,36},{8,40},{12,44},{16,48},{20,52},{24,56},{28,60},{32,6... | collective-permute-start | bytes 786440 | tf_op jit(solution)/shard_map/ppermute | solution.py:317
  279.4 8.0 %copy-start.5 = (f32[4,64,2048]{2,1,0:T(8,128)S(1)}, f32[4,64,2048]{2,1,0:T(8,128)}, u32[]{:S(2)}) copy-start(f32[4,64,2048]{2,1,0:T(8,128)} %bitcast_dynamic-update-slice_fusion.2) | copy-start | bytes 6291460
  280.6 6.8 %collective-permute-start.8 = (bf16[64,2048]{1,0:T(8,128)(2,1)S(1)}, bf16[64,2048]{1,0:T(8,128)(2,1)S(1)}, u32[]{:S(2)}, u32[]{:S(2)}) collective-permute-start(bf16[64,2048]{1,0:T(8,128)(2,1)S(1)} %fusion.25), channel_id=1, source_target_pairs={{0,96},{4,100},{8,104},{12,108},{16,112},{20,116},{24,120},{28,124... | collective-permute-start | bytes 786440 | tf_op jit(solution)/shard_map/ppermute | solution.py:318
  284.6 34.7 %slice-start = ((s8[6815744]{0:T(1024)(128)(4,1)}), s8[4194304]{0:T(1024)(128)(4,1)S(1)}, s32[]{:S(2)}) async-start(s8[6815744]{0:T(1024)(128)(4,1)} %bitcast.126), calls=%async_computation.2 | async-start | bytes 8388608
  284.7 7.7 %collective-permute-start.5 = (bf16[64,2048]{1,0:T(8,128)(2,1)S(1)}, bf16[64,2048]{1,0:T(8,128)(2,1)S(1)}, u32[]{:S(2)}, u32[]{:S(2)}) collective-permute-start(bf16[64,2048]{1,0:T(8,128)(2,1)S(1)} %fusion.22), channel_id=1, source_target_pairs={{0,32},{4,36},{8,40},{12,44},{16,48},{20,52},{24,56},{28,60},{32,6... | collective-permute-start | bytes 786440 | tf_op jit(solution)/shard_map/ppermute | solution.py:317
  287.5 7.6 %collective-permute-start.9 = (bf16[64,2048]{1,0:T(8,128)(2,1)S(1)}, bf16[64,2048]{1,0:T(8,128)(2,1)S(1)}, u32[]{:S(2)}, u32[]{:S(2)}) collective-permute-start(bf16[64,2048]{1,0:T(8,128)(2,1)S(1)} %fusion.26), channel_id=1, source_target_pairs={{0,96},{4,100},{8,104},{12,108},{16,112},{20,116},{24,120},{28,124... | collective-permute-start | bytes 786440 | tf_op jit(solution)/shard_map/ppermute | solution.py:318
  292.4 26.9 %slice-start.1 = ((s8[6815744]{0:T(1024)(128)(4,1)}), s8[2621440]{0:T(1024)(128)(4,1)S(1)}, s32[]{:S(2)}) async-start(s8[6815744]{0:T(1024)(128)(4,1)} %bitcast.126), calls=%async_computation.3 | async-start | bytes 5242880
  292.5 7.7 %collective-permute-start.6 = (bf16[64,2048]{1,0:T(8,128)(2,1)S(1)}, bf16[64,2048]{1,0:T(8,128)(2,1)S(1)}, u32[]{:S(2)}, u32[]{:S(2)}) collective-permute-start(bf16[64,2048]{1,0:T(8,128)(2,1)S(1)} %fusion.23), channel_id=1, source_target_pairs={{0,32},{4,36},{8,40},{12,44},{16,48},{20,52},{24,56},{28,60},{32,6... | collective-permute-start | bytes 786440 | tf_op jit(solution)/shard_map/ppermute | solution.py:317
  300.3 52.7 %collective-permute-start.10 = (bf16[128,2048]{1,0:T(8,128)(2,1)S(1)}, bf16[128,2048]{1,0:T(8,128)(2,1)S(1)}, u32[]{:S(2)}, u32[]{:S(2)}) collective-permute-start(bf16[128,2048]{1,0:T(8,128)(2,1)S(1)} %fusion.19), channel_id=1, source_target_pairs={{16,0},{20,4},{24,8},{28,12},{0,16},{4,20},{8,24},{12,28},{48,32},... | collective-permute-start | bytes 1572872 | tf_op jit(solution)/shard_map/ppermute | solution.py:338
  321.1 173.4 %collective-permute-start.3 = (bf16[256,2048]{1,0:T(8,128)(2,1)}, bf16[256,2048]{1,0:T(8,128)(2,1)}, u32[]{:S(2)}, u32[]{:S(2)}) collective-permute-start(bf16[256,2048]{1,0:T(8,128)(2,1)} %get-tuple-element.103), channel_id=1, source_target_pairs={{4,0},{8,4},{12,8},{16,12},{20,16},{24,20},{28,24},{32,28},{36,32}... | collective-permute-start | bytes 3145736 | tf_op jit(solution)/shard_map/ppermute | solution.py:19
  344.0 150.4 %collective-permute-start.2 = (bf16[256,2048]{1,0:T(8,128)(2,1)}, bf16[256,2048]{1,0:T(8,128)(2,1)}, u32[]{:S(2)}, u32[]{:S(2)}) collective-permute-start(bf16[256,2048]{1,0:T(8,128)(2,1)} %get-tuple-element.104), channel_id=1, source_target_pairs={{8,0},{12,4},{16,8},{20,12},{24,16},{28,20},{32,24},{36,28},{40,32... | collective-permute-start | bytes 3145736 | tf_op jit(solution)/shard_map/ppermute | solution.py:19
  347.7 128.6 %collective-permute-start = (bf16[128,2048]{1,0:T(8,128)(2,1)}, bf16[128,2048]{1,0:T(8,128)(2,1)}, u32[]{:S(2)}, u32[]{:S(2)}) collective-permute-start(bf16[128,2048]{1,0:T(8,128)(2,1)} %slice.125), channel_id=1, source_target_pairs={{16,0},{20,4},{24,8},{28,12},{32,16},{36,20},{40,24},{44,28},{48,3... | collective-permute-start | bytes 1572872 | tf_op jit(solution)/shard_map/ppermute | solution.py:19
  349.7 24.4 %copy-start.3 = (bf16[1664,1024]{0,1:T(8,128)(2,1)S(1)}, bf16[1664,1024]{0,1:T(8,128)(2,1)}, u32[]{:S(2)}) copy-start(bf16[1664,1024]{0,1:T(8,128)(2,1)} %copy.112) | copy-start | bytes 10223620
  353.0 113.0 %copy-start.8 = (bf16[128,2048]{1,0:T(8,128)(2,1)}, bf16[128,2048]{1,0:T(8,128)(2,1)S(1)}, u32[]{:S(2)}) copy-start(bf16[128,2048]{1,0:T(8,128)(2,1)S(1)} %collective-permute-done.10) | copy-start | bytes 1572868
  353.1 42.7 %collective-permute-start.12 = (bf16[128,2048]{1,0:T(8,128)(2,1)S(1)}, bf16[128,2048]{1,0:T(8,128)(2,1)S(1)}, u32[]{:S(2)}, u32[]{:S(2)}) collective-permute-start(bf16[128,2048]{1,0:T(8,128)(2,1)S(1)} %fusion.20), channel_id=1, source_target_pairs={{12,0},{0,4},{4,8},{8,12},{28,16},{16,20},{20,24},{24,28},{44,32},... | collective-permute-start | bytes 1572872 | tf_op jit(solution)/shard_map/ppermute | solution.py:349
  355.8 110.2 %collective-permute-start.11 = (bf16[128,2048]{1,0:T(8,128)(2,1)S(1)}, bf16[128,2048]{1,0:T(8,128)(2,1)S(1)}, u32[]{:S(2)}, u32[]{:S(2)}) collective-permute-start(bf16[128,2048]{1,0:T(8,128)(2,1)S(1)} %fusion.20), channel_id=1, source_target_pairs={{4,0},{8,4},{12,8},{0,12},{20,16},{24,20},{28,24},{16,28},{36,32},... | collective-permute-start | bytes 1572872 | tf_op jit(solution)/shard_map/ppermute | solution.py:348
  395.8 83.0 %copy-start.10 = (bf16[128,2048]{1,0:T(8,128)(2,1)}, bf16[128,2048]{1,0:T(8,128)(2,1)S(1)}, u32[]{:S(2)}) copy-start(bf16[128,2048]{1,0:T(8,128)(2,1)S(1)} %collective-permute-done.12) | copy-start | bytes 1572868
  395.8 125.8 %collective-permute-start.1 = (bf16[256,2048]{1,0:T(8,128)(2,1)}, bf16[256,2048]{1,0:T(8,128)(2,1)}, u32[]{:S(2)}, u32[]{:S(2)}) collective-permute-start(bf16[256,2048]{1,0:T(8,128)(2,1)} %get-tuple-element.102), channel_id=1, source_target_pairs={{12,0},{16,4},{20,8},{24,12},{28,16},{32,20},{36,24},{40,28},{44,3... | collective-permute-start | bytes 3145736 | tf_op jit(solution)/shard_map/ppermute | solution.py:19
  466.0 12.8 %copy-start.11 = (bf16[128,2048]{1,0:T(8,128)(2,1)}, bf16[128,2048]{1,0:T(8,128)(2,1)S(1)}, u32[]{:S(2)}) copy-start(bf16[128,2048]{1,0:T(8,128)(2,1)S(1)} %collective-permute-done.11) | copy-start | bytes 1572868
  467.1 25.3 %collective-permute-start.13 = (bf16[128,2048]{1,0:T(8,128)(2,1)}, bf16[128,2048]{1,0:T(8,128)(2,1)}, u32[]{:S(2)}, u32[]{:S(2)}) collective-permute-start(bf16[128,2048]{1,0:T(8,128)(2,1)} %fusion.30), channel_id=1, source_target_pairs={{4,0},{8,4},{12,8},{0,12},{20,16},{24,20},{28,24},{16,28},{36,32},... | collective-permute-start | bytes 1572872 | tf_op jit(solution)/shard_map/ppermute | solution.py:351
  476.3 16.2 %copy-start.9 = (bf16[128,2048]{1,0:T(8,128)(2,1)S(1)}, bf16[128,2048]{1,0:T(8,128)(2,1)}, u32[]{:S(2)}) copy-start(bf16[128,2048]{1,0:T(8,128)(2,1)} %copy-done.8) | copy-start | bytes 1572868
  492.5 35.5 %copy-start.1 = (bf16[256,4096]{1,0:T(8,128)(2,1)S(1)}, bf16[256,4096]{1,0:T(8,128)(2,1)}, u32[]{:S(2)}) copy-start(bf16[256,4096]{1,0:T(8,128)(2,1)} %param.23) | copy-start | bytes 6291460
Sparse Core Ops, SparseCore 0:
  178.0 324.9 reduce-scatter.1

commit v14 on v13

--- a/solution.py
+++ b/solution.py
@@ -93,20 +93,31 @@
         mine = jnp.where(sum_local == block, kv_ref[block * BLK : (block + 1) * BLK, :], mine)
     held[...] = mine
     slot = len(spans)
-    steps = [(in_ring(1), rel_lane == 1), (in_ring(2), rel_lane >= 2), (flip(), in_group >= lanes)]
-    for stage, (target, take) in enumerate(steps):
-        copy = pltpu.make_async_remote_copy(
-            src_ref=held,
-            dst_ref=hop_buf.at[stage],
-            send_sem=sends.at[slot],
-            recv_sem=recvs.at[slot],
-            device_id={"seq": target},
-            device_id_type=mesh_id,
-        )
-        copy.start()
-        copy.wait()
-        held[...] = jnp.where(take, hop_buf[stage], held[...])
-        slot += 1
+    stages = [
+        [(in_ring(1), rel_lane == 1), (in_ring(-1), rel_lane == lanes - 1)],
+        [(in_ring(1), rel_lane == 2)],
+        [(flip(), in_group >= lanes)],
+    ]
+    stage = 0
+    for moves in stages:
+        copies = []
+        for target, take in moves:
+            copy = pltpu.make_async_remote_copy(
+                src_ref=held,
+                dst_ref=hop_buf.at[stage],
+                send_sem=sends.at[slot],
+                recv_sem=recvs.at[slot],
+                device_id={"seq": target},
+                device_id_type=mesh_id,
+            )
+            copy.start()
+            copies.append((copy, stage, take))
+            slot += 1
+            stage += 1
+        for copy, _, _ in copies:
+            copy.wait()
+        for _, index, take in copies:
+            held[...] = jnp.where(take, hop_buf[index], held[...])
 
     copy = pltpu.make_async_remote_copy(
         src_ref=held,
@@ -147,7 +158,7 @@
     tok_dev, cols = kv.shape
     back_rows = sum(spans) * BLK
     groups = seq_size // group
-    copies = len(spans) + 5
+    copies = len(spans) + 6
     ctl = jnp.stack([lead, sum_local]).astype(jnp.int32)
     return pl.pallas_call(
         functools.partial(exchange_kernel, (seq_size, group, spans)),
@@ -165,7 +176,7 @@
         ),
         scratch_shapes=[
             pltpu.VMEM((back_rows, cols), kv.dtype),
-            pltpu.VMEM((3, BLK, cols), kv.dtype),
+            pltpu.VMEM((4, BLK, cols), kv.dtype),
             pltpu.VMEM((BLK, cols), kv.dtype),
             pltpu.VMEM((2, BLK, cols), kv.dtype),
             pltpu.VMEM((BLK, cols), kv.dtype),

time: 536 us -> 536 us (level)
  no operation moved by 1% of the time
where the time goes in v14:
time: 536 us; the launch traced here: 534 us
  starting transfers between devices  152 us (28%)
  Pallas kernels  144 us (27%)
  waiting for transfers between devices  71.8 us (13%)
  local copies, waits for them, and re-layouts  54 us (10%)
  matrix products  53.8 us (10%)
  other arithmetic  42.8 us (8%)
  between operations  16.7 us (3%)
    pallas_call x1, Pallas kernels, exchange(): pl.pallas_call(functools.partial(exchange_kernel, (seq_size, group, spans...  131 us
    ppermute x4, starting transfers between devices, passed_along(): return lax.ppermute(block, axis, route)  95.7 us
    ppermute x4, waiting for transfers between devices, passed_along(): return lax.ppermute(block, axis, route)  27.8 us
    ppermute x1, starting transfers between devices, local(): lax.ppermute(part.astype(jnp.bfloat16), 'seq', route).astype(jnp.float32)  19.3 us
    ppermute x1, starting transfers between devices, local(): ahead = lax.ppermute(sent, 'seq', from_lane(1)).astype(jnp.float32)  18.1 us
    ppermute x1, waiting for transfers between devices, local(): behind = lax.ppermute(sent, 'seq', from_lane(-1)).astype(jnp.float32)  17.9 us
    unnamed x43, local copies, waits for them, and re-layouts  15.3 us
    ppermute x1, waiting for transfers between devices, local(): lax.ppermute(part.astype(jnp.bfloat16), 'seq', from_lane(1))  13.6 us
  transfers between devices with their start and end apart: 15, of which 7 were waited for; matrix products, arithmetic and copies ran while one was open for 23% of the time, Pallas kernels for 0%

profile of v14, /device:TPU:40, one launch (start us, length us, event | category | flops | bytes accessed | tf_op | source)
XLA Modules:
  0.0 534.3 jit_solution(1423408660895549166)
XLA Ops:
  7.2 1.4 slice.105
  14.4 2.2 copy.90
  18.7 131.2 %shard_map.108 = (bf16[896,2048]{1,0:T(8,128)(2,1)}, bf16[4,128,2048]{2,1,0:T(8,128)(2,1)S(1)}) custom-call(s32[2]{0:T(128)S(1)} %pad_add_fusion.1.ctl_ref, bf16[256,2048]{1,0:T(8,128)(2,1)S(1)} %constant_dynamic-update-slice_fusion.kv_ref), custom_call_target="tpu_custom_call" | custom-call | tf_op jit(solution)/shard_map/pallas_call | solution.py:163
  150.0 5.6 %pad_maximum_fusion.1.k_ref.v_ref = bf16[1664,2048]{1,0:T(8,128)(2,1)} fusion(bf16[512,2048]{1,0:T(8,128)(2,1)S(1)} %bitcast.120, bf16[256,2048]{1,0:T(8,128)(2,1)S(1)} %constant_dynamic-update-slice_fusion.kv_ref, bf16[896,2048]{1,0:T(8,128)(2,1)} %get-tuple-element.78), kind=kLoop, calls=%fused_computation.16 | loop fusion | flops 20447232 | bytes 13631488 | tf_op jit(solution)/shard_map/concatenate | solution.py:265
  155.6 1.6 broadcast_select_fusion
  157.2 12.3 %shard_map.109 = bf16[256,1024]{1,0:T(8,128)(2,1)} custom-call(bf16[256,1024]{1,0:T(8,128)(2,1)} %q_ref.1, bf16[1664,2048]{1,0:T(8,128)(2,1)} %pad_maximum_fusion.1.k_ref.v_ref, bf16[1664,2048]{1,0:T(8,128)(2,1)} %pad_maximum_fusion.1.k_ref.v_ref, f32[256,1664]{1,0:T(8,128)} %get-tuple-element.100.bias_ref), custom_call_target="tpu_custom_call" | custom-call | flops 1744830464 | bytes 9568256 | tf_op jit(solution)/shard_map/pallas_call | solution.py:208
  169.4 9.1 %convolution_bitcast_fusion = f32[4096,1024]{0,1:T(8,128)} fusion(bf16[256,1024]{1,0:T(8,128)(2,1)} %shard_map.109, bf16[256,4096]{1,0:T(8,128)(2,1)S(1)} %copy-done), kind=kOutput, calls=%fused_computation.14 | convolution fusion | flops 2147483648 | bytes 19398656 | tf_op jit(solution)/shard_map/dot_general | solution.py:381
  180.6 7.4 %slice_bitcast_fusion = (bf16[208,8,8,128]{3,2,1,0:T(8,128)(2,1)}, bf16[1664,1024]{1,0:T(8,128)(2,1)}) fusion(bf16[1664,2048]{1,0:T(8,128)(2,1)} %pad_maximum_fusion.1.k_ref.v_ref), kind=kLoop, calls=%fused_computation.24 | loop fusion | bytes 13631488
  188.0 5.7 %copy.112 = bf16[1664,1024]{0,1:T(8,128)(2,1)} copy(bf16[1664,1024]{1,0:T(8,128)(2,1)} %get-tuple-element.106) | data formatting | bytes 6815744 | tf_op jit(solution)/shard_map/reshape | solution.py:266
  194.9 1.2 copy.117
  196.1 5.7 %fusion.15 = bf16[32,8,8,128]{3,1,2,0:T(8,128)(2,1)S(1)} fusion(bf16[256,4096]{1,0:T(8,128)(2,1)S(1)} %copy-done, bf16[4096,1024]{1,0:T(8,128)(2,1)} %param.24), kind=kOutput, calls=%fused_computation.34 | convolution fusion | flops 2147745792 | bytes 11010048 | tf_op jit(solution)/shard_map/dot_general | solution.py:245
  202.2 1.6 multiply_reduce_fusion
  203.9 9.4 %fusion.2 = (f32[8,256]{1,0:T(8,128)S(1)}, f32[8,1664,256]{2,1,0:T(8,128)}) fusion(pred[256,1664]{0,1:T(8,128)(4,1)S(1)} %copy.91, bf16[1664,8,128]{0,2,1:T(8,128)(2,1)} %bitcast.121, bf16[256,8,128]{0,2,1:T(8,128)(2,1)S(1)} %bitcast.128), kind=kOutput, calls=%fused_computation.13 | convolution fusion | flops 882636800 | bytes 17997824 | tf_op jit(solution)/shard_map/qhd,khd->hqk/dot_general | solution.py:293
  213.3 8.0 %exponential_reduce_fusion = f32[8,256]{1,0:T(8,128)S(1)} fusion(f32[8,1664,256]{2,1,0:T(8,128)} %get-tuple-element.112, f32[8,256]{1,0:T(8,128)S(1)} %get-tuple-element.111, pred[256,1664]{0,1:T(8,128)(4,1)S(1)} %copy.91), kind=kLoop, calls=%fused_computation.11 | loop fusion | flops 13629440 | bytes 14073856 | tf_op jit(solution)/shard_map/reduce_sum | solution.py:298
  221.3 11.3 %fusion.3 = f32[8,128,1664]{2,1,0:T(8,128)} fusion(bf16[256,8,128]{0,2,1:T(8,128)(2,1)S(1)} %copy.102, f32[8,1664,256]{2,1,0:T(8,128)} %get-tuple-element.112, f32[8,256]{1,0:T(8,128)S(1)} %log_add_fusion, pred[256,1664]{0,1:T(8,128)(4,1)S(1)} %copy.91), kind=kOutput, calls=%fused_computation.15 | convolution fusion | flops 886046720 | bytes 21405696 | tf_op jit(solution)/shard_map/hqk,qhd->khd/dot_general | solution.py:312
  232.7 7.7 %copy.105 = f32[1664,1024]{1,0:T(8,128)} copy(f32[1664,1024]{0,1:T(8,128)} %bitcast.124) | data formatting | bytes 13631488 | tf_op jit(solution)/shard_map/reshape | solution.py:316
  240.4 9.1 %multiply_convert_fusion = bf16[8,256,1664]{1,2,0:T(8,128)(2,1)S(1)} fusion(f32[8,1664,256]{2,1,0:T(8,128)} %get-tuple-element.112, f32[8,256]{1,0:T(8,128)S(1)} %copy.96, f32[8,256]{1,0:T(8,128)S(1)} %log_add_fusion, pred[256,1664]{0,1:T(8,128)(4,1)S(1)} %copy.91, bf16[256,8,128]{0,2,1:T(8,128)(2,1)S(1)} %copy.102, ...), kind=kOutput, calls=%fused_computation.9 | convolution fusion | flops 896270336 | bytes 24821760 | tf_op jit(solution)/shard_map/qhd,khd->hqk/dot_general | solution.py:306
  249.5 5.0 fusion.34
  254.5 7.7 %copy.104 = f32[1664,1024]{1,0:T(8,128)} copy(f32[1664,1024]{0,1:T(8,128)} %bitcast.123) | data formatting | bytes 13631488 | tf_op jit(solution)/shard_map/reshape | solution.py:316
  262.2 2.8 fusion.9
  265.4 1.3 copy-done.4
  266.7 1.3 collective-permute-start.7
  269.5 8.1 %fusion = bf16[1664,2048]{1,0:T(8,128)(2,1)} fusion(f32[1664,1024]{1,0:T(8,128)} %copy.105, f32[1664,1024]{1,0:T(8,128)} %copy.104), kind=kLoop, calls=%fused_computation.7 | loop fusion | flops 13631488 | bytes 20447232 | tf_op jit(solution)/shard_map/convert.4
  279.7 1.2 fusion.25
  280.9 2.5 collective-permute-start.8
  284.8 4.1 collective-permute-done.8
  289.0 3.5 collective-permute-start.9
  293.6 3.2 collective-permute-done.9
  296.9 4.3 collective-permute-done.6
  301.4 19.3 %collective-permute-start.10 = (bf16[128,2048]{1,0:T(8,128)(2,1)S(1)}, bf16[128,2048]{1,0:T(8,128)(2,1)S(1)}, u32[]{:S(2)}, u32[]{:S(2)}) collective-permute-start(bf16[128,2048]{1,0:T(8,128)(2,1)S(1)} %fusion.19), channel_id=1, source_target_pairs={{16,0},{20,4},{24,8},{28,12},{0,16},{4,20},{8,24},{12,28},{48,32},... | collective-permute-start | bytes 1572872 | tf_op jit(solution)/shard_map/ppermute | solution.py:349
  320.7 1.8 fusion.31
  322.4 21.1 %collective-permute-start.3 = (bf16[256,2048]{1,0:T(8,128)(2,1)}, bf16[256,2048]{1,0:T(8,128)(2,1)}, u32[]{:S(2)}, u32[]{:S(2)}) collective-permute-start(bf16[256,2048]{1,0:T(8,128)(2,1)} %get-tuple-element.103), channel_id=1, source_target_pairs={{4,0},{8,4},{12,8},{16,12},{20,16},{24,20},{28,24},{32,28},{36,32}... | collective-permute-start | bytes 3145736 | tf_op jit(solution)/shard_map/ppermute | solution.py:19
  343.5 2.7 collective-permute-start.2
  347.1 1.9 collective-permute-start
  349.1 3.2 fusion.12
  352.4 2.7 collective-permute-start.12
  355.1 18.1 %collective-permute-start.11 = (bf16[128,2048]{1,0:T(8,128)(2,1)S(1)}, bf16[128,2048]{1,0:T(8,128)(2,1)S(1)}, u32[]{:S(2)}, u32[]{:S(2)}) collective-permute-start(bf16[128,2048]{1,0:T(8,128)(2,1)S(1)} %fusion.20), channel_id=1, source_target_pairs={{4,0},{8,4},{12,8},{0,12},{20,16},{24,20},{28,24},{16,28},{36,32},... | collective-permute-start | bytes 1572872 | tf_op jit(solution)/shard_map/ppermute | solution.py:359
  373.2 4.1 convolution_convert_fusion
  377.3 17.9 %collective-permute-done.12 = bf16[128,2048]{1,0:T(8,128)(2,1)S(1)} collective-permute-done((bf16[128,2048]{1,0:T(8,128)(2,1)S(1)}, bf16[128,2048]{1,0:T(8,128)(2,1)S(1)}, u32[]{:S(2)}, u32[]{:S(2)}) %collective-permute-start.12) | collective-permute-done | bytes 524320 | tf_op jit(solution)/shard_map/ppermute | solution.py:360
  395.2 70.0 %collective-permute-start.1 = (bf16[256,2048]{1,0:T(8,128)(2,1)}, bf16[256,2048]{1,0:T(8,128)(2,1)}, u32[]{:S(2)}, u32[]{:S(2)}) collective-permute-start(bf16[256,2048]{1,0:T(8,128)(2,1)} %get-tuple-element.102), channel_id=1, source_target_pairs={{12,0},{16,4},{20,8},{24,12},{28,16},{32,20},{36,24},{40,28},{44,3... | collective-permute-start | bytes 3145736 | tf_op jit(solution)/shard_map/ppermute | solution.py:19
  465.2 1.1 fusion.30
  466.4 7.7 %collective-permute-start.13 = (bf16[128,2048]{1,0:T(8,128)(2,1)}, bf16[128,2048]{1,0:T(8,128)(2,1)}, u32[]{:S(2)}, u32[]{:S(2)}) collective-permute-start(bf16[128,2048]{1,0:T(8,128)(2,1)} %fusion.30), channel_id=1, source_target_pairs={{4,0},{8,4},{12,8},{0,12},{20,16},{24,20},{28,24},{16,28},{36,32},... | collective-permute-start | bytes 1572872 | tf_op jit(solution)/shard_map/ppermute | solution.py:362
  475.1 2.5 fusion.18
  477.7 13.6 %collective-permute-done.13 = bf16[128,2048]{1,0:T(8,128)(2,1)} collective-permute-done((bf16[128,2048]{1,0:T(8,128)(2,1)}, bf16[128,2048]{1,0:T(8,128)(2,1)}, u32[]{:S(2)}, u32[]{:S(2)}) %collective-permute-start.13) | collective-permute-done | bytes 524320 | tf_op jit(solution)/shard_map/ppermute | solution.py:362
  491.2 1.9 add_select_fusion
  493.2 27.8 %collective-permute-done.1 = bf16[256,2048]{1,0:T(8,128)(2,1)} collective-permute-done((bf16[256,2048]{1,0:T(8,128)(2,1)}, bf16[256,2048]{1,0:T(8,128)(2,1)}, u32[]{:S(2)}, u32[]{:S(2)}) %collective-permute-start.1) | collective-permute-done | bytes 1048608 | tf_op jit(solution)/shard_map/ppermute | solution.py:19
  521.0 3.3 fusion.14
  525.4 2.0 copy.107
  (105 shorter events, 19.2 us)
Async XLA Ops:
  7.2 162.3 %copy-start = (bf16[256,4096]{1,0:T(8,128)(2,1)S(1)}, bf16[256,4096]{1,0:T(8,128)(2,1)}, u32[]{:S(2)}) copy-start(bf16[256,4096]{1,0:T(8,128)(2,1)} %param.23) | copy-start | bytes 6291460
  7.2 518.2 %reduce-scatter.2.cloned.1.call-start = ((), (), s32[]{:S(2)}) async-start(), calls=%async_computation.1 | async-start | bytes 17301504 | tf_op jit(solution)/shard_map/reduce_scatter | solution.py:380
  149.9 5.6 %copy-start.13 = (pred[256,1664]{1,0:T(8,128)(4,1)S(1)}, pred[256,1664]{1,0:T(8,128)(4,1)}, u32[]{:S(2)}) copy-start(pred[256,1664]{1,0:T(8,128)(4,1)} %copy.90) | copy-start | bytes 1277956
  149.9 5.6 %copy-start.14 = (pred[256,1152]{1,0:T(8,128)(4,1)S(1)}, pred[256,1152]{1,0:T(8,128)(4,1)}, u32[]{:S(2)}) copy-start(pred[256,1152]{1,0:T(8,128)(4,1)} %iota_compare_fusion) | copy-start | bytes 884740
  178.6 1.0 copy-start.12
  188.0 6.7 %copy-start.6 = (bf16[256,1024]{1,0:T(8,128)(2,1)S(1)}, bf16[256,1024]{1,0:T(8,128)(2,1)}, u32[]{:S(2)}) copy-start(bf16[256,1024]{1,0:T(8,128)(2,1)} %shard_map.109) | copy-start | bytes 1572868
  201.8 2.1 copy-start.7
  249.5 5.0 copy-start.2
  265.3 1.3 copy-start.4
  266.7 12.2 %collective-permute-start.7 = (bf16[64,2048]{1,0:T(8,128)(2,1)S(1)}, bf16[64,2048]{1,0:T(8,128)(2,1)S(1)}, u32[]{:S(2)}, u32[]{:S(2)}) collective-permute-start(bf16[64,2048]{1,0:T(8,128)(2,1)S(1)} %fusion.24), channel_id=1, source_target_pairs={{0,96},{4,100},{8,104},{12,108},{16,112},{20,116},{24,120},{28,124... | collective-permute-start | bytes 786440 | tf_op jit(solution)/shard_map/ppermute | solution.py:329
  268.8 15.8 %collective-permute-start.4 = (bf16[64,2048]{1,0:T(8,128)(2,1)}, bf16[64,2048]{1,0:T(8,128)(2,1)S(1)}, u32[]{:S(2)}, u32[]{:S(2)}) collective-permute-start(bf16[64,2048]{1,0:T(8,128)(2,1)} %fusion.21), channel_id=1, source_target_pairs={{0,32},{4,36},{8,40},{12,44},{16,48},{20,52},{24,56},{28,60},{32,6... | collective-permute-start | bytes 786440 | tf_op jit(solution)/shard_map/ppermute | solution.py:328
  279.7 9.2 %copy-start.5 = (f32[4,64,2048]{2,1,0:T(8,128)S(1)}, f32[4,64,2048]{2,1,0:T(8,128)}, u32[]{:S(2)}) copy-start(f32[4,64,2048]{2,1,0:T(8,128)} %bitcast_dynamic-update-slice_fusion.2) | copy-start | bytes 6291460
  280.9 8.0 %collective-permute-start.8 = (bf16[64,2048]{1,0:T(8,128)(2,1)S(1)}, bf16[64,2048]{1,0:T(8,128)(2,1)S(1)}, u32[]{:S(2)}, u32[]{:S(2)}) collective-permute-start(bf16[64,2048]{1,0:T(8,128)(2,1)S(1)} %fusion.25), channel_id=1, source_target_pairs={{0,96},{4,100},{8,104},{12,108},{16,112},{20,116},{24,120},{28,124... | collective-permute-start | bytes 786440 | tf_op jit(solution)/shard_map/ppermute | solution.py:329
  284.6 36.1 %slice-start = ((s8[6815744]{0:T(1024)(128)(4,1)}), s8[4194304]{0:T(1024)(128)(4,1)S(1)}, s32[]{:S(2)}) async-start(s8[6815744]{0:T(1024)(128)(4,1)} %bitcast.126), calls=%async_computation.2 | async-start | bytes 8388608
  284.7 8.7 %collective-permute-start.5 = (bf16[64,2048]{1,0:T(8,128)(2,1)S(1)}, bf16[64,2048]{1,0:T(8,128)(2,1)S(1)}, u32[]{:S(2)}, u32[]{:S(2)}) collective-permute-start(bf16[64,2048]{1,0:T(8,128)(2,1)S(1)} %fusion.22), channel_id=1, source_target_pairs={{0,32},{4,36},{8,40},{12,44},{16,48},{20,52},{24,56},{28,60},{32,6... | collective-permute-start | bytes 786440 | tf_op jit(solution)/shard_map/ppermute | solution.py:328
  289.0 7.8 %collective-permute-start.9 = (bf16[64,2048]{1,0:T(8,128)(2,1)S(1)}, bf16[64,2048]{1,0:T(8,128)(2,1)S(1)}, u32[]{:S(2)}, u32[]{:S(2)}) collective-permute-start(bf16[64,2048]{1,0:T(8,128)(2,1)S(1)} %fusion.26), channel_id=1, source_target_pairs={{0,96},{4,100},{8,104},{12,108},{16,112},{20,116},{24,120},{28,124... | collective-permute-start | bytes 786440 | tf_op jit(solution)/shard_map/ppermute | solution.py:329
  293.4 27.2 %slice-start.1 = ((s8[6815744]{0:T(1024)(128)(4,1)}), s8[2621440]{0:T(1024)(128)(4,1)S(1)}, s32[]{:S(2)}) async-start(s8[6815744]{0:T(1024)(128)(4,1)} %bitcast.126), calls=%async_computation.3 | async-start | bytes 5242880
  293.5 7.8 %collective-permute-start.6 = (bf16[64,2048]{1,0:T(8,128)(2,1)S(1)}, bf16[64,2048]{1,0:T(8,128)(2,1)S(1)}, u32[]{:S(2)}, u32[]{:S(2)}) collective-permute-start(bf16[64,2048]{1,0:T(8,128)(2,1)S(1)} %fusion.23), channel_id=1, source_target_pairs={{0,32},{4,36},{8,40},{12,44},{16,48},{20,52},{24,56},{28,60},{32,6... | collective-permute-start | bytes 786440 | tf_op jit(solution)/shard_map/ppermute | solution.py:328
  301.4 50.9 %collective-permute-start.10 = (bf16[128,2048]{1,0:T(8,128)(2,1)S(1)}, bf16[128,2048]{1,0:T(8,128)(2,1)S(1)}, u32[]{:S(2)}, u32[]{:S(2)}) collective-permute-start(bf16[128,2048]{1,0:T(8,128)(2,1)S(1)} %fusion.19), channel_id=1, source_target_pairs={{16,0},{20,4},{24,8},{28,12},{0,16},{4,20},{8,24},{12,28},{48,32},... | collective-permute-start | bytes 1572872 | tf_op jit(solution)/shard_map/ppermute | solution.py:349
  322.4 170.8 %collective-permute-start.3 = (bf16[256,2048]{1,0:T(8,128)(2,1)}, bf16[256,2048]{1,0:T(8,128)(2,1)}, u32[]{:S(2)}, u32[]{:S(2)}) collective-permute-start(bf16[256,2048]{1,0:T(8,128)(2,1)} %get-tuple-element.103), channel_id=1, source_target_pairs={{4,0},{8,4},{12,8},{16,12},{20,16},{24,20},{28,24},{32,28},{36,32}... | collective-permute-start | bytes 3145736 | tf_op jit(solution)/shard_map/ppermute | solution.py:19
  343.5 149.7 %collective-permute-start.2 = (bf16[256,2048]{1,0:T(8,128)(2,1)}, bf16[256,2048]{1,0:T(8,128)(2,1)}, u32[]{:S(2)}, u32[]{:S(2)}) collective-permute-start(bf16[256,2048]{1,0:T(8,128)(2,1)} %get-tuple-element.104), channel_id=1, source_target_pairs={{8,0},{12,4},{16,8},{20,12},{24,16},{28,20},{32,24},{36,28},{40,32... | collective-permute-start | bytes 3145736 | tf_op jit(solution)/shard_map/ppermute | solution.py:19
  347.1 128.1 %collective-permute-start = (bf16[128,2048]{1,0:T(8,128)(2,1)}, bf16[128,2048]{1,0:T(8,128)(2,1)}, u32[]{:S(2)}, u32[]{:S(2)}) collective-permute-start(bf16[128,2048]{1,0:T(8,128)(2,1)} %slice.125), channel_id=1, source_target_pairs={{16,0},{20,4},{24,8},{28,12},{32,16},{36,20},{40,24},{44,28},{48,3... | collective-permute-start | bytes 1572872 | tf_op jit(solution)/shard_map/ppermute | solution.py:19
  349.1 24.1 %copy-start.3 = (bf16[1664,1024]{0,1:T(8,128)(2,1)S(1)}, bf16[1664,1024]{0,1:T(8,128)(2,1)}, u32[]{:S(2)}) copy-start(bf16[1664,1024]{0,1:T(8,128)(2,1)} %copy.112) | copy-start | bytes 10223620
  352.3 112.9 %copy-start.8 = (bf16[128,2048]{1,0:T(8,128)(2,1)}, bf16[128,2048]{1,0:T(8,128)(2,1)S(1)}, u32[]{:S(2)}) copy-start(bf16[128,2048]{1,0:T(8,128)(2,1)S(1)} %collective-permute-done.10) | copy-start | bytes 1572868
  352.4 42.8 %collective-permute-start.12 = (bf16[128,2048]{1,0:T(8,128)(2,1)S(1)}, bf16[128,2048]{1,0:T(8,128)(2,1)S(1)}, u32[]{:S(2)}, u32[]{:S(2)}) collective-permute-start(bf16[128,2048]{1,0:T(8,128)(2,1)S(1)} %fusion.20), channel_id=1, source_target_pairs={{12,0},{0,4},{4,8},{8,12},{28,16},{16,20},{20,24},{24,28},{44,32},... | collective-permute-start | bytes 1572872 | tf_op jit(solution)/shard_map/ppermute | solution.py:360
  355.1 110.1 %collective-permute-start.11 = (bf16[128,2048]{1,0:T(8,128)(2,1)S(1)}, bf16[128,2048]{1,0:T(8,128)(2,1)S(1)}, u32[]{:S(2)}, u32[]{:S(2)}) collective-permute-start(bf16[128,2048]{1,0:T(8,128)(2,1)S(1)} %fusion.20), channel_id=1, source_target_pairs={{4,0},{8,4},{12,8},{0,12},{20,16},{24,20},{28,24},{16,28},{36,32},... | collective-permute-start | bytes 1572872 | tf_op jit(solution)/shard_map/ppermute | solution.py:359
  395.2 82.4 %copy-start.10 = (bf16[128,2048]{1,0:T(8,128)(2,1)}, bf16[128,2048]{1,0:T(8,128)(2,1)S(1)}, u32[]{:S(2)}) copy-start(bf16[128,2048]{1,0:T(8,128)(2,1)S(1)} %collective-permute-done.12) | copy-start | bytes 1572868
  395.2 125.8 %collective-permute-start.1 = (bf16[256,2048]{1,0:T(8,128)(2,1)}, bf16[256,2048]{1,0:T(8,128)(2,1)}, u32[]{:S(2)}, u32[]{:S(2)}) collective-permute-start(bf16[256,2048]{1,0:T(8,128)(2,1)} %get-tuple-element.102), channel_id=1, source_target_pairs={{12,0},{16,4},{20,8},{24,12},{28,16},{32,20},{36,24},{40,28},{44,3... | collective-permute-start | bytes 3145736 | tf_op jit(solution)/shard_map/ppermute | solution.py:19
  465.2 12.4 %copy-start.11 = (bf16[128,2048]{1,0:T(8,128)(2,1)}, bf16[128,2048]{1,0:T(8,128)(2,1)S(1)}, u32[]{:S(2)}) copy-start(bf16[128,2048]{1,0:T(8,128)(2,1)S(1)} %collective-permute-done.11) | copy-start | bytes 1572868
  466.4 24.9 %collective-permute-start.13 = (bf16[128,2048]{1,0:T(8,128)(2,1)}, bf16[128,2048]{1,0:T(8,128)(2,1)}, u32[]{:S(2)}, u32[]{:S(2)}) collective-permute-start(bf16[128,2048]{1,0:T(8,128)(2,1)} %fusion.30), channel_id=1, source_target_pairs={{4,0},{8,4},{12,8},{0,12},{20,16},{24,20},{28,24},{16,28},{36,32},... | collective-permute-start | bytes 1572872 | tf_op jit(solution)/shard_map/ppermute | solution.py:362
  475.1 16.1 %copy-start.9 = (bf16[128,2048]{1,0:T(8,128)(2,1)S(1)}, bf16[128,2048]{1,0:T(8,128)(2,1)}, u32[]{:S(2)}) copy-start(bf16[128,2048]{1,0:T(8,128)(2,1)} %copy-done.8) | copy-start | bytes 1572868
  491.2 36.2 %copy-start.1 = (bf16[256,4096]{1,0:T(8,128)(2,1)S(1)}, bf16[256,4096]{1,0:T(8,128)(2,1)}, u32[]{:S(2)}) copy-start(bf16[256,4096]{1,0:T(8,128)(2,1)} %param.23) | copy-start | bytes 6291460
Sparse Core Ops, SparseCore 0:
  178.7 320.3 reduce-scatter.1

commit v15 on v14

--- a/solution.py
+++ b/solution.py
@@ -316,7 +316,17 @@
         [key_part.reshape(-1, width), value_part.reshape(-1, width)], axis=1
     )
 
+    own_grad = grad_kv[back_blocks * BLK : pool_blocks * BLK]
+    pool_start = 0
+    for distance in range(reach_back, 0, -1):
+        rows_needed = span_blocks[distance - 1] * BLK
+        back = passed_along(
+            grad_kv[pool_start : pool_start + rows_needed].astype(jnp.bfloat16), "seq", -distance
+        ).astype(jnp.float32)
+        own_grad = own_grad.at[tok_dev - rows_needed :].add(back)
+        pool_start = pool_start + rows_needed
     part = grad_kv[pool_blocks * BLK :].reshape(summary_count, BLK, 2 * width)
+    own_grad, part = lax.optimization_barrier((own_grad, part))
     half_rows = BLK // 2
     forward_acc = part[:, :half_rows]
     backward_acc = part[:, half_rows:]
@@ -365,15 +375,6 @@
     far_here = (rel == 0) & (own_local == sum_local)
     far_add = jnp.where(far_here[:, None, None], part[None], 0.0)
 
-    own_grad = grad_kv[back_blocks * BLK : pool_blocks * BLK]
-    pool_start = 0
-    for distance in range(reach_back, 0, -1):
-        rows_needed = span_blocks[distance - 1] * BLK
-        back = passed_along(
-            grad_kv[pool_start : pool_start + rows_needed].astype(jnp.bfloat16), "seq", -distance
-        ).astype(jnp.float32)
-        own_grad = own_grad.at[tok_dev - rows_needed :].add(back)
-        pool_start = pool_start + rows_needed
     total = own_grad.reshape(blocks_dev, BLK, 2 * width) + far_add
     total = total.reshape(tok_dev, 2 * width).astype(jnp.bfloat16)
 

time: 536 us -> 599 us (1.12)
  waiting for transfers between devices: 71.8 us -> 236 us
  starting transfers between devices: 152 us -> 53 us
    ppermute x4, waiting for transfers between devices: 27.8 us -> 200 us  [passed_along(): return lax.ppermute(block, axis, route)]
    ppermute x4, starting transfers between devices: 95.7 us -> 36.2 us  [passed_along(): return lax.ppermute(block, axis, route)]
    ppermute x1, starting transfers between devices: 19.3 us -> 0.09 us  [local(): lax.ppermute(part.astype(jnp.bfloat16), 'seq', route).astype(jnp.float32)]
    ppermute x1, starting transfers between devices: 18.1 us -> 3.77 us  [local(): ahead = lax.ppermute(sent, 'seq', from_lane(1)).astype(jnp.float32)]
    ppermute x1, waiting for transfers between devices: 13.6 us -> 1.17 us  [local(): lax.ppermute(part.astype(jnp.bfloat16), 'seq', from_lane(1))]
    ppermute x1, waiting for transfers between devices: 17.9 us -> 7.43 us  [local(): behind = lax.ppermute(sent, 'seq', from_lane(-1)).astype(jnp.float32)]
    ppermute x1, waiting for transfers between devices: 0.01 us -> 9.15 us  [local(): lax.ppermute(part.astype(jnp.bfloat16), 'seq', route).astype(jnp.float32)]
    ppermute x3, waiting for transfers between devices: 7.3 us -> 15.6 us  [local(): lax.ppermute(out_b.astype(jnp.bfloat16), 'seq', to_prev).astype(jnp.float32)]
  transfers between devices with their start and end apart: 15 -> 15, of which waited for: 7 -> 11; matrix products, arithmetic and copies ran while one was open for 23% -> 19% of each run, Pallas kernels for 0% -> 0%
where the time goes in v15:
time: 599 us; the launch traced here: 593 us
  waiting for transfers between devices  236 us (39%)
  Pallas kernels  144 us (24%)
  matrix products  54.8 us (9%)
  starting transfers between devices  53 us (9%)
  local copies, waits for them, and re-layouts  48.7 us (8%)
  other arithmetic  39.3 us (7%)
  between operations  16.9 us (3%)
    ppermute x4, waiting for transfers between devices, passed_along(): return lax.ppermute(block, axis, route)  200 us
    pallas_call x1, Pallas kernels, exchange(): pl.pallas_call(functools.partial(exchange_kernel, (seq_size, group, spans...  131 us
    ppermute x4, starting transfers between devices, passed_along(): return lax.ppermute(block, axis, route)  36.2 us
    ppermute x3, waiting for transfers between devices, local(): lax.ppermute(out_b.astype(jnp.bfloat16), 'seq', to_prev).astype(jnp.float32)  15.6 us
    unnamed x39, local copies, waits for them, and re-layouts  14 us
    pallas_call x1, Pallas kernels, attention_out(): pl.pallas_call(functools.partial(forward_kernel, scale), out_shape=jax.Sh...  12.3 us
  transfers between devices with their start and end apart: 15, of which 11 were waited for; matrix products, arithmetic and copies ran while one was open for 19% of the time, Pallas kernels for 0%

profile of v15, /device:TPU:40, one launch (start us, length us, event | category | flops | bytes accessed | tf_op | source)
XLA Modules:
  0.0 592.6 jit_solution(18368688066196104190)
XLA Ops:
  7.2 1.4 slice.105
  10.7 1.1 constant_dynamic-update-slice_fusion.1
  14.4 2.2 copy.90
  18.7 131.2 %shard_map.108 = (bf16[896,2048]{1,0:T(8,128)(2,1)}, bf16[4,128,2048]{2,1,0:T(8,128)(2,1)S(1)}) custom-call(s32[2]{0:T(128)S(1)} %pad_add_fusion.1.ctl_ref, bf16[256,2048]{1,0:T(8,128)(2,1)S(1)} %constant_dynamic-update-slice_fusion.kv_ref), custom_call_target="tpu_custom_call" | custom-call | tf_op jit(solution)/shard_map/pallas_call | solution.py:163
  150.0 5.6 pad_maximum_fusion.1.k_ref.v_ref
  155.6 1.6 broadcast_select_fusion
  157.2 12.3 %shard_map.109 = bf16[256,1024]{1,0:T(8,128)(2,1)} custom-call(bf16[256,1024]{1,0:T(8,128)(2,1)} %q_ref.1, bf16[1664,2048]{1,0:T(8,128)(2,1)} %pad_maximum_fusion.1.k_ref.v_ref, bf16[1664,2048]{1,0:T(8,128)(2,1)} %pad_maximum_fusion.1.k_ref.v_ref, f32[256,1664]{1,0:T(8,128)} %get-tuple-element.104.bias_ref), custom_call_target="tpu_custom_call" | custom-call | flops 1744830464 | bytes 9568256 | tf_op jit(solution)/shard_map/pallas_call | solution.py:208
  169.4 9.1 %convolution_bitcast_fusion = f32[4096,1024]{0,1:T(8,128)} fusion(bf16[256,1024]{1,0:T(8,128)(2,1)} %shard_map.109, bf16[256,4096]{1,0:T(8,128)(2,1)S(1)} %copy-done), kind=kOutput, calls=%fused_computation.14 | convolution fusion | flops 2147483648 | bytes 19398656 | tf_op jit(solution)/shard_map/dot_general | solution.py:382
  180.6 7.4 %slice_bitcast_fusion = (bf16[208,8,8,128]{3,2,1,0:T(8,128)(2,1)}, bf16[1664,1024]{1,0:T(8,128)(2,1)}) fusion(bf16[1664,2048]{1,0:T(8,128)(2,1)} %pad_maximum_fusion.1.k_ref.v_ref), kind=kLoop, calls=%fused_computation.24 | loop fusion | bytes 13631488
  188.0 5.7 copy.112
  194.9 1.2 copy.117
  196.1 5.7 fusion.15
  202.2 1.6 multiply_reduce_fusion
  203.9 9.4 %fusion.2 = (f32[8,256]{1,0:T(8,128)S(1)}, f32[8,1664,256]{2,1,0:T(8,128)}) fusion(pred[256,1664]{0,1:T(8,128)(4,1)S(1)} %copy.91, bf16[1664,8,128]{0,2,1:T(8,128)(2,1)} %bitcast.125, bf16[256,8,128]{0,2,1:T(8,128)(2,1)S(1)} %bitcast.130), kind=kOutput, calls=%fused_computation.13 | convolution fusion | flops 882636800 | bytes 17997824 | tf_op jit(solution)/shard_map/qhd,khd->hqk/dot_general | solution.py:293
  213.3 8.0 %exponential_reduce_fusion = f32[8,256]{1,0:T(8,128)S(1)} fusion(f32[8,1664,256]{2,1,0:T(8,128)} %get-tuple-element.116, f32[8,256]{1,0:T(8,128)S(1)} %get-tuple-element.115, pred[256,1664]{0,1:T(8,128)(4,1)S(1)} %copy.91), kind=kLoop, calls=%fused_computation.11 | loop fusion | flops 13629440 | bytes 14073856 | tf_op jit(solution)/shard_map/reduce_sum | solution.py:298
  221.3 11.3 %fusion.3 = f32[8,128,1664]{2,1,0:T(8,128)} fusion(bf16[256,8,128]{0,2,1:T(8,128)(2,1)S(1)} %copy.102, f32[8,1664,256]{2,1,0:T(8,128)} %get-tuple-element.116, f32[8,256]{1,0:T(8,128)S(1)} %log_add_fusion, pred[256,1664]{0,1:T(8,128)(4,1)S(1)} %copy.91), kind=kOutput, calls=%fused_computation.15 | convolution fusion | flops 886046720 | bytes 21405696 | tf_op jit(solution)/shard_map/hqk,qhd->khd/dot_general | solution.py:312
  232.7 7.7 %copy.105 = f32[1664,1024]{1,0:T(8,128)} copy(f32[1664,1024]{0,1:T(8,128)} %bitcast.128) | data formatting | bytes 13631488 | tf_op jit(solution)/shard_map/reshape | solution.py:316
  240.4 9.1 %multiply_convert_fusion = bf16[8,256,1664]{1,2,0:T(8,128)(2,1)S(1)} fusion(f32[8,1664,256]{2,1,0:T(8,128)} %get-tuple-element.116, f32[8,256]{1,0:T(8,128)S(1)} %copy.96, f32[8,256]{1,0:T(8,128)S(1)} %log_add_fusion, pred[256,1664]{0,1:T(8,128)(4,1)S(1)} %copy.91, bf16[256,8,128]{0,2,1:T(8,128)(2,1)S(1)} %copy.102, ...), kind=kOutput, calls=%fused_computation.9 | convolution fusion | flops 896270336 | bytes 24821760 | tf_op jit(solution)/shard_map/qhd,khd->hqk/dot_general | solution.py:306
  249.5 5.0 fusion.34
  254.5 7.7 %copy.104 = f32[1664,1024]{1,0:T(8,128)} copy(f32[1664,1024]{0,1:T(8,128)} %bitcast.127) | data formatting | bytes 13631488 | tf_op jit(solution)/shard_map/reshape | solution.py:316
  262.2 5.8 fusion
  268.0 1.7 fusion.31
  269.7 25.7 %collective-permute-start.3 = (bf16[256,2048]{1,0:T(8,128)(2,1)}, bf16[256,2048]{1,0:T(8,128)(2,1)S(1)}, u32[]{:S(2)}, u32[]{:S(2)}) collective-permute-start(bf16[256,2048]{1,0:T(8,128)(2,1)} %get-tuple-element.107), channel_id=1, source_target_pairs={{4,0},{8,4},{12,8},{16,12},{20,16},{24,20},{28,24},{32,28},{36,32}... | collective-permute-start | bytes 3145736 | tf_op jit(solution)/shard_map/ppermute | solution.py:19
  295.4 1.9 collective-permute-start.2
  298.2 6.4 %collective-permute-start = (bf16[128,2048]{1,0:T(8,128)(2,1)}, bf16[128,2048]{1,0:T(8,128)(2,1)}, u32[]{:S(2)}, u32[]{:S(2)}) collective-permute-start(bf16[128,2048]{1,0:T(8,128)(2,1)} %slice.125), channel_id=1, source_target_pairs={{16,0},{20,4},{24,8},{28,12},{32,16},{36,20},{40,24},{44,28},{48,3... | collective-permute-start | bytes 1572872 | tf_op jit(solution)/shard_map/ppermute | solution.py:19
  304.6 2.2 collective-permute-start.1
  307.0 1.9 fusion.12
  308.9 3.5 fusion.9
  312.4 61.6 %collective-permute-done = bf16[128,2048]{1,0:T(8,128)(2,1)} collective-permute-done((bf16[128,2048]{1,0:T(8,128)(2,1)}, bf16[128,2048]{1,0:T(8,128)(2,1)}, u32[]{:S(2)}, u32[]{:S(2)}) %collective-permute-start) | collective-permute-done | bytes 524320 | tf_op jit(solution)/shard_map/ppermute | solution.py:19
  374.0 1.2 fusion.18
  375.3 138.5 %collective-permute-done.1 = bf16[256,2048]{1,0:T(8,128)(2,1)} collective-permute-done((bf16[256,2048]{1,0:T(8,128)(2,1)}, bf16[256,2048]{1,0:T(8,128)(2,1)}, u32[]{:S(2)}, u32[]{:S(2)}) %collective-permute-start.1) | collective-permute-done | bytes 1048608 | tf_op jit(solution)/shard_map/ppermute | solution.py:19
  513.8 3.5 convert_add_fusion
  518.0 5.0 collective-permute-start.4
  523.1 5.2 collective-permute-done.7
  528.6 2.4 collective-permute-start.5
  531.0 6.4 %collective-permute-done.8 = bf16[64,2048]{1,0:T(8,128)(2,1)S(1)} collective-permute-done((bf16[64,2048]{1,0:T(8,128)(2,1)S(1)}, bf16[64,2048]{1,0:T(8,128)(2,1)S(1)}, u32[]{:S(2)}, u32[]{:S(2)}) %collective-permute-start.8) | collective-permute-done | bytes 262176 | tf_op jit(solution)/shard_map/ppermute | solution.py:339
  538.6 1.5 collective-permute-start.6
  540.1 4.1 collective-permute-done.9
  544.3 2.0 collective-permute-done.6
  546.5 9.2 %collective-permute-done.10 = bf16[128,2048]{1,0:T(8,128)(2,1)S(1)} collective-permute-done((bf16[128,2048]{1,0:T(8,128)(2,1)S(1)}, bf16[128,2048]{1,0:T(8,128)(2,1)S(1)}, u32[]{:S(2)}, u32[]{:S(2)}) %collective-permute-start.10) | collective-permute-done | bytes 524320 | tf_op jit(solution)/shard_map/ppermute | solution.py:359
  555.9 3.8 collective-permute-start.11
  559.7 7.4 %collective-permute-done.12 = bf16[128,2048]{1,0:T(8,128)(2,1)S(1)} collective-permute-done((bf16[128,2048]{1,0:T(8,128)(2,1)S(1)}, bf16[128,2048]{1,0:T(8,128)(2,1)S(1)}, u32[]{:S(2)}, u32[]{:S(2)}) %collective-permute-start.12) | collective-permute-done | bytes 524320 | tf_op jit(solution)/shard_map/ppermute | solution.py:370
  568.0 3.3 collective-permute-start.13
  571.2 5.1 convolution_convert_fusion
  577.5 1.2 collective-permute-done.13
  578.6 2.1 add_select_fusion
  580.7 1.9 fusion.14
  583.7 2.0 copy.107
  (103 shorter events, 15.0 us)
Async XLA Ops:
  7.2 162.3 %copy-start = (bf16[256,4096]{1,0:T(8,128)(2,1)S(1)}, bf16[256,4096]{1,0:T(8,128)(2,1)}, u32[]{:S(2)}) copy-start(bf16[256,4096]{1,0:T(8,128)(2,1)} %param.23) | copy-start | bytes 6291460
  7.2 576.5 %reduce-scatter.2.cloned.1.call-start = ((), (), s32[]{:S(2)}) async-start(), calls=%async_computation.1 | async-start | bytes 17301504 | tf_op jit(solution)/shard_map/reduce_scatter | solution.py:381
  149.9 5.6 copy-start.9
  149.9 5.6 copy-start.10
  178.6 1.0 copy-start.8
  188.0 6.7 %copy-start.3 = (bf16[256,1024]{1,0:T(8,128)(2,1)S(1)}, bf16[256,1024]{1,0:T(8,128)(2,1)}, u32[]{:S(2)}) copy-start(bf16[256,1024]{1,0:T(8,128)(2,1)} %shard_map.109) | copy-start | bytes 1572868
  201.8 2.1 copy-start.4
  249.5 5.0 copy-start.2
  269.7 105.5 %collective-permute-start.3 = (bf16[256,2048]{1,0:T(8,128)(2,1)}, bf16[256,2048]{1,0:T(8,128)(2,1)S(1)}, u32[]{:S(2)}, u32[]{:S(2)}) collective-permute-start(bf16[256,2048]{1,0:T(8,128)(2,1)} %get-tuple-element.107), channel_id=1, source_target_pairs={{4,0},{8,4},{12,8},{16,12},{20,16},{24,20},{28,24},{32,28},{36,32}... | collective-permute-start | bytes 3145736 | tf_op jit(solution)/shard_map/ppermute | solution.py:19
  295.4 79.8 %collective-permute-start.2 = (bf16[256,2048]{1,0:T(8,128)(2,1)}, bf16[256,2048]{1,0:T(8,128)(2,1)}, u32[]{:S(2)}, u32[]{:S(2)}) collective-permute-start(bf16[256,2048]{1,0:T(8,128)(2,1)} %get-tuple-element.108), channel_id=1, source_target_pairs={{8,0},{12,4},{16,8},{20,12},{24,16},{28,20},{32,24},{36,28},{40,32... | collective-permute-start | bytes 3145736 | tf_op jit(solution)/shard_map/ppermute | solution.py:19
  298.2 75.8 %collective-permute-start = (bf16[128,2048]{1,0:T(8,128)(2,1)}, bf16[128,2048]{1,0:T(8,128)(2,1)}, u32[]{:S(2)}, u32[]{:S(2)}) collective-permute-start(bf16[128,2048]{1,0:T(8,128)(2,1)} %slice.125), channel_id=1, source_target_pairs={{16,0},{20,4},{24,8},{28,12},{32,16},{36,20},{40,24},{44,28},{48,3... | collective-permute-start | bytes 1572872 | tf_op jit(solution)/shard_map/ppermute | solution.py:19
  304.6 209.2 %collective-permute-start.1 = (bf16[256,2048]{1,0:T(8,128)(2,1)}, bf16[256,2048]{1,0:T(8,128)(2,1)}, u32[]{:S(2)}, u32[]{:S(2)}) collective-permute-start(bf16[256,2048]{1,0:T(8,128)(2,1)} %get-tuple-element.106), channel_id=1, source_target_pairs={{12,0},{16,4},{20,8},{24,12},{28,16},{32,20},{36,24},{40,28},{44,3... | collective-permute-start | bytes 3145736 | tf_op jit(solution)/shard_map/ppermute | solution.py:19
  307.0 67.0 %slice-start = ((s8[6815744]{0:T(1024)(128)(4,1)}), s8[4194304]{0:T(1024)(128)(4,1)S(1)}, s32[]{:S(2)}) async-start(s8[6815744]{0:T(1024)(128)(4,1)} %bitcast.121), calls=%async_computation.2 | async-start | bytes 8388608
  307.0 67.0 %slice-start.2 = ((s8[6815744]{0:T(1024)(128)(4,1)}), s8[4194304]{0:T(1024)(128)(4,1)S(1)}, s32[]{:S(2)}) async-start(s8[6815744]{0:T(1024)(128)(4,1)} %bitcast.123), calls=%async_computation.4 | async-start | bytes 8388608
  308.9 65.1 %slice-start.1 = ((s8[6815744]{0:T(1024)(128)(4,1)}), s8[2621440]{0:T(1024)(128)(4,1)S(1)}, s32[]{:S(2)}) async-start(s8[6815744]{0:T(1024)(128)(4,1)} %bitcast.121), calls=%async_computation.3 | async-start | bytes 5242880
  308.9 65.1 %slice-start.3 = ((s8[6815744]{0:T(1024)(128)(4,1)}), s8[2621440]{0:T(1024)(128)(4,1)S(1)}, s32[]{:S(2)}) async-start(s8[6815744]{0:T(1024)(128)(4,1)} %bitcast.123), calls=%async_computation.5 | async-start | bytes 5242880
  517.8 10.4 %collective-permute-start.7 = (bf16[64,2048]{1,0:T(8,128)(2,1)S(1)}, bf16[64,2048]{1,0:T(8,128)(2,1)S(1)}, u32[]{:S(2)}, u32[]{:S(2)}) collective-permute-start(bf16[64,2048]{1,0:T(8,128)(2,1)S(1)} %fusion.24), channel_id=1, source_target_pairs={{0,96},{4,100},{8,104},{12,108},{16,112},{20,116},{24,120},{28,124... | collective-permute-start | bytes 786440 | tf_op jit(solution)/shard_map/ppermute | solution.py:339
  518.0 10.5 %collective-permute-start.4 = (bf16[64,2048]{1,0:T(8,128)(2,1)S(1)}, bf16[64,2048]{1,0:T(8,128)(2,1)S(1)}, u32[]{:S(2)}, u32[]{:S(2)}) collective-permute-start(bf16[64,2048]{1,0:T(8,128)(2,1)S(1)} %fusion.21), channel_id=1, source_target_pairs={{0,32},{4,36},{8,40},{12,44},{16,48},{20,52},{24,56},{28,60},{32,6... | collective-permute-start | bytes 786440 | tf_op jit(solution)/shard_map/ppermute | solution.py:338
  528.4 9.0 %collective-permute-start.8 = (bf16[64,2048]{1,0:T(8,128)(2,1)S(1)}, bf16[64,2048]{1,0:T(8,128)(2,1)S(1)}, u32[]{:S(2)}, u32[]{:S(2)}) collective-permute-start(bf16[64,2048]{1,0:T(8,128)(2,1)S(1)} %fusion.25), channel_id=1, source_target_pairs={{0,96},{4,100},{8,104},{12,108},{16,112},{20,116},{24,120},{28,124... | collective-permute-start | bytes 786440 | tf_op jit(solution)/shard_map/ppermute | solution.py:339
  528.6 9.9 %collective-permute-start.5 = (bf16[64,2048]{1,0:T(8,128)(2,1)S(1)}, bf16[64,2048]{1,0:T(8,128)(2,1)S(1)}, u32[]{:S(2)}, u32[]{:S(2)}) collective-permute-start(bf16[64,2048]{1,0:T(8,128)(2,1)S(1)} %fusion.22), channel_id=1, source_target_pairs={{0,32},{4,36},{8,40},{12,44},{16,48},{20,52},{24,56},{28,60},{32,6... | collective-permute-start | bytes 786440 | tf_op jit(solution)/shard_map/ppermute | solution.py:338
  537.5 6.7 %collective-permute-start.9 = (bf16[64,2048]{1,0:T(8,128)(2,1)S(1)}, bf16[64,2048]{1,0:T(8,128)(2,1)S(1)}, u32[]{:S(2)}, u32[]{:S(2)}) collective-permute-start(bf16[64,2048]{1,0:T(8,128)(2,1)S(1)} %fusion.26), channel_id=1, source_target_pairs={{0,96},{4,100},{8,104},{12,108},{16,112},{20,116},{24,120},{28,124... | collective-permute-start | bytes 786440 | tf_op jit(solution)/shard_map/ppermute | solution.py:339
  538.6 7.7 %collective-permute-start.6 = (bf16[64,2048]{1,0:T(8,128)(2,1)S(1)}, bf16[64,2048]{1,0:T(8,128)(2,1)S(1)}, u32[]{:S(2)}, u32[]{:S(2)}) collective-permute-start(bf16[64,2048]{1,0:T(8,128)(2,1)S(1)} %fusion.23), channel_id=1, source_target_pairs={{0,32},{4,36},{8,40},{12,44},{16,48},{20,52},{24,56},{28,60},{32,6... | collective-permute-start | bytes 786440 | tf_op jit(solution)/shard_map/ppermute | solution.py:338
  546.4 9.3 %collective-permute-start.10 = (bf16[128,2048]{1,0:T(8,128)(2,1)S(1)}, bf16[128,2048]{1,0:T(8,128)(2,1)S(1)}, u32[]{:S(2)}, u32[]{:S(2)}) collective-permute-start(bf16[128,2048]{1,0:T(8,128)(2,1)S(1)} %fusion.19), channel_id=1, source_target_pairs={{16,0},{20,4},{24,8},{28,12},{0,16},{4,20},{8,24},{12,28},{48,32},... | collective-permute-start | bytes 1572872 | tf_op jit(solution)/shard_map/ppermute | solution.py:359
  555.7 20.7 %copy-start.5 = (bf16[128,2048]{1,0:T(8,128)(2,1)}, bf16[128,2048]{1,0:T(8,128)(2,1)S(1)}, u32[]{:S(2)}) copy-start(bf16[128,2048]{1,0:T(8,128)(2,1)S(1)} %collective-permute-done.10) | copy-start | bytes 1572868
  555.8 11.3 %collective-permute-start.12 = (bf16[128,2048]{1,0:T(8,128)(2,1)S(1)}, bf16[128,2048]{1,0:T(8,128)(2,1)S(1)}, u32[]{:S(2)}, u32[]{:S(2)}) collective-permute-start(bf16[128,2048]{1,0:T(8,128)(2,1)S(1)} %fusion.20), channel_id=1, source_target_pairs={{12,0},{0,4},{4,8},{8,12},{28,16},{16,20},{20,24},{24,28},{44,32},... | collective-permute-start | bytes 1572872 | tf_op jit(solution)/shard_map/ppermute | solution.py:370
  555.9 11.7 %collective-permute-start.11 = (bf16[128,2048]{1,0:T(8,128)(2,1)S(1)}, bf16[128,2048]{1,0:T(8,128)(2,1)S(1)}, u32[]{:S(2)}, u32[]{:S(2)}) collective-permute-start(bf16[128,2048]{1,0:T(8,128)(2,1)S(1)} %fusion.20), channel_id=1, source_target_pairs={{4,0},{8,4},{12,8},{0,12},{20,16},{24,20},{28,24},{16,28},{36,32},... | collective-permute-start | bytes 1572872 | tf_op jit(solution)/shard_map/ppermute | solution.py:369
  567.1 0.9 copy-start.6
  567.6 8.7 %copy-start.7 = (bf16[128,2048]{1,0:T(8,128)(2,1)}, bf16[128,2048]{1,0:T(8,128)(2,1)S(1)}, u32[]{:S(2)}) copy-start(bf16[128,2048]{1,0:T(8,128)(2,1)S(1)} %collective-permute-done.11) | copy-start | bytes 1572868
  568.0 10.7 %collective-permute-start.13 = (bf16[128,2048]{1,0:T(8,128)(2,1)S(1)}, bf16[128,2048]{1,0:T(8,128)(2,1)}, u32[]{:S(2)}, u32[]{:S(2)}) collective-permute-start(bf16[128,2048]{1,0:T(8,128)(2,1)S(1)} %fusion.30), channel_id=1, source_target_pairs={{4,0},{8,4},{12,8},{0,12},{20,16},{24,20},{28,24},{16,28},{36,32},... | collective-permute-start | bytes 1572872 | tf_op jit(solution)/shard_map/ppermute | solution.py:372
  578.6 7.1 %copy-start.1 = (bf16[256,4096]{1,0:T(8,128)(2,1)S(1)}, bf16[256,4096]{1,0:T(8,128)(2,1)}, u32[]{:S(2)}) copy-start(bf16[256,4096]{1,0:T(8,128)(2,1)} %param.23) | copy-start | bytes 6291460
Sparse Core Ops, SparseCore 0:
  178.7 347.9 reduce-scatter.1

commit v16 on v14

--- a/solution.py
+++ b/solution.py
@@ -358,9 +358,8 @@
     sent = part.astype(jnp.bfloat16)
     ahead = lax.ppermute(sent, "seq", from_lane(1)).astype(jnp.float32)
     behind = lax.ppermute(sent, "seq", from_lane(-1)).astype(jnp.float32)
-    part = part + jnp.where(rel_lane == 1, ahead, 0.0) + jnp.where(rel_lane == 0, behind, 0.0)
-    ahead = lax.ppermute(part.astype(jnp.bfloat16), "seq", from_lane(1)).astype(jnp.float32)
-    part = jnp.where(rel_lane == 0, part + ahead, part)
+    opposite = lax.ppermute(sent, "seq", from_lane(2)).astype(jnp.float32)
+    part = jnp.where(rel_lane == 0, part + ahead + behind + opposite, part)
     own_local = jnp.arange(blocks_dev, dtype=jnp.int32)
     far_here = (rel == 0) & (own_local == sum_local)
     far_add = jnp.where(far_here[:, None, None], part[None], 0.0)

time: 536 us -> 566 us (1.056); the launches traced: 534 us -> 557 us
  starting transfers between devices: 152 us -> 198 us
  waiting for transfers between devices: 71.8 us -> 48.8 us
    ppermute x1, starting transfers between devices: 7.67 us -> 113 us  [local(): opposite = lax.ppermute(sent, 'seq', from_lane(2)).astype(jnp.float32)]
    ppermute x4, starting transfers between devices: 95.7 us -> 27.6 us  [passed_along(): return lax.ppermute(block, axis, route)]
    ppermute x1, waiting for transfers between devices: 17.9 us -> 3.5 us  [local(): behind = lax.ppermute(sent, 'seq', from_lane(-1)).astype(jnp.float32)]
    ppermute x1, starting transfers between devices: 18.1 us -> 29.6 us  [local(): ahead = lax.ppermute(sent, 'seq', from_lane(1)).astype(jnp.float32)]
    ppermute x4, waiting for transfers between devices: 27.8 us -> 17.9 us  [passed_along(): return lax.ppermute(block, axis, route)]
  transfers between devices with their start and end apart: 15 -> 15, of which waited for: 7 -> 7; matrix products, arithmetic and copies ran while one was open for 23% -> 21% of each run, Pallas kernels for 0% -> 0%
where the time goes in v16:
time: 566 us; the launch traced here: 557 us
  starting transfers between devices  198 us (35%)
  Pallas kernels  144 us (25%)
  local copies, waits for them, and re-layouts  54.6 us (10%)
  matrix products  53.8 us (10%)
  waiting for transfers between devices  48.8 us (9%)
  other arithmetic  41.6 us (7%)
  between operations  16.7 us (3%)
    pallas_call x1, Pallas kernels, exchange(): pl.pallas_call(functools.partial(exchange_kernel, (seq_size, group, spans...  131 us
    ppermute x1, starting transfers between devices, local(): opposite = lax.ppermute(sent, 'seq', from_lane(2)).astype(jnp.float32)  113 us
    ppermute x1, starting transfers between devices, local(): ahead = lax.ppermute(sent, 'seq', from_lane(1)).astype(jnp.float32)  29.6 us
    ppermute x4, starting transfers between devices, passed_along(): return lax.ppermute(block, axis, route)  27.6 us
    ppermute x1, starting transfers between devices, local(): lax.ppermute(part.astype(jnp.bfloat16), 'seq', route).astype(jnp.float32)  19.3 us
    ppermute x4, waiting for transfers between devices, passed_along(): return lax.ppermute(block, axis, route)  17.9 us
    unnamed x43, local copies, waits for them, and re-layouts  16.7 us
    ppermute x1, waiting for transfers between devices, local(): opposite = lax.ppermute(sent, 'seq', from_lane(2)).astype(jnp.float32)  15 us
  transfers between devices with their start and end apart: 15, of which 7 were waited for; matrix products, arithmetic and copies ran while one was open for 21% of the time, Pallas kernels for 0%

profile of v16, /device:TPU:40, one launch (start us, length us, event | category | flops | bytes accessed | tf_op | source)
XLA Modules:
  0.0 557.1 jit_solution(1422623759946497914)
XLA Ops:
  7.2 1.4 slice.105
  10.7 1.1 constant_dynamic-update-slice_fusion.1
  14.4 2.2 copy.90
  18.7 131.2 %shard_map.108 = (bf16[896,2048]{1,0:T(8,128)(2,1)}, bf16[4,128,2048]{2,1,0:T(8,128)(2,1)S(1)}) custom-call(s32[2]{0:T(128)S(1)} %pad_add_fusion.1.ctl_ref, bf16[256,2048]{1,0:T(8,128)(2,1)S(1)} %constant_dynamic-update-slice_fusion.kv_ref), custom_call_target="tpu_custom_call" | custom-call | tf_op jit(solution)/shard_map/pallas_call | solution.py:163
  150.0 5.6 %pad_maximum_fusion.1.k_ref.v_ref = bf16[1664,2048]{1,0:T(8,128)(2,1)} fusion(bf16[512,2048]{1,0:T(8,128)(2,1)S(1)} %bitcast.120, bf16[256,2048]{1,0:T(8,128)(2,1)S(1)} %constant_dynamic-update-slice_fusion.kv_ref, bf16[896,2048]{1,0:T(8,128)(2,1)} %get-tuple-element.78), kind=kLoop, calls=%fused_computation.16 | loop fusion | flops 20447232 | bytes 13631488 | tf_op jit(solution)/shard_map/concatenate | solution.py:265
  155.6 1.6 broadcast_select_fusion
  157.2 12.3 %shard_map.109 = bf16[256,1024]{1,0:T(8,128)(2,1)} custom-call(bf16[256,1024]{1,0:T(8,128)(2,1)} %q_ref.1, bf16[1664,2048]{1,0:T(8,128)(2,1)} %pad_maximum_fusion.1.k_ref.v_ref, bf16[1664,2048]{1,0:T(8,128)(2,1)} %pad_maximum_fusion.1.k_ref.v_ref, f32[256,1664]{1,0:T(8,128)} %get-tuple-element.100.bias_ref), custom_call_target="tpu_custom_call" | custom-call | flops 1744830464 | bytes 9568256 | tf_op jit(solution)/shard_map/pallas_call | solution.py:208
  169.4 9.1 %convolution_bitcast_fusion = f32[4096,1024]{0,1:T(8,128)} fusion(bf16[256,1024]{1,0:T(8,128)(2,1)} %shard_map.109, bf16[256,4096]{1,0:T(8,128)(2,1)S(1)} %copy-done), kind=kOutput, calls=%fused_computation.14 | convolution fusion | flops 2147483648 | bytes 19398656 | tf_op jit(solution)/shard_map/dot_general | solution.py:380
  180.6 7.4 %slice_bitcast_fusion = (bf16[208,8,8,128]{3,2,1,0:T(8,128)(2,1)}, bf16[1664,1024]{1,0:T(8,128)(2,1)}) fusion(bf16[1664,2048]{1,0:T(8,128)(2,1)} %pad_maximum_fusion.1.k_ref.v_ref), kind=kLoop, calls=%fused_computation.24 | loop fusion | bytes 13631488
  188.0 5.7 %copy.112 = bf16[1664,1024]{0,1:T(8,128)(2,1)} copy(bf16[1664,1024]{1,0:T(8,128)(2,1)} %get-tuple-element.106) | data formatting | bytes 6815744 | tf_op jit(solution)/shard_map/reshape | solution.py:266
  194.9 1.2 copy.117
  196.1 5.7 %fusion.15 = bf16[32,8,8,128]{3,1,2,0:T(8,128)(2,1)S(1)} fusion(bf16[256,4096]{1,0:T(8,128)(2,1)S(1)} %copy-done, bf16[4096,1024]{1,0:T(8,128)(2,1)} %param.24), kind=kOutput, calls=%fused_computation.33 | convolution fusion | flops 2147745792 | bytes 11010048 | tf_op jit(solution)/shard_map/dot_general | solution.py:245
  202.2 1.6 multiply_reduce_fusion
  203.9 9.4 %fusion.2 = (f32[8,256]{1,0:T(8,128)S(1)}, f32[8,1664,256]{2,1,0:T(8,128)}) fusion(pred[256,1664]{0,1:T(8,128)(4,1)S(1)} %copy.91, bf16[1664,8,128]{0,2,1:T(8,128)(2,1)} %bitcast.121, bf16[256,8,128]{0,2,1:T(8,128)(2,1)S(1)} %bitcast.128), kind=kOutput, calls=%fused_computation.13 | convolution fusion | flops 882636800 | bytes 17997824 | tf_op jit(solution)/shard_map/qhd,khd->hqk/dot_general | solution.py:293
  213.3 8.0 %exponential_reduce_fusion = f32[8,256]{1,0:T(8,128)S(1)} fusion(f32[8,1664,256]{2,1,0:T(8,128)} %get-tuple-element.112, f32[8,256]{1,0:T(8,128)S(1)} %get-tuple-element.111, pred[256,1664]{0,1:T(8,128)(4,1)S(1)} %copy.91), kind=kLoop, calls=%fused_computation.11 | loop fusion | flops 13629440 | bytes 14073856 | tf_op jit(solution)/shard_map/reduce_sum | solution.py:298
  221.3 11.3 %fusion.3 = f32[8,128,1664]{2,1,0:T(8,128)} fusion(bf16[256,8,128]{0,2,1:T(8,128)(2,1)S(1)} %copy.102, f32[8,1664,256]{2,1,0:T(8,128)} %get-tuple-element.112, f32[8,256]{1,0:T(8,128)S(1)} %log_add_fusion, pred[256,1664]{0,1:T(8,128)(4,1)S(1)} %copy.91), kind=kOutput, calls=%fused_computation.15 | convolution fusion | flops 886046720 | bytes 21405696 | tf_op jit(solution)/shard_map/hqk,qhd->khd/dot_general | solution.py:312
  232.7 7.7 %copy.105 = f32[1664,1024]{1,0:T(8,128)} copy(f32[1664,1024]{0,1:T(8,128)} %bitcast.124) | data formatting | bytes 13631488 | tf_op jit(solution)/shard_map/reshape | solution.py:316
  240.4 9.1 %multiply_convert_fusion = bf16[8,256,1664]{1,2,0:T(8,128)(2,1)S(1)} fusion(f32[8,1664,256]{2,1,0:T(8,128)} %get-tuple-element.112, f32[8,256]{1,0:T(8,128)S(1)} %copy.96, f32[8,256]{1,0:T(8,128)S(1)} %log_add_fusion, pred[256,1664]{0,1:T(8,128)(4,1)S(1)} %copy.91, bf16[256,8,128]{0,2,1:T(8,128)(2,1)S(1)} %copy.102, ...), kind=kOutput, calls=%fused_computation.9 | convolution fusion | flops 896270336 | bytes 24821760 | tf_op jit(solution)/shard_map/qhd,khd->hqk/dot_general | solution.py:306
  249.5 5.0 fusion.33
  254.5 7.7 %copy.104 = f32[1664,1024]{1,0:T(8,128)} copy(f32[1664,1024]{0,1:T(8,128)} %bitcast.123) | data formatting | bytes 13631488 | tf_op jit(solution)/shard_map/reshape | solution.py:316
  262.2 2.8 fusion.9
  265.4 1.3 copy-done.4
  266.7 1.3 collective-permute-start.7
  269.5 8.1 %fusion = bf16[1664,2048]{1,0:T(8,128)(2,1)} fusion(f32[1664,1024]{1,0:T(8,128)} %copy.105, f32[1664,1024]{1,0:T(8,128)} %copy.104), kind=kLoop, calls=%fused_computation.7 | loop fusion | flops 13631488 | bytes 20447232 | tf_op jit(solution)/shard_map/convert.4
  279.7 1.2 fusion.25
  280.9 2.5 collective-permute-start.8
  283.5 1.1 constant_dynamic-slice_fusion.1
  284.8 4.1 collective-permute-done.8
  289.0 3.5 collective-permute-start.9
  293.6 3.2 collective-permute-done.9
  296.9 4.3 collective-permute-done.6
  301.4 19.3 %collective-permute-start.10 = (bf16[128,2048]{1,0:T(8,128)(2,1)S(1)}, bf16[128,2048]{1,0:T(8,128)(2,1)S(1)}, u32[]{:S(2)}, u32[]{:S(2)}) collective-permute-start(bf16[128,2048]{1,0:T(8,128)(2,1)S(1)} %fusion.19), channel_id=1, source_target_pairs={{16,0},{20,4},{24,8},{28,12},{0,16},{4,20},{8,24},{12,28},{48,32},... | collective-permute-start | bytes 1572872 | tf_op jit(solution)/shard_map/ppermute | solution.py:349
  320.7 1.8 fusion.30
  322.4 21.1 %collective-permute-start.3 = (bf16[256,2048]{1,0:T(8,128)(2,1)}, bf16[256,2048]{1,0:T(8,128)(2,1)}, u32[]{:S(2)}, u32[]{:S(2)}) collective-permute-start(bf16[256,2048]{1,0:T(8,128)(2,1)} %get-tuple-element.103), channel_id=1, source_target_pairs={{4,0},{8,4},{12,8},{16,12},{20,16},{24,20},{28,24},{32,28},{36,32}... | collective-permute-start | bytes 3145736 | tf_op jit(solution)/shard_map/ppermute | solution.py:19
  343.5 2.7 collective-permute-start.2
  346.3 1.9 collective-permute-start
  348.2 1.9 collective-permute-start.1
  350.2 3.2 fusion.12
  354.2 113.2 %collective-permute-start.13 = (bf16[128,2048]{1,0:T(8,128)(2,1)S(1)}, bf16[128,2048]{1,0:T(8,128)(2,1)S(1)}, u32[]{:S(2)}, u32[]{:S(2)}) collective-permute-start(bf16[128,2048]{1,0:T(8,128)(2,1)S(1)} %fusion.20), channel_id=1, source_target_pairs={{8,0},{12,4},{0,8},{4,12},{24,16},{28,20},{16,24},{20,28},{40,32},... | collective-permute-start | bytes 1572872 | tf_op jit(solution)/shard_map/ppermute | solution.py:361
  467.4 4.1 convolution_convert_fusion
  471.6 15.0 %collective-permute-done.13 = bf16[128,2048]{1,0:T(8,128)(2,1)S(1)} collective-permute-done((bf16[128,2048]{1,0:T(8,128)(2,1)S(1)}, bf16[128,2048]{1,0:T(8,128)(2,1)S(1)}, u32[]{:S(2)}, u32[]{:S(2)}) %collective-permute-start.13) | collective-permute-done | bytes 524320 | tf_op jit(solution)/shard_map/ppermute | solution.py:361
  486.6 29.6 %collective-permute-start.11 = (bf16[128,2048]{1,0:T(8,128)(2,1)S(1)}, bf16[128,2048]{1,0:T(8,128)(2,1)}, u32[]{:S(2)}, u32[]{:S(2)}) collective-permute-start(bf16[128,2048]{1,0:T(8,128)(2,1)S(1)} %fusion.20), channel_id=1, source_target_pairs={{4,0},{8,4},{12,8},{0,12},{20,16},{24,20},{28,24},{16,28},{36,32},... | collective-permute-start | bytes 1572872 | tf_op jit(solution)/shard_map/ppermute | solution.py:359
  517.2 2.5 fusion.18
  519.7 3.5 collective-permute-done.12
  524.0 1.9 add_select_fusion.1
  526.0 17.9 %collective-permute-done.1 = bf16[256,2048]{1,0:T(8,128)(2,1)} collective-permute-done((bf16[256,2048]{1,0:T(8,128)(2,1)}, bf16[256,2048]{1,0:T(8,128)(2,1)}, u32[]{:S(2)}, u32[]{:S(2)}) %collective-permute-start.1) | collective-permute-done | bytes 1048608 | tf_op jit(solution)/shard_map/ppermute | solution.py:19
  543.9 3.3 fusion.14
  548.2 2.0 copy.107
  (104 shorter events, 17.7 us)
Async XLA Ops:
  7.2 162.3 %copy-start = (bf16[256,4096]{1,0:T(8,128)(2,1)S(1)}, bf16[256,4096]{1,0:T(8,128)(2,1)}, u32[]{:S(2)}) copy-start(bf16[256,4096]{1,0:T(8,128)(2,1)} %param.23) | copy-start | bytes 6291460
  7.2 541.1 %reduce-scatter.2.cloned.1.call-start = ((), (), s32[]{:S(2)}) async-start(), calls=%async_computation.1 | async-start | bytes 17301504 | tf_op jit(solution)/shard_map/reduce_scatter | solution.py:379
  149.9 5.6 %copy-start.11 = (pred[256,1664]{1,0:T(8,128)(4,1)S(1)}, pred[256,1664]{1,0:T(8,128)(4,1)}, u32[]{:S(2)}) copy-start(pred[256,1664]{1,0:T(8,128)(4,1)} %copy.90) | copy-start | bytes 1277956
  149.9 5.6 %copy-start.12 = (pred[256,1152]{1,0:T(8,128)(4,1)S(1)}, pred[256,1152]{1,0:T(8,128)(4,1)}, u32[]{:S(2)}) copy-start(pred[256,1152]{1,0:T(8,128)(4,1)} %iota_compare_fusion) | copy-start | bytes 884740
  178.6 1.0 copy-start.10
  188.0 6.7 %copy-start.6 = (bf16[256,1024]{1,0:T(8,128)(2,1)S(1)}, bf16[256,1024]{1,0:T(8,128)(2,1)}, u32[]{:S(2)}) copy-start(bf16[256,1024]{1,0:T(8,128)(2,1)} %shard_map.109) | copy-start | bytes 1572868
  201.8 2.1 copy-start.7
  249.5 5.0 copy-start.2
  265.3 1.3 copy-start.4
  266.7 12.2 %collective-permute-start.7 = (bf16[64,2048]{1,0:T(8,128)(2,1)S(1)}, bf16[64,2048]{1,0:T(8,128)(2,1)S(1)}, u32[]{:S(2)}, u32[]{:S(2)}) collective-permute-start(bf16[64,2048]{1,0:T(8,128)(2,1)S(1)} %fusion.24), channel_id=1, source_target_pairs={{0,96},{4,100},{8,104},{12,108},{16,112},{20,116},{24,120},{28,124... | collective-permute-start | bytes 786440 | tf_op jit(solution)/shard_map/ppermute | solution.py:329
  268.8 15.8 %collective-permute-start.4 = (bf16[64,2048]{1,0:T(8,128)(2,1)}, bf16[64,2048]{1,0:T(8,128)(2,1)S(1)}, u32[]{:S(2)}, u32[]{:S(2)}) collective-permute-start(bf16[64,2048]{1,0:T(8,128)(2,1)} %fusion.21), channel_id=1, source_target_pairs={{0,32},{4,36},{8,40},{12,44},{16,48},{20,52},{24,56},{28,60},{32,6... | collective-permute-start | bytes 786440 | tf_op jit(solution)/shard_map/ppermute | solution.py:328
  279.7 9.2 %copy-start.5 = (f32[4,64,2048]{2,1,0:T(8,128)S(1)}, f32[4,64,2048]{2,1,0:T(8,128)}, u32[]{:S(2)}) copy-start(f32[4,64,2048]{2,1,0:T(8,128)} %bitcast_dynamic-update-slice_fusion.2) | copy-start | bytes 6291460
  280.9 8.0 %collective-permute-start.8 = (bf16[64,2048]{1,0:T(8,128)(2,1)S(1)}, bf16[64,2048]{1,0:T(8,128)(2,1)S(1)}, u32[]{:S(2)}, u32[]{:S(2)}) collective-permute-start(bf16[64,2048]{1,0:T(8,128)(2,1)S(1)} %fusion.25), channel_id=1, source_target_pairs={{0,96},{4,100},{8,104},{12,108},{16,112},{20,116},{24,120},{28,124... | collective-permute-start | bytes 786440 | tf_op jit(solution)/shard_map/ppermute | solution.py:329
  284.6 36.1 %slice-start = ((s8[6815744]{0:T(1024)(128)(4,1)}), s8[4194304]{0:T(1024)(128)(4,1)S(1)}, s32[]{:S(2)}) async-start(s8[6815744]{0:T(1024)(128)(4,1)} %bitcast.126), calls=%async_computation.2 | async-start | bytes 8388608
  284.7 8.7 %collective-permute-start.5 = (bf16[64,2048]{1,0:T(8,128)(2,1)S(1)}, bf16[64,2048]{1,0:T(8,128)(2,1)S(1)}, u32[]{:S(2)}, u32[]{:S(2)}) collective-permute-start(bf16[64,2048]{1,0:T(8,128)(2,1)S(1)} %fusion.22), channel_id=1, source_target_pairs={{0,32},{4,36},{8,40},{12,44},{16,48},{20,52},{24,56},{28,60},{32,6... | collective-permute-start | bytes 786440 | tf_op jit(solution)/shard_map/ppermute | solution.py:328
  289.0 7.8 %collective-permute-start.9 = (bf16[64,2048]{1,0:T(8,128)(2,1)S(1)}, bf16[64,2048]{1,0:T(8,128)(2,1)S(1)}, u32[]{:S(2)}, u32[]{:S(2)}) collective-permute-start(bf16[64,2048]{1,0:T(8,128)(2,1)S(1)} %fusion.26), channel_id=1, source_target_pairs={{0,96},{4,100},{8,104},{12,108},{16,112},{20,116},{24,120},{28,124... | collective-permute-start | bytes 786440 | tf_op jit(solution)/shard_map/ppermute | solution.py:329
  293.4 27.2 %slice-start.1 = ((s8[6815744]{0:T(1024)(128)(4,1)}), s8[2621440]{0:T(1024)(128)(4,1)S(1)}, s32[]{:S(2)}) async-start(s8[6815744]{0:T(1024)(128)(4,1)} %bitcast.126), calls=%async_computation.3 | async-start | bytes 5242880
  293.5 7.8 %collective-permute-start.6 = (bf16[64,2048]{1,0:T(8,128)(2,1)S(1)}, bf16[64,2048]{1,0:T(8,128)(2,1)S(1)}, u32[]{:S(2)}, u32[]{:S(2)}) collective-permute-start(bf16[64,2048]{1,0:T(8,128)(2,1)S(1)} %fusion.23), channel_id=1, source_target_pairs={{0,32},{4,36},{8,40},{12,44},{16,48},{20,52},{24,56},{28,60},{32,6... | collective-permute-start | bytes 786440 | tf_op jit(solution)/shard_map/ppermute | solution.py:328
  301.4 52.0 %collective-permute-start.10 = (bf16[128,2048]{1,0:T(8,128)(2,1)S(1)}, bf16[128,2048]{1,0:T(8,128)(2,1)S(1)}, u32[]{:S(2)}, u32[]{:S(2)}) collective-permute-start(bf16[128,2048]{1,0:T(8,128)(2,1)S(1)} %fusion.19), channel_id=1, source_target_pairs={{16,0},{20,4},{24,8},{28,12},{0,16},{4,20},{8,24},{12,28},{48,32},... | collective-permute-start | bytes 1572872 | tf_op jit(solution)/shard_map/ppermute | solution.py:349
  322.4 203.5 %collective-permute-start.3 = (bf16[256,2048]{1,0:T(8,128)(2,1)}, bf16[256,2048]{1,0:T(8,128)(2,1)}, u32[]{:S(2)}, u32[]{:S(2)}) collective-permute-start(bf16[256,2048]{1,0:T(8,128)(2,1)} %get-tuple-element.103), channel_id=1, source_target_pairs={{4,0},{8,4},{12,8},{16,12},{20,16},{24,20},{28,24},{32,28},{36,32}... | collective-permute-start | bytes 3145736 | tf_op jit(solution)/shard_map/ppermute | solution.py:19
  343.5 182.4 %collective-permute-start.2 = (bf16[256,2048]{1,0:T(8,128)(2,1)}, bf16[256,2048]{1,0:T(8,128)(2,1)}, u32[]{:S(2)}, u32[]{:S(2)}) collective-permute-start(bf16[256,2048]{1,0:T(8,128)(2,1)} %get-tuple-element.104), channel_id=1, source_target_pairs={{8,0},{12,4},{16,8},{20,12},{24,16},{28,20},{32,24},{36,28},{40,32... | collective-permute-start | bytes 3145736 | tf_op jit(solution)/shard_map/ppermute | solution.py:19
  346.3 125.2 %collective-permute-start = (bf16[128,2048]{1,0:T(8,128)(2,1)S(1)}, bf16[128,2048]{1,0:T(8,128)(2,1)}, u32[]{:S(2)}, u32[]{:S(2)}) collective-permute-start(bf16[128,2048]{1,0:T(8,128)(2,1)S(1)} %slice.125), channel_id=1, source_target_pairs={{16,0},{20,4},{24,8},{28,12},{32,16},{36,20},{40,24},{44,28},{48,3... | collective-permute-start | bytes 1572872 | tf_op jit(solution)/shard_map/ppermute | solution.py:19
  348.2 195.7 %collective-permute-start.1 = (bf16[256,2048]{1,0:T(8,128)(2,1)}, bf16[256,2048]{1,0:T(8,128)(2,1)}, u32[]{:S(2)}, u32[]{:S(2)}) collective-permute-start(bf16[256,2048]{1,0:T(8,128)(2,1)} %get-tuple-element.102), channel_id=1, source_target_pairs={{12,0},{16,4},{20,8},{24,12},{28,16},{32,20},{36,24},{40,28},{44,3... | collective-permute-start | bytes 3145736 | tf_op jit(solution)/shard_map/ppermute | solution.py:19
  350.2 117.2 %copy-start.3 = (bf16[1664,1024]{0,1:T(8,128)(2,1)S(1)}, bf16[1664,1024]{0,1:T(8,128)(2,1)}, u32[]{:S(2)}) copy-start(bf16[1664,1024]{0,1:T(8,128)(2,1)} %copy.112) | copy-start | bytes 10223620
  353.4 0.8 copy-start.8
  354.2 132.4 %collective-permute-start.13 = (bf16[128,2048]{1,0:T(8,128)(2,1)S(1)}, bf16[128,2048]{1,0:T(8,128)(2,1)S(1)}, u32[]{:S(2)}, u32[]{:S(2)}) collective-permute-start(bf16[128,2048]{1,0:T(8,128)(2,1)S(1)} %fusion.20), channel_id=1, source_target_pairs={{8,0},{12,4},{0,8},{4,12},{24,16},{28,20},{16,24},{20,28},{40,32},... | collective-permute-start | bytes 1572872 | tf_op jit(solution)/shard_map/ppermute | solution.py:361
  471.5 51.7 %collective-permute-start.12 = (bf16[128,2048]{1,0:T(8,128)(2,1)S(1)}, bf16[128,2048]{1,0:T(8,128)(2,1)S(1)}, u32[]{:S(2)}, u32[]{:S(2)}) collective-permute-start(bf16[128,2048]{1,0:T(8,128)(2,1)S(1)} %fusion.20), channel_id=1, source_target_pairs={{12,0},{0,4},{4,8},{8,12},{28,16},{16,20},{20,24},{24,28},{44,32},... | collective-permute-start | bytes 1572872 | tf_op jit(solution)/shard_map/ppermute | solution.py:360
  486.6 33.1 %copy-start.13 = (bf16[128,2048]{1,0:T(8,128)(2,1)}, bf16[128,2048]{1,0:T(8,128)(2,1)S(1)}, u32[]{:S(2)}) copy-start(bf16[128,2048]{1,0:T(8,128)(2,1)S(1)} %collective-permute-done.13) | copy-start | bytes 1572868
  486.6 37.4 %collective-permute-start.11 = (bf16[128,2048]{1,0:T(8,128)(2,1)S(1)}, bf16[128,2048]{1,0:T(8,128)(2,1)}, u32[]{:S(2)}, u32[]{:S(2)}) collective-permute-start(bf16[128,2048]{1,0:T(8,128)(2,1)S(1)} %fusion.20), channel_id=1, source_target_pairs={{4,0},{8,4},{12,8},{0,12},{20,16},{24,20},{28,24},{16,28},{36,32},... | collective-permute-start | bytes 1572872 | tf_op jit(solution)/shard_map/ppermute | solution.py:359
  517.2 6.8 %copy-start.9 = (bf16[128,2048]{1,0:T(8,128)(2,1)S(1)}, bf16[128,2048]{1,0:T(8,128)(2,1)}, u32[]{:S(2)}) copy-start(bf16[128,2048]{1,0:T(8,128)(2,1)} %copy-done.8) | copy-start | bytes 1572868
  523.2 0.8 copy-start.14
  524.0 26.2 %copy-start.1 = (bf16[256,4096]{1,0:T(8,128)(2,1)S(1)}, bf16[256,4096]{1,0:T(8,128)(2,1)}, u32[]{:S(2)}) copy-start(bf16[256,4096]{1,0:T(8,128)(2,1)} %param.23) | copy-start | bytes 6291460
Sparse Core Ops, SparseCore 0:
  178.7 340.5 reduce-scatter.1

commit v17 on v14

--- a/solution.py
+++ b/solution.py
@@ -133,6 +133,8 @@
     pair[0] = jnp.where(upper, cross1[...], held[...])
     pair[1] = jnp.where(upper, held[...], cross1[...])
     slot += 1
+    for distance in range(len(spans), 0, -1):
+        send_window(distance)
     copy = pltpu.make_async_remote_copy(
         src_ref=pair,
         dst_ref=cross2,
@@ -143,8 +145,6 @@
     )
     copy.start()
     copy.wait()
-    for distance in range(len(spans), 0, -1):
-        send_window(distance)
     upper = ((my_group // 2) % 2) == 1
     for index in range(2):
         far_out[index] = jnp.where(upper, cross2[index], pair[index])

time: 536 us -> 540 us (level)
  waiting for transfers between devices: 71.8 us -> 106 us
  Pallas kernels: 144 us -> 124 us
  starting transfers between devices: 152 us -> 141 us
    pallas_call x1, Pallas kernels: 131 us -> 112 us  [exchange(): pl.pallas_call(functools.partial(exchange_kernel, (seq_size, group, spans...]
    ppermute x1, waiting for transfers between devices: 17.9 us -> 36.9 us  [local(): behind = lax.ppermute(sent, 'seq', from_lane(-1)).astype(jnp.float32)]
    ppermute x1, starting transfers between devices: 18.1 us -> 0.01 us  [local(): ahead = lax.ppermute(sent, 'seq', from_lane(1)).astype(jnp.float32)]
    ppermute x4, waiting for transfers between devices: 27.8 us -> 42.2 us  [passed_along(): return lax.ppermute(block, axis, route)]
    ppermute x4, starting transfers between devices: 95.7 us -> 109 us  [passed_along(): return lax.ppermute(block, axis, route)]
  transfers between devices with their start and end apart: 15 -> 15, of which waited for: 7 -> 7; matrix products, arithmetic and copies ran while one was open for 23% -> 22% of each run, Pallas kernels for 0% -> 0%
where the time goes in v17:
time: 540 us; the launch traced here: 539 us
  starting transfers between devices  141 us (26%)
  Pallas kernels  124 us (23%)
  waiting for transfers between devices  106 us (20%)
  local copies, waits for them, and re-layouts  54.2 us (10%)
  matrix products  53.6 us (10%)
  other arithmetic  42.4 us (8%)
  between operations  16.8 us (3%)
    pallas_call x1, Pallas kernels, exchange(): pl.pallas_call(functools.partial(exchange_kernel, (seq_size, group, spans...  112 us
    ppermute x4, starting transfers between devices, passed_along(): return lax.ppermute(block, axis, route)  109 us
    ppermute x4, waiting for transfers between devices, passed_along(): return lax.ppermute(block, axis, route)  42.2 us
    ppermute x1, waiting for transfers between devices, local(): behind = lax.ppermute(sent, 'seq', from_lane(-1)).astype(jnp.float32)  36.9 us
    ppermute x1, starting transfers between devices, local(): lax.ppermute(part.astype(jnp.bfloat16), 'seq', route).astype(jnp.float32)  18.5 us
    unnamed x43, local copies, waits for them, and re-layouts  15.3 us
    ppermute x1, waiting for transfers between devices, local(): lax.ppermute(part.astype(jnp.bfloat16), 'seq', from_lane(1))  14 us
    pallas_call x1, Pallas kernels, attention_out(): pl.pallas_call(functools.partial(forward_kernel, scale), out_shape=jax.Sh...  12.3 us
  transfers between devices with their start and end apart: 15, of which 7 were waited for; matrix products, arithmetic and copies ran while one was open for 22% of the time, Pallas kernels for 0%

profile of v17, /device:TPU:40, one launch (start us, length us, event | category | flops | bytes accessed | tf_op | source)
XLA Modules:
  0.0 538.9 jit_solution(14235841381973778340)
XLA Ops:
  7.2 1.4 slice.105
  14.4 2.2 copy.90
  18.7 112.2 %shard_map.108 = (bf16[896,2048]{1,0:T(8,128)(2,1)}, bf16[4,128,2048]{2,1,0:T(8,128)(2,1)S(1)}) custom-call(s32[2]{0:T(128)S(1)} %pad_add_fusion.1.ctl_ref, bf16[256,2048]{1,0:T(8,128)(2,1)S(1)} %constant_dynamic-update-slice_fusion.kv_ref), custom_call_target="tpu_custom_call" | custom-call | tf_op jit(solution)/shard_map/pallas_call | solution.py:163
  130.9 5.6 %pad_maximum_fusion.1.k_ref.v_ref = bf16[1664,2048]{1,0:T(8,128)(2,1)} fusion(bf16[512,2048]{1,0:T(8,128)(2,1)S(1)} %bitcast.120, bf16[256,2048]{1,0:T(8,128)(2,1)S(1)} %constant_dynamic-update-slice_fusion.kv_ref, bf16[896,2048]{1,0:T(8,128)(2,1)} %get-tuple-element.78), kind=kLoop, calls=%fused_computation.16 | loop fusion | flops 20447232 | bytes 13631488 | tf_op jit(solution)/shard_map/concatenate | solution.py:265
  136.5 1.6 broadcast_select_fusion
  138.1 12.3 %shard_map.109 = bf16[256,1024]{1,0:T(8,128)(2,1)} custom-call(bf16[256,1024]{1,0:T(8,128)(2,1)} %q_ref.1, bf16[1664,2048]{1,0:T(8,128)(2,1)} %pad_maximum_fusion.1.k_ref.v_ref, bf16[1664,2048]{1,0:T(8,128)(2,1)} %pad_maximum_fusion.1.k_ref.v_ref, f32[256,1664]{1,0:T(8,128)} %get-tuple-element.100.bias_ref), custom_call_target="tpu_custom_call" | custom-call | flops 1744830464 | bytes 9568256 | tf_op jit(solution)/shard_map/pallas_call | solution.py:208
  150.4 9.1 %convolution_bitcast_fusion = f32[4096,1024]{0,1:T(8,128)} fusion(bf16[256,1024]{1,0:T(8,128)(2,1)} %shard_map.109, bf16[256,4096]{1,0:T(8,128)(2,1)S(1)} %copy-done), kind=kOutput, calls=%fused_computation.14 | convolution fusion | flops 2147483648 | bytes 19398656 | tf_op jit(solution)/shard_map/dot_general | solution.py:381
  161.6 7.4 %slice_bitcast_fusion = (bf16[208,8,8,128]{3,2,1,0:T(8,128)(2,1)}, bf16[1664,1024]{1,0:T(8,128)(2,1)}) fusion(bf16[1664,2048]{1,0:T(8,128)(2,1)} %pad_maximum_fusion.1.k_ref.v_ref), kind=kLoop, calls=%fused_computation.24 | loop fusion | bytes 13631488
  168.9 5.7 %copy.112 = bf16[1664,1024]{0,1:T(8,128)(2,1)} copy(bf16[1664,1024]{1,0:T(8,128)(2,1)} %get-tuple-element.106) | data formatting | bytes 6815744 | tf_op jit(solution)/shard_map/reshape | solution.py:266
  175.8 1.2 copy.117
  177.0 5.7 %fusion.15 = bf16[32,8,8,128]{3,1,2,0:T(8,128)(2,1)S(1)} fusion(bf16[256,4096]{1,0:T(8,128)(2,1)S(1)} %copy-done, bf16[4096,1024]{1,0:T(8,128)(2,1)} %param.24), kind=kOutput, calls=%fused_computation.34 | convolution fusion | flops 2147745792 | bytes 11010048 | tf_op jit(solution)/shard_map/dot_general | solution.py:245
  183.1 1.6 multiply_reduce_fusion
  184.8 9.4 %fusion.2 = (f32[8,256]{1,0:T(8,128)S(1)}, f32[8,1664,256]{2,1,0:T(8,128)}) fusion(pred[256,1664]{0,1:T(8,128)(4,1)S(1)} %copy.91, bf16[1664,8,128]{0,2,1:T(8,128)(2,1)} %bitcast.121, bf16[256,8,128]{0,2,1:T(8,128)(2,1)S(1)} %bitcast.128), kind=kOutput, calls=%fused_computation.13 | convolution fusion | flops 882636800 | bytes 17997824 | tf_op jit(solution)/shard_map/qhd,khd->hqk/dot_general | solution.py:293
  194.2 7.6 %exponential_reduce_fusion = f32[8,256]{1,0:T(8,128)S(1)} fusion(f32[8,1664,256]{2,1,0:T(8,128)} %get-tuple-element.112, f32[8,256]{1,0:T(8,128)S(1)} %get-tuple-element.111, pred[256,1664]{0,1:T(8,128)(4,1)S(1)} %copy.91), kind=kLoop, calls=%fused_computation.11 | loop fusion | flops 13629440 | bytes 14073856 | tf_op jit(solution)/shard_map/reduce_sum | solution.py:298
  201.8 11.2 %fusion.3 = f32[8,128,1664]{2,1,0:T(8,128)} fusion(bf16[256,8,128]{0,2,1:T(8,128)(2,1)S(1)} %copy.102, f32[8,1664,256]{2,1,0:T(8,128)} %get-tuple-element.112, f32[8,256]{1,0:T(8,128)S(1)} %log_add_fusion, pred[256,1664]{0,1:T(8,128)(4,1)S(1)} %copy.91), kind=kOutput, calls=%fused_computation.15 | convolution fusion | flops 886046720 | bytes 21405696 | tf_op jit(solution)/shard_map/hqk,qhd->khd/dot_general | solution.py:312
  213.0 8.0 %copy.105 = f32[1664,1024]{1,0:T(8,128)} copy(f32[1664,1024]{0,1:T(8,128)} %bitcast.124) | data formatting | bytes 13631488 | tf_op jit(solution)/shard_map/reshape | solution.py:316
  221.0 9.1 %multiply_convert_fusion = bf16[8,256,1664]{1,2,0:T(8,128)(2,1)S(1)} fusion(f32[8,1664,256]{2,1,0:T(8,128)} %get-tuple-element.112, f32[8,256]{1,0:T(8,128)S(1)} %copy.96, f32[8,256]{1,0:T(8,128)S(1)} %log_add_fusion, pred[256,1664]{0,1:T(8,128)(4,1)S(1)} %copy.91, bf16[256,8,128]{0,2,1:T(8,128)(2,1)S(1)} %copy.102, ...), kind=kOutput, calls=%fused_computation.9 | convolution fusion | flops 896270336 | bytes 24821760 | tf_op jit(solution)/shard_map/qhd,khd->hqk/dot_general | solution.py:306
  230.1 5.0 fusion.34
  235.1 7.7 %copy.104 = f32[1664,1024]{1,0:T(8,128)} copy(f32[1664,1024]{0,1:T(8,128)} %bitcast.123) | data formatting | bytes 13631488 | tf_op jit(solution)/shard_map/reshape | solution.py:316
  242.8 2.8 fusion.9
  245.9 1.3 copy-done.4
  248.1 2.0 collective-permute-start.4
  250.1 8.1 %fusion = bf16[1664,2048]{1,0:T(8,128)(2,1)} fusion(f32[1664,1024]{1,0:T(8,128)} %copy.105, f32[1664,1024]{1,0:T(8,128)} %copy.104), kind=kLoop, calls=%fused_computation.7 | loop fusion | flops 13631488 | bytes 20447232 | tf_op jit(solution)/shard_map/convert.4
  258.2 1.1 constant_dynamic-slice_fusion.2
  260.3 1.2 fusion.25
  261.5 1.3 collective-permute-start.8
  264.9 4.9 collective-permute-done.8
  270.7 1.2 collective-permute-done.5
  272.3 4.1 collective-permute-done.9
  276.5 3.1 collective-permute-done.6
  279.8 18.5 %collective-permute-start.10 = (bf16[128,2048]{1,0:T(8,128)(2,1)S(1)}, bf16[128,2048]{1,0:T(8,128)(2,1)S(1)}, u32[]{:S(2)}, u32[]{:S(2)}) collective-permute-start(bf16[128,2048]{1,0:T(8,128)(2,1)S(1)} %fusion.19), channel_id=1, source_target_pairs={{16,0},{20,4},{24,8},{28,12},{0,16},{4,20},{8,24},{12,28},{48,32},... | collective-permute-start | bytes 1572872 | tf_op jit(solution)/shard_map/ppermute | solution.py:349
  298.3 1.8 fusion.31
  300.1 23.7 %collective-permute-start.3 = (bf16[256,2048]{1,0:T(8,128)(2,1)}, bf16[256,2048]{1,0:T(8,128)(2,1)}, u32[]{:S(2)}, u32[]{:S(2)}) collective-permute-start(bf16[256,2048]{1,0:T(8,128)(2,1)} %get-tuple-element.103), channel_id=1, source_target_pairs={{4,0},{8,4},{12,8},{16,12},{20,16},{24,20},{28,24},{32,28},{36,32}... | collective-permute-start | bytes 3145736 | tf_op jit(solution)/shard_map/ppermute | solution.py:19
  323.7 22.2 %collective-permute-start.2 = (bf16[256,2048]{1,0:T(8,128)(2,1)}, bf16[256,2048]{1,0:T(8,128)(2,1)}, u32[]{:S(2)}, u32[]{:S(2)}) collective-permute-start(bf16[256,2048]{1,0:T(8,128)(2,1)} %get-tuple-element.104), channel_id=1, source_target_pairs={{8,0},{12,4},{16,8},{20,12},{24,16},{28,20},{32,24},{36,28},{40,32... | collective-permute-start | bytes 3145736 | tf_op jit(solution)/shard_map/ppermute | solution.py:19
  346.8 1.9 collective-permute-start
  348.8 3.2 fusion.12
  352.2 2.7 collective-permute-start.12
  354.9 4.1 convolution_convert_fusion
  359.0 36.9 %collective-permute-done.12 = bf16[128,2048]{1,0:T(8,128)(2,1)S(1)} collective-permute-done((bf16[128,2048]{1,0:T(8,128)(2,1)S(1)}, bf16[128,2048]{1,0:T(8,128)(2,1)S(1)}, u32[]{:S(2)}, u32[]{:S(2)}) %collective-permute-start.12) | collective-permute-done | bytes 524320 | tf_op jit(solution)/shard_map/ppermute | solution.py:360
  395.9 61.3 %collective-permute-start.1 = (bf16[256,2048]{1,0:T(8,128)(2,1)}, bf16[256,2048]{1,0:T(8,128)(2,1)}, u32[]{:S(2)}, u32[]{:S(2)}) collective-permute-start(bf16[256,2048]{1,0:T(8,128)(2,1)} %get-tuple-element.102), channel_id=1, source_target_pairs={{12,0},{16,4},{20,8},{24,12},{28,16},{32,20},{36,24},{40,28},{44,3... | collective-permute-start | bytes 3145736 | tf_op jit(solution)/shard_map/ppermute | solution.py:19
  457.3 1.1 fusion.30
  458.4 5.5 %collective-permute-start.13 = (bf16[128,2048]{1,0:T(8,128)(2,1)}, bf16[128,2048]{1,0:T(8,128)(2,1)}, u32[]{:S(2)}, u32[]{:S(2)}) collective-permute-start(bf16[128,2048]{1,0:T(8,128)(2,1)} %fusion.30), channel_id=1, source_target_pairs={{4,0},{8,4},{12,8},{0,12},{20,16},{24,20},{28,24},{16,28},{36,32},... | collective-permute-start | bytes 1572872 | tf_op jit(solution)/shard_map/ppermute | solution.py:362
  465.0 2.5 fusion.18
  467.6 14.0 %collective-permute-done.13 = bf16[128,2048]{1,0:T(8,128)(2,1)} collective-permute-done((bf16[128,2048]{1,0:T(8,128)(2,1)}, bf16[128,2048]{1,0:T(8,128)(2,1)}, u32[]{:S(2)}, u32[]{:S(2)}) %collective-permute-start.13) | collective-permute-done | bytes 524320 | tf_op jit(solution)/shard_map/ppermute | solution.py:362
  481.5 1.9 add_select_fusion
  483.5 42.2 %collective-permute-done.1 = bf16[256,2048]{1,0:T(8,128)(2,1)} collective-permute-done((bf16[256,2048]{1,0:T(8,128)(2,1)}, bf16[256,2048]{1,0:T(8,128)(2,1)}, u32[]{:S(2)}, u32[]{:S(2)}) %collective-permute-start.1) | collective-permute-done | bytes 1048608 | tf_op jit(solution)/shard_map/ppermute | solution.py:19
  525.6 3.3 fusion.14
  530.0 2.0 copy.107
  (105 shorter events, 18.3 us)
Async XLA Ops:
  7.2 143.2 %copy-start = (bf16[256,4096]{1,0:T(8,128)(2,1)S(1)}, bf16[256,4096]{1,0:T(8,128)(2,1)}, u32[]{:S(2)}) copy-start(bf16[256,4096]{1,0:T(8,128)(2,1)} %param.23) | copy-start | bytes 6291460
  7.2 522.8 %reduce-scatter.2.cloned.1.call-start = ((), (), s32[]{:S(2)}) async-start(), calls=%async_computation.1 | async-start | bytes 17301504 | tf_op jit(solution)/shard_map/reduce_scatter | solution.py:380
  130.9 5.6 %copy-start.13 = (pred[256,1664]{1,0:T(8,128)(4,1)S(1)}, pred[256,1664]{1,0:T(8,128)(4,1)}, u32[]{:S(2)}) copy-start(pred[256,1664]{1,0:T(8,128)(4,1)} %copy.90) | copy-start | bytes 1277956
  130.9 5.6 %copy-start.14 = (pred[256,1152]{1,0:T(8,128)(4,1)S(1)}, pred[256,1152]{1,0:T(8,128)(4,1)}, u32[]{:S(2)}) copy-start(pred[256,1152]{1,0:T(8,128)(4,1)} %iota_compare_fusion) | copy-start | bytes 884740
  159.5 1.0 copy-start.12
  168.9 6.7 %copy-start.6 = (bf16[256,1024]{1,0:T(8,128)(2,1)S(1)}, bf16[256,1024]{1,0:T(8,128)(2,1)}, u32[]{:S(2)}) copy-start(bf16[256,1024]{1,0:T(8,128)(2,1)} %shard_map.109) | copy-start | bytes 1572868
  182.7 2.1 copy-start.7
  230.1 5.0 copy-start.2
  245.9 1.3 copy-start.4
  247.3 12.2 %collective-permute-start.7 = (bf16[64,2048]{1,0:T(8,128)(2,1)S(1)}, bf16[64,2048]{1,0:T(8,128)(2,1)S(1)}, u32[]{:S(2)}, u32[]{:S(2)}) collective-permute-start(bf16[64,2048]{1,0:T(8,128)(2,1)S(1)} %fusion.24), channel_id=1, source_target_pairs={{0,96},{4,100},{8,104},{12,108},{16,112},{20,116},{24,120},{28,124... | collective-permute-start | bytes 786440 | tf_op jit(solution)/shard_map/ppermute | solution.py:329
  248.1 15.8 %collective-permute-start.4 = (bf16[64,2048]{1,0:T(8,128)(2,1)}, bf16[64,2048]{1,0:T(8,128)(2,1)S(1)}, u32[]{:S(2)}, u32[]{:S(2)}) collective-permute-start(bf16[64,2048]{1,0:T(8,128)(2,1)} %fusion.21), channel_id=1, source_target_pairs={{0,32},{4,36},{8,40},{12,44},{16,48},{20,52},{24,56},{28,60},{32,6... | collective-permute-start | bytes 786440 | tf_op jit(solution)/shard_map/ppermute | solution.py:328
  260.3 9.6 %copy-start.5 = (f32[4,64,2048]{2,1,0:T(8,128)S(1)}, f32[4,64,2048]{2,1,0:T(8,128)}, u32[]{:S(2)}) copy-start(f32[4,64,2048]{2,1,0:T(8,128)} %bitcast_dynamic-update-slice_fusion.2) | copy-start | bytes 6291460
  261.5 8.3 %collective-permute-start.8 = (bf16[64,2048]{1,0:T(8,128)(2,1)S(1)}, bf16[64,2048]{1,0:T(8,128)(2,1)S(1)}, u32[]{:S(2)}, u32[]{:S(2)}) collective-permute-start(bf16[64,2048]{1,0:T(8,128)(2,1)S(1)} %fusion.25), channel_id=1, source_target_pairs={{0,96},{4,100},{8,104},{12,108},{16,112},{20,116},{24,120},{28,124... | collective-permute-start | bytes 786440 | tf_op jit(solution)/shard_map/ppermute | solution.py:329
  263.9 34.4 %slice-start = ((s8[6815744]{0:T(1024)(128)(4,1)}), s8[4194304]{0:T(1024)(128)(4,1)S(1)}, s32[]{:S(2)}) async-start(s8[6815744]{0:T(1024)(128)(4,1)} %bitcast.126), calls=%async_computation.2 | async-start | bytes 8388608
  264.1 7.8 %collective-permute-start.5 = (bf16[64,2048]{1,0:T(8,128)(2,1)S(1)}, bf16[64,2048]{1,0:T(8,128)(2,1)S(1)}, u32[]{:S(2)}, u32[]{:S(2)}) collective-permute-start(bf16[64,2048]{1,0:T(8,128)(2,1)S(1)} %fusion.22), channel_id=1, source_target_pairs={{0,32},{4,36},{8,40},{12,44},{16,48},{20,52},{24,56},{28,60},{32,6... | collective-permute-start | bytes 786440 | tf_op jit(solution)/shard_map/ppermute | solution.py:328
  270.0 6.4 %collective-permute-start.9 = (bf16[64,2048]{1,0:T(8,128)(2,1)S(1)}, bf16[64,2048]{1,0:T(8,128)(2,1)S(1)}, u32[]{:S(2)}, u32[]{:S(2)}) collective-permute-start(bf16[64,2048]{1,0:T(8,128)(2,1)S(1)} %fusion.26), channel_id=1, source_target_pairs={{0,96},{4,100},{8,104},{12,108},{16,112},{20,116},{24,120},{28,124... | collective-permute-start | bytes 786440 | tf_op jit(solution)/shard_map/ppermute | solution.py:329
  271.9 26.4 %slice-start.1 = ((s8[6815744]{0:T(1024)(128)(4,1)}), s8[2621440]{0:T(1024)(128)(4,1)S(1)}, s32[]{:S(2)}) async-start(s8[6815744]{0:T(1024)(128)(4,1)} %bitcast.126), calls=%async_computation.3 | async-start | bytes 5242880
  271.9 7.7 %collective-permute-start.6 = (bf16[64,2048]{1,0:T(8,128)(2,1)S(1)}, bf16[64,2048]{1,0:T(8,128)(2,1)S(1)}, u32[]{:S(2)}, u32[]{:S(2)}) collective-permute-start(bf16[64,2048]{1,0:T(8,128)(2,1)S(1)} %fusion.23), channel_id=1, source_target_pairs={{0,32},{4,36},{8,40},{12,44},{16,48},{20,52},{24,56},{28,60},{32,6... | collective-permute-start | bytes 786440 | tf_op jit(solution)/shard_map/ppermute | solution.py:328
  279.8 72.3 %collective-permute-start.10 = (bf16[128,2048]{1,0:T(8,128)(2,1)S(1)}, bf16[128,2048]{1,0:T(8,128)(2,1)S(1)}, u32[]{:S(2)}, u32[]{:S(2)}) collective-permute-start(bf16[128,2048]{1,0:T(8,128)(2,1)S(1)} %fusion.19), channel_id=1, source_target_pairs={{16,0},{20,4},{24,8},{28,12},{0,16},{4,20},{8,24},{12,28},{48,32},... | collective-permute-start | bytes 1572872 | tf_op jit(solution)/shard_map/ppermute | solution.py:349
  300.1 183.4 %collective-permute-start.3 = (bf16[256,2048]{1,0:T(8,128)(2,1)}, bf16[256,2048]{1,0:T(8,128)(2,1)}, u32[]{:S(2)}, u32[]{:S(2)}) collective-permute-start(bf16[256,2048]{1,0:T(8,128)(2,1)} %get-tuple-element.103), channel_id=1, source_target_pairs={{4,0},{8,4},{12,8},{16,12},{20,16},{24,20},{28,24},{32,28},{36,32}... | collective-permute-start | bytes 3145736 | tf_op jit(solution)/shard_map/ppermute | solution.py:19
  323.7 159.7 %collective-permute-start.2 = (bf16[256,2048]{1,0:T(8,128)(2,1)}, bf16[256,2048]{1,0:T(8,128)(2,1)}, u32[]{:S(2)}, u32[]{:S(2)}) collective-permute-start(bf16[256,2048]{1,0:T(8,128)(2,1)} %get-tuple-element.104), channel_id=1, source_target_pairs={{8,0},{12,4},{16,8},{20,12},{24,16},{28,20},{32,24},{36,28},{40,32... | collective-permute-start | bytes 3145736 | tf_op jit(solution)/shard_map/ppermute | solution.py:19
  346.8 118.2 %collective-permute-start = (bf16[128,2048]{1,0:T(8,128)(2,1)}, bf16[128,2048]{1,0:T(8,128)(2,1)}, u32[]{:S(2)}, u32[]{:S(2)}) collective-permute-start(bf16[128,2048]{1,0:T(8,128)(2,1)} %slice.125), channel_id=1, source_target_pairs={{16,0},{20,4},{24,8},{28,12},{32,16},{36,20},{40,24},{44,28},{48,3... | collective-permute-start | bytes 1572872 | tf_op jit(solution)/shard_map/ppermute | solution.py:19
  348.8 6.1 %copy-start.3 = (bf16[1664,1024]{0,1:T(8,128)(2,1)S(1)}, bf16[1664,1024]{0,1:T(8,128)(2,1)}, u32[]{:S(2)}) copy-start(bf16[1664,1024]{0,1:T(8,128)(2,1)} %copy.112) | copy-start | bytes 10223620
  352.0 105.2 %copy-start.8 = (bf16[128,2048]{1,0:T(8,128)(2,1)}, bf16[128,2048]{1,0:T(8,128)(2,1)S(1)}, u32[]{:S(2)}) copy-start(bf16[128,2048]{1,0:T(8,128)(2,1)S(1)} %collective-permute-done.10) | copy-start | bytes 1572868
  352.2 43.7 %collective-permute-start.12 = (bf16[128,2048]{1,0:T(8,128)(2,1)S(1)}, bf16[128,2048]{1,0:T(8,128)(2,1)S(1)}, u32[]{:S(2)}, u32[]{:S(2)}) collective-permute-start(bf16[128,2048]{1,0:T(8,128)(2,1)S(1)} %fusion.20), channel_id=1, source_target_pairs={{12,0},{0,4},{4,8},{8,12},{28,16},{16,20},{20,24},{24,28},{44,32},... | collective-permute-start | bytes 1572872 | tf_op jit(solution)/shard_map/ppermute | solution.py:360
  354.9 102.4 %collective-permute-start.11 = (bf16[128,2048]{1,0:T(8,128)(2,1)S(1)}, bf16[128,2048]{1,0:T(8,128)(2,1)S(1)}, u32[]{:S(2)}, u32[]{:S(2)}) collective-permute-start(bf16[128,2048]{1,0:T(8,128)(2,1)S(1)} %fusion.20), channel_id=1, source_target_pairs={{4,0},{8,4},{12,8},{0,12},{20,16},{24,20},{28,24},{16,28},{36,32},... | collective-permute-start | bytes 1572872 | tf_op jit(solution)/shard_map/ppermute | solution.py:359
  395.9 71.7 %copy-start.10 = (bf16[128,2048]{1,0:T(8,128)(2,1)}, bf16[128,2048]{1,0:T(8,128)(2,1)S(1)}, u32[]{:S(2)}) copy-start(bf16[128,2048]{1,0:T(8,128)(2,1)S(1)} %collective-permute-done.12) | copy-start | bytes 1572868
  395.9 129.7 %collective-permute-start.1 = (bf16[256,2048]{1,0:T(8,128)(2,1)}, bf16[256,2048]{1,0:T(8,128)(2,1)}, u32[]{:S(2)}, u32[]{:S(2)}) collective-permute-start(bf16[256,2048]{1,0:T(8,128)(2,1)} %get-tuple-element.102), channel_id=1, source_target_pairs={{12,0},{16,4},{20,8},{24,12},{28,16},{32,20},{36,24},{40,28},{44,3... | collective-permute-start | bytes 3145736 | tf_op jit(solution)/shard_map/ppermute | solution.py:19
  457.3 10.3 %copy-start.11 = (bf16[128,2048]{1,0:T(8,128)(2,1)}, bf16[128,2048]{1,0:T(8,128)(2,1)S(1)}, u32[]{:S(2)}) copy-start(bf16[128,2048]{1,0:T(8,128)(2,1)S(1)} %collective-permute-done.11) | copy-start | bytes 1572868
  458.4 23.1 %collective-permute-start.13 = (bf16[128,2048]{1,0:T(8,128)(2,1)}, bf16[128,2048]{1,0:T(8,128)(2,1)}, u32[]{:S(2)}, u32[]{:S(2)}) collective-permute-start(bf16[128,2048]{1,0:T(8,128)(2,1)} %fusion.30), channel_id=1, source_target_pairs={{4,0},{8,4},{12,8},{0,12},{20,16},{24,20},{28,24},{16,28},{36,32},... | collective-permute-start | bytes 1572872 | tf_op jit(solution)/shard_map/ppermute | solution.py:362
  465.0 16.5 %copy-start.9 = (bf16[128,2048]{1,0:T(8,128)(2,1)S(1)}, bf16[128,2048]{1,0:T(8,128)(2,1)}, u32[]{:S(2)}) copy-start(bf16[128,2048]{1,0:T(8,128)(2,1)} %copy-done.8) | copy-start | bytes 1572868
  481.5 50.5 %copy-start.1 = (bf16[256,4096]{1,0:T(8,128)(2,1)S(1)}, bf16[256,4096]{1,0:T(8,128)(2,1)}, u32[]{:S(2)}) copy-start(bf16[256,4096]{1,0:T(8,128)(2,1)} %param.23) | copy-start | bytes 6291460
Sparse Core Ops, SparseCore 0:
  159.7 349.8 reduce-scatter.1

commit v18 on v14

--- a/solution.py
+++ b/solution.py
@@ -318,29 +318,24 @@
 
     part = grad_kv[pool_blocks * BLK :].reshape(summary_count, BLK, 2 * width)
     half_rows = BLK // 2
-    forward_acc = part[:, :half_rows]
-    backward_acc = part[:, half_rows:]
     to_next = [(d, (d + group) % seq_size) for d in range(seq_size)]
     to_prev = [(d, (d - group) % seq_size) for d in range(seq_size)]
-    for step in range(groups - 1):
-        out_f = lax.dynamic_index_in_dim(forward_acc, (my_group - step - 1) % groups, 0, keepdims=False)
-        out_b = lax.dynamic_index_in_dim(backward_acc, (my_group + step + 1) % groups, 0, keepdims=False)
-        in_f = lax.ppermute(out_f.astype(jnp.bfloat16), "seq", to_next).astype(jnp.float32)
-        in_b = lax.ppermute(out_b.astype(jnp.bfloat16), "seq", to_prev).astype(jnp.float32)
-        slot_f = (my_group - step - 2) % groups
-        slot_b = (my_group + step + 2) % groups
-        forward_acc = lax.dynamic_update_index_in_dim(
-            forward_acc, lax.dynamic_index_in_dim(forward_acc, slot_f, 0, keepdims=False) + in_f, slot_f, 0
-        )
-        backward_acc = lax.dynamic_update_index_in_dim(
-            backward_acc, lax.dynamic_index_in_dim(backward_acc, slot_b, 0, keepdims=False) + in_b, slot_b, 0
-        )
-    part = jnp.concatenate(
-        [
-            lax.dynamic_index_in_dim(forward_acc, my_group, 0, keepdims=False),
-            lax.dynamic_index_in_dim(backward_acc, my_group, 0, keepdims=False),
-        ],
-        axis=0,
+
+    def slot(shift):
+        return lax.dynamic_index_in_dim(part, (my_group + shift) % groups, 0, keepdims=False)
+
+    opposite = slot(2)
+    send_next = jnp.concatenate([slot(1), opposite[:half_rows]], 0).astype(jnp.bfloat16)
+    send_prev = jnp.concatenate([slot(-1), opposite[half_rows:]], 0).astype(jnp.bfloat16)
+    from_prev = lax.ppermute(send_next, "seq", to_next)
+    from_next = lax.ppermute(send_prev, "seq", to_prev)
+    far_lo = lax.ppermute(from_prev[BLK:], "seq", to_next).astype(jnp.float32)
+    far_hi = lax.ppermute(from_next[BLK:], "seq", to_prev).astype(jnp.float32)
+    part = (
+        slot(0)
+        + from_prev[:BLK].astype(jnp.float32)
+        + from_next[:BLK].astype(jnp.float32)
+        + jnp.concatenate([far_lo, far_hi], 0)
     )
     lanes = group // 2
     lane = in_group % lanes

time: 536 us -> 541 us (level)
  waiting for transfers between devices: 71.8 us -> 77.4 us
    ppermute x4, starting transfers between devices: 95.7 us -> 106 us  [passed_along(): return lax.ppermute(block, axis, route)]
    ppermute x6 -> x4, waiting for transfers between devices: 12.4 us -> 17.7 us  [the longest x1 17.5 us: local(): from_next = lax.ppermute(send_prev, 'seq', to_prev)]
    unnamed x43 -> x41, local copies, waits for them, and re-layouts: 15.3 us -> 16.1 us
  transfers between devices with their start and end apart: 15 -> 13, of which waited for: 7 -> 5; matrix products, arithmetic and copies ran while one was open for 23% -> 22% of each run, Pallas kernels for 0% -> 0%
where the time goes in v18:
time: 541 us; the launch traced here: 540 us
  starting transfers between devices  152 us (28%)
  Pallas kernels  144 us (27%)
  waiting for transfers between devices  77.4 us (14%)
  matrix products  53.9 us (10%)
  local copies, waits for them, and re-layouts  53.1 us (10%)
  other arithmetic  43.7 us (8%)
  between operations  16.5 us (3%)
    pallas_call x1, Pallas kernels, exchange(): pl.pallas_call(functools.partial(exchange_kernel, (seq_size, group, spans...  131 us
    ppermute x4, starting transfers between devices, passed_along(): return lax.ppermute(block, axis, route)  106 us
    ppermute x4, waiting for transfers between devices, passed_along(): return lax.ppermute(block, axis, route)  27 us
    ppermute x1, waiting for transfers between devices, local(): behind = lax.ppermute(sent, 'seq', from_lane(-1)).astype(jnp.float32)  21.9 us
    ppermute x1, starting transfers between devices, local(): lax.ppermute(part.astype(jnp.bfloat16), 'seq', route).astype(jnp.float32)  18.1 us
    ppermute x1, waiting for transfers between devices, local(): from_next = lax.ppermute(send_prev, 'seq', to_prev)  17.5 us
    unnamed x41, local copies, waits for them, and re-layouts  16.1 us
    ppermute x1, starting transfers between devices, local(): ahead = lax.ppermute(sent, 'seq', from_lane(1)).astype(jnp.float32)  15.7 us
  transfers between devices with their start and end apart: 13, of which 5 were waited for; matrix products, arithmetic and copies ran while one was open for 22% of the time, Pallas kernels for 0%

profile of v18, /device:TPU:40, one launch (start us, length us, event | category | flops | bytes accessed | tf_op | source)
XLA Modules:
  0.0 540.0 jit_solution(6226985984453319590)
XLA Ops:
  7.2 1.4 slice.125
  10.7 1.1 constant_dynamic-update-slice_fusion.1
  14.4 2.2 copy.90
  17.6 1.1 constant_dynamic-update-slice_fusion.kv_ref
  18.7 131.2 %shard_map.108 = (bf16[896,2048]{1,0:T(8,128)(2,1)}, bf16[4,128,2048]{2,1,0:T(8,128)(2,1)S(1)}) custom-call(s32[2]{0:T(128)S(1)} %pad_add_fusion.1.ctl_ref, bf16[256,2048]{1,0:T(8,128)(2,1)S(1)} %constant_dynamic-update-slice_fusion.kv_ref), custom_call_target="tpu_custom_call" | custom-call | tf_op jit(solution)/shard_map/pallas_call | solution.py:163
  150.0 5.6 %pad_maximum_fusion.1.k_ref.v_ref = bf16[1664,2048]{1,0:T(8,128)(2,1)} fusion(bf16[512,2048]{1,0:T(8,128)(2,1)S(1)} %bitcast.83, bf16[256,2048]{1,0:T(8,128)(2,1)S(1)} %constant_dynamic-update-slice_fusion.kv_ref, bf16[896,2048]{1,0:T(8,128)(2,1)} %get-tuple-element.78), kind=kLoop, calls=%fused_computation.16 | loop fusion | flops 20447232 | bytes 13631488 | tf_op jit(solution)/shard_map/concatenate | solution.py:265
  155.6 1.6 broadcast_select_fusion
  157.2 12.3 %shard_map.109 = bf16[256,1024]{1,0:T(8,128)(2,1)} custom-call(bf16[256,1024]{1,0:T(8,128)(2,1)} %q_ref.1, bf16[1664,2048]{1,0:T(8,128)(2,1)} %pad_maximum_fusion.1.k_ref.v_ref, bf16[1664,2048]{1,0:T(8,128)(2,1)} %pad_maximum_fusion.1.k_ref.v_ref, f32[256,1664]{1,0:T(8,128)} %get-tuple-element.102.bias_ref), custom_call_target="tpu_custom_call" | custom-call | flops 1744830464 | bytes 9568256 | tf_op jit(solution)/shard_map/pallas_call | solution.py:208
  169.5 9.2 %convolution_bitcast_fusion = f32[4096,1024]{0,1:T(8,128)} fusion(bf16[256,1024]{1,0:T(8,128)(2,1)} %shard_map.109, bf16[256,4096]{1,0:T(8,128)(2,1)S(1)} %copy-done), kind=kOutput, calls=%fused_computation.14 | convolution fusion | flops 2147483648 | bytes 19398656 | tf_op jit(solution)/shard_map/dot_general | solution.py:376
  180.7 7.4 %slice_bitcast_fusion = (bf16[208,8,8,128]{3,2,1,0:T(8,128)(2,1)}, bf16[1664,1024]{1,0:T(8,128)(2,1)}) fusion(bf16[1664,2048]{1,0:T(8,128)(2,1)} %pad_maximum_fusion.1.k_ref.v_ref), kind=kLoop, calls=%fused_computation.24 | loop fusion | bytes 13631488
  188.0 5.7 %copy.112 = bf16[1664,1024]{0,1:T(8,128)(2,1)} copy(bf16[1664,1024]{1,0:T(8,128)(2,1)} %get-tuple-element.108) | data formatting | bytes 6815744 | tf_op jit(solution)/shard_map/reshape | solution.py:266
  194.9 1.2 copy.117
  196.1 5.8 %fusion.15 = bf16[32,8,8,128]{3,1,2,0:T(8,128)(2,1)S(1)} fusion(bf16[256,4096]{1,0:T(8,128)(2,1)S(1)} %copy-done, bf16[4096,1024]{1,0:T(8,128)(2,1)} %param.24), kind=kOutput, calls=%fused_computation.34 | convolution fusion | flops 2147745792 | bytes 11010048 | tf_op jit(solution)/shard_map/dot_general | solution.py:245
  202.3 1.6 multiply_reduce_fusion
  203.9 9.4 %fusion.2 = (f32[8,256]{1,0:T(8,128)S(1)}, f32[8,1664,256]{2,1,0:T(8,128)}) fusion(pred[256,1664]{0,1:T(8,128)(4,1)S(1)} %copy.91, bf16[1664,8,128]{0,2,1:T(8,128)(2,1)} %bitcast.84, bf16[256,8,128]{0,2,1:T(8,128)(2,1)S(1)} %bitcast.90), kind=kOutput, calls=%fused_computation.13 | convolution fusion | flops 882636800 | bytes 17997824 | tf_op jit(solution)/shard_map/qhd,khd->hqk/dot_general | solution.py:293
  213.3 8.0 %exponential_reduce_fusion = f32[8,256]{1,0:T(8,128)S(1)} fusion(f32[8,1664,256]{2,1,0:T(8,128)} %get-tuple-element.117, f32[8,256]{1,0:T(8,128)S(1)} %get-tuple-element.116, pred[256,1664]{0,1:T(8,128)(4,1)S(1)} %copy.91), kind=kLoop, calls=%fused_computation.11 | loop fusion | flops 13629440 | bytes 14073856 | tf_op jit(solution)/shard_map/reduce_sum | solution.py:298
  221.4 11.4 %fusion.3 = f32[8,128,1664]{2,1,0:T(8,128)} fusion(bf16[256,8,128]{0,2,1:T(8,128)(2,1)S(1)} %copy.102, f32[8,1664,256]{2,1,0:T(8,128)} %get-tuple-element.117, f32[8,256]{1,0:T(8,128)S(1)} %log_add_fusion, pred[256,1664]{0,1:T(8,128)(4,1)S(1)} %copy.91), kind=kOutput, calls=%fused_computation.15 | convolution fusion | flops 886046720 | bytes 21405696 | tf_op jit(solution)/shard_map/hqk,qhd->khd/dot_general | solution.py:312
  232.8 7.7 %copy.105 = f32[1664,1024]{1,0:T(8,128)} copy(f32[1664,1024]{0,1:T(8,128)} %bitcast.87) | data formatting | bytes 13631488 | tf_op jit(solution)/shard_map/reshape | solution.py:316
  240.4 9.1 %multiply_convert_fusion = bf16[8,256,1664]{1,2,0:T(8,128)(2,1)S(1)} fusion(f32[8,1664,256]{2,1,0:T(8,128)} %get-tuple-element.117, f32[8,256]{1,0:T(8,128)S(1)} %copy.96, f32[8,256]{1,0:T(8,128)S(1)} %log_add_fusion, pred[256,1664]{0,1:T(8,128)(4,1)S(1)} %copy.91, bf16[256,8,128]{0,2,1:T(8,128)(2,1)S(1)} %copy.102, ...), kind=kOutput, calls=%fused_computation.9 | convolution fusion | flops 896270336 | bytes 24821760 | tf_op jit(solution)/shard_map/qhd,khd->hqk/dot_general | solution.py:306
  249.6 5.0 fusion.32
  254.6 7.7 %copy.104 = f32[1664,1024]{1,0:T(8,128)} copy(f32[1664,1024]{0,1:T(8,128)} %bitcast.86) | data formatting | bytes 13631488 | tf_op jit(solution)/shard_map/reshape | solution.py:316
  262.3 2.8 fusion.9
  265.0 2.1 copy-done.4
  267.5 1.4 collective-permute-start.5
  269.7 17.5 %collective-permute-done.5 = bf16[192,2048]{1,0:T(8,128)(2,1)S(1)} collective-permute-done((bf16[192,2048]{1,0:T(8,128)(2,1)S(1)}, bf16[192,2048]{1,0:T(8,128)(2,1)S(1)}, u32[]{:S(2)}, u32[]{:S(2)}) %collective-permute-start.5) | collective-permute-done | bytes 786464 | tf_op jit(solution)/shard_map/ppermute | solution.py:331
  287.2 2.3 collective-permute-start.7
  289.7 8.1 %fusion = bf16[1664,2048]{1,0:T(8,128)(2,1)} fusion(f32[1664,1024]{1,0:T(8,128)} %copy.105, f32[1664,1024]{1,0:T(8,128)} %copy.104), kind=kLoop, calls=%fused_computation.7 | loop fusion | flops 13631488 | bytes 20447232 | tf_op jit(solution)/shard_map/convert.15
  297.9 2.3 fusion.28
  300.3 18.1 %collective-permute-start.8 = (bf16[128,2048]{1,0:T(8,128)(2,1)}, bf16[128,2048]{1,0:T(8,128)(2,1)S(1)}, u32[]{:S(2)}, u32[]{:S(2)}) collective-permute-start(bf16[128,2048]{1,0:T(8,128)(2,1)} %get-tuple-element.100), channel_id=1, source_target_pairs={{16,0},{20,4},{24,8},{28,12},{0,16},{4,20},{8,24},{12,28},{48,32},... | collective-permute-start | bytes 1572872 | tf_op jit(solution)/shard_map/ppermute | solution.py:344
  318.4 3.7 fusion.30
  322.1 32.3 %collective-permute-start.3 = (bf16[256,2048]{1,0:T(8,128)(2,1)}, bf16[256,2048]{1,0:T(8,128)(2,1)}, u32[]{:S(2)}, u32[]{:S(2)}) collective-permute-start(bf16[256,2048]{1,0:T(8,128)(2,1)} %get-tuple-element.105), channel_id=1, source_target_pairs={{4,0},{8,4},{12,8},{16,12},{20,16},{24,20},{28,24},{32,28},{36,32}... | collective-permute-start | bytes 3145736 | tf_op jit(solution)/shard_map/ppermute | solution.py:19
  354.4 2.6 collective-permute-start.2
  357.0 1.9 slice.151
  358.9 1.9 collective-permute-start
  360.9 3.2 fusion.12
  364.3 2.7 collective-permute-start.10
  366.9 15.7 %collective-permute-start.9 = (bf16[128,2048]{1,0:T(8,128)(2,1)S(1)}, bf16[128,2048]{1,0:T(8,128)(2,1)S(1)}, u32[]{:S(2)}, u32[]{:S(2)}) collective-permute-start(bf16[128,2048]{1,0:T(8,128)(2,1)S(1)} %fusion.21), channel_id=1, source_target_pairs={{4,0},{8,4},{12,8},{0,12},{20,16},{24,20},{28,24},{16,28},{36,32},... | collective-permute-start | bytes 1572872 | tf_op jit(solution)/shard_map/ppermute | solution.py:354
  382.6 4.1 convolution_convert_fusion
  386.7 21.9 %collective-permute-done.10 = bf16[128,2048]{1,0:T(8,128)(2,1)S(1)} collective-permute-done((bf16[128,2048]{1,0:T(8,128)(2,1)S(1)}, bf16[128,2048]{1,0:T(8,128)(2,1)S(1)}, u32[]{:S(2)}, u32[]{:S(2)}) %collective-permute-start.10) | collective-permute-done | bytes 524320 | tf_op jit(solution)/shard_map/ppermute | solution.py:355
  408.7 69.5 %collective-permute-start.1 = (bf16[256,2048]{1,0:T(8,128)(2,1)}, bf16[256,2048]{1,0:T(8,128)(2,1)}, u32[]{:S(2)}, u32[]{:S(2)}) collective-permute-start(bf16[256,2048]{1,0:T(8,128)(2,1)} %get-tuple-element.104), channel_id=1, source_target_pairs={{12,0},{16,4},{20,8},{24,12},{28,16},{32,20},{36,24},{40,28},{44,3... | collective-permute-start | bytes 3145736 | tf_op jit(solution)/shard_map/ppermute | solution.py:19
  478.2 1.1 fusion.27
  479.3 4.5 collective-permute-start.11
  485.0 2.6 fusion.18
  487.6 10.7 %collective-permute-done.11 = bf16[128,2048]{1,0:T(8,128)(2,1)} collective-permute-done((bf16[128,2048]{1,0:T(8,128)(2,1)}, bf16[128,2048]{1,0:T(8,128)(2,1)}, u32[]{:S(2)}, u32[]{:S(2)}) %collective-permute-start.11) | collective-permute-done | bytes 524320 | tf_op jit(solution)/shard_map/ppermute | solution.py:357
  498.3 1.5 add_select_fusion
  499.8 27.0 %collective-permute-done.1 = bf16[256,2048]{1,0:T(8,128)(2,1)} collective-permute-done((bf16[256,2048]{1,0:T(8,128)(2,1)}, bf16[256,2048]{1,0:T(8,128)(2,1)}, u32[]{:S(2)}, u32[]{:S(2)}) %collective-permute-start.1) | collective-permute-done | bytes 1048608 | tf_op jit(solution)/shard_map/ppermute | solution.py:19
  526.8 3.3 fusion.14
  531.2 2.0 copy.107
  (83 shorter events, 11.1 us)
Async XLA Ops:
  7.2 162.3 %copy-start = (bf16[256,4096]{1,0:T(8,128)(2,1)S(1)}, bf16[256,4096]{1,0:T(8,128)(2,1)}, u32[]{:S(2)}) copy-start(bf16[256,4096]{1,0:T(8,128)(2,1)} %param.23) | copy-start | bytes 6291460
  7.2 524.0 %reduce-scatter.2.cloned.1.call-start = ((), (), s32[]{:S(2)}) async-start(), calls=%async_computation.1 | async-start | bytes 17301504 | tf_op jit(solution)/shard_map/reduce_scatter | solution.py:375
  149.9 5.7 %copy-start.14 = (pred[256,1664]{1,0:T(8,128)(4,1)S(1)}, pred[256,1664]{1,0:T(8,128)(4,1)}, u32[]{:S(2)}) copy-start(pred[256,1664]{1,0:T(8,128)(4,1)} %copy.90) | copy-start | bytes 1277956
  149.9 5.7 %copy-start.15 = (pred[256,1152]{1,0:T(8,128)(4,1)S(1)}, pred[256,1152]{1,0:T(8,128)(4,1)}, u32[]{:S(2)}) copy-start(pred[256,1152]{1,0:T(8,128)(4,1)} %iota_compare_fusion) | copy-start | bytes 884740
  178.6 1.0 copy-start.13
  188.0 6.7 %copy-start.5 = (bf16[256,1024]{1,0:T(8,128)(2,1)S(1)}, bf16[256,1024]{1,0:T(8,128)(2,1)}, u32[]{:S(2)}) copy-start(bf16[256,1024]{1,0:T(8,128)(2,1)} %shard_map.109) | copy-start | bytes 1572868
  196.1 7.9 %copy-start.6 = (bf16[256,1024]{0,1:T(8,128)(2,1)S(1)}, bf16[256,1024]{0,1:T(8,128)(2,1)}, u32[]{:S(2)}) copy-start(bf16[256,1024]{0,1:T(8,128)(2,1)} %copy.113) | copy-start | bytes 1572868
  249.6 5.0 copy-start.2
  265.0 2.1 copy-start.4
  267.5 19.7 %collective-permute-start.5 = (bf16[192,2048]{1,0:T(8,128)(2,1)S(1)}, bf16[192,2048]{1,0:T(8,128)(2,1)S(1)}, u32[]{:S(2)}, u32[]{:S(2)}) collective-permute-start(bf16[192,2048]{1,0:T(8,128)(2,1)S(1)} %pad_maximum_fusion.3), channel_id=1, source_target_pairs={{0,96},{4,100},{8,104},{12,108},{16,112},{20,116},{24,120},{28,124... | collective-permute-start | bytes 2359304 | tf_op jit(solution)/shard_map/ppermute | solution.py:331
  268.9 20.7 %collective-permute-start.4 = (bf16[192,2048]{1,0:T(8,128)(2,1)S(1)}, bf16[192,2048]{1,0:T(8,128)(2,1)S(1)}, u32[]{:S(2)}, u32[]{:S(2)}) collective-permute-start(bf16[192,2048]{1,0:T(8,128)(2,1)S(1)} %pad_maximum_fusion.2), channel_id=1, source_target_pairs={{0,32},{4,36},{8,40},{12,44},{16,48},{20,52},{24,56},{28,60},{32,6... | collective-permute-start | bytes 2359304 | tf_op jit(solution)/shard_map/ppermute | solution.py:330
  287.2 10.5 %collective-permute-start.7 = (bf16[64,2048]{1,0:T(8,128)(2,1)S(1)}, bf16[64,2048]{1,0:T(8,128)(2,1)S(1)}, u32[]{:S(2)}, u32[]{:S(2)}) collective-permute-start(bf16[64,2048]{1,0:T(8,128)(2,1)S(1)} %slice.162), channel_id=1, source_target_pairs={{0,96},{4,100},{8,104},{12,108},{16,112},{20,116},{24,120},{28,124... | collective-permute-start | bytes 786440 | tf_op jit(solution)/shard_map/ppermute | solution.py:333
  289.6 8.4 %collective-permute-start.6 = (bf16[64,2048]{1,0:T(8,128)(2,1)S(1)}, bf16[64,2048]{1,0:T(8,128)(2,1)S(1)}, u32[]{:S(2)}, u32[]{:S(2)}) collective-permute-start(bf16[64,2048]{1,0:T(8,128)(2,1)S(1)} %slice.161), channel_id=1, source_target_pairs={{0,32},{4,36},{8,40},{12,44},{16,48},{20,52},{24,56},{28,60},{32,6... | collective-permute-start | bytes 786440 | tf_op jit(solution)/shard_map/ppermute | solution.py:332
  300.3 63.8 %collective-permute-start.8 = (bf16[128,2048]{1,0:T(8,128)(2,1)}, bf16[128,2048]{1,0:T(8,128)(2,1)S(1)}, u32[]{:S(2)}, u32[]{:S(2)}) collective-permute-start(bf16[128,2048]{1,0:T(8,128)(2,1)} %get-tuple-element.100), channel_id=1, source_target_pairs={{16,0},{20,4},{24,8},{28,12},{0,16},{4,20},{8,24},{12,28},{48,32},... | collective-permute-start | bytes 1572872 | tf_op jit(solution)/shard_map/ppermute | solution.py:344
  322.1 177.7 %collective-permute-start.3 = (bf16[256,2048]{1,0:T(8,128)(2,1)}, bf16[256,2048]{1,0:T(8,128)(2,1)}, u32[]{:S(2)}, u32[]{:S(2)}) collective-permute-start(bf16[256,2048]{1,0:T(8,128)(2,1)} %get-tuple-element.105), channel_id=1, source_target_pairs={{4,0},{8,4},{12,8},{16,12},{20,16},{24,20},{28,24},{32,28},{36,32}... | collective-permute-start | bytes 3145736 | tf_op jit(solution)/shard_map/ppermute | solution.py:19
  354.4 145.4 %collective-permute-start.2 = (bf16[256,2048]{1,0:T(8,128)(2,1)}, bf16[256,2048]{1,0:T(8,128)(2,1)}, u32[]{:S(2)}, u32[]{:S(2)}) collective-permute-start(bf16[256,2048]{1,0:T(8,128)(2,1)} %get-tuple-element.106), channel_id=1, source_target_pairs={{8,0},{12,4},{16,8},{20,12},{24,16},{28,20},{32,24},{36,28},{40,32... | collective-permute-start | bytes 3145736 | tf_op jit(solution)/shard_map/ppermute | solution.py:19
  358.9 126.0 %collective-permute-start = (bf16[128,2048]{1,0:T(8,128)(2,1)}, bf16[128,2048]{1,0:T(8,128)(2,1)}, u32[]{:S(2)}, u32[]{:S(2)}) collective-permute-start(bf16[128,2048]{1,0:T(8,128)(2,1)} %slice.151), channel_id=1, source_target_pairs={{16,0},{20,4},{24,8},{28,12},{32,16},{36,20},{40,24},{44,28},{48,3... | collective-permute-start | bytes 1572872 | tf_op jit(solution)/shard_map/ppermute | solution.py:19
  360.9 21.7 %copy-start.3 = (bf16[1664,1024]{0,1:T(8,128)(2,1)S(1)}, bf16[1664,1024]{0,1:T(8,128)(2,1)}, u32[]{:S(2)}) copy-start(bf16[1664,1024]{0,1:T(8,128)(2,1)} %copy.112) | copy-start | bytes 10223620
  364.1 114.0 %copy-start.7 = (bf16[128,2048]{1,0:T(8,128)(2,1)}, bf16[128,2048]{1,0:T(8,128)(2,1)S(1)}, u32[]{:S(2)}) copy-start(bf16[128,2048]{1,0:T(8,128)(2,1)S(1)} %collective-permute-done.8) | copy-start | bytes 1572868
  364.3 44.4 %collective-permute-start.10 = (bf16[128,2048]{1,0:T(8,128)(2,1)S(1)}, bf16[128,2048]{1,0:T(8,128)(2,1)S(1)}, u32[]{:S(2)}, u32[]{:S(2)}) collective-permute-start(bf16[128,2048]{1,0:T(8,128)(2,1)S(1)} %fusion.21), channel_id=1, source_target_pairs={{12,0},{0,4},{4,8},{8,12},{28,16},{16,20},{20,24},{24,28},{44,32},... | collective-permute-start | bytes 1572872 | tf_op jit(solution)/shard_map/ppermute | solution.py:355
  366.9 111.2 %collective-permute-start.9 = (bf16[128,2048]{1,0:T(8,128)(2,1)S(1)}, bf16[128,2048]{1,0:T(8,128)(2,1)S(1)}, u32[]{:S(2)}, u32[]{:S(2)}) collective-permute-start(bf16[128,2048]{1,0:T(8,128)(2,1)S(1)} %fusion.21), channel_id=1, source_target_pairs={{4,0},{8,4},{12,8},{0,12},{20,16},{24,20},{28,24},{16,28},{36,32},... | collective-permute-start | bytes 1572872 | tf_op jit(solution)/shard_map/ppermute | solution.py:354
  408.7 76.2 %copy-start.9 = (bf16[128,2048]{1,0:T(8,128)(2,1)}, bf16[128,2048]{1,0:T(8,128)(2,1)S(1)}, u32[]{:S(2)}) copy-start(bf16[128,2048]{1,0:T(8,128)(2,1)S(1)} %collective-permute-done.10) | copy-start | bytes 1572868
  408.7 118.1 %collective-permute-start.1 = (bf16[256,2048]{1,0:T(8,128)(2,1)}, bf16[256,2048]{1,0:T(8,128)(2,1)}, u32[]{:S(2)}, u32[]{:S(2)}) collective-permute-start(bf16[256,2048]{1,0:T(8,128)(2,1)} %get-tuple-element.104), channel_id=1, source_target_pairs={{12,0},{16,4},{20,8},{24,12},{28,16},{32,20},{36,24},{40,28},{44,3... | collective-permute-start | bytes 3145736 | tf_op jit(solution)/shard_map/ppermute | solution.py:19
  478.2 6.8 %copy-start.11 = (bf16[128,2048]{1,0:T(8,128)(2,1)}, bf16[128,2048]{1,0:T(8,128)(2,1)S(1)}, u32[]{:S(2)}) copy-start(bf16[128,2048]{1,0:T(8,128)(2,1)S(1)} %collective-permute-done.9) | copy-start | bytes 1572868
  479.3 19.0 %collective-permute-start.11 = (bf16[128,2048]{1,0:T(8,128)(2,1)}, bf16[128,2048]{1,0:T(8,128)(2,1)}, u32[]{:S(2)}, u32[]{:S(2)}) collective-permute-start(bf16[128,2048]{1,0:T(8,128)(2,1)} %fusion.27), channel_id=1, source_target_pairs={{4,0},{8,4},{12,8},{0,12},{20,16},{24,20},{28,24},{16,28},{36,32},... | collective-permute-start | bytes 1572872 | tf_op jit(solution)/shard_map/ppermute | solution.py:357
  484.9 13.4 %copy-start.8 = (bf16[128,2048]{1,0:T(8,128)(2,1)S(1)}, bf16[128,2048]{1,0:T(8,128)(2,1)}, u32[]{:S(2)}) copy-start(bf16[128,2048]{1,0:T(8,128)(2,1)} %copy-done.7) | copy-start | bytes 1572868
  484.9 13.4 %copy-start.10 = (bf16[128,2048]{1,0:T(8,128)(2,1)S(1)}, bf16[128,2048]{1,0:T(8,128)(2,1)}, u32[]{:S(2)}) copy-start(bf16[128,2048]{1,0:T(8,128)(2,1)} %copy-done.9) | copy-start | bytes 1572868
  484.9 13.4 %copy-start.12 = (bf16[128,2048]{1,0:T(8,128)(2,1)S(1)}, bf16[128,2048]{1,0:T(8,128)(2,1)}, u32[]{:S(2)}) copy-start(bf16[128,2048]{1,0:T(8,128)(2,1)} %copy-done.11) | copy-start | bytes 1572868
  484.9 48.2 %copy-start.1 = (bf16[256,4096]{1,0:T(8,128)(2,1)S(1)}, bf16[256,4096]{1,0:T(8,128)(2,1)}, u32[]{:S(2)}) copy-start(bf16[256,4096]{1,0:T(8,128)(2,1)} %param.23) | copy-start | bytes 6291460
Sparse Core Ops, SparseCore 0:
  178.8 321.1 reduce-scatter.1
